TPU v7x, 32 devices: a whole 2x2x4 slice. The times are simulated.
32 devices in a mesh: lon: 8 (over z, x), lat: 4 (over y, core).
Axes of the slice: x: 2, y: 2, z: 4, core: 2. Of those that a mesh axis runs over, the one named last changes fastest.
Arguments:
- fields: bfloat16 [128, 256, 256], P('lat', 'lon'), may hold values from -6 to 6
- cotangent: bfloat16 [128, 256, 256], P('lat', 'lon'), may hold values from -6 to 6
- dw_kernel: bfloat16 [7, 7, 256], replicated, may hold values from -0.875 to 0.875
- dw_bias: bfloat16 [256], replicated, may hold values from -3 to 3
- norm_gain: bfloat16 [256], replicated, may hold values from 0.099609375 to 1.8984375
- layer_norm_offset: bfloat16 [256], replicated, may hold values from -3 to 3
- w_expand: bfloat16 [256, 1024], replicated, may hold values from -0.375 to 0.375
- b_expand: bfloat16 [1024], replicated, may hold values from -3 to 3
- w_project: bfloat16 [1024, 256], replicated, may hold values from -0.1875 to 0.1875
- b_project: bfloat16 [256], replicated, may hold values from -3 to 3
Outputs:
- block_out: bfloat16 [128, 256, 256], P('lat', 'lon')
- grad_fields: bfloat16 [128, 256, 256], P('lat', 'lon')
- grad_kernel: float32 [7, 7, 256], replicated
- grad_dw_bias: float32 [256], replicated
- grad_gain: float32 [256], replicated
- grad_shift: float32 [256], replicated
- grad_expand: float32 [256, 1024], replicated
- grad_b_expand: float32 [1024], replicated
- grad_project: float32 [1024, 256], replicated
- grad_b_project: float32 [256], replicated
All inputs are finite; a program needn't handle non-finite values.
Results may differ from a plain program's by a relative error of at most 0.0075.
Values may be sent and summed in bfloat16 or wider, within the bound.
No kernel may reach another device: no remote copies, remote signals or barrier semaphores. Data moves between devices by JAX's collectives and lax.ppermute only.
A program may use at most 64 MiB of HBM per device.

v0:
```python
import math

import jax
import jax.numpy as jnp
from jax import lax
from jax.sharding import PartitionSpec as P

EPS = 1e-06


def extended(array, sides, width, wrap):
    for axis, dim in sides:
        size, length = (lax.axis_size(axis), array.shape[dim])
        up = [(i, (i + 1) % size) for i in range(size if wrap else size - 1)]
        down = [(j, i) for i, j in up]
        last = lax.slice_in_dim(array, length - width, length, axis=dim)
        first = lax.slice_in_dim(array, 0, width, axis=dim)
        before = lax.ppermute(last, axis, up)
        after = lax.ppermute(first, axis, down)
        array = jnp.concatenate([before, array, after], axis=dim)
    return array


def from_behind(value, axis, steps):
    count = lax.axis_size(axis)
    pairs = [(source, (source + steps) % count) for source in range(count)]
    return lax.ppermute(value, axis, pairs)


def gelu_parts(values):
    normal_cdf = 0.5 * (1.0 + jax.scipy.special.erf(values * (1.0 / math.sqrt(2.0))))
    density = jnp.exp(-0.5 * values * values) * (1.0 / math.sqrt(2.0 * math.pi))
    return (values * normal_cdf, normal_cdf + values * density)


def contract_rows(left, right):
    return lax.dot_general(
        left, right, (((0,), (0,)), ((), ())), preferred_element_type=jnp.float32
    )


def sphere_pad(field):
    lat_index = lax.axis_index("lat")
    north = lat_index == 0
    south = lat_index == lax.axis_size("lat") - 1
    wide = extended(field, (("lon", 1),), 3, True)
    outgoing = jnp.where(north, wide[2::-1], wide[:-4:-1])
    partner = from_behind(outgoing, "lon", lax.axis_size("lon") // 2)
    tall = extended(wide, (("lat", 0),), 3, False)
    top_rows = jnp.where(north, partner, tall[:3])
    bottom_rows = jnp.where(south, partner, tall[-3:])
    return (jnp.concatenate([top_rows, tall[3:-3], bottom_rows], axis=0), north, south)


def local(
    fields,
    cotangent,
    dw_kernel,
    dw_bias,
    norm_gain,
    layer_norm_offset,
    w_expand,
    b_expand,
    w_project,
    b_project,
):
    rows = fields.shape[0]
    cols = fields.shape[1]
    chans = fields.shape[2]
    scale_factor = 1.0 / math.sqrt(rows * cols * lax.axis_size("lat") * lax.axis_size("lon"))
    weights = dw_kernel.astype(jnp.float32)
    norm_scale_factor = norm_gain.astype(jnp.float32)
    padded, north, south = sphere_pad(fields)
    conv = jnp.zeros((rows, cols, chans), jnp.float32)
    for row_off in range(7):
        for col_off in range(7):
            conv = conv + weights[row_off, col_off] * padded[
                row_off : row_off + rows, col_off : col_off + cols
            ].astype(jnp.float32)
    conv = conv.reshape(-1, chans) + dw_bias.astype(jnp.float32)
    mean_removed = conv - jnp.mean(conv, axis=-1, keepdims=True)
    inverse_deviation = lax.rsqrt(
        jnp.mean(mean_removed * mean_removed, axis=-1, keepdims=True) + EPS
    )
    standardized_input = mean_removed * inverse_deviation
    normalized_input = (
        standardized_input * norm_scale_factor + layer_norm_offset.astype(jnp.float32)
    ).astype(jnp.bfloat16)
    pre = jnp.dot(normalized_input, w_expand, preferred_element_type=jnp.float32) + b_expand.astype(
        jnp.float32
    )
    active, slope = gelu_parts(pre)
    hidden = active.astype(jnp.bfloat16)
    branch = jnp.dot(hidden, w_project, preferred_element_type=jnp.float32) + b_project.astype(
        jnp.float32
    )
    flat_fields = fields.reshape(-1, chans)
    block_out = (
        (flat_fields.astype(jnp.float32) + branch).astype(jnp.bfloat16).reshape(rows, cols, chans)
    )
    flat_cot = cotangent.reshape(-1, chans)
    grad_proj = contract_rows(hidden, flat_cot) * scale_factor
    grad_bproj = jnp.sum(flat_cot.astype(jnp.float32), axis=0) * scale_factor
    d_hidden = jnp.dot(flat_cot, w_project.T, preferred_element_type=jnp.float32)
    d_pre = (d_hidden * slope).astype(jnp.bfloat16)
    grad_exp = contract_rows(normalized_input, d_pre) * scale_factor
    grad_bexp = jnp.sum(d_pre.astype(jnp.float32), axis=0) * scale_factor
    normalized_gradient = jnp.dot(d_pre, w_expand.T, preferred_element_type=jnp.float32)
    gain_gradient = jnp.sum(normalized_gradient * standardized_input, axis=0) * scale_factor
    grad_sh = jnp.sum(normalized_gradient, axis=0) * scale_factor
    scaled_output = normalized_gradient * norm_scale_factor
    conv_gradient = inverse_deviation * (
        scaled_output
        - jnp.mean(scaled_output, axis=-1, keepdims=True)
        - standardized_input * jnp.mean(scaled_output * standardized_input, axis=-1, keepdims=True)
    )
    conv_gradient = conv_gradient.astype(jnp.bfloat16).reshape(rows, cols, chans)
    grad_dwb = jnp.sum(conv_gradient.astype(jnp.float32), axis=(0, 1)) * scale_factor
    dconv_wide = conv_gradient.astype(jnp.float32)
    kern_terms = []
    for row_off in range(7):
        for col_off in range(7):
            window = padded[row_off : row_off + rows, col_off : col_off + cols].astype(jnp.float32)
            kern_terms.append(jnp.sum(dconv_wide * window, axis=(0, 1)))
    grad_kern = jnp.stack(kern_terms, axis=0).reshape(7, 7, chans) * scale_factor
    dpad, north, south = sphere_pad(conv_gradient)
    zero_rows = jnp.zeros((3, cols + 6, chans), jnp.bfloat16)
    inner = jnp.concatenate(
        [jnp.where(north, zero_rows, dpad[:3]), dpad[3:-3], jnp.where(south, zero_rows, dpad[-3:])],
        axis=0,
    )
    spacer = jnp.zeros((6, cols + 6, chans), jnp.bfloat16)
    fold_north = jnp.concatenate([jnp.where(north, dpad[:3], zero_rows), spacer], axis=0)
    fold_south = jnp.concatenate([spacer, jnp.where(south, dpad[-3:], zero_rows)], axis=0)
    adjoint = jnp.zeros((rows, cols, chans), jnp.float32)
    north_term = jnp.zeros((3, cols, chans), jnp.float32)
    south_term = jnp.zeros((3, cols, chans), jnp.float32)
    for row_off in range(7):
        for col_off in range(7):
            weight = weights[row_off, col_off]
            col_from = 6 - col_off
            adjoint = adjoint + weight * inner[
                6 - row_off : 6 - row_off + rows, col_from : col_from + cols
            ].astype(jnp.float32)
            north_term = north_term + weight * fold_north[
                row_off : row_off + 3, col_from : col_from + cols
            ].astype(jnp.float32)
            south_term = south_term + weight * fold_south[
                row_off : row_off + 3, col_from : col_from + cols
            ].astype(jnp.float32)
    adjoint = adjoint.at[:3].add(north_term)
    adjoint = adjoint.at[rows - 3 :].add(south_term)
    grad_fields = (cotangent.astype(jnp.float32) + adjoint).astype(jnp.bfloat16)
    sum_kern, sum_dwb, sum_gn, sum_sh, sum_exp, sum_bexp, sum_proj, sum_bproj = lax.psum(
        (grad_kern, grad_dwb, gain_gradient, grad_sh, grad_exp, grad_bexp, grad_proj, grad_bproj),
        ("lon", "lat"),
    )
    return (
        block_out,
        grad_fields,
        sum_kern,
        sum_dwb,
        sum_gn,
        sum_sh,
        sum_exp,
        sum_bexp,
        sum_proj,
        sum_bproj,
    )


def solution(mesh):
    placed = (P("lat", "lon", None), P("lat", "lon", None), P(), P(), P(), P(), P(), P(), P(), P())
    return jax.shard_map(
        local,
        mesh=mesh,
        in_specs=placed,
        out_specs=(
            P("lat", "lon", None),
            P("lat", "lon", None),
            P(),
            P(),
            P(),
            P(),
            P(),
            P(),
            P(),
            P(),
        ),
        check_vma=False,
    )
```

profile of v0, /device:TPU:0, one launch (start us, length us, event | category | flops | bytes accessed | tf_op | source)
XLA Modules:
  0.0 221.7 jit_solution(7986544816358134473)
XLA Ops:
  7.2 1.1 fusion.150
  8.4 3.0 %collective-permute-start = (bf16[32,3,256]{2,1,0:T(4,128)(2,1)S(1)}, bf16[32,3,256]{2,1,0:T(4,128)(2,1)S(1)}, u32[]{:S(2)}, u32[]{:S(2)}) collective-permute-start(bf16[32,3,256]{2,1,0:T(4,128)(2,1)S(1)} %get-tuple-element.121), channel_id=1, source_target_pairs={{0,4},{4,8},{8,12},{12,16},{16,20},{20,24},{24,28},{28,0},{1,5},{5... | collective-permute-start | bytes 147464 | tf_op jit(solution)/shard_map/ppermute | solution.py:18
  11.4 3.1 %collective-permute-start.1 = (bf16[32,3,256]{2,1,0:T(4,128)(2,1)S(1)}, bf16[32,3,256]{2,1,0:T(4,128)(2,1)S(1)}, u32[]{:S(2)}, u32[]{:S(2)}) collective-permute-start(bf16[32,3,256]{2,1,0:T(4,128)(2,1)S(1)} %get-tuple-element.122), channel_id=1, source_target_pairs={{4,0},{8,4},{12,8},{16,12},{20,16},{24,20},{28,24},{0,28},{5,1},{9... | collective-permute-start | bytes 147464 | tf_op jit(solution)/shard_map/ppermute | solution.py:19
  14.5 1.0 fusion.151
  15.5 1.0 fusion.152
  21.6 1.1 constant_dynamic-update-slice_fusion.1
  25.3 1.2 convert_element_type.582
  27.4 1.5 collective-permute-start.3
  28.9 1.3 collective-permute-start.4
  31.1 4.3 %collective-permute-done.2 = bf16[3,38,256]{2,1,0:T(8,128)(2,1)S(1)} collective-permute-done((bf16[3,38,256]{2,1,0:T(8,128)(2,1)S(1)}, bf16[3,38,256]{2,1,0:T(8,128)(2,1)S(1)}, u32[]{:S(2)}, u32[]{:S(2)}) %collective-permute-start.2) | collective-permute-done | bytes 58400 | tf_op jit(solution)/shard_map/ppermute | solution.py:27
  35.9 8.6 %add_reduce_fusion = (f32[32,32]{1,0:T(8,128)S(1)}, f32[32,32,256]{2,1,0:T(8,128)}) fusion(f32[256]{0:T(256)S(1)} %convert_element_type.576, bf16[35,38,256]{2,1,0:T(8,128)(2,1)S(1)} %get-tuple-element.114, f32[256]{0:T(256)S(1)} %bitcast.258, f32[256]{0:T(256)S(1)} %bitcast.254, f32[256]{0:T(256)S(1)} %bitcast.250, f32[256]{0:T(256)S(1)} %bitcast.246, ...), kind=kLoop, calls=%fused_computation.247 | loop fusion | flops 41155584 | bytes 25270272 | tf_op jit(solution)/shard_map/reduce_sum | solution.py:81
  44.5 1.6 multiply_reduce_fusion.2
  46.2 1.6 fusion.132
  47.8 1.2 multiply_convert_fusion
  49.0 2.5 %convert_reduce_fusion = (f32[1024]{0:T(1024)S(1)}, bf16[1024,1024]{1,0:T(8,128)(2,1)S(1)}) fusion(f32[1024,1024]{1,0:T(8,128)S(1)} %get-tuple-element.181, f32[1024]{0:T(1024)S(1)} %convert_element_type.580, bf16[1024,256]{1,0:T(8,128)(2,1)S(1)} %bitcast.175, bf16[1024,256]{1,0:T(8,128)(2,1)S(1)} %copy-done.22), kind=kOutput, calls=%fused_computation.57 | convolution fusion | flops 550501376 | bytes 7348224 | tf_op jit(solution)/shard_map/dot_general | solution.py:104
  51.5 1.7 convolution_multiply_fusion.1
  53.3 1.4 multiply_reduce_fusion
  55.6 3.2 %fusion.130 = (f32[256]{0:T(256)S(1)}, f32[256]{0:T(256)S(1)}, f32[256]{0:T(256)S(1)}, f32[256]{0:T(256)S(1)}, f32[256]{0:T(256)S(1)}, /*index=5*/f32[256]{0:T(2...) fusion(bf16[35,38,256]{2,1,0:T(8,128)(2,1)S(1)} %get-tuple-elem, ...), kind=kLoop, calls=%fused_computation.237 | loop fusion | flops 14413312 | bytes 9979904 | tf_op jit(solution)/shard_map/reduce_sum | solution.py:124
  58.8 3.2 %fusion.102 = (f32[256]{0:T(256)}, f32[256]{0:T(256)}, f32[256]{0:T(256)}, f32[256]{0:T(256)}, f32[256]{0:T(256)}, /*index=5*/f32[256]{0:T(256)}, f32[256]{0:T(2...) fusion(bf16[35,38,256]{2,1,0:T(8,128)(2,1)S(1)} %get-tuple-elem, ...), kind=kLoop, calls=%fused_computation.209 | loop fusion | flops 14413312 | bytes 9979904 | tf_op jit(solution)/shard_map/reduce_sum | solution.py:124
  62.1 1.7 convolution_multiply_fusion
  63.8 3.5 %fusion.112 = (f32[256]{0:T(256)S(1)}, f32[256]{0:T(256)S(1)}, f32[256]{0:T(256)S(1)}, f32[256]{0:T(256)S(1)}, f32[256]{0:T(256)S(1)}, /*index=5*/f32[256]{0:T(2...) fusion(bf16[35,38,256]{2,1,0:T(8,128)(2,1)S(1)} %get-tuple-elem, ...), kind=kLoop, calls=%fused_computation.219 | loop fusion | flops 12841728 | bytes 5829632 | tf_op jit(solution)/shard_map/reduce_sum | solution.py:124
  67.4 4.4 %stack.199 = f32[49,256]{1,0:T(8,128)S(1)} concatenate(f32[1,256]{1,0:T(1,128)S(1)} %bitcast.376, f32[1,256]{1,0:T(1,128)S(1)} %bitcast.377, f32[1,256]{1,0:T(1,128)S(1)} %bitcast.378, f32[1,256]{1,0:T(1,128)} %bitcast.421, f32[1,256]{1,0:T(1,128)} %bitcast.420, f32[1,256]{1,0:T(1,128)} %bitcast.419, f32[1,256]{1,0:T(1,128)} %bitcast.418, f32[1,256]{1,0:T(1,128)} %bitcast.417, ...), dimensions={0} | concatenate | bytes 100352 | tf_op jit(solution)/shard_map/stack | solution.py:125
  71.9 4.7 %collective-permute-start.6 = (bf16[32,3,256]{2,1,0:T(4,128)(2,1)S(1)}, bf16[32,3,256]{2,1,0:T(4,128)(2,1)S(1)}, u32[]{:S(2)}, u32[]{:S(2)}) collective-permute-start(bf16[32,3,256]{2,1,0:T(4,128)(2,1)S(1)} %get-tuple-element.119), channel_id=1, source_target_pairs={{4,0},{8,4},{12,8},{16,12},{20,16},{24,20},{28,24},{0,28},{5,1},{9... | collective-permute-start | bytes 147464 | tf_op jit(solution)/shard_map/ppermute | solution.py:19
  76.7 3.1 %fusion.7 = bf16[1024,256]{1,0:T(8,128)(2,1)} fusion(bf16[1024,1024]{1,0:T(8,128)(2,1)} %copy-done.4, bf16[1024,256]{1,0:T(8,128)(2,1)S(1)} %copy-done.23, f32[256]{0:T(256)S(1)} %copy-done.24, bf16[1024,256]{1,0:T(8,128)(2,1)S(1)} %bitcast.174), kind=kOutput, calls=%fused_computation.114 | convolution fusion | flops 537919488 | bytes 3671040 | tf_op jit(solution)/shard_map/dot_general | solution.py:94
  79.8 1.3 collective-permute-start.8
  81.2 3.7 %collective-permute-start.9 = (bf16[3,38,256]{2,1,0:T(8,128)(2,1)S(1)}, bf16[3,38,256]{2,1,0:T(8,128)(2,1)S(1)}, u32[]{:S(2)}, u32[]{:S(2)}) collective-permute-start(bf16[3,38,256]{2,1,0:T(8,128)(2,1)S(1)} %get-tuple-element.112), channel_id=1, source_target_pairs={{0,1},{1,2},{2,3},{4,5},{5,6},{6,7},{8,9},{9,10},{10,11},{12,13},{... | collective-permute-start | bytes 175112 | tf_op jit(solution)/shard_map/ppermute | solution.py:18
  85.0 6.9 %collective-permute-done.7 = bf16[3,38,256]{2,1,0:T(8,128)(2,1)S(1)} collective-permute-done((bf16[3,38,256]{2,1,0:T(8,128)(2,1)S(1)}, bf16[3,38,256]{2,1,0:T(8,128)(2,1)S(1)}, u32[]{:S(2)}, u32[]{:S(2)}) %collective-permute-start.7) | collective-permute-done | bytes 58400 | tf_op jit(solution)/shard_map/ppermute | solution.py:27
  92.5 8.0 %fusion.81 = f32[32,32,256]{2,1,0:T(8,128)S(1)} fusion(bf16[32,32,256]{2,1,0:T(8,128)(2,1)S(1)} %bitcast.173, bf16[32,3,256]{2,1,0:T(4,128)(2,1)S(1)} %collective-permute-done.5, bf16[32,3,256]{2,1,0:T(4,128)(2,1)S(1)} %collective-permute-done.6, bf16[35,38,256]{2,1,0:T(8,128)(2,1)S(1)} %get-tuple-element.110, ...), kind=kLoop, calls=%fused_computation.188 | loop fusion | flops 42991616 | bytes 23741440 | tf_op jit(solution)/shard_map/add | solution.py:142
  101.3 1.1 convert_reduce_fusion.1
  102.3 41.5 %all-reduce.2 = (f32[7,7,256]{2,1,0:T(8,128)}, f32[256]{0:T(256)}, f32[256]{0:T(256)}, f32[256]{0:T(256)}, f32[1024]{0:T(1024)}, /*index=5*/f32[256]{0:T(256)}) all-reduce(f32[7,7,256]{2,1,0:T(8,128)S(1)} %mul.2248, f32[256]{0:T(256)S(1)} %broadcast_multiply_fusion.8, ...), channel_id=1, replica_groups=mesh['lon'=8,'lat'=4] {'lon','lat'}, use_global_device_ids=true, to_apply=%region_53.54 | all-reduce | flops 14592 | bytes 116736 | tf_op jit(solution)/shard_map/psum | solution.py:154
  143.8 67.6 %all-reduce.6.cloned.1.call-done = (f32[256,1024]{1,0:T(8,128)}, f32[1024,256]{1,0:T(8,128)}) async-done(((f32[256,1024]{1,0:T(8,128)}, f32[1024,256]{1,0:T(8,128)}), (f32[256,1024]{1,0:T(8,128)}, f32[1024,256]{1,0:T(8,128)})) %all-reduce.6.cloned.1.call-update) | async-done | bytes 2097168 | tf_op jit(solution)/shard_map/psum | solution.py:154
  211.5 2.4 %copy.25 = f32[256,1024]{1,0:T(8,128)} copy(f32[256,1024]{1,0:T(8,128)} %get-tuple-element.223) | data formatting | bytes 2097152
  (108 shorter events, 13.4 us)
Async XLA Ops:
  7.2 40.6 %copy-start = (bf16[256,1024]{1,0:T(8,128)(2,1)S(1)}, bf16[256,1024]{1,0:T(8,128)(2,1)}, u32[]{:S(2)}) copy-start(bf16[256,1024]{1,0:T(8,128)(2,1)} %param.20) | copy-start | bytes 1572868
  7.2 28.3 %copy-start.2 = (bf16[32,32,256]{2,1,0:T(8,128)(2,1)S(1)}, bf16[32,32,256]{2,1,0:T(8,128)(2,1)}, u32[]{:S(2)}) copy-start(bf16[32,32,256]{2,1,0:T(8,128)(2,1)} %param.14) | copy-start | bytes 1572868
  7.2 204.3 %all-reduce.6.cloned.1.call-start = ((), (), s32[]{:S(2)}) async-start(), calls=%async_computation | async-start | bytes 4194304 | tf_op jit(solution)/shard_map/psum | solution.py:154
  8.4 18.2 %collective-permute-start = (bf16[32,3,256]{2,1,0:T(4,128)(2,1)S(1)}, bf16[32,3,256]{2,1,0:T(4,128)(2,1)S(1)}, u32[]{:S(2)}, u32[]{:S(2)}) collective-permute-start(bf16[32,3,256]{2,1,0:T(4,128)(2,1)S(1)} %get-tuple-element.121), channel_id=1, source_target_pairs={{0,4},{4,8},{8,12},{12,16},{16,20},{20,24},{24,28},{28,0},{1,5},{5... | collective-permute-start | bytes 147464 | tf_op jit(solution)/shard_map/ppermute | solution.py:18
  11.4 15.2 %collective-permute-start.1 = (bf16[32,3,256]{2,1,0:T(4,128)(2,1)S(1)}, bf16[32,3,256]{2,1,0:T(4,128)(2,1)S(1)}, u32[]{:S(2)}, u32[]{:S(2)}) collective-permute-start(bf16[32,3,256]{2,1,0:T(4,128)(2,1)S(1)} %get-tuple-element.122), channel_id=1, source_target_pairs={{4,0},{8,4},{12,8},{16,12},{20,16},{24,20},{28,24},{0,28},{5,1},{9... | collective-permute-start | bytes 147464 | tf_op jit(solution)/shard_map/ppermute | solution.py:19
  27.4 8.0 %collective-permute-start.3 = (bf16[3,38,256]{2,1,0:T(8,128)(2,1)S(1)}, bf16[3,38,256]{2,1,0:T(8,128)(2,1)S(1)}, u32[]{:S(2)}, u32[]{:S(2)}) collective-permute-start(bf16[3,38,256]{2,1,0:T(8,128)(2,1)S(1)} %get-tuple-element.116), channel_id=1, source_target_pairs={{0,1},{1,2},{2,3},{4,5},{5,6},{6,7},{8,9},{9,10},{10,11},{12,13},{... | collective-permute-start | bytes 175112 | tf_op jit(solution)/shard_map/ppermute | solution.py:18
  28.9 6.5 %collective-permute-start.4 = (bf16[3,38,256]{2,1,0:T(8,128)(2,1)S(1)}, bf16[3,38,256]{2,1,0:T(8,128)(2,1)S(1)}, u32[]{:S(2)}, u32[]{:S(2)}) collective-permute-start(bf16[3,38,256]{2,1,0:T(8,128)(2,1)S(1)} %get-tuple-element.115), channel_id=1, source_target_pairs={{1,0},{2,1},{3,2},{5,4},{6,5},{7,6},{9,8},{10,9},{11,10},{13,12},{... | collective-permute-start | bytes 175112 | tf_op jit(solution)/shard_map/ppermute | solution.py:19
  30.2 5.2 %collective-permute-start.2 = (bf16[3,38,256]{2,1,0:T(8,128)(2,1)S(1)}, bf16[3,38,256]{2,1,0:T(8,128)(2,1)S(1)}, u32[]{:S(2)}, u32[]{:S(2)}) collective-permute-start(bf16[3,38,256]{2,1,0:T(8,128)(2,1)S(1)} %reverse_select_fusion.1), channel_id=1, source_target_pairs={{0,16},{4,20},{8,24},{12,28},{16,0},{20,4},{24,8},{28,12},{1,17},{... | collective-permute-start | bytes 175112 | tf_op jit(solution)/shard_map/ppermute | solution.py:27
  49.0 13.1 %copy-start.4 = (bf16[1024,1024]{1,0:T(8,128)(2,1)}, bf16[1024,1024]{1,0:T(8,128)(2,1)S(1)}, u32[]{:S(2)}) copy-start(bf16[1024,1024]{1,0:T(8,128)(2,1)S(1)} %get-tuple-element.180) | copy-start | bytes 6291460
  67.3 9.3 %copy-start.3 = (bf16[32,32,256]{2,1,0:T(8,128)(2,1)S(1)}, bf16[32,32,256]{2,1,0:T(8,128)(2,1)}, u32[]{:S(2)}) copy-start(bf16[32,32,256]{2,1,0:T(8,128)(2,1)} %param.14) | copy-start | bytes 1572868
  67.3 9.3 %copy-start.23 = (bf16[1024,256]{1,0:T(8,128)(2,1)S(1)}, bf16[1024,256]{1,0:T(8,128)(2,1)}, u32[]{:S(2)}) copy-start(bf16[1024,256]{1,0:T(8,128)(2,1)} %param.22) | copy-start | bytes 1572868
  67.4 9.3 %copy-start.24 = (f32[256]{0:T(256)S(1)}, f32[256]{0:T(256)}, u32[]{:S(2)}) copy-start(f32[256]{0:T(256)} %convert_element_type.582) | copy-start | bytes 3076
  71.8 8.0 %collective-permute-start.5 = (bf16[32,3,256]{2,1,0:T(4,128)(2,1)S(1)}, bf16[32,3,256]{2,1,0:T(4,128)(2,1)S(1)}, u32[]{:S(2)}, u32[]{:S(2)}) collective-permute-start(bf16[32,3,256]{2,1,0:T(4,128)(2,1)S(1)} %get-tuple-element.120), channel_id=1, source_target_pairs={{0,4},{4,8},{8,12},{12,16},{16,20},{20,24},{24,28},{28,0},{1,5},{5... | collective-permute-start | bytes 147464 | tf_op jit(solution)/shard_map/ppermute | solution.py:18
  71.9 7.9 %collective-permute-start.6 = (bf16[32,3,256]{2,1,0:T(4,128)(2,1)S(1)}, bf16[32,3,256]{2,1,0:T(4,128)(2,1)S(1)}, u32[]{:S(2)}, u32[]{:S(2)}) collective-permute-start(bf16[32,3,256]{2,1,0:T(4,128)(2,1)S(1)} %get-tuple-element.119), channel_id=1, source_target_pairs={{4,0},{8,4},{12,8},{16,12},{20,16},{24,20},{28,24},{0,28},{5,1},{9... | collective-permute-start | bytes 147464 | tf_op jit(solution)/shard_map/ppermute | solution.py:19
  76.6 3.1 %copy-start.20 = (f32[256]{0:T(256)S(1)}, f32[256]{0:T(256)}, u32[]{:S(2)}) copy-start(f32[256]{0:T(256)} %get-tuple-element.34) | copy-start | bytes 3076
  76.6 3.1 %copy-start.21 = (f32[256]{0:T(256)S(1)}, f32[256]{0:T(256)}, u32[]{:S(2)}) copy-start(f32[256]{0:T(256)} %get-tuple-element.85) | copy-start | bytes 3076
  79.8 12.1 %collective-permute-start.8 = (bf16[3,38,256]{2,1,0:T(8,128)(2,1)S(1)}, bf16[3,38,256]{2,1,0:T(8,128)(2,1)S(1)}, u32[]{:S(2)}, u32[]{:S(2)}) collective-permute-start(bf16[3,38,256]{2,1,0:T(8,128)(2,1)S(1)} %get-tuple-element.111), channel_id=1, source_target_pairs={{1,0},{2,1},{3,2},{5,4},{6,5},{7,6},{9,8},{10,9},{11,10},{13,12},{... | collective-permute-start | bytes 175112 | tf_op jit(solution)/shard_map/ppermute | solution.py:19
  81.2 10.7 %collective-permute-start.9 = (bf16[3,38,256]{2,1,0:T(8,128)(2,1)S(1)}, bf16[3,38,256]{2,1,0:T(8,128)(2,1)S(1)}, u32[]{:S(2)}, u32[]{:S(2)}) collective-permute-start(bf16[3,38,256]{2,1,0:T(8,128)(2,1)S(1)} %get-tuple-element.112), channel_id=1, source_target_pairs={{0,1},{1,2},{2,3},{4,5},{5,6},{6,7},{8,9},{9,10},{10,11},{12,13},{... | collective-permute-start | bytes 175112 | tf_op jit(solution)/shard_map/ppermute | solution.py:18
  84.8 7.1 %collective-permute-start.7 = (bf16[3,38,256]{2,1,0:T(8,128)(2,1)S(1)}, bf16[3,38,256]{2,1,0:T(8,128)(2,1)S(1)}, u32[]{:S(2)}, u32[]{:S(2)}) collective-permute-start(bf16[3,38,256]{2,1,0:T(8,128)(2,1)S(1)} %reverse_select_fusion), channel_id=1, source_target_pairs={{0,16},{4,20},{8,24},{12,28},{16,0},{20,4},{24,8},{28,12},{1,17},{... | collective-permute-start | bytes 175112 | tf_op jit(solution)/shard_map/ppermute | solution.py:27
  92.3 8.2 %copy-start.8 = (f32[256]{0:T(256)S(1)}, f32[256]{0:T(256)}, u32[]{:S(2)}) copy-start(f32[256]{0:T(256)} %get-tuple-element.200) | copy-start | bytes 3076
  92.3 8.2 %copy-start.9 = (f32[256]{0:T(256)S(1)}, f32[256]{0:T(256)}, u32[]{:S(2)}) copy-start(f32[256]{0:T(256)} %get-tuple-element.189) | copy-start | bytes 3076
  92.4 8.2 %copy-start.10 = (f32[256]{0:T(256)S(1)}, f32[256]{0:T(256)}, u32[]{:S(2)}) copy-start(f32[256]{0:T(256)} %get-tuple-element.190) | copy-start | bytes 3076
  92.4 8.2 %copy-start.11 = (f32[256]{0:T(256)S(1)}, f32[256]{0:T(256)}, u32[]{:S(2)}) copy-start(f32[256]{0:T(256)} %get-tuple-element.191) | copy-start | bytes 3076
  92.4 8.2 %copy-start.12 = (f32[256]{0:T(256)S(1)}, f32[256]{0:T(256)}, u32[]{:S(2)}) copy-start(f32[256]{0:T(256)} %get-tuple-element.192) | copy-start | bytes 3076
  92.4 8.2 %copy-start.13 = (f32[256]{0:T(256)S(1)}, f32[256]{0:T(256)}, u32[]{:S(2)}) copy-start(f32[256]{0:T(256)} %get-tuple-element.193) | copy-start | bytes 3076
  92.4 8.2 %copy-start.14 = (f32[256]{0:T(256)S(1)}, f32[256]{0:T(256)}, u32[]{:S(2)}) copy-start(f32[256]{0:T(256)} %get-tuple-element.194) | copy-start | bytes 3076
  92.4 8.2 %copy-start.15 = (f32[256]{0:T(256)S(1)}, f32[256]{0:T(256)}, u32[]{:S(2)}) copy-start(f32[256]{0:T(256)} %get-tuple-element.195) | copy-start | bytes 3076
  92.4 8.2 %copy-start.16 = (f32[256]{0:T(256)S(1)}, f32[256]{0:T(256)}, u32[]{:S(2)}) copy-start(f32[256]{0:T(256)} %get-tuple-element.196) | copy-start | bytes 3076
  92.4 8.2 %copy-start.17 = (f32[256]{0:T(256)S(1)}, f32[256]{0:T(256)}, u32[]{:S(2)}) copy-start(f32[256]{0:T(256)} %get-tuple-element.197) | copy-start | bytes 3076
  92.4 8.2 %copy-start.18 = (f32[256]{0:T(256)S(1)}, f32[256]{0:T(256)}, u32[]{:S(2)}) copy-start(f32[256]{0:T(256)} %get-tuple-element.198) | copy-start | bytes 3076
  92.5 8.6 %copy-start.19 = (f32[256]{0:T(256)S(1)}, f32[256]{0:T(256)}, u32[]{:S(2)}) copy-start(f32[256]{0:T(256)} %fusion.147) | copy-start | bytes 3076
  92.5 8.8 %copy-start.7 = (bf16[32,32,256]{2,1,0:T(8,128)(2,1)S(1)}, bf16[32,32,256]{2,1,0:T(8,128)(2,1)}, u32[]{:S(2)}) copy-start(bf16[32,32,256]{2,1,0:T(8,128)(2,1)} %param.15) | copy-start | bytes 1572868
  (4 other events, 6.2 us)
Sparse Core Ops, SparseCore 0:
  76.7 134.6 all-reduce.5
where the time goes:
time: 223 us; the launch traced here: 222 us
  waiting for transfers between devices  78.9 us (35%)
  other arithmetic  42.2 us (19%)
  blocking collectives  41.5 us (19%)
  starting transfers between devices  19.5 us (9%)
  between operations  14.7 us (7%)
  local copies, waits for them, and re-layouts  13.3 us (6%)
  matrix products  11.6 us (5%)
    psum x1, waiting for transfers between devices, local(): lax.psum((grad_kern, grad_dwb, gain_gradient, grad_sh, grad_exp, grad_bex...  67.6 us
    psum x1, blocking collectives, local(): lax.psum((grad_kern, grad_dwb, gain_gradient, grad_sh, grad_exp, grad_bex...  41.5 us
    ppermute x2, waiting for transfers between devices, from_behind(): return lax.ppermute(value, axis, pairs)  11.3 us
    ppermute x4, starting transfers between devices, extended(): after = lax.ppermute(first, axis, down)  10.4 us
    reduce_sum x3, other arithmetic, local(): kern_terms.append(jnp.sum(dconv_wide * window, axis=(0, 1)))  10 us
    reduce_sum x1, other arithmetic, local(): mean_removed = conv - jnp.mean(conv, axis=-1, keepdims=True)  8.57 us
    ppermute x4, starting transfers between devices, extended(): before = lax.ppermute(last, axis, up)  8.18 us
    add x1, other arithmetic, local(): adjoint + weight * inner[6 - row_off:6 - row_off + rows, col_from:col_fro...  8.02 us
  transfers between devices with their start and end apart: 11, of which 3 were waited for; matrix products, arithmetic and copies ran while one was open for 11% of the time, Pallas kernels for 0%

commit v1 on v0

--- a/solution.py
+++ b/solution.py
@@ -8,23 +8,107 @@
 EPS = 1e-06
 
 
-def extended(array, sides, width, wrap):
-    for axis, dim in sides:
-        size, length = (lax.axis_size(axis), array.shape[dim])
-        up = [(i, (i + 1) % size) for i in range(size if wrap else size - 1)]
-        down = [(j, i) for i, j in up]
-        last = lax.slice_in_dim(array, length - width, length, axis=dim)
-        first = lax.slice_in_dim(array, 0, width, axis=dim)
-        before = lax.ppermute(last, axis, up)
-        after = lax.ppermute(first, axis, down)
-        array = jnp.concatenate([before, array, after], axis=dim)
-    return array
-
-
-def from_behind(value, axis, steps):
-    count = lax.axis_size(axis)
-    pairs = [(source, (source + steps) % count) for source in range(count)]
-    return lax.ppermute(value, axis, pairs)
+def flat_pairs(target):
+    lons, lats = lax.axis_size("lon"), lax.axis_size("lat")
+    pairs = []
+    for lon in range(lons):
+        for lat in range(lats):
+            to_lon, to_lat = target(lon, lat)
+            pairs.append((lon * lats + lat, to_lon * lats + to_lat))
+    return pairs
+
+
+def send(value, target):
+    return lax.ppermute(value, ("lon", "lat"), flat_pairs(target))
+
+
+def lon_margins(field):
+    lons = lax.axis_size("lon")
+    odd = lax.axis_index("lon") % 2 == 1
+    first, last = field[:, :3], field[:, -3:]
+    inner = send(jnp.where(odd, first, last), lambda lon, lat: (lon ^ 1, lat))
+    outer = send(
+        jnp.where(odd, last, first),
+        lambda lon, lat: ((lon + 1) % lons if lon % 2 else (lon - 1) % lons, lat),
+    )
+    west = jnp.where(odd, inner, outer)
+    east = jnp.where(odd, outer, inner)
+    return jnp.concatenate([west, field, east], axis=1)
+
+
+def lat_margins(wide):
+    lons, lats = lax.axis_size("lon"), lax.axis_size("lat")
+    lat = lax.axis_index("lat")
+    odd = lat % 2 == 1
+    pole = (lat == 0) | (lat == lats - 1)
+    first, last = wide[:3], wide[-3:]
+
+    def beyond(lon, lat):
+        if lat == 0 or lat == lats - 1:
+            return ((lon + lons // 2) % lons, lat)
+        return (lon, lat + 1 if lat % 2 else lat - 1)
+
+    outgoing = jnp.where(odd, last, first)
+    outgoing = jnp.where(pole, outgoing[::-1], outgoing)
+    far = send(outgoing, beyond)
+    near = send(jnp.where(odd, first, last), lambda lon, lat: (lon, lat ^ 1))
+    north = jnp.where(odd, near, far)
+    south = jnp.where(odd, far, near)
+    return north, south
+
+
+def axis_bits():
+    lon_bits = [("lon", bit) for bit in range((lax.axis_size("lon") - 1).bit_length())]
+    lat_bits = [("lat", bit) for bit in range(1, (lax.axis_size("lat") - 1).bit_length())]
+    steps = []
+    while lon_bits or lat_bits:
+        if lon_bits:
+            steps.append(lon_bits.pop(0))
+        if lat_bits:
+            steps.append(lat_bits.pop(0))
+    return steps
+
+
+def flip(place, step):
+    lon, lat = place
+    axis, bit = step
+    return (lon ^ (1 << bit), lat) if axis == "lon" else (lon, lat ^ (1 << bit))
+
+
+def summed(keep, give):
+    core = lax.axis_index("lat") % 2
+    steps = axis_bits()
+    other = list(steps)
+    for at in range(0, len(steps) - 1, 2):
+        other[at], other[at + 1] = other[at + 1], other[at]
+
+    def exchange(value, at):
+        return send(value, lambda lon, lat: flip((lon, lat), (other if lat % 2 else steps)[at]))
+
+    def bit_of(at):
+        def bit(step):
+            return lax.shift_right_logical(lax.axis_index(step[0]), step[1]) & 1
+
+        return jnp.where(core == 1, bit(other[at]), bit(steps[at]))
+
+    total = keep + send(give, lambda lon, lat: (lon, lat ^ 1)).astype(jnp.float32)
+    halvings = min(2, len(steps))
+    for at in range(halvings):
+        half = total.shape[0] // 2
+        bit = bit_of(at)
+        outgoing = lax.dynamic_slice_in_dim(total, (1 - bit) * half, half, 0)
+        mine = lax.dynamic_slice_in_dim(total, bit * half, half, 0)
+        total = mine + exchange(outgoing.astype(jnp.bfloat16), at).astype(jnp.float32)
+    sent = total.astype(jnp.bfloat16)
+    for at in range(halvings, len(steps)):
+        got = exchange(sent, at)
+        sent = (sent.astype(jnp.float32) + got.astype(jnp.float32)).astype(jnp.bfloat16)
+    for at in reversed(range(halvings)):
+        got = exchange(sent, at)
+        low = bit_of(at) == 0
+        sent = jnp.concatenate([jnp.where(low, sent, got), jnp.where(low, got, sent)], axis=0)
+    got = send(sent, lambda lon, lat: (lon, lat ^ 1))
+    return jnp.where(core == 0, sent, got), jnp.where(core == 0, got, sent)
 
 
 def gelu_parts(values):
@@ -40,16 +124,14 @@
 
 
 def sphere_pad(field):
-    lat_index = lax.axis_index("lat")
-    north = lat_index == 0
-    south = lat_index == lax.axis_size("lat") - 1
-    wide = extended(field, (("lon", 1),), 3, True)
-    outgoing = jnp.where(north, wide[2::-1], wide[:-4:-1])
-    partner = from_behind(outgoing, "lon", lax.axis_size("lon") // 2)
-    tall = extended(wide, (("lat", 0),), 3, False)
-    top_rows = jnp.where(north, partner, tall[:3])
-    bottom_rows = jnp.where(south, partner, tall[-3:])
-    return (jnp.concatenate([top_rows, tall[3:-3], bottom_rows], axis=0), north, south)
+    lat = lax.axis_index("lat")
+    wide = lon_margins(field)
+    top, bottom = lat_margins(wide)
+    return (
+        jnp.concatenate([top, wide, bottom], axis=0),
+        lat == 0,
+        lat == lax.axis_size("lat") - 1,
+    )
 
 
 def local(
@@ -151,10 +233,32 @@
     adjoint = adjoint.at[:3].add(north_term)
     adjoint = adjoint.at[rows - 3 :].add(south_term)
     grad_fields = (cotangent.astype(jnp.float32) + adjoint).astype(jnp.bfloat16)
-    sum_kern, sum_dwb, sum_gn, sum_sh, sum_exp, sum_bexp, sum_proj, sum_bproj = lax.psum(
-        (grad_kern, grad_dwb, gain_gradient, grad_sh, grad_exp, grad_bexp, grad_proj, grad_bproj),
-        ("lon", "lat"),
-    )
+    hidden_units = w_expand.shape[1]
+    pieces = hidden_units // chans
+    small = [
+        grad_kern.reshape(49, chans),
+        grad_dwb.reshape(1, chans),
+        gain_gradient.reshape(1, chans),
+        grad_sh.reshape(1, chans),
+        grad_bproj.reshape(1, chans),
+        grad_bexp.reshape(pieces, chans),
+        jnp.zeros((128 - 53 - pieces, chans), jnp.float32),
+    ]
+    expand_rows = grad_exp.reshape(chans, pieces, chans).swapaxes(0, 1).reshape(-1, chans)
+    first = jnp.concatenate([expand_rows, jnp.concatenate(small, axis=0)[:64]], axis=0)
+    second = jnp.concatenate([grad_proj, jnp.concatenate(small, axis=0)[64:128]], axis=0)
+    core = lax.axis_index("lat") % 2
+    keep = jnp.where(core == 0, first, second)
+    give = jnp.where(core == 0, second, first).astype(jnp.bfloat16)
+    first, second = summed(keep, give)
+    first = first.astype(jnp.float32)
+    second = second.astype(jnp.float32)
+    sum_exp = first[:hidden_units].reshape(pieces, chans, chans).swapaxes(0, 1).reshape(chans, -1)
+    sum_proj = second[:hidden_units]
+    rest = first[hidden_units:]
+    sum_kern = rest[:49].reshape(7, 7, chans)
+    sum_dwb, sum_gn, sum_sh, sum_bproj = rest[49], rest[50], rest[51], rest[52]
+    sum_bexp = rest[53 : 53 + pieces].reshape(-1)
     return (
         block_out,
         grad_fields,

time: 223 us -> 148 us (0.66)
  waiting for transfers between devices: 78.9 us -> 35.9 us
  blocking collectives: 41.5 us -> 0 us
  other arithmetic: 42.2 us -> 60.8 us
  between operations: 14.7 us -> 3.08 us
  matrix products: 11.6 us -> 15.2 us
    psum x1 -> x0, waiting for transfers between devices: 67.6 us -> none  [local(): lax.psum((grad_kern, grad_dwb, gain_gradient, grad_sh, grad_exp, grad_bex...]
    psum x1 -> x0, blocking collectives: 41.5 us -> none  [local(): lax.psum((grad_kern, grad_dwb, gain_gradient, grad_sh, grad_exp, grad_bex...]
    ppermute x10 -> x16, waiting for transfers between devices: 11.3 us -> 35.9 us  [send(): return lax.ppermute(value, ('lon', 'lat'), flat_pairs(target))]
    mul x14, other arithmetic: 3.47 us -> 10.9 us  [local(): weight * fold_north[row_off:row_off + 3, col_from:col_from + cols].astype...]
    add x0 -> x2, other arithmetic: none -> 3.54 us  [the longest x1 2.43 us: summed(): keep + send(give, lambda lon, lat: (lon, lat ^ 1)).astype(jnp.float32)]
    reshape x0 -> x3, local copies, waits for them, and re-layouts: none -> 3.18 us  [the longest x1 1.44 us: local(): grad_exp.reshape(chans, pieces, chans).swapaxes(0, 1).reshape(-1, chans)]
    another operation x1, local copies, waits for them, and re-layouts: 4.36 us -> 1.53 us  [local(): jnp.stack(kern_terms, axis=0).reshape(7, 7, chans) * scale_factor]
    unnamed x53 -> x286, local copies, waits for them, and re-layouts: 4.58 us -> 1.86 us
  transfers between devices with their start and end apart: 11 -> 16, of which waited for: 3 -> 10; matrix products, arithmetic and copies ran while one was open for 11% -> 19% of each run, Pallas kernels for 0% -> 0%
where the time goes in v1:
time: 148 us; the launch traced here: 147 us
  other arithmetic  60.8 us (41%)
  waiting for transfers between devices  35.9 us (24%)
  starting transfers between devices  17.5 us (12%)
  matrix products  15.2 us (10%)
  local copies, waits for them, and re-layouts  14.5 us (10%)
  between operations  3.08 us (2%)
    ppermute x16, waiting for transfers between devices, send(): return lax.ppermute(value, ('lon', 'lat'), flat_pairs(target))  35.9 us
    ppermute x16, starting transfers between devices, send(): return lax.ppermute(value, ('lon', 'lat'), flat_pairs(target))  17.5 us
    mul x14, other arithmetic, local(): weight * fold_north[row_off:row_off + 3, col_from:col_from + cols].astype...  10.9 us
    reduce_sum x1, other arithmetic, local(): mean_removed = conv - jnp.mean(conv, axis=-1, keepdims=True)  9.54 us
    reduce_sum x4, other arithmetic, local(): kern_terms.append(jnp.sum(dconv_wide * window, axis=(0, 1)))  9.45 us
    add x1, other arithmetic, local(): adjoint + weight * inner[6 - row_off:6 - row_off + rows, col_from:col_fro...  8.82 us
    dot_general x2, matrix products, contract_rows(): lax.dot_general(left, right, (((0,), (0,)), ((), ())), preferred_element_...  4.05 us
    slice x3, local copies, waits for them, and re-layouts, local(): weights[row_off, col_off]  3.6 us
  transfers between devices with their start and end apart: 16, of which 10 were waited for; matrix products, arithmetic and copies ran while one was open for 19% of the time, Pallas kernels for 0%

profile of v1, /device:TPU:0, one launch (start us, length us, event | category | flops | bytes accessed | tf_op | source)
XLA Modules:
  0.0 146.9 jit_solution(7340964366663517288)
XLA Ops:
  1.9 3.0 %collective-permute-start = (bf16[32,3,256]{2,1,0:T(4,128)(2,1)S(1)}, bf16[32,3,256]{2,1,0:T(4,128)(2,1)S(1)}, u32[]{:S(2)}, u32[]{:S(2)}) collective-permute-start(bf16[32,3,256]{2,1,0:T(4,128)(2,1)S(1)} %get-tuple-element.117), channel_id=1, source_target_pairs={{0,4},{1,5},{2,6},{3,7},{4,0},{5,1},{6,2},{7,3},{8,12},{9,13},{10,... | collective-permute-start | bytes 147464 | tf_op jit(solution)/shard_map/ppermute | solution.py:22
  4.9 3.6 %collective-permute-start.1 = (bf16[32,3,256]{2,1,0:T(4,128)(2,1)S(1)}, bf16[32,3,256]{2,1,0:T(4,128)(2,1)S(1)}, u32[]{:S(2)}, u32[]{:S(2)}) collective-permute-start(bf16[32,3,256]{2,1,0:T(4,128)(2,1)S(1)} %get-tuple-element.118), channel_id=1, source_target_pairs={{0,28},{1,29},{2,30},{3,31},{4,8},{5,9},{6,10},{7,11},{8,4},{9,5},... | collective-permute-start | bytes 147464 | tf_op jit(solution)/shard_map/ppermute | solution.py:22
  9.6 1.6 %fusion.156 = (f32[1,1,256]{2,1,0:T(1,128)S(1)}, f32[1,1,256]{2,1,0:T(1,128)}, f32[1,1,256]{2,1,0:T(1,128)}, f32[1,1,256]{2,1,0:T(1,128)}, f32[1,1,256]{2,1,0:T(...) fusion(bf16[7,7,256]{2,1,0:T(8,128)(2,1)} %param.16), kind=kLoop, calls=%fused_computation.411 | loop fusion | bytes 38912 | tf_op jit(solution)/shard_map/slice | solution.py:159
  22.1 1.3 fusion.152
  25.5 1.6 %collective-permute-start.2 = (bf16[3,38,256]{2,1,0:T(8,128)(2,1)S(1)}, bf16[3,38,256]{2,1,0:T(8,128)(2,1)S(1)}, u32[]{:S(2)}, u32[]{:S(2)}) collective-permute-start(bf16[3,38,256]{2,1,0:T(8,128)(2,1)S(1)} %get-tuple-element.100), channel_id=1, source_target_pairs={{0,1},{1,0},{2,3},{3,2},{4,5},{5,4},{6,7},{7,6},{8,9},{9,8},{10,11... | collective-permute-start | bytes 175112 | tf_op jit(solution)/shard_map/ppermute | solution.py:22
  31.1 9.5 %add_reduce_fusion = (f32[32,32]{1,0:T(8,128)S(1)}, f32[32,32,256]{2,1,0:T(8,128)S(1)}) fusion(f32[256]{0:T(256)S(1)} %convert_element_type.619, bf16[35,38,256]{2,1,0:T(8,128)(2,1)S(1)} %get-tuple-element.110, f32[256]{0:T(256)} %bitcast.281, f32[256]{0:T(256)} %bitcast.277, f32[256]{0:T(256)} %bitcast.273, f32[256]{0:T(256)} %bitcast.269, ...), kind=kLoop, calls=%fused_computation.250 | loop fusion | flops 43514880 | bytes 23746560 | tf_op jit(solution)/shard_map/reduce_sum | solution.py:163
  43.0 3.5 %multiply_convert_fusion = (bf16[1024,1024]{1,0:T(8,128)(2,1)}, f32[1024,1024]{1,0:T(8,128)S(1)}) fusion(f32[1024]{0:T(1024)} %convert_element_type.623, bf16[256,1024]{1,0:T(8,128)(2,1)S(1)} %copy-done, f32[1024,256]{1,0:T(8,128)S(1)} %fusion.132, f32[256]{0:T(256)} %convert_element_type.621, f32[256]{0:T(256)} %convert_element_type.620), kind=kOutput, calls=%fused_computation.58 | convolution fusion | flops 543948800 | bytes 7870464 | tf_op jit(solution)/shard_map/dot_general | solution.py:171
  46.5 3.1 %convert_reduce_fusion = (f32[1024]{0:T(1024)}, bf16[1024,1024]{1,0:T(8,128)(2,1)S(1)}) fusion(f32[1024,1024]{1,0:T(8,128)S(1)} %get-tuple-element.181, f32[1024]{0:T(1024)S(1)} %copy-done.89, bf16[1024,256]{1,0:T(8,128)(2,1)S(1)} %bitcast.198, bf16[1024,256]{1,0:T(8,128)(2,1)S(1)} %copy-done.136), kind=kOutput, calls=%fused_computation.57 | convolution fusion | flops 550501376 | bytes 7348224 | tf_op jit(solution)/shard_map/dot_general | solution.py:186
  49.6 1.4 multiply_reduce_fusion
  51.0 1.5 %convert_reduce_fusion.2 = (f32[256]{0:T(256)}, bf16[1024,256]{1,0:T(8,128)(2,1)S(1)}) fusion(f32[1024]{0:T(1024)S(1)} %get-tuple-element.185, f32[1024]{0:T(1024)S(1)} %get-tuple-element.186, f32[1024,256]{1,0:T(8,128)S(1)} %get-tuple-element.182, f32[256]{0:T(256)S(1)} %copy-done.85, f32[1024]{0:T(1024)S(1)} %rsqrt.12, f32[1024]{0:T(1024)S(1)} %div.15, ...), kind=kLoop, calls=%fused_computation.245 | loop fusion | flops 2883328 | bytes 2640896 | tf_op jit(solution)/shard_map/reduce_sum | solution.py:200
  52.5 1.5 %fusion.112 = (f32[256]{0:T(256)}, f32[256]{0:T(256)}, f32[256]{0:T(256)}, f32[256]{0:T(256)}, f32[256]{0:T(256)}, /*index=5*/f32[256]{0:T(256)}) fusion(bf16[35,38,256]{2,1,0:T(8,128)(2,1)S(1)} %get-tuple-element.110, bf16[1024,256]{1,0:T(8,128)(2,1)S(1)} %get-tuple-element.94, bf16[35,38,256]{2,1,0:T(8,128)(2,1)S(1)} %get-tuple-element.109), kind=kLoop, calls=%fused_computation.222 | loop fusion | flops 4979200 | bytes 3676160 | tf_op jit(solution)/shard_map/reduce_sum | solution.py:206
  54.0 3.2 %fusion.130 = (f32[256]{0:T(256)}, f32[256]{0:T(256)}, f32[256]{0:T(256)}, f32[256]{0:T(256)}, f32[256]{0:T(256)}, /*index=5*/f32[256]{0:T(256)}, f32[256]{0:T(2...) fusion(bf16[35,38,256]{2,1,0:T(8,128)(2,1)S(1)} %get-tuple-elem, ...), kind=kLoop, calls=%fused_computation.240 | loop fusion | flops 14413312 | bytes 9979904 | tf_op jit(solution)/shard_map/reduce_sum | solution.py:206
  57.3 3.3 %fusion.102 = (f32[256]{0:T(256)}, f32[256]{0:T(256)}, f32[256]{0:T(256)}, f32[256]{0:T(256)}, f32[256]{0:T(256)}, /*index=5*/f32[256]{0:T(256)}, f32[256]{0:T(2...) fusion(bf16[35,38,256]{2,1,0:T(8,128)(2,1)S(1)} %get-tuple-elem, ...), kind=kLoop, calls=%fused_computation.212 | loop fusion | flops 14413312 | bytes 9979904 | tf_op jit(solution)/shard_map/reduce_sum | solution.py:206
  60.5 1.5 %fusion.109 = (f32[256]{0:T(256)S(1)}, f32[256]{0:T(256)S(1)}, f32[256]{0:T(256)S(1)}, f32[256]{0:T(256)S(1)}, f32[256]{0:T(256)S(1)}, /*index=5*/f32[256]{0:T(256)S(1)}, f32[256]{0:T(256)S(1)}) fusion(bf16[32,3,256]{2,1,0:T(4,128)(2,1)S(1)} %copy-done.6, bf16[32,32,256]{2,1,0:T(8,128)(2,1)S(1)} %copy-done.2, bf16[1024,256]{1,0:T(8,128)(2,1)S(1)} %get-tuple-element.94, ...), kind=kLoop, calls=%fused_computation.219 | loop fusion | flops 10483968 | bytes 1154048 | tf_op jit(solution)/shard_map/reduce_sum | solution.py:206
  63.5 1.5 %stack.199 = f32[49,256]{1,0:T(8,128)S(1)} concatenate(f32[1,256]{1,0:T(1,128)S(1)} %bitcast.379, f32[1,256]{1,0:T(1,128)S(1)} %bitcast.380, f32[1,256]{1,0:T(1,128)S(1)} %bitcast.381, f32[1,256]{1,0:T(1,128)} %bitcast.417, f32[1,256]{1,0:T(1,128)} %bitcast.416, f32[1,256]{1,0:T(1,128)} %bitcast.415, f32[1,256]{1,0:T(1,128)} %bitcast.414, f32[1,256]{1,0:T(1,128)} %bitcast.413, ...), dimensions={0} | concatenate | bytes 100352 | tf_op jit(solution)/shard_map/stack | solution.py:207
  65.8 2.6 %collective-permute-start.5 = (bf16[32,3,256]{2,1,0:T(4,128)(2,1)S(1)}, bf16[32,3,256]{2,1,0:T(4,128)(2,1)S(1)}, u32[]{:S(2)}, u32[]{:S(2)}) collective-permute-start(bf16[32,3,256]{2,1,0:T(4,128)(2,1)S(1)} %get-tuple-element.115), channel_id=1, source_target_pairs={{0,28},{1,29},{2,30},{3,31},{4,8},{5,9},{6,10},{7,11},{8,4},{9,5},... | collective-permute-start | bytes 147464 | tf_op jit(solution)/shard_map/ppermute | solution.py:22
  68.4 3.3 %convolution_multiply_fusion = f32[1024,256]{1,0:T(8,128)} fusion(bf16[1024,1024]{1,0:T(8,128)(2,1)} %get-tuple-element.180, bf16[1024,256]{1,0:T(8,128)(2,1)S(1)} %bitcast.199), kind=kOutput, calls=%fused_computation.60 | convolution fusion | flops 537133056 | bytes 3670016 | tf_op jit(solution)/shard_map/dot_general | solution.py:121
  74.5 1.4 reshape.216
  75.9 1.4 copy.20
  80.5 8.8 %fusion.81 = f32[32,32,256]{2,1,0:T(8,128)S(1)} fusion(bf16[32,32,256]{2,1,0:T(8,128)(2,1)S(1)} %bitcast.191, bf16[32,3,256]{2,1,0:T(4,128)(2,1)S(1)} %get-tuple-element.122, bf16[32,3,256]{2,1,0:T(4,128)(2,1)S(1)} %get-tuple-element.121, bf16[35,38,256]{2,1,0:T(8,128)(2,1)S(1)} %get-tuple-element.108, bf16[35,38,256]{2,1,0:T(8,128)(2,1)S(1)} %get-tuple-element.107, ...), kind=kLoop, calls=%fused_computation.191 | loop fusion | flops 42991616 | bytes 23741440 | tf_op jit(solution)/shard_map/add | solution.py:224
  93.0 1.4 select_convert_fusion
  94.5 1.9 %collective-permute-done.8 = bf16[1088,256]{1,0:T(8,128)(2,1)S(1)} collective-permute-done((bf16[1088,256]{1,0:T(8,128)(2,1)S(1)}, bf16[1088,256]{1,0:T(8,128)(2,1)S(1)}, u32[]{:S(2)}, u32[]{:S(2)}) %collective-permute-start.8) | collective-permute-done | bytes 557088 | tf_op jit(solution)/shard_map/ppermute | solution.py:22
  96.4 2.4 %convert_add_fusion.1 = f32[1088,256]{1,0:T(8,128)} fusion(bf16[1088,256]{1,0:T(8,128)(2,1)S(1)} %collective-permute-done.8, f32[1024,256]{1,0:T(8,128)} %convolution_multiply_fusion, f32[64,256]{1,0:T(8,128)S(1)} %slice.1238, f32[1024,256]{1,0:T(8,128)S(1)} %bitcast.194, pred[]{:T(512)S(6)} %eq.45), kind=kLoop, calls=%fused_computation.116 | loop fusion | flops 1114112 | bytes 3833857 | tf_op jit(solution)/shard_map/add | solution.py:94
  100.4 6.2 %collective-permute-done.9 = bf16[544,256]{1,0:T(8,128)(2,1)S(1)} collective-permute-done((bf16[544,256]{1,0:T(8,128)(2,1)S(1)}, bf16[544,256]{1,0:T(8,128)(2,1)S(1)}, u32[]{:S(2)}, u32[]{:S(2)}) %collective-permute-start.9) | collective-permute-done | bytes 278560 | tf_op jit(solution)/shard_map/ppermute | solution.py:22
  107.7 1.6 %collective-permute-start.10 = (bf16[272,256]{1,0:T(8,128)(2,1)S(1)}, bf16[272,256]{1,0:T(8,128)(2,1)S(1)}, u32[]{:S(2)}, u32[]{:S(2)}) collective-permute-start(bf16[272,256]{1,0:T(8,128)(2,1)S(1)} %dynamic-slice_convert_fusion.1), channel_id=1, source_target_pairs={{0,2},{1,5},{2,0},{3,7},{4,6},{5,1},{6,4},{7,3},{8,10},{9,13},{10,... | collective-permute-start | bytes 417800 | tf_op jit(solution)/shard_map/ppermute | solution.py:22
  109.3 3.5 %collective-permute-done.10 = bf16[272,256]{1,0:T(8,128)(2,1)S(1)} collective-permute-done((bf16[272,256]{1,0:T(8,128)(2,1)S(1)}, bf16[272,256]{1,0:T(8,128)(2,1)S(1)}, u32[]{:S(2)}, u32[]{:S(2)}) %collective-permute-start.10) | collective-permute-done | bytes 139296 | tf_op jit(solution)/shard_map/ppermute | solution.py:22
  113.9 4.4 %collective-permute-done.11 = bf16[272,256]{1,0:T(8,128)(2,1)S(1)} collective-permute-done((bf16[272,256]{1,0:T(8,128)(2,1)S(1)}, bf16[272,256]{1,0:T(8,128)(2,1)S(1)}, u32[]{:S(2)}, u32[]{:S(2)}) %collective-permute-start.11) | collective-permute-done | bytes 139296 | tf_op jit(solution)/shard_map/ppermute | solution.py:22
  118.4 2.0 %collective-permute-start.12 = (bf16[272,256]{1,0:T(8,128)(2,1)S(1)}, bf16[272,256]{1,0:T(8,128)(2,1)S(1)}, u32[]{:S(2)}, u32[]{:S(2)}) collective-permute-start(bf16[272,256]{1,0:T(8,128)(2,1)S(1)} %add_convert_fusion.2), channel_id=1, source_target_pairs={{0,16},{1,9},{2,18},{3,11},{4,20},{5,13},{6,22},{7,15},{8,24},{9,1... | collective-permute-start | bytes 417800 | tf_op jit(solution)/shard_map/ppermute | solution.py:22
  120.4 5.5 %collective-permute-done.12 = bf16[272,256]{1,0:T(8,128)(2,1)S(1)} collective-permute-done((bf16[272,256]{1,0:T(8,128)(2,1)S(1)}, bf16[272,256]{1,0:T(8,128)(2,1)S(1)}, u32[]{:S(2)}, u32[]{:S(2)}) %collective-permute-start.12) | collective-permute-done | bytes 139296 | tf_op jit(solution)/shard_map/ppermute | solution.py:22
  127.0 5.6 %collective-permute-done.13 = bf16[272,256]{1,0:T(8,128)(2,1)S(1)} collective-permute-done((bf16[272,256]{1,0:T(8,128)(2,1)S(1)}, bf16[272,256]{1,0:T(8,128)(2,1)S(1)}, u32[]{:S(2)}, u32[]{:S(2)}) %collective-permute-start.13) | collective-permute-done | bytes 139296 | tf_op jit(solution)/shard_map/ppermute | solution.py:22
  132.7 6.5 %collective-permute-done.14 = bf16[544,256]{1,0:T(8,128)(2,1)S(1)} collective-permute-done((bf16[544,256]{1,0:T(8,128)(2,1)S(1)}, bf16[544,256]{1,0:T(8,128)(2,1)S(1)}, u32[]{:S(2)}, u32[]{:S(2)}) %collective-permute-start.14) | collective-permute-done | bytes 278560 | tf_op jit(solution)/shard_map/ppermute | solution.py:22
  139.5 3.1 %fusion.7 = bf16[1024,256]{1,0:T(8,128)(2,1)} fusion(bf16[1024,1024]{1,0:T(8,128)(2,1)} %get-tuple-element.180, bf16[1024,256]{1,0:T(8,128)(2,1)S(1)} %copy-done.137, f32[256]{0:T(256)S(1)} %convert_element_type.625, bf16[1024,256]{1,0:T(8,128)(2,1)S(1)} %bitcast.192), kind=kOutput, calls=%fused_computation.114 | convolution fusion | flops 537919488 | bytes 3671040 | tf_op jit(solution)/shard_map/dot_general | solution.py:176
  (377 shorter events, 40.8 us)
Async XLA Ops:
  0.6 42.3 %copy-start = (bf16[256,1024]{1,0:T(8,128)(2,1)S(1)}, bf16[256,1024]{1,0:T(8,128)(2,1)}, u32[]{:S(2)}) copy-start(bf16[256,1024]{1,0:T(8,128)(2,1)} %param.20) | copy-start | bytes 1572868
  0.7 30.0 %copy-start.1 = (bf16[32,32,256]{2,1,0:T(8,128)(2,1)S(1)}, bf16[32,32,256]{2,1,0:T(8,128)(2,1)}, u32[]{:S(2)}) copy-start(bf16[32,32,256]{2,1,0:T(8,128)(2,1)} %param.14) | copy-start | bytes 1572868
  0.7 27.0 %copy-start.138 = (bf16[256]{0:T(256)(128)(2,1)S(1)}, bf16[256]{0:T(256)(128)(2,1)}, u32[]{:S(2)}) copy-start(bf16[256]{0:T(256)(128)(2,1)} %param.17) | copy-start | bytes 1540
  0.7 27.0 %copy-start.139 = (bf16[256]{0:T(256)(128)(2,1)S(1)}, bf16[256]{0:T(256)(128)(2,1)}, u32[]{:S(2)}) copy-start(bf16[256]{0:T(256)(128)(2,1)} %param.18) | copy-start | bytes 1540
  0.7 27.6 %copy-start.133 = (bf16[1024]{0:T(1024)(128)(2,1)S(1)}, bf16[1024]{0:T(1024)(128)(2,1)}, u32[]{:S(2)}) copy-start(bf16[1024]{0:T(1024)(128)(2,1)} %param.21) | copy-start | bytes 6148
  0.7 28.2 %copy-start.140 = (bf16[256]{0:T(256)(128)(2,1)S(1)}, bf16[256]{0:T(256)(128)(2,1)}, u32[]{:S(2)}) copy-start(bf16[256]{0:T(256)(128)(2,1)} %param.19) | copy-start | bytes 1540
  1.9 22.2 %collective-permute-start = (bf16[32,3,256]{2,1,0:T(4,128)(2,1)S(1)}, bf16[32,3,256]{2,1,0:T(4,128)(2,1)S(1)}, u32[]{:S(2)}, u32[]{:S(2)}) collective-permute-start(bf16[32,3,256]{2,1,0:T(4,128)(2,1)S(1)} %get-tuple-element.117), channel_id=1, source_target_pairs={{0,4},{1,5},{2,6},{3,7},{4,0},{5,1},{6,2},{7,3},{8,12},{9,13},{10,... | collective-permute-start | bytes 147464 | tf_op jit(solution)/shard_map/ppermute | solution.py:22
  4.9 19.5 %collective-permute-start.1 = (bf16[32,3,256]{2,1,0:T(4,128)(2,1)S(1)}, bf16[32,3,256]{2,1,0:T(4,128)(2,1)S(1)}, u32[]{:S(2)}, u32[]{:S(2)}) collective-permute-start(bf16[32,3,256]{2,1,0:T(4,128)(2,1)S(1)} %get-tuple-element.118), channel_id=1, source_target_pairs={{0,28},{1,29},{2,30},{3,31},{4,8},{5,9},{6,10},{7,11},{8,4},{9,5},... | collective-permute-start | bytes 147464 | tf_op jit(solution)/shard_map/ppermute | solution.py:22
  9.4 14.6 %copy-start.45 = (f32[1,1,256]{2,1,0:T(1,128)}, f32[1,1,256]{2,1,0:T(1,128)S(1)}, u32[]{:S(2)}) copy-start(f32[1,1,256]{2,1,0:T(1,128)S(1)} %get-tuple-element.131) | copy-start | bytes 3076
  9.5 14.6 %copy-start.47 = (f32[1,1,256]{2,1,0:T(1,128)}, f32[1,1,256]{2,1,0:T(1,128)S(1)}, u32[]{:S(2)}) copy-start(f32[1,1,256]{2,1,0:T(1,128)S(1)} %get-tuple-element.132) | copy-start | bytes 3076
  9.5 14.6 %copy-start.49 = (f32[1,1,256]{2,1,0:T(1,128)}, f32[1,1,256]{2,1,0:T(1,128)S(1)}, u32[]{:S(2)}) copy-start(f32[1,1,256]{2,1,0:T(1,128)S(1)} %get-tuple-element.133) | copy-start | bytes 3076
  9.5 14.6 %copy-start.51 = (f32[1,1,256]{2,1,0:T(1,128)}, f32[1,1,256]{2,1,0:T(1,128)S(1)}, u32[]{:S(2)}) copy-start(f32[1,1,256]{2,1,0:T(1,128)S(1)} %get-tuple-element.134) | copy-start | bytes 3076
  9.5 14.6 %copy-start.53 = (f32[1,1,256]{2,1,0:T(1,128)}, f32[1,1,256]{2,1,0:T(1,128)S(1)}, u32[]{:S(2)}) copy-start(f32[1,1,256]{2,1,0:T(1,128)S(1)} %get-tuple-element.135) | copy-start | bytes 3076
  11.3 19.8 %copy-start.83 = (f32[1,1,256]{2,1,0:T(1,128)}, f32[1,1,256]{2,1,0:T(1,128)S(1)}, u32[]{:S(2)}) copy-start(f32[1,1,256]{2,1,0:T(1,128)S(1)} %get-tuple-element.150) | copy-start | bytes 3076
  11.3 19.8 %copy-start.11 = (f32[1,1,256]{2,1,0:T(1,128)}, f32[1,1,256]{2,1,0:T(1,128)S(1)}, u32[]{:S(2)}) copy-start(f32[1,1,256]{2,1,0:T(1,128)S(1)} %get-tuple-element.163) | copy-start | bytes 3076
  11.3 19.8 %copy-start.13 = (f32[1,1,256]{2,1,0:T(1,128)}, f32[1,1,256]{2,1,0:T(1,128)S(1)}, u32[]{:S(2)}) copy-start(f32[1,1,256]{2,1,0:T(1,128)S(1)} %get-tuple-element.164) | copy-start | bytes 3076
  12.4 18.7 %copy-start.25 = (f32[1,1,256]{2,1,0:T(1,128)}, f32[1,1,256]{2,1,0:T(1,128)S(1)}, u32[]{:S(2)}) copy-start(f32[1,1,256]{2,1,0:T(1,128)S(1)} %get-tuple-element.170) | copy-start | bytes 3076
  12.4 18.7 %copy-start.27 = (f32[1,1,256]{2,1,0:T(1,128)}, f32[1,1,256]{2,1,0:T(1,128)S(1)}, u32[]{:S(2)}) copy-start(f32[1,1,256]{2,1,0:T(1,128)S(1)} %get-tuple-element.171) | copy-start | bytes 3076
  25.4 5.2 %collective-permute-start.3 = (bf16[3,38,256]{2,1,0:T(8,128)(2,1)S(1)}, bf16[3,38,256]{2,1,0:T(8,128)(2,1)S(1)}, u32[]{:S(2)}, u32[]{:S(2)}) collective-permute-start(bf16[3,38,256]{2,1,0:T(8,128)(2,1)S(1)} %reverse_select_fusion.1), channel_id=1, source_target_pairs={{0,16},{1,2},{2,1},{3,19},{4,20},{5,6},{6,5},{7,23},{8,24},{9,10},... | collective-permute-start | bytes 175112 | tf_op jit(solution)/shard_map/ppermute | solution.py:22
  25.5 5.1 %collective-permute-start.2 = (bf16[3,38,256]{2,1,0:T(8,128)(2,1)S(1)}, bf16[3,38,256]{2,1,0:T(8,128)(2,1)S(1)}, u32[]{:S(2)}, u32[]{:S(2)}) collective-permute-start(bf16[3,38,256]{2,1,0:T(8,128)(2,1)S(1)} %get-tuple-element.100), channel_id=1, source_target_pairs={{0,1},{1,0},{2,3},{3,2},{4,5},{5,4},{6,7},{7,6},{8,9},{9,8},{10,11... | collective-permute-start | bytes 175112 | tf_op jit(solution)/shard_map/ppermute | solution.py:22
  65.7 6.5 %collective-permute-start.4 = (bf16[32,3,256]{2,1,0:T(4,128)(2,1)S(1)}, bf16[32,3,256]{2,1,0:T(4,128)(2,1)S(1)}, u32[]{:S(2)}, u32[]{:S(2)}) collective-permute-start(bf16[32,3,256]{2,1,0:T(4,128)(2,1)S(1)} %get-tuple-element.116), channel_id=1, source_target_pairs={{0,4},{1,5},{2,6},{3,7},{4,0},{5,1},{6,2},{7,3},{8,12},{9,13},{10,... | collective-permute-start | bytes 147464 | tf_op jit(solution)/shard_map/ppermute | solution.py:22
  65.8 7.0 %collective-permute-start.5 = (bf16[32,3,256]{2,1,0:T(4,128)(2,1)S(1)}, bf16[32,3,256]{2,1,0:T(4,128)(2,1)S(1)}, u32[]{:S(2)}, u32[]{:S(2)}) collective-permute-start(bf16[32,3,256]{2,1,0:T(4,128)(2,1)S(1)} %get-tuple-element.115), channel_id=1, source_target_pairs={{0,28},{1,29},{2,30},{3,31},{4,8},{5,9},{6,10},{7,11},{8,4},{9,5},... | collective-permute-start | bytes 147464 | tf_op jit(solution)/shard_map/ppermute | solution.py:22
  73.0 4.8 %collective-permute-start.7 = (bf16[3,38,256]{2,1,0:T(8,128)(2,1)S(1)}, bf16[3,38,256]{2,1,0:T(8,128)(2,1)S(1)}, u32[]{:S(2)}, u32[]{:S(2)}) collective-permute-start(bf16[3,38,256]{2,1,0:T(8,128)(2,1)S(1)} %broadcast_select_fusion.18), channel_id=1, source_target_pairs={{0,1},{1,0},{2,3},{3,2},{4,5},{5,4},{6,7},{7,6},{8,9},{9,8},{10,11... | collective-permute-start | bytes 175112 | tf_op jit(solution)/shard_map/ppermute | solution.py:22
  73.1 5.7 %collective-permute-start.6 = (bf16[3,38,256]{2,1,0:T(8,128)(2,1)S(1)}, bf16[3,38,256]{2,1,0:T(8,128)(2,1)}, u32[]{:S(2)}, u32[]{:S(2)}) collective-permute-start(bf16[3,38,256]{2,1,0:T(8,128)(2,1)S(1)} %reverse_select_fusion), channel_id=1, source_target_pairs={{0,16},{1,2},{2,1},{3,19},{4,20},{5,6},{6,5},{7,23},{8,24},{9,10},... | collective-permute-start | bytes 175112 | tf_op jit(solution)/shard_map/ppermute | solution.py:22
  94.4 2.0 %collective-permute-start.8 = (bf16[1088,256]{1,0:T(8,128)(2,1)S(1)}, bf16[1088,256]{1,0:T(8,128)(2,1)S(1)}, u32[]{:S(2)}, u32[]{:S(2)}) collective-permute-start(bf16[1088,256]{1,0:T(8,128)(2,1)S(1)} %select_convert_fusion), channel_id=1, source_target_pairs={{0,1},{1,0},{2,3},{3,2},{4,5},{5,4},{6,7},{7,6},{8,9},{9,8},{10,11... | collective-permute-start | bytes 1671176 | tf_op jit(solution)/shard_map/ppermute | solution.py:22
  99.9 6.6 %collective-permute-start.9 = (bf16[544,256]{1,0:T(8,128)(2,1)S(1)}, bf16[544,256]{1,0:T(8,128)(2,1)S(1)}, u32[]{:S(2)}, u32[]{:S(2)}) collective-permute-start(bf16[544,256]{1,0:T(8,128)(2,1)S(1)} %dynamic-slice_convert_fusion), channel_id=1, source_target_pairs={{0,4},{1,3},{2,6},{3,1},{4,0},{5,7},{6,2},{7,5},{8,12},{9,11},{10,... | collective-permute-start | bytes 835592 | tf_op jit(solution)/shard_map/ppermute | solution.py:22
  107.7 5.1 %collective-permute-start.10 = (bf16[272,256]{1,0:T(8,128)(2,1)S(1)}, bf16[272,256]{1,0:T(8,128)(2,1)S(1)}, u32[]{:S(2)}, u32[]{:S(2)}) collective-permute-start(bf16[272,256]{1,0:T(8,128)(2,1)S(1)} %dynamic-slice_convert_fusion.1), channel_id=1, source_target_pairs={{0,2},{1,5},{2,0},{3,7},{4,6},{5,1},{6,4},{7,3},{8,10},{9,13},{10,... | collective-permute-start | bytes 417800 | tf_op jit(solution)/shard_map/ppermute | solution.py:22
  112.9 5.5 %collective-permute-start.11 = (bf16[272,256]{1,0:T(8,128)(2,1)S(1)}, bf16[272,256]{1,0:T(8,128)(2,1)S(1)}, u32[]{:S(2)}, u32[]{:S(2)}) collective-permute-start(bf16[272,256]{1,0:T(8,128)(2,1)S(1)} %add_convert_fusion.3), channel_id=1, source_target_pairs={{0,8},{1,17},{2,10},{3,19},{4,12},{5,21},{6,14},{7,23},{8,0},{9,25... | collective-permute-start | bytes 417800 | tf_op jit(solution)/shard_map/ppermute | solution.py:22
  118.4 7.5 %collective-permute-start.12 = (bf16[272,256]{1,0:T(8,128)(2,1)S(1)}, bf16[272,256]{1,0:T(8,128)(2,1)S(1)}, u32[]{:S(2)}, u32[]{:S(2)}) collective-permute-start(bf16[272,256]{1,0:T(8,128)(2,1)S(1)} %add_convert_fusion.2), channel_id=1, source_target_pairs={{0,16},{1,9},{2,18},{3,11},{4,20},{5,13},{6,22},{7,15},{8,24},{9,1... | collective-permute-start | bytes 417800 | tf_op jit(solution)/shard_map/ppermute | solution.py:22
  126.0 6.6 %collective-permute-start.13 = (bf16[272,256]{1,0:T(8,128)(2,1)S(1)}, bf16[272,256]{1,0:T(8,128)(2,1)S(1)}, u32[]{:S(2)}, u32[]{:S(2)}) collective-permute-start(bf16[272,256]{1,0:T(8,128)(2,1)S(1)} %add_convert_fusion.1), channel_id=1, source_target_pairs={{0,2},{1,5},{2,0},{3,7},{4,6},{5,1},{6,4},{7,3},{8,10},{9,13},{10,... | collective-permute-start | bytes 417800 | tf_op jit(solution)/shard_map/ppermute | solution.py:22
  132.6 6.6 %collective-permute-start.14 = (bf16[544,256]{1,0:T(8,128)(2,1)S(1)}, bf16[544,256]{1,0:T(8,128)(2,1)S(1)}, u32[]{:S(2)}, u32[]{:S(2)}) collective-permute-start(bf16[544,256]{1,0:T(8,128)(2,1)S(1)} %pad_maximum_fusion.8), channel_id=1, source_target_pairs={{0,4},{1,3},{2,6},{3,1},{4,0},{5,7},{6,2},{7,5},{8,12},{9,11},{10,... | collective-permute-start | bytes 835592 | tf_op jit(solution)/shard_map/ppermute | solution.py:22
  139.4 3.2 %collective-permute-start.15 = (bf16[1088,256]{1,0:T(8,128)(2,1)S(1)}, bf16[1088,256]{1,0:T(8,128)(2,1)S(1)}, u32[]{:S(2)}, u32[]{:S(2)}) collective-permute-start(bf16[1088,256]{1,0:T(8,128)(2,1)S(1)} %pad_maximum_fusion.3), channel_id=1, source_target_pairs={{0,1},{1,0},{2,3},{3,2},{4,5},{5,4},{6,7},{7,6},{8,9},{9,8},{10,11... | collective-permute-start | bytes 1671176 | tf_op jit(solution)/shard_map/ppermute | solution.py:22
  (126 other events, 633.9 us)

commit v2 on v1

v2 whole, which is shorter than its diff:
```python
import functools
import math

import jax
import jax.numpy as jnp
from jax import lax
from jax.experimental import pallas as pl
from jax.experimental.pallas import tpu as pltpu
from jax.sharding import PartitionSpec as P

EPS = 1e-06


def flat_pairs(target):
    lons, lats = lax.axis_size("lon"), lax.axis_size("lat")
    pairs = []
    for lon in range(lons):
        for lat in range(lats):
            to_lon, to_lat = target(lon, lat)
            pairs.append((lon * lats + lat, to_lon * lats + to_lat))
    return pairs


def send(value, target):
    return lax.ppermute(value, ("lon", "lat"), flat_pairs(target))


def lon_margins(field):
    lons = lax.axis_size("lon")
    odd = lax.axis_index("lon") % 2 == 1
    first, last = field[:, :3], field[:, -3:]
    inner = send(jnp.where(odd, first, last), lambda lon, lat: (lon ^ 1, lat))
    outer = send(
        jnp.where(odd, last, first),
        lambda lon, lat: ((lon + 1) % lons if lon % 2 else (lon - 1) % lons, lat),
    )
    west = jnp.where(odd, inner, outer)
    east = jnp.where(odd, outer, inner)
    return jnp.concatenate([west, field, east], axis=1)


def lat_margins(wide):
    lons, lats = lax.axis_size("lon"), lax.axis_size("lat")
    lat = lax.axis_index("lat")
    odd = lat % 2 == 1
    pole = (lat == 0) | (lat == lats - 1)
    first, last = wide[:3], wide[-3:]

    def beyond(lon, lat):
        if lat == 0 or lat == lats - 1:
            return ((lon + lons // 2) % lons, lat)
        return (lon, lat + 1 if lat % 2 else lat - 1)

    outgoing = jnp.where(odd, last, first)
    outgoing = jnp.where(pole, outgoing[::-1], outgoing)
    far = send(outgoing, beyond)
    near = send(jnp.where(odd, first, last), lambda lon, lat: (lon, lat ^ 1))
    north = jnp.where(odd, near, far)
    south = jnp.where(odd, far, near)
    return north, south


def axis_bits():
    lon_bits = [("lon", bit) for bit in range((lax.axis_size("lon") - 1).bit_length())]
    lat_bits = [("lat", bit) for bit in range(1, (lax.axis_size("lat") - 1).bit_length())]
    steps = []
    while lon_bits or lat_bits:
        if lon_bits:
            steps.append(lon_bits.pop(0))
        if lat_bits:
            steps.append(lat_bits.pop(0))
    return steps


def flip(place, step):
    lon, lat = place
    axis, bit = step
    return (lon ^ (1 << bit), lat) if axis == "lon" else (lon, lat ^ (1 << bit))


def summed(keep, give):
    core = lax.axis_index("lat") % 2
    steps = axis_bits()
    other = list(steps)
    for at in range(0, len(steps) - 1, 2):
        other[at], other[at + 1] = other[at + 1], other[at]

    def exchange(value, at):
        return send(value, lambda lon, lat: flip((lon, lat), (other if lat % 2 else steps)[at]))

    def bit_of(at):
        def bit(step):
            return lax.shift_right_logical(lax.axis_index(step[0]), step[1]) & 1

        return jnp.where(core == 1, bit(other[at]), bit(steps[at]))

    total = keep + send(give, lambda lon, lat: (lon, lat ^ 1)).astype(jnp.float32)
    halvings = min(2, len(steps))
    for at in range(halvings):
        half = total.shape[0] // 2
        bit = bit_of(at)
        outgoing = lax.dynamic_slice_in_dim(total, (1 - bit) * half, half, 0)
        mine = lax.dynamic_slice_in_dim(total, bit * half, half, 0)
        total = mine + exchange(outgoing.astype(jnp.bfloat16), at).astype(jnp.float32)
    sent = total.astype(jnp.bfloat16)
    for at in range(halvings, len(steps)):
        got = exchange(sent, at)
        sent = (sent.astype(jnp.float32) + got.astype(jnp.float32)).astype(jnp.bfloat16)
    for at in reversed(range(halvings)):
        got = exchange(sent, at)
        low = bit_of(at) == 0
        sent = jnp.concatenate([jnp.where(low, sent, got), jnp.where(low, got, sent)], axis=0)
    got = send(sent, lambda lon, lat: (lon, lat ^ 1))
    return jnp.where(core == 0, sent, got), jnp.where(core == 0, got, sent)


def gelu_parts(values):
    normal_cdf = 0.5 * (1.0 + jax.scipy.special.erf(values * (1.0 / math.sqrt(2.0))))
    density = jnp.exp(-0.5 * values * values) * (1.0 / math.sqrt(2.0 * math.pi))
    return (values * normal_cdf, normal_cdf + values * density)


LANES = 128
SUBLANES = 8


def slot_rows(ref, lane, row, start, count):
    return ref[lane, row, pl.ds(start, SUBLANES, stride=count), :]


def spread_weights(weight_ref, spread_ref):
    for lane in range(spread_ref.shape[0]):
        for tap in range(49):
            row = weight_ref[tap : tap + 1, lane * LANES : (lane + 1) * LANES]
            spread_ref[lane, tap] = jnp.broadcast_to(row.astype(jnp.float32), (SUBLANES, LANES))


def split_lanes(source_ref, wide_ref):
    rows = source_ref.shape[0]

    def body(row, carry):
        for lane in range(wide_ref.shape[0]):
            wide_ref[lane, row] = source_ref[row, :, lane * LANES : (lane + 1) * LANES].astype(
                jnp.float32
            )
        return carry

    lax.fori_loop(0, rows, body, 0)


def main_kernel(
    scale_factor,
    padded_ref,
    fields_ref,
    cot_ref,
    dw_ref,
    chan_ref,
    b_expand_ref,
    w_expand_ref,
    w_project_ref,
    out_ref,
    dconv_ref,
    expand_ref,
    project_ref,
    small_ref,
    wide_ref,
    spread_ref,
    conv_ref,
    dwide_ref,
):
    tiles = wide_ref.shape[0]
    rows = conv_ref.shape[1]
    cols = conv_ref.shape[2]
    chans = tiles * LANES
    slots = cols // SUBLANES
    hidden_units = w_expand_ref.shape[1]
    pieces = hidden_units // chans
    block_rows = 8
    blocks = rows // block_rows
    cells = block_rows * cols
    spread_weights(dw_ref, spread_ref)
    split_lanes(padded_ref, wide_ref)

    def conv_block(at, carry):
        lane, start = at // (rows // 4), (at % (rows // 4)) * 4
        totals = [[jnp.zeros((SUBLANES, LANES), jnp.float32)] * slots for unused in range(4)]
        for row in range(10):
            loaded = [
                slot_rows(wide_ref, lane, start + row, place, slots) for place in range(slots + 6)
            ]
            for row_off in range(7):
                to = row - row_off
                if 0 <= to < 4:
                    for col_off in range(7):
                        weight = spread_ref[lane, row_off * 7 + col_off]
                        for slot in range(slots):
                            totals[to][slot] = totals[to][slot] + weight * loaded[slot + col_off]
        for to in range(4):
            for slot in range(slots):
                conv_ref[lane, start + to, pl.ds(slot, SUBLANES, stride=slots), :] = totals[to][slot]
        return carry

    lax.fori_loop(0, tiles * (rows // 4), conv_block, 0)

    expand_ref[...] = jnp.zeros_like(expand_ref)
    project_ref[...] = jnp.zeros_like(project_ref)
    small_ref[...] = jnp.zeros_like(small_ref)
    dw_bias = chan_ref[0:1].astype(jnp.float32)
    gain = chan_ref[1:2].astype(jnp.float32)
    offset = chan_ref[2:3].astype(jnp.float32)
    b_project = chan_ref[3:4].astype(jnp.float32)

    def mlp_block(block, carry):
        row = block * block_rows
        conv = jnp.concatenate(
            [conv_ref[lane, pl.ds(row, block_rows)].reshape(cells, LANES) for lane in range(tiles)],
            axis=1,
        )
        conv = conv + dw_bias
        removed = conv - jnp.mean(conv, axis=-1, keepdims=True)
        deviation = lax.rsqrt(jnp.mean(removed * removed, axis=-1, keepdims=True) + EPS)
        xhat = removed * deviation
        normed = (xhat * gain + offset).astype(jnp.bfloat16)
        cot = cot_ref[pl.ds(block * cells, cells), :]
        branch = jnp.zeros((cells, chans), jnp.float32)
        d_normed = jnp.zeros((cells, chans), jnp.float32)
        for piece in range(pieces):
            part = slice(piece * chans, (piece + 1) * chans)
            w_in = w_expand_ref[:, part]
            w_out = w_project_ref[part, :]
            pre = jnp.dot(normed, w_in, preferred_element_type=jnp.float32)
            pre = pre + b_expand_ref[0:1, part].astype(jnp.float32)
            active, slope = gelu_parts(pre)
            hidden = active.astype(jnp.bfloat16)
            branch = branch + jnp.dot(hidden, w_out, preferred_element_type=jnp.float32)
            d_hidden = contract(cot, w_out, 1, 1)
            d_pre_wide = d_hidden * slope
            d_pre = d_pre_wide.astype(jnp.bfloat16)
            project_ref[part, :] += contract(hidden, cot, 0, 0)
            expand_ref[part, :] += contract(normed, d_pre, 0, 0)
            small_ref[53 + piece : 54 + piece] += jnp.sum(
                d_pre.astype(jnp.float32), axis=0, keepdims=True
            )
            d_normed = d_normed + contract(d_pre, w_in, 1, 1)
        plain = fields_ref[pl.ds(block * cells, cells), :].astype(jnp.float32)
        out_ref[pl.ds(block * cells, cells), :] = (plain + (branch + b_project)).astype(jnp.bfloat16)
        small_ref[50:51] += jnp.sum(d_normed * xhat, axis=0, keepdims=True)
        small_ref[51:52] += jnp.sum(d_normed, axis=0, keepdims=True)
        small_ref[52:53] += jnp.sum(cot.astype(jnp.float32), axis=0, keepdims=True)
        scaled = d_normed * gain
        d_conv = deviation * (
            scaled
            - jnp.mean(scaled, axis=-1, keepdims=True)
            - xhat * jnp.mean(scaled * xhat, axis=-1, keepdims=True)
        )
        d_conv = d_conv.astype(jnp.bfloat16)
        dconv_ref[pl.ds(block * cells, cells), :] = d_conv
        d_conv = d_conv.astype(jnp.float32)
        small_ref[49:50] += jnp.sum(d_conv, axis=0, keepdims=True)
        for lane in range(tiles):
            dwide_ref[lane, pl.ds(row, block_rows)] = d_conv[
                :, lane * LANES : (lane + 1) * LANES
            ].reshape(block_rows, cols, LANES)
        return carry

    lax.fori_loop(0, blocks, mlp_block, 0)

    for lane in range(tiles):
        for row_off in range(7):

            def kernel_row(row, totals):
                grads = [slot_rows(dwide_ref, lane, row, slot, slots) for slot in range(slots)]
                loaded = [
                    slot_rows(wide_ref, lane, row + row_off, place, slots)
                    for place in range(slots + 6)
                ]
                return tuple(
                    totals[col_off] + sum(grads[slot] * loaded[slot + col_off] for slot in range(slots))
                    for col_off in range(7)
                )

            zeros = tuple(jnp.zeros((SUBLANES, LANES), jnp.float32) for unused in range(7))
            totals = lax.fori_loop(0, rows, kernel_row, zeros, unroll=4)
            for col_off in range(7):
                tap = row_off * 7 + col_off
                small_ref[tap : tap + 1, lane * LANES : (lane + 1) * LANES] = jnp.sum(
                    totals[col_off], axis=0, keepdims=True
                )
    small_ref[...] = small_ref[...] * scale_factor
    expand_ref[...] = expand_ref[...] * scale_factor
    project_ref[...] = project_ref[...] * scale_factor


def contract(left, right, left_dim, right_dim):
    return lax.dot_general(
        left,
        right,
        (((left_dim,), (right_dim,)), ((), ())),
        preferred_element_type=jnp.float32,
    )


def main_pass(
    padded, fields, cot, dw_kernel, chan_params, b_expand, w_expand, w_project, scale_factor
):
    rows, cols = padded.shape[0] - 6, fields.shape[0] // (padded.shape[0] - 6)
    chans = fields.shape[1]
    hidden_units = w_expand.shape[1]
    tiles = chans // LANES
    cells = rows * cols
    pad_cols = padded.shape[1]
    return pl.pallas_call(
        functools.partial(main_kernel, scale_factor),
        out_shape=[
            jax.ShapeDtypeStruct((cells, chans), jnp.bfloat16),
            jax.ShapeDtypeStruct((cells, chans), jnp.bfloat16),
            jax.ShapeDtypeStruct((hidden_units, chans), jnp.float32),
            jax.ShapeDtypeStruct((hidden_units, chans), jnp.float32),
            jax.ShapeDtypeStruct((64, chans), jnp.float32),
        ],
        in_specs=[pl.BlockSpec(memory_space=pltpu.VMEM)] * 8,
        out_specs=[pl.BlockSpec(memory_space=pltpu.VMEM)] * 5,
        scratch_shapes=[
            pltpu.VMEM((tiles, rows + 6, pad_cols, LANES), jnp.float32),
            pltpu.VMEM((tiles, 49, SUBLANES, LANES), jnp.float32),
            pltpu.VMEM((tiles, rows, cols, LANES), jnp.float32),
            pltpu.VMEM((tiles, rows, cols, LANES), jnp.float32),
        ],
        compiler_params=pltpu.CompilerParams(vmem_limit_bytes=48 << 20),
        cost_estimate=pl.CostEstimate(
            flops=12 * cells * chans * hidden_units,
            bytes_accessed=8 << 20,
            transcendentals=2 * cells * hidden_units,
        ),
        name="block_main",
    )(padded, fields, cot, dw_kernel, chan_params, b_expand, w_expand, w_project)


def adjoint_kernel(
    poles_ref,
    padded_ref,
    cot_ref,
    dw_ref,
    out_ref,
    wide_ref,
    spread_ref,
    edge_ref,
    sum_ref,
):
    tiles = wide_ref.shape[0]
    rows = sum_ref.shape[1]
    cols = sum_ref.shape[2]
    slots = cols // SUBLANES
    spread_weights(dw_ref, spread_ref)
    split_lanes(padded_ref, wide_ref)
    for side in range(2):
        at_pole = poles_ref[side] == 1
        for lane in range(tiles):
            for row_off in range(3):
                near = row_off if side == 0 else 6 - row_off
                for col_off in range(7):
                    plain = spread_ref[lane, (6 - near) * 7 + col_off]
                    turned = spread_ref[lane, near * 7 + col_off]
                    edge_ref[side, lane, row_off * 7 + col_off] = jnp.where(at_pole, turned, plain)

    def block_of(lane, start, first, last):
        totals = [[jnp.zeros((SUBLANES, LANES), jnp.float32)] * slots for unused in range(4)]
        for row in range(10):
            loaded = [
                slot_rows(wide_ref, lane, start + row, place, slots) for place in range(slots + 6)
            ]
            for row_off in range(7):
                to = row - row_off
                if 0 <= to < 4:
                    for col_off in range(7):
                        tap = 6 - col_off
                        if first and row < 3:
                            weight = edge_ref[0, lane, row_off * 7 + tap]
                        elif last and row >= 7:
                            weight = edge_ref[1, lane, (6 - row_off) * 7 + tap]
                        else:
                            weight = spread_ref[lane, (6 - row_off) * 7 + tap]
                        for slot in range(slots):
                            totals[to][slot] = totals[to][slot] + weight * loaded[slot + col_off]
        for to in range(4):
            for slot in range(slots):
                sum_ref[lane, start + to, pl.ds(slot, SUBLANES, stride=slots), :] = totals[to][slot]

    inner = rows // 4 - 2

    def inner_block(at, carry):
        block_of(at // inner, (1 + at % inner) * 4, False, False)
        return carry

    def edge_block(lane, carry):
        block_of(lane, 0, True, False)
        block_of(lane, rows - 4, False, True)
        return carry

    lax.fori_loop(0, tiles * inner, inner_block, 0)
    lax.fori_loop(0, tiles, edge_block, 0)

    def finish(row, carry):
        total = jnp.concatenate([sum_ref[lane, row] for lane in range(tiles)], axis=1)
        out_ref[row] = (cot_ref[row].astype(jnp.float32) + total).astype(jnp.bfloat16)
        return carry

    lax.fori_loop(0, rows, finish, 0)


def adjoint_pass(padded, cot, dw_kernel, poles):
    rows, cols, chans = cot.shape
    tiles = chans // LANES
    return pl.pallas_call(
        adjoint_kernel,
        out_shape=jax.ShapeDtypeStruct(cot.shape, jnp.bfloat16),
        in_specs=[pl.BlockSpec(memory_space=pltpu.SMEM)]
        + [pl.BlockSpec(memory_space=pltpu.VMEM)] * 3,
        out_specs=pl.BlockSpec(memory_space=pltpu.VMEM),
        scratch_shapes=[
            pltpu.VMEM((tiles, rows + 6, padded.shape[1], LANES), jnp.float32),
            pltpu.VMEM((tiles, 49, SUBLANES, LANES), jnp.float32),
            pltpu.VMEM((2, tiles, 21, SUBLANES, LANES), jnp.float32),
            pltpu.VMEM((tiles, rows, cols, LANES), jnp.float32),
        ],
        compiler_params=pltpu.CompilerParams(vmem_limit_bytes=32 << 20),
        cost_estimate=pl.CostEstimate(
            flops=98 * rows * cols * chans, bytes_accessed=3 << 20, transcendentals=0
        ),
        name="block_adjoint",
    )(poles, padded, cot, dw_kernel)


def sphere_pad(field):
    wide = lon_margins(field)
    top, bottom = lat_margins(wide)
    return jnp.concatenate([top, wide, bottom], axis=0)


def local(
    fields,
    cotangent,
    dw_kernel,
    dw_bias,
    norm_gain,
    layer_norm_offset,
    w_expand,
    b_expand,
    w_project,
    b_project,
):
    rows = fields.shape[0]
    cols = fields.shape[1]
    chans = fields.shape[2]
    scale_factor = 1.0 / math.sqrt(rows * cols * lax.axis_size("lat") * lax.axis_size("lon"))
    lat = lax.axis_index("lat")
    poles = jnp.stack([lat == 0, lat == lax.axis_size("lat") - 1]).astype(jnp.int32)
    taps = dw_kernel.reshape(49, chans)
    chan_params = jnp.stack([dw_bias, norm_gain, layer_norm_offset, b_project])
    flat_cot = cotangent.reshape(-1, chans)
    block_out, conv_gradient, grad_exp, grad_proj, small = main_pass(
        sphere_pad(fields),
        fields.reshape(-1, chans),
        flat_cot,
        taps,
        chan_params,
        b_expand.reshape(1, -1),
        w_expand,
        w_project,
        scale_factor,
    )
    block_out = block_out.reshape(fields.shape)
    grad_fields = adjoint_pass(
        sphere_pad(conv_gradient.reshape(fields.shape)), cotangent, taps, poles
    )
    hidden_units = w_expand.shape[1]
    pieces = hidden_units // chans
    first = jnp.concatenate([grad_exp, small], axis=0)
    second = jnp.concatenate([grad_proj, jnp.zeros_like(small)], axis=0)
    core = lax.axis_index("lat") % 2
    keep = jnp.where(core == 0, first, second)
    give = jnp.where(core == 0, second, first).astype(jnp.bfloat16)
    first, second = summed(keep, give)
    first = first.astype(jnp.float32)
    second = second.astype(jnp.float32)
    sum_exp = first[:hidden_units].reshape(pieces, chans, chans).swapaxes(0, 1).reshape(chans, -1)
    sum_proj = second[:hidden_units]
    rest = first[hidden_units:]
    sum_kern = rest[:49].reshape(7, 7, chans)
    sum_dwb, sum_gn, sum_sh, sum_bproj = rest[49], rest[50], rest[51], rest[52]
    sum_bexp = rest[53 : 53 + pieces].reshape(-1)
    return (
        block_out,
        grad_fields,
        sum_kern,
        sum_dwb,
        sum_gn,
        sum_sh,
        sum_exp,
        sum_bexp,
        sum_proj,
        sum_bproj,
    )


def solution(mesh):
    placed = (P("lat", "lon", None), P("lat", "lon", None), P(), P(), P(), P(), P(), P(), P(), P())
    return jax.shard_map(
        local,
        mesh=mesh,
        in_specs=placed,
        out_specs=(
            P("lat", "lon", None),
            P("lat", "lon", None),
            P(),
            P(),
            P(),
            P(),
            P(),
            P(),
            P(),
            P(),
        ),
        check_vma=False,
    )
```

time: 148 us -> 97 us (0.66)
  other arithmetic: 60.8 us -> 8.32 us
  Pallas kernels: 0 us -> 22.6 us
  matrix products: 15.2 us -> 0 us
  local copies, waits for them, and re-layouts: 14.5 us -> 8.64 us
  waiting for transfers between devices: 35.9 us -> 41.7 us
  starting transfers between devices: 17.5 us -> 14.3 us
  between operations: 3.08 us -> 1 us
    reduce_sum x8 -> x0, other arithmetic: 22.6 us -> none  [the longest x1 9.54 us: local(): mean_removed = conv - jnp.mean(conv, axis=-1, keepdims=True)]
    pallas_call x0 -> x2, Pallas kernels: none -> 22.6 us  [the longest x1 16.7 us: main_pass(): pl.pallas_call(functools.partial(main_kernel, scale_factor), out_shape=[j...]
    dot_general x6 -> x0, matrix products: 15.2 us -> none  [the longest x2 4.05 us: contract_rows(): lax.dot_general(left, right, (((0,), (0,)), ((), ())), preferred_element_...]
    mul x20 -> x0, other arithmetic: 13.7 us -> none  [the longest x14 10.9 us: local(): weight * fold_north[row_off:row_off + 3, col_from:col_from + cols].astype...]
    add x2 -> x0, other arithmetic: 10.1 us -> none  [the longest x1 8.82 us: local(): adjoint + weight * inner[6 - row_off:6 - row_off + rows, col_from:col_fro...]
    ppermute x16, waiting for transfers between devices: 35.9 us -> 41.7 us  [send(): return lax.ppermute(value, ('lon', 'lat'), flat_pairs(target))]
    slice x4 -> x0, local copies, waits for them, and re-layouts: 3.6 us -> none  [the longest x3 3.6 us: local(): weights[row_off, col_off]]
    ppermute x16, starting transfers between devices: 17.5 us -> 14.3 us  [send(): return lax.ppermute(value, ('lon', 'lat'), flat_pairs(target))]
  transfers between devices with their start and end apart: 16 -> 16, of which waited for: 10 -> 10; matrix products, arithmetic and copies ran while one was open for 19% -> 5% of each run, Pallas kernels for 0% -> 6%
where the time goes in v2:
time: 97 us; the launch traced here: 96.6 us
  waiting for transfers between devices  41.7 us (43%)
  Pallas kernels  22.6 us (23%)
  starting transfers between devices  14.3 us (15%)
  local copies, waits for them, and re-layouts  8.64 us (9%)
  other arithmetic  8.32 us (9%)
  between operations  1 us (1%)
    ppermute x16, waiting for transfers between devices, send(): return lax.ppermute(value, ('lon', 'lat'), flat_pairs(target))  41.7 us
    pallas_call x1, Pallas kernels, main_pass(): pl.pallas_call(functools.partial(main_kernel, scale_factor), out_shape=[j...  16.7 us
    ppermute x16, starting transfers between devices, send(): return lax.ppermute(value, ('lon', 'lat'), flat_pairs(target))  14.3 us
    pallas_call x1, Pallas kernels, adjoint_pass(): pl.pallas_call(adjoint_kernel, out_shape=jax.ShapeDtypeStruct(cot.shape,...  5.87 us
    another operation x4, local copies, waits for them, and re-layouts, local(): chan_params = jnp.stack([dw_bias, norm_gain, layer_norm_offset, b_project])  2.63 us
    unnamed x17, local copies, waits for them, and re-layouts  2.04 us
  transfers between devices with their start and end apart: 16, of which 10 were waited for; matrix products, arithmetic and copies ran while one was open for 5% of the time, Pallas kernels for 6%

profile of v2, /device:TPU:0, one launch (start us, length us, event | category | flops | bytes accessed | tf_op | source)
XLA Modules:
  0.0 96.6 jit_solution(1375411754493948829)
XLA Ops:
  0.7 1.1 %broadcast_select_fusion.11 = (bf16[32,3,256]{2,1,0:T(4,128)(2,1)S(1)}, bf16[32,3,256]{2,1,0:T(4,128)(2,1)S(1)}) fusion(pred[]{:T(512)S(6)} %eq.42, bf16[32,32,256]{2,1,0:T(8,128)(2,1)} %param.10), kind=kLoop, calls=%fused_computation.31 | loop fusion | flops 49152 | bytes 196609 | tf_op jit(solution)/shard_map/jit(_where)/select_n | solution.py:32
  1.8 3.0 %collective-permute-start = (bf16[32,3,256]{2,1,0:T(4,128)(2,1)S(1)}, bf16[32,3,256]{2,1,0:T(4,128)(2,1)S(1)}, u32[]{:S(2)}, u32[]{:S(2)}) collective-permute-start(bf16[32,3,256]{2,1,0:T(4,128)(2,1)S(1)} %get-tuple-element.34), channel_id=1, source_target_pairs={{0,4},{1,5},{2,6},{3,7},{4,0},{5,1},{6,2},{7,3},{8,12},{9,13},{10,... | collective-permute-start | bytes 147464 | tf_op jit(solution)/shard_map/ppermute | solution.py:25
  4.8 3.6 %collective-permute-start.1 = (bf16[32,3,256]{2,1,0:T(4,128)(2,1)S(1)}, bf16[32,3,256]{2,1,0:T(4,128)(2,1)S(1)}, u32[]{:S(2)}, u32[]{:S(2)}) collective-permute-start(bf16[32,3,256]{2,1,0:T(4,128)(2,1)S(1)} %get-tuple-element.35), channel_id=1, source_target_pairs={{0,28},{1,29},{2,30},{3,31},{4,8},{5,9},{6,10},{7,11},{8,4},{9,5},... | collective-permute-start | bytes 147464 | tf_op jit(solution)/shard_map/ppermute | solution.py:25
  8.3 0.7 stack.24
  9.0 0.7 stack.25
  9.7 0.7 stack.26
  10.3 0.7 stack.27
  11.0 0.7 reshape.53.b_expand_ref
  11.7 0.8 reshape.52.dw_ref
  12.5 0.9 broadcast_select_fusion.19
  13.6 1.6 %collective-permute-start.2 = (bf16[3,38,256]{2,1,0:T(8,128)(2,1)S(1)}, bf16[3,38,256]{2,1,0:T(8,128)(2,1)S(1)}, u32[]{:S(2)}, u32[]{:S(2)}) collective-permute-start(bf16[3,38,256]{2,1,0:T(8,128)(2,1)S(1)} %get-tuple-element.23), channel_id=1, source_target_pairs={{0,1},{1,0},{2,3},{3,2},{4,5},{5,4},{6,7},{7,6},{8,9},{9,8},{10,11... | collective-permute-start | bytes 175112 | tf_op jit(solution)/shard_map/ppermute | solution.py:25
  15.2 3.5 %collective-permute-done.3 = bf16[3,38,256]{2,1,0:T(8,128)(2,1)S(1)} collective-permute-done((bf16[3,38,256]{2,1,0:T(8,128)(2,1)S(1)}, bf16[3,38,256]{2,1,0:T(8,128)(2,1)S(1)}, u32[]{:S(2)}, u32[]{:S(2)}) %collective-permute-start.3) | collective-permute-done | bytes 58400 | tf_op jit(solution)/shard_map/ppermute | solution.py:25
  19.1 16.7 %block_main.1 = (bf16[1024,256]{1,0:T(8,128)(2,1)}, bf16[1024,256]{1,0:T(8,128)(2,1)S(1)}, f32[1024,256]{1,0:T(8,128)S(1)}, f32[1024,256]{1,0:T(8,128)S(1)}, f32[64,256]{1,0:T(8,128)S(1)}) custom-call(bf16[38,38,256]{2,1,0:T(8,128)(2,1)S(1)} %pad_maximum_fusion.padded_ref, bf16[1024,256]{1,0:T(8,128)(2,1)S(1)} %bitcast.18, bf16[1024,256]{1,0:T(8,128)(2,1)S(1)} %bitcast.22, ...), custom_call_target="tpu_custom_call" | custom-call | flops 3221225472 | bytes 8388608 | tf_op jit(solution)/shard_map/block_main/pallas_call | solution.py:312
  36.0 1.1 %select_convert_fusion = bf16[1088,256]{1,0:T(8,128)(2,1)} fusion(f32[1088,256]{1,0:T(8,128)S(1)} %constant_dynamic-update-slice_fusion, f32[1024,256]{1,0:T(8,128)S(1)} %get-tuple-element.19, pred[]{:T(512)S(6)} %eq.45), kind=kLoop, calls=%fused_computation.1 | loop fusion | flops 278528 | bytes 2719745 | tf_op jit(solution)/shard_map/convert_element_type | solution.py:482
  37.2 2.2 %collective-permute-done.8 = bf16[1088,256]{1,0:T(8,128)(2,1)S(1)} collective-permute-done((bf16[1088,256]{1,0:T(8,128)(2,1)}, bf16[1088,256]{1,0:T(8,128)(2,1)S(1)}, u32[]{:S(2)}, u32[]{:S(2)}) %collective-permute-start.8) | collective-permute-done | bytes 557088 | tf_op jit(solution)/shard_map/ppermute | solution.py:25
  39.3 1.4 %convert_add_fusion = f32[1088,256]{1,0:T(8,128)S(1)} fusion(bf16[1088,256]{1,0:T(8,128)(2,1)S(1)} %collective-permute-done.8, f32[1088,256]{1,0:T(8,128)} %copy-done.4, f32[1024,256]{1,0:T(8,128)S(1)} %get-tuple-element.19, pred[]{:T(512)S(6)} %eq.45), kind=kLoop, calls=%fused_computation | loop fusion | flops 835584 | bytes 3833857 | tf_op jit(solution)/shard_map/add | solution.py:97
  40.7 1.0 %copy-done.6 = f32[1088,256]{1,0:T(8,128)} copy-done((f32[1088,256]{1,0:T(8,128)}, f32[1088,256]{1,0:T(8,128)S(1)}, u32[]{:S(2)}) %copy-start.6) | copy-done | bytes 1114136
  41.8 6.5 %collective-permute-done.9 = bf16[544,256]{1,0:T(8,128)(2,1)S(1)} collective-permute-done((bf16[544,256]{1,0:T(8,128)(2,1)S(1)}, bf16[544,256]{1,0:T(8,128)(2,1)S(1)}, u32[]{:S(2)}, u32[]{:S(2)}) %collective-permute-start.9) | collective-permute-done | bytes 278560 | tf_op jit(solution)/shard_map/ppermute | solution.py:25
  48.4 1.1 %convert_add_fusion.1 = f32[544,256]{1,0:T(8,128)S(1)} fusion(bf16[544,256]{1,0:T(8,128)(2,1)S(1)} %collective-permute-done.9, f32[1088,256]{1,0:T(8,128)} %copy-done.6, s32[]{:T(128)S(6)} %select_n.197), kind=kLoop, calls=%fused_computation.8 | loop fusion | flops 278528 | bytes 1392644 | tf_op jit(solution)/shard_map/add | solution.py:104
  49.6 5.0 %collective-permute-done.10 = bf16[272,256]{1,0:T(8,128)(2,1)S(1)} collective-permute-done((bf16[272,256]{1,0:T(8,128)(2,1)S(1)}, bf16[272,256]{1,0:T(8,128)(2,1)S(1)}, u32[]{:S(2)}, u32[]{:S(2)}) %collective-permute-start.10) | collective-permute-done | bytes 139296 | tf_op jit(solution)/shard_map/ppermute | solution.py:25
  54.8 5.0 %collective-permute-done.11 = bf16[272,256]{1,0:T(8,128)(2,1)S(1)} collective-permute-done((bf16[272,256]{1,0:T(8,128)(2,1)S(1)}, bf16[272,256]{1,0:T(8,128)(2,1)S(1)}, u32[]{:S(2)}, u32[]{:S(2)}) %collective-permute-start.11) | collective-permute-done | bytes 139296 | tf_op jit(solution)/shard_map/ppermute | solution.py:25
  60.2 2.1 %collective-permute-start.4 = (bf16[32,3,256]{2,1,0:T(4,128)(2,1)S(1)}, bf16[32,3,256]{2,1,0:T(4,128)(2,1)S(1)}, u32[]{:S(2)}, u32[]{:S(2)}) collective-permute-start(bf16[32,3,256]{2,1,0:T(4,128)(2,1)S(1)} %get-tuple-element.32), channel_id=1, source_target_pairs={{0,4},{1,5},{2,6},{3,7},{4,0},{5,1},{6,2},{7,3},{8,12},{9,13},{10,... | collective-permute-start | bytes 147464 | tf_op jit(solution)/shard_map/ppermute | solution.py:25
  62.2 1.7 %collective-permute-start.5 = (bf16[32,3,256]{2,1,0:T(4,128)(2,1)S(1)}, bf16[32,3,256]{2,1,0:T(4,128)(2,1)S(1)}, u32[]{:S(2)}, u32[]{:S(2)}) collective-permute-start(bf16[32,3,256]{2,1,0:T(4,128)(2,1)S(1)} %get-tuple-element.33), channel_id=1, source_target_pairs={{0,28},{1,29},{2,30},{3,31},{4,8},{5,9},{6,10},{7,11},{8,4},{9,5},... | collective-permute-start | bytes 147464 | tf_op jit(solution)/shard_map/ppermute | solution.py:25
  63.9 3.0 %collective-permute-done.12 = bf16[272,256]{1,0:T(8,128)(2,1)S(1)} collective-permute-done((bf16[272,256]{1,0:T(8,128)(2,1)S(1)}, bf16[272,256]{1,0:T(8,128)(2,1)S(1)}, u32[]{:S(2)}, u32[]{:S(2)}) %collective-permute-start.12) | collective-permute-done | bytes 139296 | tf_op jit(solution)/shard_map/ppermute | solution.py:25
  67.2 2.0 %collective-permute-done.5 = bf16[32,3,256]{2,1,0:T(4,128)(2,1)S(1)} collective-permute-done((bf16[32,3,256]{2,1,0:T(4,128)(2,1)S(1)}, bf16[32,3,256]{2,1,0:T(4,128)(2,1)S(1)}, u32[]{:S(2)}, u32[]{:S(2)}) %collective-permute-start.5) | collective-permute-done | bytes 49184 | tf_op jit(solution)/shard_map/ppermute | solution.py:25
  69.2 4.4 %collective-permute-done.13 = bf16[272,256]{1,0:T(8,128)(2,1)S(1)} collective-permute-done((bf16[272,256]{1,0:T(8,128)(2,1)S(1)}, bf16[272,256]{1,0:T(8,128)(2,1)S(1)}, u32[]{:S(2)}, u32[]{:S(2)}) %collective-permute-start.13) | collective-permute-done | bytes 139296 | tf_op jit(solution)/shard_map/ppermute | solution.py:25
  73.7 0.9 collective-permute-start.14
  74.6 5.7 %collective-permute-done.14 = bf16[544,256]{1,0:T(8,128)(2,1)S(1)} collective-permute-done((bf16[544,256]{1,0:T(8,128)(2,1)S(1)}, bf16[544,256]{1,0:T(8,128)(2,1)S(1)}, u32[]{:S(2)}, u32[]{:S(2)}) %collective-permute-start.14) | collective-permute-done | bytes 278560 | tf_op jit(solution)/shard_map/ppermute | solution.py:25
  81.2 4.5 %collective-permute-done.7 = bf16[3,38,256]{2,1,0:T(8,128)(2,1)S(1)} collective-permute-done((bf16[3,38,256]{2,1,0:T(8,128)(2,1)S(1)}, bf16[3,38,256]{2,1,0:T(8,128)(2,1)S(1)}, u32[]{:S(2)}, u32[]{:S(2)}) %collective-permute-start.7) | collective-permute-done | bytes 58400 | tf_op jit(solution)/shard_map/ppermute | solution.py:25
  86.1 5.9 %block_adjoint.1 = bf16[32,32,256]{2,1,0:T(8,128)(2,1)} custom-call(s32[2]{0:T(128)S(1)} %add_convert_fusion.3.poles_ref, bf16[38,38,256]{2,1,0:T(8,128)(2,1)S(1)} %pad_maximum_fusion.1.padded_ref, bf16[32,32,256]{2,1,0:T(8,128)(2,1)S(1)} %copy-done.1, bf16[49,256]{1,0:T(8,128)(2,1)S(1)} %reshape.52.dw_ref), custom_call_target="tpu_custom_call" | custom-call | flops 25690112 | bytes 3145728 | tf_op jit(solution)/shard_map/block_adjoint/pallas_call | solution.py:414
  93.7 1.1 %copy.21 = f32[4,32,8,256]{3,2,0,1:T(8,128)} copy(f32[4,32,8,256]{3,2,1,0:T(8,128)S(1)} %bitcast.23) | data formatting | bytes 2097152 | tf_op jit(solution)/shard_map/reshape | solution.py:486
  95.5 1.1 %fusion.2 = f32[1024,256]{1,0:T(8,128)} fusion(bf16[544,256]{1,0:T(8,128)(2,1)S(1)} %get-tuple-element.30, bf16[544,256]{1,0:T(8,128)(2,1)S(1)} %get-tuple-element.31, bf16[1088,256]{1,0:T(8,128)(2,1)S(1)} %collective-permute-done.15, pred[]{:T(512)S(6)} %eq.45), kind=kLoop, calls=%fused_computation.12 | loop fusion | flops 1572864 | bytes 2129921 | tf_op jit(solution)/shard_map/slice | solution.py:487
  (62 shorter events, 5.6 us)
Async XLA Ops:
  0.6 18.1 %copy-start = (bf16[32,32,256]{2,1,0:T(8,128)(2,1)S(1)}, bf16[32,32,256]{2,1,0:T(8,128)(2,1)}, u32[]{:S(2)}) copy-start(bf16[32,32,256]{2,1,0:T(8,128)(2,1)} %param.10) | copy-start | bytes 1572868
  1.8 10.7 %collective-permute-start = (bf16[32,3,256]{2,1,0:T(4,128)(2,1)S(1)}, bf16[32,3,256]{2,1,0:T(4,128)(2,1)S(1)}, u32[]{:S(2)}, u32[]{:S(2)}) collective-permute-start(bf16[32,3,256]{2,1,0:T(4,128)(2,1)S(1)} %get-tuple-element.34), channel_id=1, source_target_pairs={{0,4},{1,5},{2,6},{3,7},{4,0},{5,1},{6,2},{7,3},{8,12},{9,13},{10,... | collective-permute-start | bytes 147464 | tf_op jit(solution)/shard_map/ppermute | solution.py:25
  4.8 7.7 %collective-permute-start.1 = (bf16[32,3,256]{2,1,0:T(4,128)(2,1)S(1)}, bf16[32,3,256]{2,1,0:T(4,128)(2,1)S(1)}, u32[]{:S(2)}, u32[]{:S(2)}) collective-permute-start(bf16[32,3,256]{2,1,0:T(4,128)(2,1)S(1)} %get-tuple-element.35), channel_id=1, source_target_pairs={{0,28},{1,29},{2,30},{3,31},{4,8},{5,9},{6,10},{7,11},{8,4},{9,5},... | collective-permute-start | bytes 147464 | tf_op jit(solution)/shard_map/ppermute | solution.py:25
  13.4 5.7 %copy-start.1 = (bf16[32,32,256]{2,1,0:T(8,128)(2,1)S(1)}, bf16[32,32,256]{2,1,0:T(8,128)(2,1)}, u32[]{:S(2)}) copy-start(bf16[32,32,256]{2,1,0:T(8,128)(2,1)} %cot_ref.1) | copy-start | bytes 1572868
  13.4 5.7 %copy-start.2 = (bf16[256,1024]{1,0:T(8,128)(2,1)S(1)}, bf16[256,1024]{1,0:T(8,128)(2,1)}, u32[]{:S(2)}) copy-start(bf16[256,1024]{1,0:T(8,128)(2,1)} %w_expand_ref.1) | copy-start | bytes 1572868
  13.4 5.7 %copy-start.3 = (bf16[1024,256]{1,0:T(8,128)(2,1)S(1)}, bf16[1024,256]{1,0:T(8,128)(2,1)}, u32[]{:S(2)}) copy-start(bf16[1024,256]{1,0:T(8,128)(2,1)} %w_project_ref.1) | copy-start | bytes 1572868
  13.5 5.2 %collective-permute-start.3 = (bf16[3,38,256]{2,1,0:T(8,128)(2,1)S(1)}, bf16[3,38,256]{2,1,0:T(8,128)(2,1)S(1)}, u32[]{:S(2)}, u32[]{:S(2)}) collective-permute-start(bf16[3,38,256]{2,1,0:T(8,128)(2,1)S(1)} %reverse_select_fusion.1), channel_id=1, source_target_pairs={{0,16},{1,2},{2,1},{3,19},{4,20},{5,6},{6,5},{7,23},{8,24},{9,10},... | collective-permute-start | bytes 175112 | tf_op jit(solution)/shard_map/ppermute | solution.py:25
  13.6 5.1 %collective-permute-start.2 = (bf16[3,38,256]{2,1,0:T(8,128)(2,1)S(1)}, bf16[3,38,256]{2,1,0:T(8,128)(2,1)S(1)}, u32[]{:S(2)}, u32[]{:S(2)}) collective-permute-start(bf16[3,38,256]{2,1,0:T(8,128)(2,1)S(1)} %get-tuple-element.23), channel_id=1, source_target_pairs={{0,1},{1,0},{2,3},{3,2},{4,5},{5,4},{6,7},{7,6},{8,9},{9,8},{10,11... | collective-permute-start | bytes 175112 | tf_op jit(solution)/shard_map/ppermute | solution.py:25
  36.0 1.2 %copy-start.4 = (f32[1088,256]{1,0:T(8,128)}, f32[1088,256]{1,0:T(8,128)S(1)}, u32[]{:S(2)}) copy-start(f32[1088,256]{1,0:T(8,128)S(1)} %constant_dynamic-update-slice_fusion) | copy-start | bytes 3342340
  37.2 2.2 %collective-permute-start.8 = (bf16[1088,256]{1,0:T(8,128)(2,1)}, bf16[1088,256]{1,0:T(8,128)(2,1)S(1)}, u32[]{:S(2)}, u32[]{:S(2)}) collective-permute-start(bf16[1088,256]{1,0:T(8,128)(2,1)} %select_convert_fusion), channel_id=1, source_target_pairs={{0,1},{1,0},{2,3},{3,2},{4,5},{5,4},{6,7},{7,6},{8,9},{9,8},{10,11... | collective-permute-start | bytes 1671176 | tf_op jit(solution)/shard_map/ppermute | solution.py:25
  40.7 1.0 %copy-start.6 = (f32[1088,256]{1,0:T(8,128)}, f32[1088,256]{1,0:T(8,128)S(1)}, u32[]{:S(2)}) copy-start(f32[1088,256]{1,0:T(8,128)S(1)} %convert_add_fusion) | copy-start | bytes 3342340
  41.7 6.6 %collective-permute-start.9 = (bf16[544,256]{1,0:T(8,128)(2,1)S(1)}, bf16[544,256]{1,0:T(8,128)(2,1)S(1)}, u32[]{:S(2)}, u32[]{:S(2)}) collective-permute-start(bf16[544,256]{1,0:T(8,128)(2,1)S(1)} %dynamic-slice_convert_fusion), channel_id=1, source_target_pairs={{0,4},{1,3},{2,6},{3,1},{4,0},{5,7},{6,2},{7,5},{8,12},{9,11},{10,... | collective-permute-start | bytes 835592 | tf_op jit(solution)/shard_map/ppermute | solution.py:25
  49.5 5.1 %collective-permute-start.10 = (bf16[272,256]{1,0:T(8,128)(2,1)S(1)}, bf16[272,256]{1,0:T(8,128)(2,1)S(1)}, u32[]{:S(2)}, u32[]{:S(2)}) collective-permute-start(bf16[272,256]{1,0:T(8,128)(2,1)S(1)} %dynamic-slice_convert_fusion.1), channel_id=1, source_target_pairs={{0,2},{1,5},{2,0},{3,7},{4,6},{5,1},{6,4},{7,3},{8,10},{9,13},{10,... | collective-permute-start | bytes 417800 | tf_op jit(solution)/shard_map/ppermute | solution.py:25
  54.7 5.1 %collective-permute-start.11 = (bf16[272,256]{1,0:T(8,128)(2,1)S(1)}, bf16[272,256]{1,0:T(8,128)(2,1)S(1)}, u32[]{:S(2)}, u32[]{:S(2)}) collective-permute-start(bf16[272,256]{1,0:T(8,128)(2,1)S(1)} %add_convert_fusion.2), channel_id=1, source_target_pairs={{0,8},{1,17},{2,10},{3,19},{4,12},{5,21},{6,14},{7,23},{8,0},{9,25... | collective-permute-start | bytes 417800 | tf_op jit(solution)/shard_map/ppermute | solution.py:25
  59.8 7.1 %collective-permute-start.12 = (bf16[272,256]{1,0:T(8,128)(2,1)S(1)}, bf16[272,256]{1,0:T(8,128)(2,1)S(1)}, u32[]{:S(2)}, u32[]{:S(2)}) collective-permute-start(bf16[272,256]{1,0:T(8,128)(2,1)S(1)} %add_convert_fusion.1), channel_id=1, source_target_pairs={{0,16},{1,9},{2,18},{3,11},{4,20},{5,13},{6,22},{7,15},{8,24},{9,1... | collective-permute-start | bytes 417800 | tf_op jit(solution)/shard_map/ppermute | solution.py:25
  60.2 7.0 %collective-permute-start.4 = (bf16[32,3,256]{2,1,0:T(4,128)(2,1)S(1)}, bf16[32,3,256]{2,1,0:T(4,128)(2,1)S(1)}, u32[]{:S(2)}, u32[]{:S(2)}) collective-permute-start(bf16[32,3,256]{2,1,0:T(4,128)(2,1)S(1)} %get-tuple-element.32), channel_id=1, source_target_pairs={{0,4},{1,5},{2,6},{3,7},{4,0},{5,1},{6,2},{7,3},{8,12},{9,13},{10,... | collective-permute-start | bytes 147464 | tf_op jit(solution)/shard_map/ppermute | solution.py:25
  62.2 7.0 %collective-permute-start.5 = (bf16[32,3,256]{2,1,0:T(4,128)(2,1)S(1)}, bf16[32,3,256]{2,1,0:T(4,128)(2,1)S(1)}, u32[]{:S(2)}, u32[]{:S(2)}) collective-permute-start(bf16[32,3,256]{2,1,0:T(4,128)(2,1)S(1)} %get-tuple-element.33), channel_id=1, source_target_pairs={{0,28},{1,29},{2,30},{3,31},{4,8},{5,9},{6,10},{7,11},{8,4},{9,5},... | collective-permute-start | bytes 147464 | tf_op jit(solution)/shard_map/ppermute | solution.py:25
  66.9 6.7 %collective-permute-start.13 = (bf16[272,256]{1,0:T(8,128)(2,1)S(1)}, bf16[272,256]{1,0:T(8,128)(2,1)S(1)}, u32[]{:S(2)}, u32[]{:S(2)}) collective-permute-start(bf16[272,256]{1,0:T(8,128)(2,1)S(1)} %add_convert_fusion), channel_id=1, source_target_pairs={{0,2},{1,5},{2,0},{3,7},{4,6},{5,1},{6,4},{7,3},{8,10},{9,13},{10,... | collective-permute-start | bytes 417800 | tf_op jit(solution)/shard_map/ppermute | solution.py:25
  73.7 6.6 %collective-permute-start.14 = (bf16[544,256]{1,0:T(8,128)(2,1)S(1)}, bf16[544,256]{1,0:T(8,128)(2,1)S(1)}, u32[]{:S(2)}, u32[]{:S(2)}) collective-permute-start(bf16[544,256]{1,0:T(8,128)(2,1)S(1)} %pad_maximum_fusion.3), channel_id=1, source_target_pairs={{0,4},{1,3},{2,6},{3,1},{4,0},{5,7},{6,2},{7,5},{8,12},{9,11},{10,... | collective-permute-start | bytes 835592 | tf_op jit(solution)/shard_map/ppermute | solution.py:25
  80.4 11.6 %collective-permute-start.15 = (bf16[1088,256]{1,0:T(8,128)(2,1)S(1)}, bf16[1088,256]{1,0:T(8,128)(2,1)S(1)}, u32[]{:S(2)}, u32[]{:S(2)}) collective-permute-start(bf16[1088,256]{1,0:T(8,128)(2,1)S(1)} %pad_maximum_fusion.2), channel_id=1, source_target_pairs={{0,1},{1,0},{2,3},{3,2},{4,5},{5,4},{6,7},{7,6},{8,9},{9,8},{10,11... | collective-permute-start | bytes 1671176 | tf_op jit(solution)/shard_map/ppermute | solution.py:25
  80.5 5.2 %collective-permute-start.7 = (bf16[3,38,256]{2,1,0:T(8,128)(2,1)S(1)}, bf16[3,38,256]{2,1,0:T(8,128)(2,1)S(1)}, u32[]{:S(2)}, u32[]{:S(2)}) collective-permute-start(bf16[3,38,256]{2,1,0:T(8,128)(2,1)S(1)} %reverse_select_fusion), channel_id=1, source_target_pairs={{0,16},{1,2},{2,1},{3,19},{4,20},{5,6},{6,5},{7,23},{8,24},{9,10},... | collective-permute-start | bytes 175112 | tf_op jit(solution)/shard_map/ppermute | solution.py:25
  80.6 5.1 %collective-permute-start.6 = (bf16[3,38,256]{2,1,0:T(8,128)(2,1)S(1)}, bf16[3,38,256]{2,1,0:T(8,128)(2,1)S(1)}, u32[]{:S(2)}, u32[]{:S(2)}) collective-permute-start(bf16[3,38,256]{2,1,0:T(8,128)(2,1)S(1)} %get-tuple-element.20), channel_id=1, source_target_pairs={{0,1},{1,0},{2,3},{3,2},{4,5},{5,4},{6,7},{7,6},{8,9},{9,8},{10,11... | collective-permute-start | bytes 175112 | tf_op jit(solution)/shard_map/ppermute | solution.py:25
  92.1 1.0 %copy-start.5 = (f32[1088,256]{1,0:T(8,128)}, f32[1088,256]{1,0:T(8,128)S(1)}, u32[]{:S(2)}) copy-start(f32[1088,256]{1,0:T(8,128)S(1)} %select_convert_fusion.1) | copy-start | bytes 3342340
  93.7 1.1 %slice-start = ((f32[1088,256]{1,0:T(8,128)}), f32[49,256]{1,0:T(8,128)S(1)}, s32[]{:S(2)}) async-start(f32[1088,256]{1,0:T(8,128)} %copy-done.5), calls=%async_computation | async-start | bytes 114688 | tf_op jit(solution)/shard_map/slice | solution.py:489

commit v3 on v2

--- a/solution.py
+++ b/solution.py
@@ -29,11 +29,11 @@
     lons = lax.axis_size("lon")
     odd = lax.axis_index("lon") % 2 == 1
     first, last = field[:, :3], field[:, -3:]
-    inner = send(jnp.where(odd, first, last), lambda lon, lat: (lon ^ 1, lat))
     outer = send(
         jnp.where(odd, last, first),
         lambda lon, lat: ((lon + 1) % lons if lon % 2 else (lon - 1) % lons, lat),
     )
+    inner = send(jnp.where(odd, first, last), lambda lon, lat: (lon ^ 1, lat))
     west = jnp.where(odd, inner, outer)
     east = jnp.where(odd, outer, inner)
     return jnp.concatenate([west, field, east], axis=1)
@@ -78,7 +78,7 @@
     return (lon ^ (1 << bit), lat) if axis == "lon" else (lon, lat ^ (1 << bit))
 
 
-def summed(keep, give):
+def partner_steps():
     core = lax.axis_index("lat") % 2
     steps = axis_bits()
     other = list(steps)
@@ -94,24 +94,22 @@
 
         return jnp.where(core == 1, bit(other[at]), bit(steps[at]))
 
-    total = keep + send(give, lambda lon, lat: (lon, lat ^ 1)).astype(jnp.float32)
-    halvings = min(2, len(steps))
-    for at in range(halvings):
-        half = total.shape[0] // 2
-        bit = bit_of(at)
-        outgoing = lax.dynamic_slice_in_dim(total, (1 - bit) * half, half, 0)
-        mine = lax.dynamic_slice_in_dim(total, bit * half, half, 0)
-        total = mine + exchange(outgoing.astype(jnp.bfloat16), at).astype(jnp.float32)
-    sent = total.astype(jnp.bfloat16)
-    for at in range(halvings, len(steps)):
-        got = exchange(sent, at)
-        sent = (sent.astype(jnp.float32) + got.astype(jnp.float32)).astype(jnp.bfloat16)
-    for at in reversed(range(halvings)):
-        got = exchange(sent, at)
-        low = bit_of(at) == 0
-        sent = jnp.concatenate([jnp.where(low, sent, got), jnp.where(low, got, sent)], axis=0)
-    got = send(sent, lambda lon, lat: (lon, lat ^ 1))
-    return jnp.where(core == 0, sent, got), jnp.where(core == 0, got, sent)
+    return len(steps), exchange, bit_of
+
+
+def within_pair(value):
+    return send(value, lambda lon, lat: (lon, lat ^ 1))
+
+
+def halves(total, bit):
+    half = total.shape[0] // 2
+    outgoing = lax.dynamic_slice_in_dim(total, (1 - bit) * half, half, 0)
+    mine = lax.dynamic_slice_in_dim(total, bit * half, half, 0)
+    return mine, outgoing.astype(jnp.bfloat16)
+
+
+def rounded_sum(left, right):
+    return (left.astype(jnp.float32) + right.astype(jnp.float32)).astype(jnp.bfloat16)
 
 
 def gelu_parts(values):
@@ -131,7 +129,7 @@
 def spread_weights(weight_ref, spread_ref):
     for lane in range(spread_ref.shape[0]):
         for tap in range(49):
-            row = weight_ref[tap : tap + 1, lane * LANES : (lane + 1) * LANES]
+            row = weight_ref[tap // 7, tap % 7 : tap % 7 + 1, lane * LANES : (lane + 1) * LANES]
             spread_ref[lane, tap] = jnp.broadcast_to(row.astype(jnp.float32), (SUBLANES, LANES))
 
 
@@ -150,23 +148,28 @@
 
 def main_kernel(
     scale_factor,
+    core_ref,
     padded_ref,
     fields_ref,
     cot_ref,
     dw_ref,
-    chan_ref,
+    dw_bias_ref,
+    gain_ref,
+    offset_ref,
+    b_project_ref,
     b_expand_ref,
     w_expand_ref,
     w_project_ref,
     out_ref,
     dconv_ref,
-    expand_ref,
-    project_ref,
+    keep_ref,
+    give_ref,
     small_ref,
     wide_ref,
     spread_ref,
     conv_ref,
-    dwide_ref,
+    expand_ref,
+    project_ref,
 ):
     tiles = wide_ref.shape[0]
     rows = conv_ref.shape[1]
@@ -205,10 +208,11 @@
     expand_ref[...] = jnp.zeros_like(expand_ref)
     project_ref[...] = jnp.zeros_like(project_ref)
     small_ref[...] = jnp.zeros_like(small_ref)
-    dw_bias = chan_ref[0:1].astype(jnp.float32)
-    gain = chan_ref[1:2].astype(jnp.float32)
-    offset = chan_ref[2:3].astype(jnp.float32)
-    b_project = chan_ref[3:4].astype(jnp.float32)
+    dw_bias, gain, offset, b_project = (
+        ref[...].astype(jnp.float32).reshape(1, chans)
+        for ref in (dw_bias_ref, gain_ref, offset_ref, b_project_ref)
+    )
+    b_expand = b_expand_ref[...].astype(jnp.float32).reshape(1, hidden_units)
 
     def mlp_block(block, carry):
         row = block * block_rows
@@ -229,7 +233,7 @@
             w_in = w_expand_ref[:, part]
             w_out = w_project_ref[part, :]
             pre = jnp.dot(normed, w_in, preferred_element_type=jnp.float32)
-            pre = pre + b_expand_ref[0:1, part].astype(jnp.float32)
+            pre = pre + b_expand[:, part]
             active, slope = gelu_parts(pre)
             hidden = active.astype(jnp.bfloat16)
             branch = branch + jnp.dot(hidden, w_out, preferred_element_type=jnp.float32)
@@ -238,15 +242,15 @@
             d_pre = d_pre_wide.astype(jnp.bfloat16)
             project_ref[part, :] += contract(hidden, cot, 0, 0)
             expand_ref[part, :] += contract(normed, d_pre, 0, 0)
-            small_ref[53 + piece : 54 + piece] += jnp.sum(
+            small_ref[8 + piece : 9 + piece] += jnp.sum(
                 d_pre.astype(jnp.float32), axis=0, keepdims=True
             )
             d_normed = d_normed + contract(d_pre, w_in, 1, 1)
         plain = fields_ref[pl.ds(block * cells, cells), :].astype(jnp.float32)
         out_ref[pl.ds(block * cells, cells), :] = (plain + (branch + b_project)).astype(jnp.bfloat16)
-        small_ref[50:51] += jnp.sum(d_normed * xhat, axis=0, keepdims=True)
-        small_ref[51:52] += jnp.sum(d_normed, axis=0, keepdims=True)
-        small_ref[52:53] += jnp.sum(cot.astype(jnp.float32), axis=0, keepdims=True)
+        small_ref[0:1] += jnp.sum(d_normed * xhat, axis=0, keepdims=True)
+        small_ref[1:2] += jnp.sum(d_normed, axis=0, keepdims=True)
+        small_ref[2:3] += jnp.sum(cot.astype(jnp.float32), axis=0, keepdims=True)
         scaled = d_normed * gain
         d_conv = deviation * (
             scaled
@@ -255,40 +259,28 @@
         )
         d_conv = d_conv.astype(jnp.bfloat16)
         dconv_ref[pl.ds(block * cells, cells), :] = d_conv
-        d_conv = d_conv.astype(jnp.float32)
-        small_ref[49:50] += jnp.sum(d_conv, axis=0, keepdims=True)
-        for lane in range(tiles):
-            dwide_ref[lane, pl.ds(row, block_rows)] = d_conv[
-                :, lane * LANES : (lane + 1) * LANES
-            ].reshape(block_rows, cols, LANES)
         return carry
 
     lax.fori_loop(0, blocks, mlp_block, 0)
 
-    for lane in range(tiles):
-        for row_off in range(7):
-
-            def kernel_row(row, totals):
-                grads = [slot_rows(dwide_ref, lane, row, slot, slots) for slot in range(slots)]
-                loaded = [
-                    slot_rows(wide_ref, lane, row + row_off, place, slots)
-                    for place in range(slots + 6)
-                ]
-                return tuple(
-                    totals[col_off] + sum(grads[slot] * loaded[slot + col_off] for slot in range(slots))
-                    for col_off in range(7)
-                )
-
-            zeros = tuple(jnp.zeros((SUBLANES, LANES), jnp.float32) for unused in range(7))
-            totals = lax.fori_loop(0, rows, kernel_row, zeros, unroll=4)
-            for col_off in range(7):
-                tap = row_off * 7 + col_off
-                small_ref[tap : tap + 1, lane * LANES : (lane + 1) * LANES] = jnp.sum(
-                    totals[col_off], axis=0, keepdims=True
-                )
     small_ref[...] = small_ref[...] * scale_factor
-    expand_ref[...] = expand_ref[...] * scale_factor
-    project_ref[...] = project_ref[...] * scale_factor
+
+    def finish(mine, other):
+        def body(at, carry):
+            part = pl.ds(at * 64, 64)
+            keep_ref[part] = mine[part] * scale_factor
+            give_ref[part] = (other[part] * scale_factor).astype(jnp.bfloat16)
+            return carry
+
+        lax.fori_loop(0, hidden_units // 64, body, 0)
+
+    @pl.when(core_ref[0] == 0)
+    def first():
+        finish(expand_ref, project_ref)
+
+    @pl.when(core_ref[0] != 0)
+    def second():
+        finish(project_ref, expand_ref)
 
 
 def contract(left, right, left_dim, right_dim):
@@ -301,7 +293,7 @@
 
 
 def main_pass(
-    padded, fields, cot, dw_kernel, chan_params, b_expand, w_expand, w_project, scale_factor
+    core, padded, fields, cot, dw_kernel, vectors, w_expand, w_project, scale_factor
 ):
     rows, cols = padded.shape[0] - 6, fields.shape[0] // (padded.shape[0] - 6)
     chans = fields.shape[1]
@@ -315,25 +307,152 @@
             jax.ShapeDtypeStruct((cells, chans), jnp.bfloat16),
             jax.ShapeDtypeStruct((cells, chans), jnp.bfloat16),
             jax.ShapeDtypeStruct((hidden_units, chans), jnp.float32),
-            jax.ShapeDtypeStruct((hidden_units, chans), jnp.float32),
-            jax.ShapeDtypeStruct((64, chans), jnp.float32),
+            jax.ShapeDtypeStruct((hidden_units, chans), jnp.bfloat16),
+            jax.ShapeDtypeStruct((8 + hidden_units // chans, chans), jnp.float32),
         ],
-        in_specs=[pl.BlockSpec(memory_space=pltpu.VMEM)] * 8,
+        in_specs=[pl.BlockSpec(memory_space=pltpu.SMEM)]
+        + [pl.BlockSpec(memory_space=pltpu.VMEM)] * 11,
         out_specs=[pl.BlockSpec(memory_space=pltpu.VMEM)] * 5,
         scratch_shapes=[
             pltpu.VMEM((tiles, rows + 6, pad_cols, LANES), jnp.float32),
             pltpu.VMEM((tiles, 49, SUBLANES, LANES), jnp.float32),
             pltpu.VMEM((tiles, rows, cols, LANES), jnp.float32),
-            pltpu.VMEM((tiles, rows, cols, LANES), jnp.float32),
+            pltpu.VMEM((hidden_units, chans), jnp.float32),
+            pltpu.VMEM((hidden_units, chans), jnp.float32),
         ],
-        compiler_params=pltpu.CompilerParams(vmem_limit_bytes=48 << 20),
+        compiler_params=pltpu.CompilerParams(vmem_limit_bytes=14 << 20),
         cost_estimate=pl.CostEstimate(
             flops=12 * cells * chans * hidden_units,
             bytes_accessed=8 << 20,
             transcendentals=2 * cells * hidden_units,
         ),
         name="block_main",
-    )(padded, fields, cot, dw_kernel, chan_params, b_expand, w_expand, w_project)
+    )(core, padded, fields, cot, dw_kernel, *vectors, w_expand, w_project)
+
+
+def taps_kernel(scale_factor, padded_ref, dconv_ref, small_ref, out_ref, wide_ref, dwide_ref, sums_ref):
+    tiles, rows, cols = dwide_ref.shape[0], dwide_ref.shape[1], dwide_ref.shape[2]
+    slots = cols // SUBLANES
+    split_lanes(padded_ref, wide_ref)
+    split_lanes(dconv_ref, dwide_ref)
+    sums_ref[...] = jnp.zeros_like(sums_ref)
+    for lane in range(tiles):
+        lanes = slice(lane * LANES, (lane + 1) * LANES)
+        for row_off in range(7):
+
+            def kernel_row(row, totals):
+                grads = [slot_rows(dwide_ref, lane, row, slot, slots) for slot in range(slots)]
+                loaded = [
+                    slot_rows(wide_ref, lane, row + row_off, place, slots)
+                    for place in range(slots + 6)
+                ]
+                sums = [
+                    totals[col_off] + sum(grads[slot] * loaded[slot + col_off] for slot in range(slots))
+                    for col_off in range(7)
+                ]
+                if row_off == 0:
+                    sums.append(totals[7] + sum(grads))
+                return tuple(sums)
+
+            count = 8 if row_off == 0 else 7
+            zeros = tuple(jnp.zeros((SUBLANES, LANES), jnp.float32) for unused in range(count))
+            totals = lax.fori_loop(0, rows, kernel_row, zeros, unroll=4)
+            for col_off in range(count):
+                tap = row_off * 7 + col_off if col_off < 7 else 49
+                sums_ref[tap : tap + 1, lanes] = jnp.sum(totals[col_off], axis=0, keepdims=True)
+    sums_ref[...] = sums_ref[...] * scale_factor
+    pieces = small_ref.shape[0] - 8
+    sums_ref[50:53] = small_ref[0:3]
+    sums_ref[53 : 53 + pieces] = small_ref[8 : 8 + pieces]
+    out_ref[...] = sums_ref[...].astype(jnp.bfloat16)
+
+
+def taps_pass(padded, conv_gradient, small, scale_factor):
+    rows, cols, chans = conv_gradient.shape
+    tiles = chans // LANES
+    height = -(-(45 + small.shape[0]) // 32) * 32
+    return pl.pallas_call(
+        functools.partial(taps_kernel, scale_factor),
+        out_shape=jax.ShapeDtypeStruct((height, chans), jnp.bfloat16),
+        in_specs=[pl.BlockSpec(memory_space=pltpu.VMEM)] * 3,
+        out_specs=pl.BlockSpec(memory_space=pltpu.VMEM),
+        scratch_shapes=[
+            pltpu.VMEM((tiles,) + padded.shape[:2] + (LANES,), jnp.float32),
+            pltpu.VMEM((tiles, rows, cols, LANES), jnp.float32),
+            pltpu.VMEM((height, chans), jnp.float32),
+        ],
+        compiler_params=pltpu.CompilerParams(vmem_limit_bytes=6 << 20),
+        cost_estimate=pl.CostEstimate(
+            flops=98 * rows * cols * chans, bytes_accessed=3 << 20, transcendentals=0
+        ),
+        name="block_taps",
+    )(padded, conv_gradient, small)
+
+
+def finish_kernel(
+    core_ref,
+    mine_ref,
+    got_ref,
+    kern_ref,
+    dwb_ref,
+    gain_ref,
+    shift_ref,
+    expand_ref,
+    b_expand_ref,
+    project_ref,
+    b_project_ref,
+    sums_ref,
+):
+    hidden_units, chans = project_ref.shape
+    pieces = hidden_units // chans
+    small = slice(hidden_units, mine_ref.shape[0])
+    sums_ref[...] = mine_ref[small].astype(jnp.float32) + got_ref[small].astype(jnp.float32)
+    for row_off in range(7):
+        kern_ref[row_off] = sums_ref[row_off * 7 : row_off * 7 + 7]
+    dwb_ref[...] = sums_ref[49]
+    gain_ref[...] = sums_ref[50]
+    shift_ref[...] = sums_ref[51]
+    b_project_ref[...] = sums_ref[52]
+    for piece in range(pieces):
+        b_expand_ref[piece * chans : (piece + 1) * chans] = sums_ref[53 + piece]
+
+    def write(first_ref, second_ref):
+        for piece in range(pieces):
+            part = slice(piece * chans, (piece + 1) * chans)
+            expand_ref[:, part] = first_ref[part].astype(jnp.float32)
+            project_ref[part] = second_ref[part].astype(jnp.float32)
+
+    @pl.when(core_ref[0] == 0)
+    def first():
+        write(mine_ref, got_ref)
+
+    @pl.when(core_ref[0] != 0)
+    def second():
+        write(got_ref, mine_ref)
+
+
+def finish_pass(core, mine, got, hidden_units):
+    chans = mine.shape[1]
+    one = jax.ShapeDtypeStruct((chans,), jnp.float32)
+    return pl.pallas_call(
+        finish_kernel,
+        out_shape=[
+            jax.ShapeDtypeStruct((7, 7, chans), jnp.float32),
+            one,
+            one,
+            one,
+            jax.ShapeDtypeStruct((chans, hidden_units), jnp.float32),
+            jax.ShapeDtypeStruct((hidden_units,), jnp.float32),
+            jax.ShapeDtypeStruct((hidden_units, chans), jnp.float32),
+            one,
+        ],
+        in_specs=[pl.BlockSpec(memory_space=pltpu.SMEM)]
+        + [pl.BlockSpec(memory_space=pltpu.VMEM)] * 2,
+        out_specs=[pl.BlockSpec(memory_space=pltpu.VMEM)] * 8,
+        scratch_shapes=[pltpu.VMEM((mine.shape[0] - hidden_units, chans), jnp.float32)],
+        compiler_params=pltpu.CompilerParams(vmem_limit_bytes=8 << 20),
+        name="block_finish",
+    )(core, mine, got)
 
 
 def adjoint_kernel(
@@ -423,7 +542,7 @@
             pltpu.VMEM((2, tiles, 21, SUBLANES, LANES), jnp.float32),
             pltpu.VMEM((tiles, rows, cols, LANES), jnp.float32),
         ],
-        compiler_params=pltpu.CompilerParams(vmem_limit_bytes=32 << 20),
+        compiler_params=pltpu.CompilerParams(vmem_limit_bytes=6 << 20),
         cost_estimate=pl.CostEstimate(
             flops=98 * rows * cols * chans, bytes_accessed=3 << 20, transcendentals=0
         ),
@@ -453,42 +572,70 @@
     cols = fields.shape[1]
     chans = fields.shape[2]
     scale_factor = 1.0 / math.sqrt(rows * cols * lax.axis_size("lat") * lax.axis_size("lon"))
+    hidden_units = w_expand.shape[1]
     lat = lax.axis_index("lat")
     poles = jnp.stack([lat == 0, lat == lax.axis_size("lat") - 1]).astype(jnp.int32)
-    taps = dw_kernel.reshape(49, chans)
-    chan_params = jnp.stack([dw_bias, norm_gain, layer_norm_offset, b_project])
-    flat_cot = cotangent.reshape(-1, chans)
-    block_out, conv_gradient, grad_exp, grad_proj, small = main_pass(
-        sphere_pad(fields),
+    core = (lat % 2).reshape(1)
+    padded = sphere_pad(fields)
+    block_out, conv_gradient, keep, give, small = main_pass(
+        core,
+        padded,
         fields.reshape(-1, chans),
-        flat_cot,
-        taps,
-        chan_params,
-        b_expand.reshape(1, -1),
+        cotangent.reshape(-1, chans),
+        dw_kernel,
+        (dw_bias, norm_gain, layer_norm_offset, b_project, b_expand),
         w_expand,
         w_project,
         scale_factor,
     )
     block_out = block_out.reshape(fields.shape)
-    grad_fields = adjoint_pass(
-        sphere_pad(conv_gradient.reshape(fields.shape)), cotangent, taps, poles
+    conv_gradient = conv_gradient.reshape(fields.shape)
+    barrier = lax.optimization_barrier
+    count, exchange, bit_of = partner_steps()
+    total = keep + within_pair(give).astype(jnp.float32)
+    mine, outgoing = halves(total, bit_of(0))
+    outgoing, taps_in = barrier((outgoing, conv_gradient))
+    got = exchange(outgoing, 0)
+    small = taps_pass(padded, taps_in, small, scale_factor)
+    got, small, conv_gradient = barrier((got, small, conv_gradient))
+    mine, outgoing = halves(mine + got.astype(jnp.float32), bit_of(1))
+    outgoing, conv_gradient = barrier((outgoing, conv_gradient))
+    got = exchange(outgoing, 1)
+    wide = lon_margins(conv_gradient)
+    payload = (mine + got.astype(jnp.float32)).astype(jnp.bfloat16)
+    payload = jnp.concatenate([payload, small], axis=0)
+    for at in range(2, count):
+        got = exchange(payload, at)
+        if at == 2:
+            got, wide = barrier((got, wide))
+            top, bottom = lat_margins(wide)
+        payload = rounded_sum(payload, got)
+    if count > 2:
+        payload, top, bottom = barrier((payload, top, bottom))
+    else:
+        top, bottom = lat_margins(wide)
+    padded_gradient = jnp.concatenate([top, wide, bottom], axis=0)
+    for at in (1, 0):
+        if at == 0:
+            payload, padded_gradient = barrier((payload, padded_gradient))
+            grad_fields = adjoint_pass(padded_gradient, cotangent, dw_kernel, poles)
+        got = exchange(payload, at)
+        if at == 0:
+            got, grad_fields = barrier((got, grad_fields))
+        own = payload.shape[0] - small.shape[0]
+        low = bit_of(at) == 0
+        here, there = payload[:own], got[:own]
+        payload = jnp.concatenate(
+            [
+                jnp.where(low, here, there),
+                jnp.where(low, there, here),
+                rounded_sum(payload[own:], got[own:]),
+            ],
+            axis=0,
+        )
+    sum_kern, sum_dwb, sum_gn, sum_sh, sum_exp, sum_bexp, sum_proj, sum_bproj = finish_pass(
+        core, payload, within_pair(payload), hidden_units
     )
-    hidden_units = w_expand.shape[1]
-    pieces = hidden_units // chans
-    first = jnp.concatenate([grad_exp, small], axis=0)
-    second = jnp.concatenate([grad_proj, jnp.zeros_like(small)], axis=0)
-    core = lax.axis_index("lat") % 2
-    keep = jnp.where(core == 0, first, second)
-    give = jnp.where(core == 0, second, first).astype(jnp.bfloat16)
-    first, second = summed(keep, give)
-    first = first.astype(jnp.float32)
-    second = second.astype(jnp.float32)
-    sum_exp = first[:hidden_units].reshape(pieces, chans, chans).swapaxes(0, 1).reshape(chans, -1)
-    sum_proj = second[:hidden_units]
-    rest = first[hidden_units:]
-    sum_kern = rest[:49].reshape(7, 7, chans)
-    sum_dwb, sum_gn, sum_sh, sum_bproj = rest[49], rest[50], rest[51], rest[52]
-    sum_bexp = rest[53 : 53 + pieces].reshape(-1)
     return (
         block_out,
         grad_fields,

time: 97 us -> 78.4 us (0.81)
  waiting for transfers between devices: 41.7 us -> 28.2 us
  local copies, waits for them, and re-layouts: 8.64 us -> 1.78 us
  other arithmetic: 8.32 us -> 3.68 us
  starting transfers between devices: 14.3 us -> 17.7 us
  Pallas kernels: 22.6 us -> 25 us
    ppermute x16, waiting for transfers between devices: 41.7 us -> 28.2 us  [send(): return lax.ppermute(value, ('lon', 'lat'), flat_pairs(target))]
    pallas_call x0 -> x2, Pallas kernels: none -> 6.06 us  [the longest x1 4.54 us: taps_pass(): pl.pallas_call(functools.partial(taps_kernel, scale_factor), out_shape=ja...]
    pallas_call x1, Pallas kernels: 16.7 us -> 13 us  [main_pass(): pl.pallas_call(functools.partial(main_kernel, scale_factor), out_shape=[j...]
    ppermute x16, starting transfers between devices: 14.3 us -> 17.7 us  [send(): return lax.ppermute(value, ('lon', 'lat'), flat_pairs(target))]
    reshape x4 -> x0, local copies, waits for them, and re-layouts: 3.19 us -> none  [the longest x1 1.11 us: local(): first[:hidden_units].reshape(pieces, chans, chans).swapaxes(0, 1)]
    another operation x4 -> x0, local copies, waits for them, and re-layouts: 2.63 us -> none  [local(): chan_params = jnp.stack([dw_bias, norm_gain, layer_norm_offset, b_project])]
    add x2, other arithmetic: 2.51 us -> 0.16 us  [the longest x1 0.1 us: local(): total = keep + within_pair(give).astype(jnp.float32)]
    convert_element_type x5, other arithmetic: 1.33 us -> 0.14 us  [the longest x4 0.11 us: rounded_sum(): (left.astype(jnp.float32) + right.astype(jnp.float32)).astype(jnp.bfloat16)]
  transfers between devices with their start and end apart: 16 -> 16, of which waited for: 10 -> 12; matrix products, arithmetic and copies ran while one was open for 5% -> 1% of each run, Pallas kernels for 6% -> 14%
where the time goes in v3:
time: 78.4 us; the launch traced here: 77.4 us
  waiting for transfers between devices  28.2 us (36%)
  Pallas kernels  25 us (32%)
  starting transfers between devices  17.7 us (23%)
  other arithmetic  3.68 us (5%)
  local copies, waits for them, and re-layouts  1.78 us (2%)
  between operations  1 us (1%)
    ppermute x16, waiting for transfers between devices, send(): return lax.ppermute(value, ('lon', 'lat'), flat_pairs(target))  28.2 us
    ppermute x16, starting transfers between devices, send(): return lax.ppermute(value, ('lon', 'lat'), flat_pairs(target))  17.7 us
    pallas_call x1, Pallas kernels, main_pass(): pl.pallas_call(functools.partial(main_kernel, scale_factor), out_shape=[j...  13 us
    pallas_call x1, Pallas kernels, adjoint_pass(): pl.pallas_call(adjoint_kernel, out_shape=jax.ShapeDtypeStruct(cot.shape,...  5.93 us
    pallas_call x1, Pallas kernels, taps_pass(): pl.pallas_call(functools.partial(taps_kernel, scale_factor), out_shape=ja...  4.54 us
  transfers between devices with their start and end apart: 16, of which 12 were waited for; matrix products, arithmetic and copies ran while one was open for 1% of the time, Pallas kernels for 14%

profile of v3, /device:TPU:0, one launch (start us, length us, event | category | flops | bytes accessed | tf_op | source)
XLA Modules:
  0.0 77.4 jit_solution(5527966893764814067)
XLA Ops:
  0.7 1.1 %broadcast_select_fusion.11 = (bf16[32,3,256]{2,1,0:T(4,128)(2,1)S(1)}, bf16[32,3,256]{2,1,0:T(4,128)(2,1)S(1)}) fusion(pred[]{:T(512)S(6)} %eq.36, bf16[32,32,256]{2,1,0:T(8,128)(2,1)} %param.10), kind=kLoop, calls=%fused_computation.28 | loop fusion | flops 49152 | bytes 196609 | tf_op jit(solution)/shard_map/jit(_where)/select_n | solution.py:36
  1.8 3.0 %collective-permute-start = (bf16[32,3,256]{2,1,0:T(4,128)(2,1)S(1)}, bf16[32,3,256]{2,1,0:T(4,128)(2,1)S(1)}, u32[]{:S(2)}, u32[]{:S(2)}) collective-permute-start(bf16[32,3,256]{2,1,0:T(4,128)(2,1)S(1)} %get-tuple-element.77), channel_id=1, source_target_pairs={{0,4},{1,5},{2,6},{3,7},{4,0},{5,1},{6,2},{7,3},{8,12},{9,13},{10,... | collective-permute-start | bytes 147464 | tf_op jit(solution)/shard_map/ppermute | solution.py:25
  4.8 3.6 %collective-permute-start.1 = (bf16[32,3,256]{2,1,0:T(4,128)(2,1)S(1)}, bf16[32,3,256]{2,1,0:T(4,128)(2,1)S(1)}, u32[]{:S(2)}, u32[]{:S(2)}) collective-permute-start(bf16[32,3,256]{2,1,0:T(4,128)(2,1)S(1)} %get-tuple-element.78), channel_id=1, source_target_pairs={{0,28},{1,29},{2,30},{3,31},{4,8},{5,9},{6,10},{7,11},{8,4},{9,5},... | collective-permute-start | bytes 147464 | tf_op jit(solution)/shard_map/ppermute | solution.py:25
  8.4 3.4 %collective-permute-done.1 = bf16[32,3,256]{2,1,0:T(4,128)(2,1)S(1)} collective-permute-done((bf16[32,3,256]{2,1,0:T(4,128)(2,1)S(1)}, bf16[32,3,256]{2,1,0:T(4,128)(2,1)S(1)}, u32[]{:S(2)}, u32[]{:S(2)}) %collective-permute-start.1) | collective-permute-done | bytes 49184 | tf_op jit(solution)/shard_map/ppermute | solution.py:25
  11.8 0.9 %broadcast_select_fusion.19 = (bf16[3,38,256]{2,1,0:T(8,128)(2,1)S(1)}, bf16[3,38,256]{2,1,0:T(8,128)(2,1)S(1)}, bf16[3,38,256]{2,1,0:T(8,128)(2,1)S(1)}) fusion(pred[]{:T(512)S(6)} %eq.35, bf16[32,3,256]{2,1,0:T(4,128)(2,1)S(1)} %get-tuple-element.84, bf16[32,32,256]{2,1,0:T(8,128)(2,1)} %param.10, bf16[32,3,256]{2,1,0:T(4,128)(2,1)S(1)} %get-tuple-element.83), kind=kLoop, calls=%fused_computation.39 | loop fusion | flops 379392 | bytes 797697 | tf_op jit(solution)/shard_map/jit(_where)/select_n | solution.py:57
  12.8 0.9 %collective-permute-start.3 = (bf16[3,38,256]{2,1,0:T(8,128)(2,1)S(1)}, bf16[3,38,256]{2,1,0:T(8,128)(2,1)S(1)}, u32[]{:S(2)}, u32[]{:S(2)}) collective-permute-start(bf16[3,38,256]{2,1,0:T(8,128)(2,1)S(1)} %reverse_select_fusion.1), channel_id=1, source_target_pairs={{0,16},{1,2},{2,1},{3,19},{4,20},{5,6},{6,5},{7,23},{8,24},{9,10},... | collective-permute-start | bytes 175112 | tf_op jit(solution)/shard_map/ppermute | solution.py:25
  13.7 0.8 %collective-permute-start.2 = (bf16[3,38,256]{2,1,0:T(8,128)(2,1)S(1)}, bf16[3,38,256]{2,1,0:T(8,128)(2,1)S(1)}, u32[]{:S(2)}, u32[]{:S(2)}) collective-permute-start(bf16[3,38,256]{2,1,0:T(8,128)(2,1)S(1)} %get-tuple-element.68), channel_id=1, source_target_pairs={{0,1},{1,0},{2,3},{3,2},{4,5},{5,4},{6,7},{7,6},{8,9},{9,8},{10,11... | collective-permute-start | bytes 175112 | tf_op jit(solution)/shard_map/ppermute | solution.py:25
  14.5 3.5 %collective-permute-done.3 = bf16[3,38,256]{2,1,0:T(8,128)(2,1)S(1)} collective-permute-done((bf16[3,38,256]{2,1,0:T(8,128)(2,1)S(1)}, bf16[3,38,256]{2,1,0:T(8,128)(2,1)S(1)}, u32[]{:S(2)}, u32[]{:S(2)}) %collective-permute-start.3) | collective-permute-done | bytes 58400 | tf_op jit(solution)/shard_map/ppermute | solution.py:25
  18.1 0.4 pad_maximum_fusion.padded_ref
  18.6 13.0 %block_main.1 = (bf16[1024,256]{1,0:T(8,128)(2,1)}, bf16[1024,256]{1,0:T(8,128)(2,1)S(1)}, f32[1024,256]{1,0:T(8,128)S(1)}, bf16[1024,256]{1,0:T(8,128)(2,1)}, f32[12,256]{1,0:T(8,128)S(1)}) custom-call(s32[1]{0:T(128)} %bitcast.core_ref, bf16[38,38,256]{2,1,0:T(8,128)(2,1)S(1)} %pad_maximum_fusion.padded_ref, bf16[1024,256]{1,0:T(8,128)(2,1)S(1)} %bitcast.7, ...), custom_call_target="tpu_custom_call" | custom-call | flops 3221225472 | bytes 8388608 | tf_op jit(solution)/shard_map/block_main/pallas_call | solution.py:304
  31.5 2.1 %collective-permute-done.4 = bf16[1024,256]{1,0:T(8,128)(2,1)S(1)} collective-permute-done((bf16[1024,256]{1,0:T(8,128)(2,1)}, bf16[1024,256]{1,0:T(8,128)(2,1)S(1)}, u32[]{:S(2)}, u32[]{:S(2)}) %collective-permute-start.4) | collective-permute-done | bytes 524320 | tf_op jit(solution)/shard_map/ppermute | solution.py:25
  33.8 1.0 %copy-done.10 = f32[1024,256]{1,0:T(8,128)} copy-done((f32[1024,256]{1,0:T(8,128)}, f32[1024,256]{1,0:T(8,128)S(1)}, u32[]{:S(2)}) %copy-start.10) | copy-done | bytes 1048600
  34.7 0.7 dynamic-slice_convert_fusion
  35.5 4.5 %block_taps.1 = bf16[64,256]{1,0:T(8,128)(2,1)S(1)} custom-call(bf16[38,38,256]{2,1,0:T(8,128)(2,1)S(1)} %pad_maximum_fusion.padded_ref, bf16[32,32,256]{2,1,0:T(8,128)(2,1)S(1)} %bitcast.8, f32[12,256]{1,0:T(8,128)S(1)} %get-tuple-element.45.small_ref), custom_call_target="tpu_custom_call" | custom-call | flops 25690112 | bytes 3145728 | tf_op jit(solution)/shard_map/block_taps/pallas_call | solution.py:374
  40.0 2.0 %collective-permute-done.5 = bf16[512,256]{1,0:T(8,128)(2,1)S(1)} collective-permute-done((bf16[512,256]{1,0:T(8,128)(2,1)}, bf16[512,256]{1,0:T(8,128)(2,1)S(1)}, u32[]{:S(2)}, u32[]{:S(2)}) %collective-permute-start.5) | collective-permute-done | bytes 262176 | tf_op jit(solution)/shard_map/ppermute | solution.py:25
  42.4 3.8 %collective-permute-start.9 = (bf16[32,3,256]{2,1,0:T(4,128)(2,1)S(1)}, bf16[32,3,256]{2,1,0:T(4,128)(2,1)S(1)}, u32[]{:S(2)}, u32[]{:S(2)}) collective-permute-start(bf16[32,3,256]{2,1,0:T(4,128)(2,1)S(1)} %get-tuple-element.76), channel_id=1, source_target_pairs={{0,28},{1,29},{2,30},{3,31},{4,8},{5,9},{6,10},{7,11},{8,4},{9,5},... | collective-permute-start | bytes 147464 | tf_op jit(solution)/shard_map/ppermute | solution.py:25
  46.2 1.0 %collective-permute-done.6 = bf16[256,256]{1,0:T(8,128)(2,1)S(1)} collective-permute-done((bf16[256,256]{1,0:T(8,128)(2,1)S(1)}, bf16[256,256]{1,0:T(8,128)(2,1)S(1)}, u32[]{:S(2)}, u32[]{:S(2)}) %collective-permute-start.6) | collective-permute-done | bytes 131104 | tf_op jit(solution)/shard_map/ppermute | solution.py:25
  47.3 2.6 %collective-permute-done.9 = bf16[32,3,256]{2,1,0:T(4,128)(2,1)S(1)} collective-permute-done((bf16[32,3,256]{2,1,0:T(4,128)(2,1)S(1)}, bf16[32,3,256]{2,1,0:T(4,128)(2,1)S(1)}, u32[]{:S(2)}, u32[]{:S(2)}) %collective-permute-start.9) | collective-permute-done | bytes 49184 | tf_op jit(solution)/shard_map/ppermute | solution.py:25
  49.9 0.4 pad_maximum_fusion.2
  50.3 3.7 %collective-permute-done.7 = bf16[320,256]{1,0:T(8,128)(2,1)S(1)} collective-permute-done((bf16[320,256]{1,0:T(8,128)(2,1)S(1)}, bf16[320,256]{1,0:T(8,128)(2,1)S(1)}, u32[]{:S(2)}, u32[]{:S(2)}) %collective-permute-start.7) | collective-permute-done | bytes 163872 | tf_op jit(solution)/shard_map/ppermute | solution.py:25
  54.1 0.7 collective-permute-start.12
  54.8 0.2 collective-permute-start.11
  55.0 2.2 %collective-permute-start.10 = (bf16[320,256]{1,0:T(8,128)(2,1)S(1)}, bf16[320,256]{1,0:T(8,128)(2,1)S(1)}, u32[]{:S(2)}, u32[]{:S(2)}) collective-permute-start(bf16[320,256]{1,0:T(8,128)(2,1)S(1)} %add_convert_fusion.1), channel_id=1, source_target_pairs={{0,16},{1,9},{2,18},{3,11},{4,20},{5,13},{6,22},{7,15},{8,24},{9,1... | collective-permute-start | bytes 491528 | tf_op jit(solution)/shard_map/ppermute | solution.py:25
  57.2 2.4 %collective-permute-done.12 = bf16[3,38,256]{2,1,0:T(8,128)(2,1)S(1)} collective-permute-done((bf16[3,38,256]{2,1,0:T(8,128)(2,1)S(1)}, bf16[3,38,256]{2,1,0:T(8,128)(2,1)S(1)}, u32[]{:S(2)}, u32[]{:S(2)}) %collective-permute-start.12) | collective-permute-done | bytes 58400 | tf_op jit(solution)/shard_map/ppermute | solution.py:25
  59.6 1.8 %collective-permute-done.10 = bf16[320,256]{1,0:T(8,128)(2,1)S(1)} collective-permute-done((bf16[320,256]{1,0:T(8,128)(2,1)S(1)}, bf16[320,256]{1,0:T(8,128)(2,1)S(1)}, u32[]{:S(2)}, u32[]{:S(2)}) %collective-permute-start.10) | collective-permute-done | bytes 163872 | tf_op jit(solution)/shard_map/ppermute | solution.py:25
  61.5 1.7 %collective-permute-start.13 = (bf16[320,256]{1,0:T(8,128)(2,1)S(1)}, bf16[320,256]{1,0:T(8,128)(2,1)S(1)}, u32[]{:S(2)}, u32[]{:S(2)}) collective-permute-start(bf16[320,256]{1,0:T(8,128)(2,1)S(1)} %add_convert_fusion), channel_id=1, source_target_pairs={{0,2},{1,5},{2,0},{3,7},{4,6},{5,1},{6,4},{7,3},{8,10},{9,13},{10,... | collective-permute-start | bytes 491528 | tf_op jit(solution)/shard_map/ppermute | solution.py:25
  63.3 3.6 %collective-permute-done.13 = bf16[320,256]{1,0:T(8,128)(2,1)S(1)} collective-permute-done((bf16[320,256]{1,0:T(8,128)(2,1)S(1)}, bf16[320,256]{1,0:T(8,128)(2,1)S(1)}, u32[]{:S(2)}, u32[]{:S(2)}) %collective-permute-start.13) | collective-permute-done | bytes 163872 | tf_op jit(solution)/shard_map/ppermute | solution.py:25
  67.0 0.6 collective-permute-start.14
  67.7 5.9 %block_adjoint.1 = bf16[32,32,256]{2,1,0:T(8,128)(2,1)} custom-call(s32[2]{0:T(128)S(1)} %add_convert_fusion.5.poles_ref, bf16[38,38,256]{2,1,0:T(8,128)(2,1)S(1)} %pad_maximum_fusion.1.padded_ref, bf16[32,32,256]{2,1,0:T(8,128)(2,1)S(1)} %copy-done.1, bf16[7,7,256]{2,1,0:T(8,128)(2,1)S(1)} %copy-done.2), custom_call_target="tpu_custom_call" | custom-call | flops 25690112 | bytes 3145728 | tf_op jit(solution)/shard_map/block_adjoint/pallas_call | solution.py:533
  73.6 0.2 collective-permute-done.14
  73.9 1.9 %collective-permute-done.15.got_ref = bf16[1088,256]{1,0:T(8,128)(2,1)S(1)} collective-permute-done((bf16[1088,256]{1,0:T(8,128)(2,1)S(1)}, bf16[1088,256]{1,0:T(8,128)(2,1)S(1)}, u32[]{:S(2)}, u32[]{:S(2)}) %collective-permute-start.15) | collective-permute-done | bytes 557088 | tf_op jit(solution)/shard_map/ppermute | solution.py:25
  75.9 1.5 %block_finish.1 = (f32[7,7,256]{2,1,0:T(8,128)}, f32[256]{0:T(256)}, f32[256]{0:T(256)}, f32[256]{0:T(256)}, f32[256,1024]{1,0:T(8,128)}, /*index=5*/f32[1024]{0:T(1024)}, f32[1024,256]{1,0:T(8,128)}, f32[256]{0:T(256)}) custom-call(s32[1]{0:T(128)} %bitcast.core_ref, bf16[1088,256]{1,0:T(8,128)(2,1)S(1)} %pad_maximum_fusion.3.mine_ref, ...), custom_call_target="tpu_custom_call" | custom-call | tf_op jit(solution)/shard_map/block_finish/pallas_call | solution.py:437
  (57 shorter events, 1.3 us)
Async XLA Ops:
  0.6 17.4 %copy-start = (bf16[32,32,256]{2,1,0:T(8,128)(2,1)S(1)}, bf16[32,32,256]{2,1,0:T(8,128)(2,1)}, u32[]{:S(2)}) copy-start(bf16[32,32,256]{2,1,0:T(8,128)(2,1)} %param.10) | copy-start | bytes 1572868
  1.8 6.6 %collective-permute-start = (bf16[32,3,256]{2,1,0:T(4,128)(2,1)S(1)}, bf16[32,3,256]{2,1,0:T(4,128)(2,1)S(1)}, u32[]{:S(2)}, u32[]{:S(2)}) collective-permute-start(bf16[32,3,256]{2,1,0:T(4,128)(2,1)S(1)} %get-tuple-element.77), channel_id=1, source_target_pairs={{0,4},{1,5},{2,6},{3,7},{4,0},{5,1},{6,2},{7,3},{8,12},{9,13},{10,... | collective-permute-start | bytes 147464 | tf_op jit(solution)/shard_map/ppermute | solution.py:25
  4.8 7.0 %collective-permute-start.1 = (bf16[32,3,256]{2,1,0:T(4,128)(2,1)S(1)}, bf16[32,3,256]{2,1,0:T(4,128)(2,1)S(1)}, u32[]{:S(2)}, u32[]{:S(2)}) collective-permute-start(bf16[32,3,256]{2,1,0:T(4,128)(2,1)S(1)} %get-tuple-element.78), channel_id=1, source_target_pairs={{0,28},{1,29},{2,30},{3,31},{4,8},{5,9},{6,10},{7,11},{8,4},{9,5},... | collective-permute-start | bytes 147464 | tf_op jit(solution)/shard_map/ppermute | solution.py:25
  12.7 5.8 %copy-start.1 = (bf16[32,32,256]{2,1,0:T(8,128)(2,1)S(1)}, bf16[32,32,256]{2,1,0:T(8,128)(2,1)}, u32[]{:S(2)}) copy-start(bf16[32,32,256]{2,1,0:T(8,128)(2,1)} %cot_ref.1) | copy-start | bytes 1572868
  12.7 5.8 %copy-start.2 = (bf16[7,7,256]{2,1,0:T(8,128)(2,1)S(1)}, bf16[7,7,256]{2,1,0:T(8,128)(2,1)}, u32[]{:S(2)}) copy-start(bf16[7,7,256]{2,1,0:T(8,128)(2,1)} %dw_ref.3) | copy-start | bytes 75268
  12.7 5.8 %copy-start.3 = (bf16[256,1024]{1,0:T(8,128)(2,1)S(1)}, bf16[256,1024]{1,0:T(8,128)(2,1)}, u32[]{:S(2)}) copy-start(bf16[256,1024]{1,0:T(8,128)(2,1)} %w_expand_ref.1) | copy-start | bytes 1572868
  12.7 5.8 %copy-start.4 = (bf16[1024,256]{1,0:T(8,128)(2,1)S(1)}, bf16[1024,256]{1,0:T(8,128)(2,1)}, u32[]{:S(2)}) copy-start(bf16[1024,256]{1,0:T(8,128)(2,1)} %w_project_ref.1) | copy-start | bytes 1572868
  12.7 5.8 %copy-start.5 = (bf16[1024]{0:T(1024)(128)(2,1)S(1)}, bf16[1024]{0:T(1024)(128)(2,1)}, u32[]{:S(2)}) copy-start(bf16[1024]{0:T(1024)(128)(2,1)} %b_expand_ref.1) | copy-start | bytes 6148
  12.7 5.8 %copy-start.6 = (bf16[256]{0:T(256)(128)(2,1)S(1)}, bf16[256]{0:T(256)(128)(2,1)}, u32[]{:S(2)}) copy-start(bf16[256]{0:T(256)(128)(2,1)} %dw_bias_ref.1) | copy-start | bytes 1540
  12.8 5.8 %copy-start.7 = (bf16[256]{0:T(256)(128)(2,1)S(1)}, bf16[256]{0:T(256)(128)(2,1)}, u32[]{:S(2)}) copy-start(bf16[256]{0:T(256)(128)(2,1)} %gain_ref.1) | copy-start | bytes 1540
  12.8 5.8 %copy-start.8 = (bf16[256]{0:T(256)(128)(2,1)S(1)}, bf16[256]{0:T(256)(128)(2,1)}, u32[]{:S(2)}) copy-start(bf16[256]{0:T(256)(128)(2,1)} %offset_ref.1) | copy-start | bytes 1540
  12.8 5.8 %copy-start.9 = (bf16[256]{0:T(256)(128)(2,1)S(1)}, bf16[256]{0:T(256)(128)(2,1)}, u32[]{:S(2)}) copy-start(bf16[256]{0:T(256)(128)(2,1)} %b_project_ref.1) | copy-start | bytes 1540
  12.8 5.2 %collective-permute-start.3 = (bf16[3,38,256]{2,1,0:T(8,128)(2,1)S(1)}, bf16[3,38,256]{2,1,0:T(8,128)(2,1)S(1)}, u32[]{:S(2)}, u32[]{:S(2)}) collective-permute-start(bf16[3,38,256]{2,1,0:T(8,128)(2,1)S(1)} %reverse_select_fusion.1), channel_id=1, source_target_pairs={{0,16},{1,2},{2,1},{3,19},{4,20},{5,6},{6,5},{7,23},{8,24},{9,10},... | collective-permute-start | bytes 175112 | tf_op jit(solution)/shard_map/ppermute | solution.py:25
  13.7 4.3 %collective-permute-start.2 = (bf16[3,38,256]{2,1,0:T(8,128)(2,1)S(1)}, bf16[3,38,256]{2,1,0:T(8,128)(2,1)S(1)}, u32[]{:S(2)}, u32[]{:S(2)}) collective-permute-start(bf16[3,38,256]{2,1,0:T(8,128)(2,1)S(1)} %get-tuple-element.68), channel_id=1, source_target_pairs={{0,1},{1,0},{2,3},{3,2},{4,5},{5,4},{6,7},{7,6},{8,9},{9,8},{10,11... | collective-permute-start | bytes 175112 | tf_op jit(solution)/shard_map/ppermute | solution.py:25
  31.5 2.1 %collective-permute-start.4 = (bf16[1024,256]{1,0:T(8,128)(2,1)}, bf16[1024,256]{1,0:T(8,128)(2,1)S(1)}, u32[]{:S(2)}, u32[]{:S(2)}) collective-permute-start(bf16[1024,256]{1,0:T(8,128)(2,1)} %get-tuple-element.41), channel_id=1, source_target_pairs={{0,1},{1,0},{2,3},{3,2},{4,5},{5,4},{6,7},{7,6},{8,9},{9,8},{10,11... | collective-permute-start | bytes 1572872 | tf_op jit(solution)/shard_map/ppermute | solution.py:25
  33.7 1.0 %copy-start.10 = (f32[1024,256]{1,0:T(8,128)}, f32[1024,256]{1,0:T(8,128)S(1)}, u32[]{:S(2)}) copy-start(f32[1024,256]{1,0:T(8,128)S(1)} %convert_add_fusion) | copy-start | bytes 3145732
  35.4 6.6 %copy-start.11 = (f32[1024,256]{1,0:T(8,128)S(1)}, f32[1024,256]{1,0:T(8,128)}, u32[]{:S(2)}) copy-start(f32[1024,256]{1,0:T(8,128)} %copy-done.10) | copy-start | bytes 3145732
  35.5 6.6 %collective-permute-start.5 = (bf16[512,256]{1,0:T(8,128)(2,1)}, bf16[512,256]{1,0:T(8,128)(2,1)S(1)}, u32[]{:S(2)}, u32[]{:S(2)}) collective-permute-start(bf16[512,256]{1,0:T(8,128)(2,1)} %dynamic-slice_convert_fusion), channel_id=1, source_target_pairs={{0,4},{1,3},{2,6},{3,1},{4,0},{5,7},{6,2},{7,5},{8,12},{9,11},{10,... | collective-permute-start | bytes 786440 | tf_op jit(solution)/shard_map/ppermute | solution.py:25
  42.1 5.0 %collective-permute-start.6 = (bf16[256,256]{1,0:T(8,128)(2,1)S(1)}, bf16[256,256]{1,0:T(8,128)(2,1)S(1)}, u32[]{:S(2)}, u32[]{:S(2)}) collective-permute-start(bf16[256,256]{1,0:T(8,128)(2,1)S(1)} %dynamic-slice_convert_fusion.1), channel_id=1, source_target_pairs={{0,2},{1,5},{2,0},{3,7},{4,6},{5,1},{6,4},{7,3},{8,10},{9,13},{10,... | collective-permute-start | bytes 393224 | tf_op jit(solution)/shard_map/ppermute | solution.py:25
  42.3 5.0 %collective-permute-start.8 = (bf16[32,3,256]{2,1,0:T(4,128)(2,1)S(1)}, bf16[32,3,256]{2,1,0:T(4,128)(2,1)S(1)}, u32[]{:S(2)}, u32[]{:S(2)}) collective-permute-start(bf16[32,3,256]{2,1,0:T(4,128)(2,1)S(1)} %get-tuple-element.75), channel_id=1, source_target_pairs={{0,4},{1,5},{2,6},{3,7},{4,0},{5,1},{6,2},{7,3},{8,12},{9,13},{10,... | collective-permute-start | bytes 147464 | tf_op jit(solution)/shard_map/ppermute | solution.py:25
  42.4 7.5 %collective-permute-start.9 = (bf16[32,3,256]{2,1,0:T(4,128)(2,1)S(1)}, bf16[32,3,256]{2,1,0:T(4,128)(2,1)S(1)}, u32[]{:S(2)}, u32[]{:S(2)}) collective-permute-start(bf16[32,3,256]{2,1,0:T(4,128)(2,1)S(1)} %get-tuple-element.76), channel_id=1, source_target_pairs={{0,28},{1,29},{2,30},{3,31},{4,8},{5,9},{6,10},{7,11},{8,4},{9,5},... | collective-permute-start | bytes 147464 | tf_op jit(solution)/shard_map/ppermute | solution.py:25
  47.2 6.8 %collective-permute-start.7 = (bf16[320,256]{1,0:T(8,128)(2,1)S(1)}, bf16[320,256]{1,0:T(8,128)(2,1)S(1)}, u32[]{:S(2)}, u32[]{:S(2)}) collective-permute-start(bf16[320,256]{1,0:T(8,128)(2,1)S(1)} %pad_maximum_fusion.5), channel_id=1, source_target_pairs={{0,8},{1,17},{2,10},{3,19},{4,12},{5,21},{6,14},{7,23},{8,0},{9,25... | collective-permute-start | bytes 491528 | tf_op jit(solution)/shard_map/ppermute | solution.py:25
  54.1 5.5 %collective-permute-start.12 = (bf16[3,38,256]{2,1,0:T(8,128)(2,1)S(1)}, bf16[3,38,256]{2,1,0:T(8,128)(2,1)S(1)}, u32[]{:S(2)}, u32[]{:S(2)}) collective-permute-start(bf16[3,38,256]{2,1,0:T(8,128)(2,1)S(1)} %reverse_select_fusion), channel_id=1, source_target_pairs={{0,16},{1,2},{2,1},{3,19},{4,20},{5,6},{6,5},{7,23},{8,24},{9,10},... | collective-permute-start | bytes 175112 | tf_op jit(solution)/shard_map/ppermute | solution.py:25
  54.8 4.8 %collective-permute-start.11 = (bf16[3,38,256]{2,1,0:T(8,128)(2,1)S(1)}, bf16[3,38,256]{2,1,0:T(8,128)(2,1)S(1)}, u32[]{:S(2)}, u32[]{:S(2)}) collective-permute-start(bf16[3,38,256]{2,1,0:T(8,128)(2,1)S(1)} %get-tuple-element.72), channel_id=1, source_target_pairs={{0,1},{1,0},{2,3},{3,2},{4,5},{5,4},{6,7},{7,6},{8,9},{9,8},{10,11... | collective-permute-start | bytes 175112 | tf_op jit(solution)/shard_map/ppermute | solution.py:25
  55.0 6.4 %collective-permute-start.10 = (bf16[320,256]{1,0:T(8,128)(2,1)S(1)}, bf16[320,256]{1,0:T(8,128)(2,1)S(1)}, u32[]{:S(2)}, u32[]{:S(2)}) collective-permute-start(bf16[320,256]{1,0:T(8,128)(2,1)S(1)} %add_convert_fusion.1), channel_id=1, source_target_pairs={{0,16},{1,9},{2,18},{3,11},{4,20},{5,13},{6,22},{7,15},{8,24},{9,1... | collective-permute-start | bytes 491528 | tf_op jit(solution)/shard_map/ppermute | solution.py:25
  61.5 5.4 %collective-permute-start.13 = (bf16[320,256]{1,0:T(8,128)(2,1)S(1)}, bf16[320,256]{1,0:T(8,128)(2,1)S(1)}, u32[]{:S(2)}, u32[]{:S(2)}) collective-permute-start(bf16[320,256]{1,0:T(8,128)(2,1)S(1)} %add_convert_fusion), channel_id=1, source_target_pairs={{0,2},{1,5},{2,0},{3,7},{4,6},{5,1},{6,4},{7,3},{8,10},{9,13},{10,... | collective-permute-start | bytes 491528 | tf_op jit(solution)/shard_map/ppermute | solution.py:25
  67.0 6.8 %collective-permute-start.14 = (bf16[576,256]{1,0:T(8,128)(2,1)S(1)}, bf16[576,256]{1,0:T(8,128)(2,1)S(1)}, u32[]{:S(2)}, u32[]{:S(2)}) collective-permute-start(bf16[576,256]{1,0:T(8,128)(2,1)S(1)} %pad_maximum_fusion.4), channel_id=1, source_target_pairs={{0,4},{1,3},{2,6},{3,1},{4,0},{5,7},{6,2},{7,5},{8,12},{9,11},{10,... | collective-permute-start | bytes 884744 | tf_op jit(solution)/shard_map/ppermute | solution.py:25
  73.9 2.0 %collective-permute-start.15 = (bf16[1088,256]{1,0:T(8,128)(2,1)S(1)}, bf16[1088,256]{1,0:T(8,128)(2,1)S(1)}, u32[]{:S(2)}, u32[]{:S(2)}) collective-permute-start(bf16[1088,256]{1,0:T(8,128)(2,1)S(1)} %pad_maximum_fusion.3.mine_ref), channel_id=1, source_target_pairs={{0,1},{1,0},{2,3},{3,2},{4,5},{5,4},{6,7},{7,6},{8,9},{9,8},{10,11... | collective-permute-start | bytes 1671176 | tf_op jit(solution)/shard_map/ppermute | solution.py:25

commit v4 on v3

v4 whole, which is shorter than its diff:
```python
import functools
import math

import jax
import jax.numpy as jnp
from jax import lax
from jax.experimental import pallas as pl
from jax.experimental.pallas import tpu as pltpu
from jax.sharding import PartitionSpec as P

EPS = 1e-06


def flat_pairs(target):
    lons, lats = lax.axis_size("lon"), lax.axis_size("lat")
    pairs = []
    for lon in range(lons):
        for lat in range(lats):
            to_lon, to_lat = target(lon, lat)
            pairs.append((lon * lats + lat, to_lon * lats + to_lat))
    return pairs


def send(value, target):
    return lax.ppermute(value, ("lon", "lat"), flat_pairs(target))


def lon_margins(field):
    lons = lax.axis_size("lon")
    odd = lax.axis_index("lon") % 2 == 1
    first, last = field[:, :3], field[:, -3:]
    outer = send(
        jnp.where(odd, last, first),
        lambda lon, lat: ((lon + 1) % lons if lon % 2 else (lon - 1) % lons, lat),
    )
    inner = send(jnp.where(odd, first, last), lambda lon, lat: (lon ^ 1, lat))
    west = jnp.where(odd, inner, outer)
    east = jnp.where(odd, outer, inner)
    return jnp.concatenate([west, field, east], axis=1)


def lat_margins(wide):
    lons, lats = lax.axis_size("lon"), lax.axis_size("lat")
    lat = lax.axis_index("lat")
    odd = lat % 2 == 1
    pole = (lat == 0) | (lat == lats - 1)
    first, last = wide[:3], wide[-3:]

    def beyond(lon, lat):
        if lat == 0 or lat == lats - 1:
            return ((lon + lons // 2) % lons, lat)
        return (lon, lat + 1 if lat % 2 else lat - 1)

    outgoing = jnp.where(odd, last, first)
    outgoing = jnp.where(pole, outgoing[::-1], outgoing)
    far = send(outgoing, beyond)
    near = send(jnp.where(odd, first, last), lambda lon, lat: (lon, lat ^ 1))
    north = jnp.where(odd, near, far)
    south = jnp.where(odd, far, near)
    return north, south


def axis_bits():
    lon_bits = [("lon", bit) for bit in range((lax.axis_size("lon") - 1).bit_length())]
    lat_bits = [("lat", bit) for bit in range(1, (lax.axis_size("lat") - 1).bit_length())]
    steps = []
    while lon_bits or lat_bits:
        if lon_bits:
            steps.append(lon_bits.pop(0))
        if lat_bits:
            steps.append(lat_bits.pop(0))
    return steps


def flip(place, step):
    lon, lat = place
    axis, bit = step
    return (lon ^ (1 << bit), lat) if axis == "lon" else (lon, lat ^ (1 << bit))


def partner_steps():
    core = lax.axis_index("lat") % 2
    steps = axis_bits()
    other = list(steps)
    for at in range(0, len(steps) - 1, 2):
        other[at], other[at + 1] = other[at + 1], other[at]

    def exchange(value, at):
        return send(value, lambda lon, lat: flip((lon, lat), (other if lat % 2 else steps)[at]))

    def order(first):
        high, low = (
            lax.shift_right_logical(lax.axis_index(axis), bit) & 1 for axis, bit in first[:2]
        )
        return 2 * high + low

    own, pair = order(steps), order(other)
    place = jnp.stack([core, jnp.where(core == 0, own, pair), jnp.where(core == 0, pair, own)])
    return len(steps), exchange, place.astype(jnp.int32)


def within_pair(value):
    return send(value, lambda lon, lat: (lon, lat ^ 1))


def halves(held, got):
    half = held.shape[0] // 2
    mine = held[:half] + got[:half].astype(jnp.float32)
    return mine, (held[half:] + got[half:].astype(jnp.float32)).astype(jnp.bfloat16)


def rounded_sum(left, right):
    return (left.astype(jnp.float32) + right.astype(jnp.float32)).astype(jnp.bfloat16)


def gelu_parts(values):
    normal_cdf = 0.5 * (1.0 + jax.scipy.special.erf(values * (1.0 / math.sqrt(2.0))))
    density = jnp.exp(-0.5 * values * values) * (1.0 / math.sqrt(2.0 * math.pi))
    return (values * normal_cdf, normal_cdf + values * density)


LANES = 128
SUBLANES = 8


def slot_rows(ref, lane, row, start, count):
    return ref[lane, row, pl.ds(start, SUBLANES, stride=count), :]


def spread_weights(weight_ref, spread_ref):
    for lane in range(spread_ref.shape[0]):
        for tap in range(49):
            row = weight_ref[tap // 7, tap % 7 : tap % 7 + 1, lane * LANES : (lane + 1) * LANES]
            spread_ref[lane, tap] = jnp.broadcast_to(row.astype(jnp.float32), (SUBLANES, LANES))


def split_lanes(source_ref, wide_ref, start=0, to=0, count=None):
    count = source_ref.shape[0] if count is None else count

    def body(row, carry):
        for lane in range(wide_ref.shape[0]):
            wide_ref[lane, to + row] = source_ref[
                start + row, :, lane * LANES : (lane + 1) * LANES
            ].astype(jnp.float32)
        return carry

    lax.fori_loop(0, count, body, 0)


def split_padded(top_ref, wide_ref, bottom_ref, out_ref):
    split_lanes(top_ref, out_ref)
    split_lanes(wide_ref, out_ref, to=3)
    split_lanes(bottom_ref, out_ref, to=3 + wide_ref.shape[0])


def window_sums(source_ref, lane, start, weight_of):
    slots = (source_ref.shape[2] - 6) // SUBLANES
    totals = [[jnp.zeros((SUBLANES, LANES), jnp.float32)] * slots for unused in range(4)]
    for row in range(10):
        loaded = [
            slot_rows(source_ref, lane, start + row, place, slots) for place in range(slots + 6)
        ]
        for row_off in range(7):
            to = row - row_off
            if 0 <= to < 4:
                for col_off in range(7):
                    weight = weight_of(row, row_off, col_off)
                    for slot in range(slots):
                        totals[to][slot] = totals[to][slot] + weight * loaded[slot + col_off]
    return totals


def store_sums(totals, out_ref, lane, start):
    slots = len(totals[0])
    for to in range(4):
        for slot in range(slots):
            out_ref[lane, start + to, pl.ds(slot, SUBLANES, stride=slots), :] = totals[to][slot]


def inner_conv_kernel(wide_ref, dw_ref, out_ref, split_ref, spread_ref):
    tiles, rows = out_ref.shape[0], out_ref.shape[1]
    spread_weights(dw_ref, spread_ref)
    split_lanes(wide_ref, split_ref)

    def body(at, carry):
        lane, start = at // (rows // 4), (at % (rows // 4)) * 4
        totals = window_sums(
            split_ref, lane, start + 1, lambda row, row_off, col_off: spread_ref[lane, row_off * 7 + col_off]
        )
        store_sums(totals, out_ref, lane, start)
        return carry

    lax.fori_loop(0, tiles * (rows // 4), body, 0)


def inner_conv(wide, dw_kernel):
    rows, chans = wide.shape[0], wide.shape[2]
    cols = wide.shape[1] - 6
    tiles = chans // LANES
    return pl.pallas_call(
        inner_conv_kernel,
        out_shape=jax.ShapeDtypeStruct((tiles, rows - 8, cols, LANES), jnp.float32),
        in_specs=[pl.BlockSpec(memory_space=pltpu.VMEM)] * 2,
        out_specs=pl.BlockSpec(memory_space=pltpu.VMEM),
        scratch_shapes=[
            pltpu.VMEM((tiles,) + wide.shape[:2] + (LANES,), jnp.float32),
            pltpu.VMEM((tiles, 49, SUBLANES, LANES), jnp.float32),
        ],
        compiler_params=pltpu.CompilerParams(vmem_limit_bytes=6 << 20),
        cost_estimate=pl.CostEstimate(
            flops=98 * rows * cols * chans, bytes_accessed=2 << 20, transcendentals=0
        ),
        name="block_inner_conv",
    )(wide, dw_kernel)


def main_kernel(
    scale_factor,
    place_ref,
    top_ref,
    wide_ref,
    bottom_ref,
    inner_ref,
    fields_ref,
    cot_ref,
    dw_ref,
    dw_bias_ref,
    gain_ref,
    offset_ref,
    b_project_ref,
    b_expand_ref,
    w_expand_ref,
    w_project_ref,
    out_ref,
    dconv_ref,
    keep_ref,
    give_ref,
    small_ref,
    split_ref,
    spread_ref,
    edge_ref,
    expand_ref,
    project_ref,
):
    tiles, inner_rows, cols = inner_ref.shape[:3]
    rows = inner_rows + 8
    chans = tiles * LANES
    hidden_units = w_expand_ref.shape[1]
    pieces = hidden_units // chans
    spread_weights(dw_ref, spread_ref)
    split_lanes(top_ref, split_ref)
    split_lanes(wide_ref, split_ref, to=3, count=7)
    split_lanes(wide_ref, split_ref, start=rows - 7, to=10, count=7)
    split_lanes(bottom_ref, split_ref, to=17)

    def conv_edge(at, carry):
        lane, side = at // 2, at % 2
        totals = window_sums(
            split_ref,
            lane,
            side * 10,
            lambda row, row_off, col_off: spread_ref[lane, row_off * 7 + col_off],
        )
        store_sums(totals, edge_ref, lane, side * 4)
        return carry

    lax.fori_loop(0, tiles * 2, conv_edge, 0)
    small_ref[...] = jnp.zeros_like(small_ref)
    dw_bias, gain, offset, b_project = (
        ref[...].astype(jnp.float32).reshape(1, chans)
        for ref in (dw_bias_ref, gain_ref, offset_ref, b_project_ref)
    )
    b_expand = b_expand_ref[...].astype(jnp.float32).reshape(1, hidden_units)

    conv = jnp.concatenate(
        [
            jnp.concatenate(
                [edge_ref[lane, :4], inner_ref[lane], edge_ref[lane, 4:]], axis=0
            ).reshape(rows * cols, LANES)
            for lane in range(tiles)
        ],
        axis=1,
    )
    conv = conv + dw_bias
    removed = conv - jnp.mean(conv, axis=-1, keepdims=True)
    deviation = lax.rsqrt(jnp.mean(removed * removed, axis=-1, keepdims=True) + EPS)
    xhat = removed * deviation
    normed = (xhat * gain + offset).astype(jnp.bfloat16)
    cot = cot_ref[...]
    branch = jnp.zeros((rows * cols, chans), jnp.float32)
    d_normed = jnp.zeros((rows * cols, chans), jnp.float32)
    for piece in range(pieces):
        part = slice(piece * chans, (piece + 1) * chans)
        w_in = w_expand_ref[:, part]
        w_out = w_project_ref[part, :]
        pre = jnp.dot(normed, w_in, preferred_element_type=jnp.float32)
        pre = pre + b_expand[:, part]
        active, slope = gelu_parts(pre)
        hidden = active.astype(jnp.bfloat16)
        branch = branch + jnp.dot(hidden, w_out, preferred_element_type=jnp.float32)
        d_hidden = contract(cot, w_out, 1, 1)
        d_pre_wide = d_hidden * slope
        d_pre = d_pre_wide.astype(jnp.bfloat16)
        project_ref[part, :] = contract(hidden, cot, 0, 0)
        expand_ref[part, :] = contract(normed, d_pre, 0, 0)
        small_ref[8 + piece : 9 + piece] = jnp.sum(
            d_pre.astype(jnp.float32), axis=0, keepdims=True
        )
        d_normed = d_normed + contract(d_pre, w_in, 1, 1)
    plain = fields_ref[...].astype(jnp.float32)
    out_ref[...] = (plain + (branch + b_project)).astype(jnp.bfloat16)
    small_ref[0:1] = jnp.sum(d_normed * xhat, axis=0, keepdims=True)
    small_ref[1:2] = jnp.sum(d_normed, axis=0, keepdims=True)
    small_ref[2:3] = jnp.sum(cot.astype(jnp.float32), axis=0, keepdims=True)
    scaled = d_normed * gain
    d_conv = deviation * (
        scaled
        - jnp.mean(scaled, axis=-1, keepdims=True)
        - xhat * jnp.mean(scaled * xhat, axis=-1, keepdims=True)
    )
    d_conv = d_conv.astype(jnp.bfloat16)
    dconv_ref[...] = d_conv
    small_ref[...] = small_ref[...] * scale_factor
    quarter = hidden_units // 4

    def finish(mine, other):
        for at in range(4):
            part = slice(at * quarter, (at + 1) * quarter)
            here = pl.multiple_of((at ^ place_ref[1]) * quarter, quarter)
            there = pl.multiple_of((at ^ place_ref[2]) * quarter, quarter)
            keep_ref[pl.ds(here, quarter)] = mine[part] * scale_factor
            give_ref[pl.ds(there, quarter)] = (other[part] * scale_factor).astype(jnp.bfloat16)

    @pl.when(place_ref[0] == 0)
    def first():
        finish(expand_ref, project_ref)

    @pl.when(place_ref[0] != 0)
    def second():
        finish(project_ref, expand_ref)


def contract(left, right, left_dim, right_dim):
    return lax.dot_general(
        left,
        right,
        (((left_dim,), (right_dim,)), ((), ())),
        preferred_element_type=jnp.float32,
    )


def main_pass(
    place, top, wide, bottom, inner, fields, cot, dw_kernel, vectors, w_expand, w_project, scale_factor
):
    rows, cols = wide.shape[0], wide.shape[1] - 6
    chans = fields.shape[1]
    hidden_units = w_expand.shape[1]
    tiles = chans // LANES
    cells = rows * cols
    return pl.pallas_call(
        functools.partial(main_kernel, scale_factor),
        out_shape=[
            jax.ShapeDtypeStruct((cells, chans), jnp.bfloat16),
            jax.ShapeDtypeStruct((cells, chans), jnp.bfloat16),
            jax.ShapeDtypeStruct((hidden_units, chans), jnp.float32),
            jax.ShapeDtypeStruct((hidden_units, chans), jnp.bfloat16),
            jax.ShapeDtypeStruct((8 + hidden_units // chans, chans), jnp.float32),
        ],
        in_specs=[pl.BlockSpec(memory_space=pltpu.SMEM)]
        + [pl.BlockSpec(memory_space=pltpu.VMEM)] * 14,
        out_specs=[pl.BlockSpec(memory_space=pltpu.VMEM)] * 5,
        scratch_shapes=[
            pltpu.VMEM((tiles, 20, wide.shape[1], LANES), jnp.float32),
            pltpu.VMEM((tiles, 49, SUBLANES, LANES), jnp.float32),
            pltpu.VMEM((tiles, 8, cols, LANES), jnp.float32),
            pltpu.VMEM((hidden_units, chans), jnp.float32),
            pltpu.VMEM((hidden_units, chans), jnp.float32),
        ],
        compiler_params=pltpu.CompilerParams(vmem_limit_bytes=28 << 20),
        cost_estimate=pl.CostEstimate(
            flops=12 * cells * chans * hidden_units,
            bytes_accessed=8 << 20,
            transcendentals=2 * cells * hidden_units,
        ),
        name="block_main",
    )(place, top, wide, bottom, inner, fields, cot, dw_kernel, *vectors, w_expand, w_project)


def taps_kernel(
    scale_factor,
    top_ref,
    band_ref,
    bottom_ref,
    dconv_ref,
    small_ref,
    out_ref,
    wide_ref,
    dwide_ref,
    sums_ref,
):
    tiles, rows, cols = dwide_ref.shape[0], dwide_ref.shape[1], dwide_ref.shape[2]
    slots = cols // SUBLANES
    split_padded(top_ref, band_ref, bottom_ref, wide_ref)
    split_lanes(dconv_ref, dwide_ref)
    sums_ref[...] = jnp.zeros_like(sums_ref)
    for lane in range(tiles):
        lanes = slice(lane * LANES, (lane + 1) * LANES)
        for row_off in range(7):

            def kernel_row(row, totals):
                grads = [slot_rows(dwide_ref, lane, row, slot, slots) for slot in range(slots)]
                loaded = [
                    slot_rows(wide_ref, lane, row + row_off, place, slots)
                    for place in range(slots + 6)
                ]
                sums = [
                    totals[col_off] + sum(grads[slot] * loaded[slot + col_off] for slot in range(slots))
                    for col_off in range(7)
                ]
                if row_off == 0:
                    sums.append(totals[7] + sum(grads))
                return tuple(sums)

            count = 8 if row_off == 0 else 7
            zeros = tuple(jnp.zeros((SUBLANES, LANES), jnp.float32) for unused in range(count))
            totals = lax.fori_loop(0, rows, kernel_row, zeros, unroll=4)
            for col_off in range(count):
                tap = row_off * 7 + col_off if col_off < 7 else 49
                sums_ref[tap : tap + 1, lanes] = jnp.sum(totals[col_off], axis=0, keepdims=True)
    sums_ref[...] = sums_ref[...] * scale_factor
    pieces = small_ref.shape[0] - 8
    sums_ref[50:53] = small_ref[0:3]
    sums_ref[53 : 53 + pieces] = small_ref[8 : 8 + pieces]
    out_ref[...] = sums_ref[...].astype(jnp.bfloat16)


def taps_pass(top, wide, bottom, conv_gradient, small, scale_factor):
    rows, cols, chans = conv_gradient.shape
    tiles = chans // LANES
    height = -(-(45 + small.shape[0]) // 32) * 32
    return pl.pallas_call(
        functools.partial(taps_kernel, scale_factor),
        out_shape=jax.ShapeDtypeStruct((height, chans), jnp.bfloat16),
        in_specs=[pl.BlockSpec(memory_space=pltpu.VMEM)] * 5,
        out_specs=pl.BlockSpec(memory_space=pltpu.VMEM),
        scratch_shapes=[
            pltpu.VMEM((tiles, rows + 6, cols + 6, LANES), jnp.float32),
            pltpu.VMEM((tiles, rows, cols, LANES), jnp.float32),
            pltpu.VMEM((height, chans), jnp.float32),
        ],
        compiler_params=pltpu.CompilerParams(vmem_limit_bytes=6 << 20),
        cost_estimate=pl.CostEstimate(
            flops=98 * rows * cols * chans, bytes_accessed=3 << 20, transcendentals=0
        ),
        name="block_taps",
    )(top, wide, bottom, conv_gradient, small)


def finish_kernel(
    place_ref,
    mine_ref,
    got_ref,
    kern_ref,
    dwb_ref,
    gain_ref,
    shift_ref,
    expand_ref,
    b_expand_ref,
    project_ref,
    b_project_ref,
    sums_ref,
):
    hidden_units, chans = project_ref.shape
    pieces = hidden_units // chans
    small = slice(hidden_units, mine_ref.shape[0])
    sums_ref[...] = mine_ref[small].astype(jnp.float32) + got_ref[small].astype(jnp.float32)
    for row_off in range(7):
        kern_ref[row_off] = sums_ref[row_off * 7 : row_off * 7 + 7]
    dwb_ref[...] = sums_ref[49]
    gain_ref[...] = sums_ref[50]
    shift_ref[...] = sums_ref[51]
    b_project_ref[...] = sums_ref[52]
    for piece in range(pieces):
        b_expand_ref[piece * chans : (piece + 1) * chans] = sums_ref[53 + piece]

    def write(first_ref, first_order, second_ref, second_order):
        for at in range(pieces):
            part = slice(at * chans, (at + 1) * chans)
            columns = pl.multiple_of((at ^ first_order) * chans, chans)
            expand_ref[:, pl.ds(columns, chans)] = first_ref[part].astype(jnp.float32)
            to = pl.multiple_of((at ^ second_order) * chans, chans)
            project_ref[pl.ds(to, chans)] = second_ref[part].astype(jnp.float32)

    @pl.when(place_ref[0] == 0)
    def first():
        write(mine_ref, place_ref[1], got_ref, place_ref[2])

    @pl.when(place_ref[0] != 0)
    def second():
        write(got_ref, place_ref[2], mine_ref, place_ref[1])


def finish_pass(place, mine, got, hidden_units):
    chans = mine.shape[1]
    one = jax.ShapeDtypeStruct((chans,), jnp.float32)
    return pl.pallas_call(
        finish_kernel,
        out_shape=[
            jax.ShapeDtypeStruct((7, 7, chans), jnp.float32),
            one,
            one,
            one,
            jax.ShapeDtypeStruct((chans, hidden_units), jnp.float32),
            jax.ShapeDtypeStruct((hidden_units,), jnp.float32),
            jax.ShapeDtypeStruct((hidden_units, chans), jnp.float32),
            one,
        ],
        in_specs=[pl.BlockSpec(memory_space=pltpu.SMEM)]
        + [pl.BlockSpec(memory_space=pltpu.VMEM)] * 2,
        out_specs=[pl.BlockSpec(memory_space=pltpu.VMEM)] * 8,
        scratch_shapes=[pltpu.VMEM((mine.shape[0] - hidden_units, chans), jnp.float32)],
        compiler_params=pltpu.CompilerParams(vmem_limit_bytes=8 << 20),
        name="block_finish",
    )(place, mine, got)


def adjoint_kernel(
    poles_ref,
    top_ref,
    band_ref,
    bottom_ref,
    cot_ref,
    dw_ref,
    out_ref,
    wide_ref,
    spread_ref,
    edge_ref,
    sum_ref,
):
    tiles = wide_ref.shape[0]
    rows = sum_ref.shape[1]
    spread_weights(dw_ref, spread_ref)
    split_padded(top_ref, band_ref, bottom_ref, wide_ref)
    for side in range(2):
        at_pole = poles_ref[side] == 1
        for lane in range(tiles):
            for row_off in range(3):
                near = row_off if side == 0 else 6 - row_off
                for col_off in range(7):
                    plain = spread_ref[lane, (6 - near) * 7 + col_off]
                    turned = spread_ref[lane, near * 7 + col_off]
                    edge_ref[side, lane, row_off * 7 + col_off] = jnp.where(at_pole, turned, plain)

    def block_of(lane, start, first, last):
        def weight_of(row, row_off, col_off):
            if first and row < 3:
                return edge_ref[0, lane, row_off * 7 + 6 - col_off]
            if last and row >= 7:
                return edge_ref[1, lane, (6 - row_off) * 7 + 6 - col_off]
            return spread_ref[lane, (6 - row_off) * 7 + 6 - col_off]

        store_sums(window_sums(wide_ref, lane, start, weight_of), sum_ref, lane, start)

    inner = rows // 4 - 2

    def inner_block(at, carry):
        block_of(at // inner, (1 + at % inner) * 4, False, False)
        return carry

    def edge_block(lane, carry):
        block_of(lane, 0, True, False)
        block_of(lane, rows - 4, False, True)
        return carry

    lax.fori_loop(0, tiles * inner, inner_block, 0)
    lax.fori_loop(0, tiles, edge_block, 0)

    def finish(row, carry):
        total = jnp.concatenate([sum_ref[lane, row] for lane in range(tiles)], axis=1)
        out_ref[row] = (cot_ref[row].astype(jnp.float32) + total).astype(jnp.bfloat16)
        return carry

    lax.fori_loop(0, rows, finish, 0)


def adjoint_pass(top, wide, bottom, cot, dw_kernel, poles):
    rows, cols, chans = cot.shape
    tiles = chans // LANES
    return pl.pallas_call(
        adjoint_kernel,
        out_shape=jax.ShapeDtypeStruct(cot.shape, jnp.bfloat16),
        in_specs=[pl.BlockSpec(memory_space=pltpu.SMEM)]
        + [pl.BlockSpec(memory_space=pltpu.VMEM)] * 5,
        out_specs=pl.BlockSpec(memory_space=pltpu.VMEM),
        scratch_shapes=[
            pltpu.VMEM((tiles, rows + 6, cols + 6, LANES), jnp.float32),
            pltpu.VMEM((tiles, 49, SUBLANES, LANES), jnp.float32),
            pltpu.VMEM((2, tiles, 21, SUBLANES, LANES), jnp.float32),
            pltpu.VMEM((tiles, rows, cols, LANES), jnp.float32),
        ],
        compiler_params=pltpu.CompilerParams(vmem_limit_bytes=6 << 20),
        cost_estimate=pl.CostEstimate(
            flops=98 * rows * cols * chans, bytes_accessed=3 << 20, transcendentals=0
        ),
        name="block_adjoint",
    )(poles, top, wide, bottom, cot, dw_kernel)


def local(
    fields,
    cotangent,
    dw_kernel,
    dw_bias,
    norm_gain,
    layer_norm_offset,
    w_expand,
    b_expand,
    w_project,
    b_project,
):
    rows = fields.shape[0]
    cols = fields.shape[1]
    chans = fields.shape[2]
    scale_factor = 1.0 / math.sqrt(rows * cols * lax.axis_size("lat") * lax.axis_size("lon"))
    hidden_units = w_expand.shape[1]
    lat = lax.axis_index("lat")
    poles = jnp.stack([lat == 0, lat == lax.axis_size("lat") - 1]).astype(jnp.int32)
    count, exchange, place = partner_steps()
    wide = lon_margins(fields)
    inner = inner_conv(wide, dw_kernel)
    edges = lat_margins(wide)
    block_out, conv_gradient, keep, give, small = main_pass(
        place,
        edges[0],
        wide,
        edges[1],
        inner,
        fields.reshape(-1, chans),
        cotangent.reshape(-1, chans),
        dw_kernel,
        (dw_bias, norm_gain, layer_norm_offset, b_project, b_expand),
        w_expand,
        w_project,
        scale_factor,
    )
    block_out = block_out.reshape(fields.shape)
    conv_gradient = conv_gradient.reshape(fields.shape)
    barrier = lax.optimization_barrier
    mine, outgoing = halves(keep, within_pair(give))
    outgoing, taps_in = barrier((outgoing, conv_gradient))
    got = exchange(outgoing, 0)
    small = taps_pass(edges[0], wide, edges[1], taps_in, small, scale_factor)
    got, small, conv_gradient = barrier((got, small, conv_gradient))
    mine, outgoing = halves(mine, got)
    outgoing, conv_gradient = barrier((outgoing, conv_gradient))
    got = exchange(outgoing, 1)
    wide = lon_margins(conv_gradient)
    payload = (mine + got.astype(jnp.float32)).astype(jnp.bfloat16)
    payload = jnp.concatenate([payload, small], axis=0)
    for at in range(2, count):
        got = exchange(payload, at)
        if at == 2:
            got, wide = barrier((got, wide))
            top, bottom = lat_margins(wide)
        payload = rounded_sum(payload, got)
    if count > 2:
        payload, top, bottom = barrier((payload, top, bottom))
    else:
        top, bottom = lat_margins(wide)
    for at in (1, 0):
        if at == 0:
            payload, top, wide, bottom = barrier((payload, top, wide, bottom))
            grad_fields = adjoint_pass(top, wide, bottom, cotangent, dw_kernel, poles)
        got = exchange(payload, at)
        if at == 0:
            got, grad_fields = barrier((got, grad_fields))
        own = payload.shape[0] - small.shape[0]
        payload = jnp.concatenate(
            [payload[:own], got[:own], rounded_sum(payload[own:], got[own:])], axis=0
        )
    sum_kern, sum_dwb, sum_gn, sum_sh, sum_exp, sum_bexp, sum_proj, sum_bproj = finish_pass(
        place, payload, within_pair(payload), hidden_units
    )
    return (
        block_out,
        grad_fields,
        sum_kern,
        sum_dwb,
        sum_gn,
        sum_sh,
        sum_exp,
        sum_bexp,
        sum_proj,
        sum_bproj,
    )


def solution(mesh):
    placed = (P("lat", "lon", None), P("lat", "lon", None), P(), P(), P(), P(), P(), P(), P(), P())
    return jax.shard_map(
        local,
        mesh=mesh,
        in_specs=placed,
        out_specs=(
            P("lat", "lon", None),
            P("lat", "lon", None),
            P(),
            P(),
            P(),
            P(),
            P(),
            P(),
            P(),
            P(),
        ),
        check_vma=False,
    )
```

time: 78.4 us -> 72.8 us (0.929); the launches traced: 77.4 us -> 72.6 us
  Pallas kernels: 25 us -> 23.3 us
  local copies, waits for them, and re-layouts: 1.78 us -> 0.12 us
  waiting for transfers between devices: 28.2 us -> 26.6 us
    pallas_call x1, Pallas kernels: 13 us -> 7.5 us  [main_pass(): pl.pallas_call(functools.partial(main_kernel, scale_factor), out_shape=[j...]
    pallas_call x0 -> x1, Pallas kernels: none -> 3.26 us  [inner_conv(): pl.pallas_call(inner_conv_kernel, out_shape=jax.ShapeDtypeStruct((tiles,...]
    ppermute x16, waiting for transfers between devices: 28.2 us -> 26.6 us  [send(): return lax.ppermute(value, ('lon', 'lat'), flat_pairs(target))]
    concatenate x1 -> x2, other arithmetic: 0.4 us -> 1.8 us  [lon_margins(): return jnp.concatenate([west, field, east], axis=1)]
    unnamed x24 -> x20, local copies, waits for them, and re-layouts: 1.03 us -> 0.06 us
    select_n x4 -> x0, other arithmetic: 0.96 us -> none  [the longest x1 0.88 us: lat_margins(): near = send(jnp.where(odd, first, last), lambda lon, lat: (lon, lat ^ 1))]
  transfers between devices with their start and end apart: 16 -> 16, of which waited for: 12 -> 11; matrix products, arithmetic and copies ran while one was open for 1% -> 1% of each run, Pallas kernels for 14% -> 19%
where the time goes in v4:
time: 72.8 us; the launch traced here: 72.6 us
  waiting for transfers between devices  26.6 us (37%)
  Pallas kernels  23.3 us (32%)
  starting transfers between devices  17.9 us (25%)
  other arithmetic  3.68 us (5%)
  between operations  0.96 us (1%)
    ppermute x16, waiting for transfers between devices, send(): return lax.ppermute(value, ('lon', 'lat'), flat_pairs(target))  26.6 us
    ppermute x16, starting transfers between devices, send(): return lax.ppermute(value, ('lon', 'lat'), flat_pairs(target))  17.9 us
    pallas_call x1, Pallas kernels, main_pass(): pl.pallas_call(functools.partial(main_kernel, scale_factor), out_shape=[j...  7.5 us
    pallas_call x1, Pallas kernels, adjoint_pass(): pl.pallas_call(adjoint_kernel, out_shape=jax.ShapeDtypeStruct(cot.shape,...  5.94 us
    pallas_call x1, Pallas kernels, taps_pass(): pl.pallas_call(functools.partial(taps_kernel, scale_factor), out_shape=ja...  4.55 us
    pallas_call x1, Pallas kernels, inner_conv(): pl.pallas_call(inner_conv_kernel, out_shape=jax.ShapeDtypeStruct((tiles,...  3.26 us
    pallas_call x1, Pallas kernels, finish_pass(): pl.pallas_call(finish_kernel, out_shape=[jax.ShapeDtypeStruct((7, 7, chan...  2.06 us
    concatenate x2, other arithmetic, lon_margins(): return jnp.concatenate([west, field, east], axis=1)  1.8 us
  transfers between devices with their start and end apart: 16, of which 11 were waited for; matrix products, arithmetic and copies ran while one was open for 1% of the time, Pallas kernels for 19%

profile of v4, /device:TPU:0, one launch (start us, length us, event | category | flops | bytes accessed | tf_op | source)
XLA Modules:
  0.0 72.6 jit_solution(2426735791065274783)
XLA Ops:
  0.7 1.0 %broadcast_select_fusion.7 = (bf16[32,3,256]{2,1,0:T(4,128)(2,1)S(1)}, bf16[32,3,256]{2,1,0:T(4,128)(2,1)S(1)}) fusion(pred[]{:T(512)S(6)} %eq.30, bf16[32,32,256]{2,1,0:T(8,128)(2,1)} %param.10), kind=kLoop, calls=%fused_computation.25 | loop fusion | flops 49152 | bytes 196609 | tf_op jit(solution)/shard_map/jit(_where)/select_n | solution.py:36
  1.7 3.0 %collective-permute-start = (bf16[32,3,256]{2,1,0:T(4,128)(2,1)S(1)}, bf16[32,3,256]{2,1,0:T(4,128)(2,1)S(1)}, u32[]{:S(2)}, u32[]{:S(2)}) collective-permute-start(bf16[32,3,256]{2,1,0:T(4,128)(2,1)S(1)} %get-tuple-element.80), channel_id=1, source_target_pairs={{0,4},{1,5},{2,6},{3,7},{4,0},{5,1},{6,2},{7,3},{8,12},{9,13},{10,... | collective-permute-start | bytes 147464 | tf_op jit(solution)/shard_map/ppermute | solution.py:25
  4.7 3.6 %collective-permute-start.1 = (bf16[32,3,256]{2,1,0:T(4,128)(2,1)S(1)}, bf16[32,3,256]{2,1,0:T(4,128)(2,1)S(1)}, u32[]{:S(2)}, u32[]{:S(2)}) collective-permute-start(bf16[32,3,256]{2,1,0:T(4,128)(2,1)S(1)} %get-tuple-element.81), channel_id=1, source_target_pairs={{0,28},{1,29},{2,30},{3,31},{4,8},{5,9},{6,10},{7,11},{8,4},{9,5},... | collective-permute-start | bytes 147464 | tf_op jit(solution)/shard_map/ppermute | solution.py:25
  8.3 3.4 %collective-permute-done.1 = bf16[32,3,256]{2,1,0:T(4,128)(2,1)S(1)} collective-permute-done((bf16[32,3,256]{2,1,0:T(4,128)(2,1)S(1)}, bf16[32,3,256]{2,1,0:T(4,128)(2,1)S(1)}, u32[]{:S(2)}, u32[]{:S(2)}) %collective-permute-start.1) | collective-permute-done | bytes 49184 | tf_op jit(solution)/shard_map/ppermute | solution.py:25
  11.7 1.4 %pad_maximum_fusion.wide_ref.band_ref = bf16[32,38,256]{2,1,0:T(8,128)(2,1)S(1)} fusion(bf16[32,3,256]{2,1,0:T(4,128)(2,1)S(1)} %get-tuple-element.85, bf16[32,32,256]{2,1,0:T(8,128)(2,1)} %param.10, bf16[32,3,256]{2,1,0:T(4,128)(2,1)S(1)} %get-tuple-element.84), kind=kLoop, calls=%fused_computation | loop fusion | flops 1867776 | bytes 1245184 | tf_op jit(solution)/shard_map/concatenate | solution.py:39
  13.3 0.9 %collective-permute-start.3 = (bf16[3,38,256]{2,1,0:T(8,128)(2,1)S(1)}, bf16[3,38,256]{2,1,0:T(8,128)(2,1)S(1)}, u32[]{:S(2)}, u32[]{:S(2)}) collective-permute-start(bf16[3,38,256]{2,1,0:T(8,128)(2,1)S(1)} %reverse_select_fusion.1), channel_id=1, source_target_pairs={{0,16},{1,2},{2,1},{3,19},{4,20},{5,6},{6,5},{7,23},{8,24},{9,10},... | collective-permute-start | bytes 175112 | tf_op jit(solution)/shard_map/ppermute | solution.py:25
  14.2 0.8 %collective-permute-start.2 = (bf16[3,38,256]{2,1,0:T(8,128)(2,1)S(1)}, bf16[3,38,256]{2,1,0:T(8,128)(2,1)S(1)}, u32[]{:S(2)}, u32[]{:S(2)}) collective-permute-start(bf16[3,38,256]{2,1,0:T(8,128)(2,1)S(1)} %get-tuple-element.77), channel_id=1, source_target_pairs={{0,1},{1,0},{2,3},{3,2},{4,5},{5,4},{6,7},{7,6},{8,9},{9,8},{10,11... | collective-permute-start | bytes 175112 | tf_op jit(solution)/shard_map/ppermute | solution.py:25
  15.1 3.3 %block_inner_conv.1.inner_ref = f32[2,24,32,128]{3,2,1,0:T(8,128)S(1)} custom-call(bf16[32,38,256]{2,1,0:T(8,128)(2,1)S(1)} %pad_maximum_fusion.wide_ref.band_ref, bf16[7,7,256]{2,1,0:T(8,128)(2,1)S(1)} %copy-done.2), custom_call_target="tpu_custom_call" | custom-call | flops 25690112 | bytes 2097152 | tf_op jit(solution)/shard_map/block_inner_conv/pallas_call | solution.py:200
  18.4 0.1 collective-permute-done.3
  18.6 7.5 %block_main.1 = (bf16[1024,256]{1,0:T(8,128)(2,1)}, bf16[1024,256]{1,0:T(8,128)(2,1)S(1)}, f32[1024,256]{1,0:T(8,128)S(1)}, bf16[1024,256]{1,0:T(8,128)(2,1)S(1)}, f32[12,256]{1,0:T(8,128)S(1)}) custom-call(s32[3]{0:T(128)S(1)} %pad_add_fusion.place_ref, bf16[3,38,256]{2,1,0:T(8,128)(2,1)S(1)} %get-tuple-element.89.top_ref, ...), custom_call_target="tpu_custom_call" | custom-call | flops 3221225472 | bytes 8388608 | tf_op jit(solution)/shard_map/block_main/pallas_call | solution.py:360
  26.1 1.9 %collective-permute-done.4 = bf16[1024,256]{1,0:T(8,128)(2,1)S(1)} collective-permute-done((bf16[1024,256]{1,0:T(8,128)(2,1)S(1)}, bf16[1024,256]{1,0:T(8,128)(2,1)S(1)}, u32[]{:S(2)}, u32[]{:S(2)}) %collective-permute-start.4) | collective-permute-done | bytes 524320 | tf_op jit(solution)/shard_map/ppermute | solution.py:25
  28.0 0.1 convert_add_fusion
  28.2 4.5 %block_taps.1 = bf16[64,256]{1,0:T(8,128)(2,1)S(1)} custom-call(bf16[3,38,256]{2,1,0:T(8,128)(2,1)S(1)} %get-tuple-element.89.top_ref, bf16[32,38,256]{2,1,0:T(8,128)(2,1)S(1)} %pad_maximum_fusion.wide_ref.band_ref, bf16[3,38,256]{2,1,0:T(8,128)(2,1)S(1)} %get-tuple-element.88.bottom_ref, bf16[32,32,256]{2,1,0:T(8,128)(2,1)S(1)} %bitcast.9, ...), custom_call_target="tpu_custom_call" | custom-call | flops 25690112 | bytes 3145728 | tf_op jit(solution)/shard_map/block_taps/pallas_call | solution.py:441
  32.8 1.8 %collective-permute-done.5 = bf16[512,256]{1,0:T(8,128)(2,1)S(1)} collective-permute-done((bf16[512,256]{1,0:T(8,128)(2,1)S(1)}, bf16[512,256]{1,0:T(8,128)(2,1)S(1)}, u32[]{:S(2)}, u32[]{:S(2)}) %collective-permute-start.5) | collective-permute-done | bytes 262176 | tf_op jit(solution)/shard_map/ppermute | solution.py:25
  34.6 0.1 collective-permute-start.6
  34.8 0.3 collective-permute-start.8
  35.1 3.6 %collective-permute-start.9 = (bf16[32,3,256]{2,1,0:T(4,128)(2,1)S(1)}, bf16[32,3,256]{2,1,0:T(4,128)(2,1)S(1)}, u32[]{:S(2)}, u32[]{:S(2)}) collective-permute-start(bf16[32,3,256]{2,1,0:T(4,128)(2,1)S(1)} %get-tuple-element.79), channel_id=1, source_target_pairs={{0,28},{1,29},{2,30},{3,31},{4,8},{5,9},{6,10},{7,11},{8,4},{9,5},... | collective-permute-start | bytes 147464 | tf_op jit(solution)/shard_map/ppermute | solution.py:25
  38.7 1.0 %collective-permute-done.6 = bf16[256,256]{1,0:T(8,128)(2,1)S(1)} collective-permute-done((bf16[256,256]{1,0:T(8,128)(2,1)S(1)}, bf16[256,256]{1,0:T(8,128)(2,1)S(1)}, u32[]{:S(2)}, u32[]{:S(2)}) %collective-permute-start.6) | collective-permute-done | bytes 131104 | tf_op jit(solution)/shard_map/ppermute | solution.py:25
  39.7 1.3 %collective-permute-start.7 = (bf16[320,256]{1,0:T(8,128)(2,1)S(1)}, bf16[320,256]{1,0:T(8,128)(2,1)S(1)}, u32[]{:S(2)}, u32[]{:S(2)}) collective-permute-start(bf16[320,256]{1,0:T(8,128)(2,1)S(1)} %pad_maximum_fusion.4), channel_id=1, source_target_pairs={{0,8},{1,17},{2,10},{3,19},{4,12},{5,21},{6,14},{7,23},{8,0},{9,25... | collective-permute-start | bytes 491528 | tf_op jit(solution)/shard_map/ppermute | solution.py:25
  41.1 1.3 %collective-permute-done.9 = bf16[32,3,256]{2,1,0:T(4,128)(2,1)S(1)} collective-permute-done((bf16[32,3,256]{2,1,0:T(4,128)(2,1)S(1)}, bf16[32,3,256]{2,1,0:T(4,128)(2,1)S(1)}, u32[]{:S(2)}, u32[]{:S(2)}) %collective-permute-start.9) | collective-permute-done | bytes 49184 | tf_op jit(solution)/shard_map/ppermute | solution.py:25
  42.4 0.4 pad_maximum_fusion.1.band_ref
  42.8 3.7 %collective-permute-done.7 = bf16[320,256]{1,0:T(8,128)(2,1)S(1)} collective-permute-done((bf16[320,256]{1,0:T(8,128)(2,1)S(1)}, bf16[320,256]{1,0:T(8,128)(2,1)S(1)}, u32[]{:S(2)}, u32[]{:S(2)}) %collective-permute-start.7) | collective-permute-done | bytes 163872 | tf_op jit(solution)/shard_map/ppermute | solution.py:25
  46.6 0.8 %collective-permute-start.12 = (bf16[3,38,256]{2,1,0:T(8,128)(2,1)S(1)}, bf16[3,38,256]{2,1,0:T(8,128)(2,1)S(1)}, u32[]{:S(2)}, u32[]{:S(2)}) collective-permute-start(bf16[3,38,256]{2,1,0:T(8,128)(2,1)S(1)} %reverse_select_fusion), channel_id=1, source_target_pairs={{0,16},{1,2},{2,1},{3,19},{4,20},{5,6},{6,5},{7,23},{8,24},{9,10},... | collective-permute-start | bytes 175112 | tf_op jit(solution)/shard_map/ppermute | solution.py:25
  47.4 0.4 collective-permute-start.11
  47.8 1.9 %collective-permute-start.10 = (bf16[320,256]{1,0:T(8,128)(2,1)S(1)}, bf16[320,256]{1,0:T(8,128)(2,1)S(1)}, u32[]{:S(2)}, u32[]{:S(2)}) collective-permute-start(bf16[320,256]{1,0:T(8,128)(2,1)S(1)} %add_convert_fusion.2), channel_id=1, source_target_pairs={{0,16},{1,9},{2,18},{3,11},{4,20},{5,13},{6,22},{7,15},{8,24},{9,1... | collective-permute-start | bytes 491528 | tf_op jit(solution)/shard_map/ppermute | solution.py:25
  49.7 2.5 %collective-permute-done.12 = bf16[3,38,256]{2,1,0:T(8,128)(2,1)S(1)} collective-permute-done((bf16[3,38,256]{2,1,0:T(8,128)(2,1)S(1)}, bf16[3,38,256]{2,1,0:T(8,128)(2,1)S(1)}, u32[]{:S(2)}, u32[]{:S(2)}) %collective-permute-start.12) | collective-permute-done | bytes 58400 | tf_op jit(solution)/shard_map/ppermute | solution.py:25
  52.2 3.6 %collective-permute-done.10 = bf16[320,256]{1,0:T(8,128)(2,1)S(1)} collective-permute-done((bf16[320,256]{1,0:T(8,128)(2,1)S(1)}, bf16[320,256]{1,0:T(8,128)(2,1)S(1)}, u32[]{:S(2)}, u32[]{:S(2)}) %collective-permute-start.10) | collective-permute-done | bytes 163872 | tf_op jit(solution)/shard_map/ppermute | solution.py:25
  56.0 5.3 %collective-permute-done.13 = bf16[320,256]{1,0:T(8,128)(2,1)S(1)} collective-permute-done((bf16[320,256]{1,0:T(8,128)(2,1)S(1)}, bf16[320,256]{1,0:T(8,128)(2,1)S(1)}, u32[]{:S(2)}, u32[]{:S(2)}) %collective-permute-start.13) | collective-permute-done | bytes 163872 | tf_op jit(solution)/shard_map/ppermute | solution.py:25
  61.4 1.0 %collective-permute-start.14 = (bf16[576,256]{1,0:T(8,128)(2,1)S(1)}, bf16[576,256]{1,0:T(8,128)(2,1)S(1)}, u32[]{:S(2)}, u32[]{:S(2)}) collective-permute-start(bf16[576,256]{1,0:T(8,128)(2,1)S(1)} %pad_maximum_fusion.3), channel_id=1, source_target_pairs={{0,4},{1,3},{2,6},{3,1},{4,0},{5,7},{6,2},{7,5},{8,12},{9,11},{10,... | collective-permute-start | bytes 884744 | tf_op jit(solution)/shard_map/ppermute | solution.py:25
  62.5 5.9 %block_adjoint.1 = bf16[32,32,256]{2,1,0:T(8,128)(2,1)} custom-call(s32[2]{0:T(128)S(1)} %add_convert_fusion.5.poles_ref, bf16[3,38,256]{2,1,0:T(8,128)(2,1)S(1)} %get-tuple-element.59.top_ref, bf16[32,38,256]{2,1,0:T(8,128)(2,1)S(1)} %pad_maximum_fusion.1.band_ref, bf16[3,38,256]{2,1,0:T(8,128)(2,1)S(1)} %get-tuple-element.61.bottom_ref, ...), custom_call_target="tpu_custom_call" | custom-call | flops 25690112 | bytes 3145728 | tf_op jit(solution)/shard_map/block_adjoint/pallas_call | solution.py:589
  68.6 1.9 %collective-permute-done.15.got_ref = bf16[1088,256]{1,0:T(8,128)(2,1)S(1)} collective-permute-done((bf16[1088,256]{1,0:T(8,128)(2,1)S(1)}, bf16[1088,256]{1,0:T(8,128)(2,1)S(1)}, u32[]{:S(2)}, u32[]{:S(2)}) %collective-permute-start.15) | collective-permute-done | bytes 557088 | tf_op jit(solution)/shard_map/ppermute | solution.py:25
  70.5 2.1 %block_finish.1 = (f32[7,7,256]{2,1,0:T(8,128)}, f32[256]{0:T(256)}, f32[256]{0:T(256)}, f32[256]{0:T(256)}, f32[256,1024]{1,0:T(8,128)}, /*index=5*/f32[1024]{0:T(1024)}, f32[1024,256]{1,0:T(8,128)}, f32[256]{0:T(256)}) custom-call(s32[3]{0:T(128)S(1)} %pad_add_fusion.place_ref, bf16[1088,256]{1,0:T(8,128)(2,1)S(1)} %pad_maximum_fusion.2.mine_ref, ...), custom_call_target="tpu_custom_call" | custom-call | tf_op jit(solution)/shard_map/block_finish/pallas_call | solution.py:506
  (53 shorter events, 1.1 us)
Async XLA Ops:
  1.7 13.4 %copy-start.2 = (bf16[7,7,256]{2,1,0:T(8,128)(2,1)S(1)}, bf16[7,7,256]{2,1,0:T(8,128)(2,1)}, u32[]{:S(2)}) copy-start(bf16[7,7,256]{2,1,0:T(8,128)(2,1)} %dw_ref.5) | copy-start | bytes 75268
  1.7 6.6 %collective-permute-start = (bf16[32,3,256]{2,1,0:T(4,128)(2,1)S(1)}, bf16[32,3,256]{2,1,0:T(4,128)(2,1)S(1)}, u32[]{:S(2)}, u32[]{:S(2)}) collective-permute-start(bf16[32,3,256]{2,1,0:T(4,128)(2,1)S(1)} %get-tuple-element.80), channel_id=1, source_target_pairs={{0,4},{1,5},{2,6},{3,7},{4,0},{5,1},{6,2},{7,3},{8,12},{9,13},{10,... | collective-permute-start | bytes 147464 | tf_op jit(solution)/shard_map/ppermute | solution.py:25
  4.7 7.0 %collective-permute-start.1 = (bf16[32,3,256]{2,1,0:T(4,128)(2,1)S(1)}, bf16[32,3,256]{2,1,0:T(4,128)(2,1)S(1)}, u32[]{:S(2)}, u32[]{:S(2)}) collective-permute-start(bf16[32,3,256]{2,1,0:T(4,128)(2,1)S(1)} %get-tuple-element.81), channel_id=1, source_target_pairs={{0,28},{1,29},{2,30},{3,31},{4,8},{5,9},{6,10},{7,11},{8,4},{9,5},... | collective-permute-start | bytes 147464 | tf_op jit(solution)/shard_map/ppermute | solution.py:25
  13.2 5.4 %copy-start = (bf16[32,32,256]{2,1,0:T(8,128)(2,1)S(1)}, bf16[32,32,256]{2,1,0:T(8,128)(2,1)}, u32[]{:S(2)}) copy-start(bf16[32,32,256]{2,1,0:T(8,128)(2,1)} %param.10) | copy-start | bytes 1572868
  13.2 5.4 %copy-start.1 = (bf16[32,32,256]{2,1,0:T(8,128)(2,1)S(1)}, bf16[32,32,256]{2,1,0:T(8,128)(2,1)}, u32[]{:S(2)}) copy-start(bf16[32,32,256]{2,1,0:T(8,128)(2,1)} %cot_ref.1) | copy-start | bytes 1572868
  13.2 5.4 %copy-start.3 = (bf16[256,1024]{1,0:T(8,128)(2,1)S(1)}, bf16[256,1024]{1,0:T(8,128)(2,1)}, u32[]{:S(2)}) copy-start(bf16[256,1024]{1,0:T(8,128)(2,1)} %w_expand_ref.1) | copy-start | bytes 1572868
  13.2 5.4 %copy-start.4 = (bf16[1024,256]{1,0:T(8,128)(2,1)S(1)}, bf16[1024,256]{1,0:T(8,128)(2,1)}, u32[]{:S(2)}) copy-start(bf16[1024,256]{1,0:T(8,128)(2,1)} %w_project_ref.1) | copy-start | bytes 1572868
  13.2 5.4 %copy-start.5 = (bf16[1024]{0:T(1024)(128)(2,1)S(1)}, bf16[1024]{0:T(1024)(128)(2,1)}, u32[]{:S(2)}) copy-start(bf16[1024]{0:T(1024)(128)(2,1)} %b_expand_ref.1) | copy-start | bytes 6148
  13.2 5.4 %copy-start.6 = (bf16[256]{0:T(256)(128)(2,1)S(1)}, bf16[256]{0:T(256)(128)(2,1)}, u32[]{:S(2)}) copy-start(bf16[256]{0:T(256)(128)(2,1)} %dw_bias_ref.1) | copy-start | bytes 1540
  13.2 5.3 %copy-start.7 = (bf16[256]{0:T(256)(128)(2,1)S(1)}, bf16[256]{0:T(256)(128)(2,1)}, u32[]{:S(2)}) copy-start(bf16[256]{0:T(256)(128)(2,1)} %gain_ref.1) | copy-start | bytes 1540
  13.2 5.3 %copy-start.8 = (bf16[256]{0:T(256)(128)(2,1)S(1)}, bf16[256]{0:T(256)(128)(2,1)}, u32[]{:S(2)}) copy-start(bf16[256]{0:T(256)(128)(2,1)} %offset_ref.1) | copy-start | bytes 1540
  13.2 5.3 %copy-start.9 = (bf16[256]{0:T(256)(128)(2,1)S(1)}, bf16[256]{0:T(256)(128)(2,1)}, u32[]{:S(2)}) copy-start(bf16[256]{0:T(256)(128)(2,1)} %b_project_ref.1) | copy-start | bytes 1540
  13.3 5.2 %collective-permute-start.3 = (bf16[3,38,256]{2,1,0:T(8,128)(2,1)S(1)}, bf16[3,38,256]{2,1,0:T(8,128)(2,1)S(1)}, u32[]{:S(2)}, u32[]{:S(2)}) collective-permute-start(bf16[3,38,256]{2,1,0:T(8,128)(2,1)S(1)} %reverse_select_fusion.1), channel_id=1, source_target_pairs={{0,16},{1,2},{2,1},{3,19},{4,20},{5,6},{6,5},{7,23},{8,24},{9,10},... | collective-permute-start | bytes 175112 | tf_op jit(solution)/shard_map/ppermute | solution.py:25
  14.2 4.3 %collective-permute-start.2 = (bf16[3,38,256]{2,1,0:T(8,128)(2,1)S(1)}, bf16[3,38,256]{2,1,0:T(8,128)(2,1)S(1)}, u32[]{:S(2)}, u32[]{:S(2)}) collective-permute-start(bf16[3,38,256]{2,1,0:T(8,128)(2,1)S(1)} %get-tuple-element.77), channel_id=1, source_target_pairs={{0,1},{1,0},{2,3},{3,2},{4,5},{5,4},{6,7},{7,6},{8,9},{9,8},{10,11... | collective-permute-start | bytes 175112 | tf_op jit(solution)/shard_map/ppermute | solution.py:25
  26.1 1.9 %collective-permute-start.4 = (bf16[1024,256]{1,0:T(8,128)(2,1)S(1)}, bf16[1024,256]{1,0:T(8,128)(2,1)S(1)}, u32[]{:S(2)}, u32[]{:S(2)}) collective-permute-start(bf16[1024,256]{1,0:T(8,128)(2,1)S(1)} %get-tuple-element.43), channel_id=1, source_target_pairs={{0,1},{1,0},{2,3},{3,2},{4,5},{5,4},{6,7},{7,6},{8,9},{9,8},{10,11... | collective-permute-start | bytes 1572872 | tf_op jit(solution)/shard_map/ppermute | solution.py:25
  28.2 6.4 %collective-permute-start.5 = (bf16[512,256]{1,0:T(8,128)(2,1)S(1)}, bf16[512,256]{1,0:T(8,128)(2,1)S(1)}, u32[]{:S(2)}, u32[]{:S(2)}) collective-permute-start(bf16[512,256]{1,0:T(8,128)(2,1)S(1)} %get-tuple-element.45), channel_id=1, source_target_pairs={{0,4},{1,3},{2,6},{3,1},{4,0},{5,7},{6,2},{7,5},{8,12},{9,11},{10,... | collective-permute-start | bytes 786440 | tf_op jit(solution)/shard_map/ppermute | solution.py:25
  34.6 5.0 %collective-permute-start.6 = (bf16[256,256]{1,0:T(8,128)(2,1)S(1)}, bf16[256,256]{1,0:T(8,128)(2,1)S(1)}, u32[]{:S(2)}, u32[]{:S(2)}) collective-permute-start(bf16[256,256]{1,0:T(8,128)(2,1)S(1)} %fusion), channel_id=1, source_target_pairs={{0,2},{1,5},{2,0},{3,7},{4,6},{5,1},{6,4},{7,3},{8,10},{9,13},{10,... | collective-permute-start | bytes 393224 | tf_op jit(solution)/shard_map/ppermute | solution.py:25
  34.8 6.3 %collective-permute-start.8 = (bf16[32,3,256]{2,1,0:T(4,128)(2,1)S(1)}, bf16[32,3,256]{2,1,0:T(4,128)(2,1)S(1)}, u32[]{:S(2)}, u32[]{:S(2)}) collective-permute-start(bf16[32,3,256]{2,1,0:T(4,128)(2,1)S(1)} %get-tuple-element.78), channel_id=1, source_target_pairs={{0,4},{1,5},{2,6},{3,7},{4,0},{5,1},{6,2},{7,3},{8,12},{9,13},{10,... | collective-permute-start | bytes 147464 | tf_op jit(solution)/shard_map/ppermute | solution.py:25
  35.1 7.3 %collective-permute-start.9 = (bf16[32,3,256]{2,1,0:T(4,128)(2,1)S(1)}, bf16[32,3,256]{2,1,0:T(4,128)(2,1)S(1)}, u32[]{:S(2)}, u32[]{:S(2)}) collective-permute-start(bf16[32,3,256]{2,1,0:T(4,128)(2,1)S(1)} %get-tuple-element.79), channel_id=1, source_target_pairs={{0,28},{1,29},{2,30},{3,31},{4,8},{5,9},{6,10},{7,11},{8,4},{9,5},... | collective-permute-start | bytes 147464 | tf_op jit(solution)/shard_map/ppermute | solution.py:25
  39.7 6.8 %collective-permute-start.7 = (bf16[320,256]{1,0:T(8,128)(2,1)S(1)}, bf16[320,256]{1,0:T(8,128)(2,1)S(1)}, u32[]{:S(2)}, u32[]{:S(2)}) collective-permute-start(bf16[320,256]{1,0:T(8,128)(2,1)S(1)} %pad_maximum_fusion.4), channel_id=1, source_target_pairs={{0,8},{1,17},{2,10},{3,19},{4,12},{5,21},{6,14},{7,23},{8,0},{9,25... | collective-permute-start | bytes 491528 | tf_op jit(solution)/shard_map/ppermute | solution.py:25
  46.6 5.6 %collective-permute-start.12 = (bf16[3,38,256]{2,1,0:T(8,128)(2,1)S(1)}, bf16[3,38,256]{2,1,0:T(8,128)(2,1)S(1)}, u32[]{:S(2)}, u32[]{:S(2)}) collective-permute-start(bf16[3,38,256]{2,1,0:T(8,128)(2,1)S(1)} %reverse_select_fusion), channel_id=1, source_target_pairs={{0,16},{1,2},{2,1},{3,19},{4,20},{5,6},{6,5},{7,23},{8,24},{9,10},... | collective-permute-start | bytes 175112 | tf_op jit(solution)/shard_map/ppermute | solution.py:25
  47.4 4.9 %collective-permute-start.11 = (bf16[3,38,256]{2,1,0:T(8,128)(2,1)S(1)}, bf16[3,38,256]{2,1,0:T(8,128)(2,1)S(1)}, u32[]{:S(2)}, u32[]{:S(2)}) collective-permute-start(bf16[3,38,256]{2,1,0:T(8,128)(2,1)S(1)} %get-tuple-element.75), channel_id=1, source_target_pairs={{0,1},{1,0},{2,3},{3,2},{4,5},{5,4},{6,7},{7,6},{8,9},{9,8},{10,11... | collective-permute-start | bytes 175112 | tf_op jit(solution)/shard_map/ppermute | solution.py:25
  47.8 8.0 %collective-permute-start.10 = (bf16[320,256]{1,0:T(8,128)(2,1)S(1)}, bf16[320,256]{1,0:T(8,128)(2,1)S(1)}, u32[]{:S(2)}, u32[]{:S(2)}) collective-permute-start(bf16[320,256]{1,0:T(8,128)(2,1)S(1)} %add_convert_fusion.2), channel_id=1, source_target_pairs={{0,16},{1,9},{2,18},{3,11},{4,20},{5,13},{6,22},{7,15},{8,24},{9,1... | collective-permute-start | bytes 491528 | tf_op jit(solution)/shard_map/ppermute | solution.py:25
  55.9 5.4 %collective-permute-start.13 = (bf16[320,256]{1,0:T(8,128)(2,1)S(1)}, bf16[320,256]{1,0:T(8,128)(2,1)S(1)}, u32[]{:S(2)}, u32[]{:S(2)}) collective-permute-start(bf16[320,256]{1,0:T(8,128)(2,1)S(1)} %add_convert_fusion.1), channel_id=1, source_target_pairs={{0,2},{1,5},{2,0},{3,7},{4,6},{5,1},{6,4},{7,3},{8,10},{9,13},{10,... | collective-permute-start | bytes 491528 | tf_op jit(solution)/shard_map/ppermute | solution.py:25
  61.4 7.1 %collective-permute-start.14 = (bf16[576,256]{1,0:T(8,128)(2,1)S(1)}, bf16[576,256]{1,0:T(8,128)(2,1)S(1)}, u32[]{:S(2)}, u32[]{:S(2)}) collective-permute-start(bf16[576,256]{1,0:T(8,128)(2,1)S(1)} %pad_maximum_fusion.3), channel_id=1, source_target_pairs={{0,4},{1,3},{2,6},{3,1},{4,0},{5,7},{6,2},{7,5},{8,12},{9,11},{10,... | collective-permute-start | bytes 884744 | tf_op jit(solution)/shard_map/ppermute | solution.py:25
  68.5 2.0 %collective-permute-start.15 = (bf16[1088,256]{1,0:T(8,128)(2,1)S(1)}, bf16[1088,256]{1,0:T(8,128)(2,1)S(1)}, u32[]{:S(2)}, u32[]{:S(2)}) collective-permute-start(bf16[1088,256]{1,0:T(8,128)(2,1)S(1)} %pad_maximum_fusion.2.mine_ref), channel_id=1, source_target_pairs={{0,1},{1,0},{2,3},{3,2},{4,5},{5,4},{6,7},{7,6},{8,9},{9,8},{10,11... | collective-permute-start | bytes 1671176 | tf_op jit(solution)/shard_map/ppermute | solution.py:25

commit v5 on v4

--- a/solution.py
+++ b/solution.py
@@ -36,15 +36,16 @@
     inner = send(jnp.where(odd, first, last), lambda lon, lat: (lon ^ 1, lat))
     west = jnp.where(odd, inner, outer)
     east = jnp.where(odd, outer, inner)
-    return jnp.concatenate([west, field, east], axis=1)
-
-
-def lat_margins(wide):
+    return west, field, east
+
+
+def lat_margins(band):
     lons, lats = lax.axis_size("lon"), lax.axis_size("lat")
     lat = lax.axis_index("lat")
     odd = lat % 2 == 1
     pole = (lat == 0) | (lat == lats - 1)
-    first, last = wide[:3], wide[-3:]
+    first = jnp.concatenate([part[:3] for part in band], axis=1)
+    last = jnp.concatenate([part[-3:] for part in band], axis=1)
 
     def beyond(lon, lat):
         if lat == 0 or lat == lats - 1:
@@ -103,10 +104,11 @@
     return send(value, lambda lon, lat: (lon, lat ^ 1))
 
 
-def halves(held, got):
-    half = held.shape[0] // 2
-    mine = held[:half] + got[:half].astype(jnp.float32)
-    return mine, (held[half:] + got[half:].astype(jnp.float32)).astype(jnp.bfloat16)
+def widened_sum(*terms):
+    total = terms[0].astype(jnp.float32)
+    for term in terms[1:]:
+        total = total + term.astype(jnp.float32)
+    return total
 
 
 def rounded_sum(left, right):
@@ -147,10 +149,25 @@
     lax.fori_loop(0, count, body, 0)
 
 
-def split_padded(top_ref, wide_ref, bottom_ref, out_ref):
+def split_band(band_refs, out_ref, start=0, to=0, count=None):
+    count = band_refs[1].shape[0] if count is None else count
+
+    def body(row, carry):
+        for lane in range(out_ref.shape[0]):
+            column = 0
+            for ref in band_refs:
+                part = ref[start + row, :, lane * LANES : (lane + 1) * LANES]
+                out_ref[lane, to + row, column : column + ref.shape[1]] = part.astype(jnp.float32)
+                column += ref.shape[1]
+        return carry
+
+    lax.fori_loop(0, count, body, 0)
+
+
+def split_padded(top_ref, band_refs, bottom_ref, out_ref):
     split_lanes(top_ref, out_ref)
-    split_lanes(wide_ref, out_ref, to=3)
-    split_lanes(bottom_ref, out_ref, to=3 + wide_ref.shape[0])
+    split_band(band_refs, out_ref, to=3)
+    split_lanes(bottom_ref, out_ref, to=3 + band_refs[1].shape[0])
 
 
 def window_sums(source_ref, lane, start, weight_of):
@@ -177,33 +194,36 @@
             out_ref[lane, start + to, pl.ds(slot, SUBLANES, stride=slots), :] = totals[to][slot]
 
 
-def inner_conv_kernel(wide_ref, dw_ref, out_ref, split_ref, spread_ref):
+def inner_conv_kernel(
+    flipped, west_ref, field_ref, east_ref, dw_ref, out_ref, split_ref, spread_ref
+):
     tiles, rows = out_ref.shape[0], out_ref.shape[1]
     spread_weights(dw_ref, spread_ref)
-    split_lanes(wide_ref, split_ref)
+    split_band((west_ref, field_ref, east_ref), split_ref)
 
     def body(at, carry):
         lane, start = at // (rows // 4), (at % (rows // 4)) * 4
-        totals = window_sums(
-            split_ref, lane, start + 1, lambda row, row_off, col_off: spread_ref[lane, row_off * 7 + col_off]
-        )
-        store_sums(totals, out_ref, lane, start)
+
+        def weight_of(row, row_off, col_off):
+            tap = row_off * 7 + col_off
+            return spread_ref[lane, 48 - tap if flipped else tap]
+
+        store_sums(window_sums(split_ref, lane, start + 1, weight_of), out_ref, lane, start)
         return carry
 
     lax.fori_loop(0, tiles * (rows // 4), body, 0)
 
 
-def inner_conv(wide, dw_kernel):
-    rows, chans = wide.shape[0], wide.shape[2]
-    cols = wide.shape[1] - 6
+def inner_conv(band, dw_kernel, flipped):
+    rows, cols, chans = band[1].shape
     tiles = chans // LANES
     return pl.pallas_call(
-        inner_conv_kernel,
+        functools.partial(inner_conv_kernel, flipped),
         out_shape=jax.ShapeDtypeStruct((tiles, rows - 8, cols, LANES), jnp.float32),
-        in_specs=[pl.BlockSpec(memory_space=pltpu.VMEM)] * 2,
+        in_specs=[pl.BlockSpec(memory_space=pltpu.VMEM)] * 4,
         out_specs=pl.BlockSpec(memory_space=pltpu.VMEM),
         scratch_shapes=[
-            pltpu.VMEM((tiles,) + wide.shape[:2] + (LANES,), jnp.float32),
+            pltpu.VMEM((tiles, rows, cols + 6, LANES), jnp.float32),
             pltpu.VMEM((tiles, 49, SUBLANES, LANES), jnp.float32),
         ],
         compiler_params=pltpu.CompilerParams(vmem_limit_bytes=6 << 20),
@@ -211,17 +231,18 @@
             flops=98 * rows * cols * chans, bytes_accessed=2 << 20, transcendentals=0
         ),
         name="block_inner_conv",
-    )(wide, dw_kernel)
+    )(*band, dw_kernel)
 
 
 def main_kernel(
     scale_factor,
     place_ref,
     top_ref,
-    wide_ref,
+    west_ref,
+    fields_ref,
+    east_ref,
     bottom_ref,
     inner_ref,
-    fields_ref,
     cot_ref,
     dw_ref,
     dw_bias_ref,
@@ -249,8 +270,9 @@
     pieces = hidden_units // chans
     spread_weights(dw_ref, spread_ref)
     split_lanes(top_ref, split_ref)
-    split_lanes(wide_ref, split_ref, to=3, count=7)
-    split_lanes(wide_ref, split_ref, start=rows - 7, to=10, count=7)
+    band_refs = (west_ref, fields_ref, east_ref)
+    split_band(band_refs, split_ref, to=3, count=7)
+    split_band(band_refs, split_ref, start=rows - 7, to=10, count=7)
     split_lanes(bottom_ref, split_ref, to=17)
 
     def conv_edge(at, carry):
@@ -307,7 +329,7 @@
             d_pre.astype(jnp.float32), axis=0, keepdims=True
         )
         d_normed = d_normed + contract(d_pre, w_in, 1, 1)
-    plain = fields_ref[...].astype(jnp.float32)
+    plain = fields_ref[...].reshape(rows * cols, chans).astype(jnp.float32)
     out_ref[...] = (plain + (branch + b_project)).astype(jnp.bfloat16)
     small_ref[0:1] = jnp.sum(d_normed * xhat, axis=0, keepdims=True)
     small_ref[1:2] = jnp.sum(d_normed, axis=0, keepdims=True)
@@ -350,10 +372,9 @@
 
 
 def main_pass(
-    place, top, wide, bottom, inner, fields, cot, dw_kernel, vectors, w_expand, w_project, scale_factor
+    place, top, band, bottom, inner, cot, dw_kernel, vectors, w_expand, w_project, scale_factor
 ):
-    rows, cols = wide.shape[0], wide.shape[1] - 6
-    chans = fields.shape[1]
+    rows, cols, chans = band[1].shape
     hidden_units = w_expand.shape[1]
     tiles = chans // LANES
     cells = rows * cols
@@ -367,10 +388,10 @@
             jax.ShapeDtypeStruct((8 + hidden_units // chans, chans), jnp.float32),
         ],
         in_specs=[pl.BlockSpec(memory_space=pltpu.SMEM)]
-        + [pl.BlockSpec(memory_space=pltpu.VMEM)] * 14,
+        + [pl.BlockSpec(memory_space=pltpu.VMEM)] * 15,
         out_specs=[pl.BlockSpec(memory_space=pltpu.VMEM)] * 5,
         scratch_shapes=[
-            pltpu.VMEM((tiles, 20, wide.shape[1], LANES), jnp.float32),
+            pltpu.VMEM((tiles, 20, cols + 6, LANES), jnp.float32),
             pltpu.VMEM((tiles, 49, SUBLANES, LANES), jnp.float32),
             pltpu.VMEM((tiles, 8, cols, LANES), jnp.float32),
             pltpu.VMEM((hidden_units, chans), jnp.float32),
@@ -383,13 +404,15 @@
             transcendentals=2 * cells * hidden_units,
         ),
         name="block_main",
-    )(place, top, wide, bottom, inner, fields, cot, dw_kernel, *vectors, w_expand, w_project)
+    )(place, top, *band, bottom, inner, cot, dw_kernel, *vectors, w_expand, w_project)
 
 
 def taps_kernel(
     scale_factor,
     top_ref,
-    band_ref,
+    west_ref,
+    field_ref,
+    east_ref,
     bottom_ref,
     dconv_ref,
     small_ref,
@@ -400,7 +423,7 @@
 ):
     tiles, rows, cols = dwide_ref.shape[0], dwide_ref.shape[1], dwide_ref.shape[2]
     slots = cols // SUBLANES
-    split_padded(top_ref, band_ref, bottom_ref, wide_ref)
+    split_padded(top_ref, (west_ref, field_ref, east_ref), bottom_ref, wide_ref)
     split_lanes(dconv_ref, dwide_ref)
     sums_ref[...] = jnp.zeros_like(sums_ref)
     for lane in range(tiles):
@@ -434,14 +457,14 @@
     out_ref[...] = sums_ref[...].astype(jnp.bfloat16)
 
 
-def taps_pass(top, wide, bottom, conv_gradient, small, scale_factor):
+def taps_pass(top, band, bottom, conv_gradient, small, scale_factor):
     rows, cols, chans = conv_gradient.shape
     tiles = chans // LANES
     height = -(-(45 + small.shape[0]) // 32) * 32
     return pl.pallas_call(
         functools.partial(taps_kernel, scale_factor),
         out_shape=jax.ShapeDtypeStruct((height, chans), jnp.bfloat16),
-        in_specs=[pl.BlockSpec(memory_space=pltpu.VMEM)] * 5,
+        in_specs=[pl.BlockSpec(memory_space=pltpu.VMEM)] * 7,
         out_specs=pl.BlockSpec(memory_space=pltpu.VMEM),
         scratch_shapes=[
             pltpu.VMEM((tiles, rows + 6, cols + 6, LANES), jnp.float32),
@@ -453,13 +476,15 @@
             flops=98 * rows * cols * chans, bytes_accessed=3 << 20, transcendentals=0
         ),
         name="block_taps",
-    )(top, wide, bottom, conv_gradient, small)
+    )(top, *band, bottom, conv_gradient, small)
 
 
 def finish_kernel(
     place_ref,
     mine_ref,
-    got_ref,
+    last_ref,
+    pair_ref,
+    pair_last_ref,
     kern_ref,
     dwb_ref,
     gain_ref,
@@ -472,8 +497,9 @@
 ):
     hidden_units, chans = project_ref.shape
     pieces = hidden_units // chans
-    small = slice(hidden_units, mine_ref.shape[0])
-    sums_ref[...] = mine_ref[small].astype(jnp.float32) + got_ref[small].astype(jnp.float32)
+    early = mine_ref.shape[0] // chans
+    small = slice(hidden_units - early * chans, last_ref.shape[0])
+    sums_ref[...] = last_ref[small].astype(jnp.float32) + pair_last_ref[small].astype(jnp.float32)
     for row_off in range(7):
         kern_ref[row_off] = sums_ref[row_off * 7 : row_off * 7 + 7]
     dwb_ref[...] = sums_ref[49]
@@ -483,24 +509,27 @@
     for piece in range(pieces):
         b_expand_ref[piece * chans : (piece + 1) * chans] = sums_ref[53 + piece]
 
-    def write(first_ref, first_order, second_ref, second_order):
+    def write(first_refs, first_order, second_refs, second_order):
         for at in range(pieces):
-            part = slice(at * chans, (at + 1) * chans)
+            late = at >= early
+            part = pl.ds((at - early if late else at) * chans, chans)
             columns = pl.multiple_of((at ^ first_order) * chans, chans)
-            expand_ref[:, pl.ds(columns, chans)] = first_ref[part].astype(jnp.float32)
+            expand_ref[:, pl.ds(columns, chans)] = first_refs[late][part].astype(jnp.float32)
             to = pl.multiple_of((at ^ second_order) * chans, chans)
-            project_ref[pl.ds(to, chans)] = second_ref[part].astype(jnp.float32)
+            project_ref[pl.ds(to, chans)] = second_refs[late][part].astype(jnp.float32)
+
+    mine_refs, pair_refs = (mine_ref, last_ref), (pair_ref, pair_last_ref)
 
     @pl.when(place_ref[0] == 0)
     def first():
-        write(mine_ref, place_ref[1], got_ref, place_ref[2])
+        write(mine_refs, place_ref[1], pair_refs, place_ref[2])
 
     @pl.when(place_ref[0] != 0)
     def second():
-        write(got_ref, place_ref[2], mine_ref, place_ref[1])
-
-
-def finish_pass(place, mine, got, hidden_units):
+        write(pair_refs, place_ref[2], mine_refs, place_ref[1])
+
+
+def finish_pass(place, mine, last, pair, pair_last, hidden_units):
     chans = mine.shape[1]
     one = jax.ShapeDtypeStruct((chans,), jnp.float32)
     return pl.pallas_call(
@@ -516,31 +545,38 @@
             one,
         ],
         in_specs=[pl.BlockSpec(memory_space=pltpu.SMEM)]
-        + [pl.BlockSpec(memory_space=pltpu.VMEM)] * 2,
+        + [pl.BlockSpec(memory_space=pltpu.VMEM)] * 4,
         out_specs=[pl.BlockSpec(memory_space=pltpu.VMEM)] * 8,
-        scratch_shapes=[pltpu.VMEM((mine.shape[0] - hidden_units, chans), jnp.float32)],
+        scratch_shapes=[pltpu.VMEM((mine.shape[0] + last.shape[0] - hidden_units, chans), jnp.float32)],
         compiler_params=pltpu.CompilerParams(vmem_limit_bytes=8 << 20),
         name="block_finish",
-    )(place, mine, got)
+    )(place, mine, last, pair, pair_last)
 
 
 def adjoint_kernel(
     poles_ref,
     top_ref,
-    band_ref,
+    west_ref,
+    field_ref,
+    east_ref,
     bottom_ref,
+    inner_ref,
     cot_ref,
     dw_ref,
     out_ref,
-    wide_ref,
+    split_ref,
     spread_ref,
     edge_ref,
     sum_ref,
 ):
-    tiles = wide_ref.shape[0]
-    rows = sum_ref.shape[1]
+    tiles = split_ref.shape[0]
+    rows = cot_ref.shape[0]
     spread_weights(dw_ref, spread_ref)
-    split_padded(top_ref, band_ref, bottom_ref, wide_ref)
+    band_refs = (west_ref, field_ref, east_ref)
+    split_lanes(top_ref, split_ref)
+    split_band(band_refs, split_ref, to=3, count=7)
+    split_band(band_refs, split_ref, start=rows - 7, to=10, count=7)
+    split_lanes(bottom_ref, split_ref, to=17)
     for side in range(2):
         at_pole = poles_ref[side] == 1
         for lane in range(tiles):
@@ -551,59 +587,56 @@
                     turned = spread_ref[lane, near * 7 + col_off]
                     edge_ref[side, lane, row_off * 7 + col_off] = jnp.where(at_pole, turned, plain)
 
-    def block_of(lane, start, first, last):
-        def weight_of(row, row_off, col_off):
-            if first and row < 3:
-                return edge_ref[0, lane, row_off * 7 + 6 - col_off]
-            if last and row >= 7:
-                return edge_ref[1, lane, (6 - row_off) * 7 + 6 - col_off]
-            return spread_ref[lane, (6 - row_off) * 7 + 6 - col_off]
-
-        store_sums(window_sums(wide_ref, lane, start, weight_of), sum_ref, lane, start)
-
-    inner = rows // 4 - 2
-
-    def inner_block(at, carry):
-        block_of(at // inner, (1 + at % inner) * 4, False, False)
+    def edge_block(lane, carry):
+        for side in range(2):
+
+            def weight_of(row, row_off, col_off):
+                if side == 0 and row < 3:
+                    return edge_ref[0, lane, row_off * 7 + 6 - col_off]
+                if side == 1 and row >= 7:
+                    return edge_ref[1, lane, (6 - row_off) * 7 + 6 - col_off]
+                return spread_ref[lane, 48 - (row_off * 7 + col_off)]
+
+            totals = window_sums(split_ref, lane, side * 10, weight_of)
+            store_sums(totals, sum_ref, lane, side * 4)
         return carry
 
-    def edge_block(lane, carry):
-        block_of(lane, 0, True, False)
-        block_of(lane, rows - 4, False, True)
-        return carry
-
-    lax.fori_loop(0, tiles * inner, inner_block, 0)
     lax.fori_loop(0, tiles, edge_block, 0)
 
-    def finish(row, carry):
-        total = jnp.concatenate([sum_ref[lane, row] for lane in range(tiles)], axis=1)
-        out_ref[row] = (cot_ref[row].astype(jnp.float32) + total).astype(jnp.bfloat16)
-        return carry
-
-    lax.fori_loop(0, rows, finish, 0)
-
-
-def adjoint_pass(top, wide, bottom, cot, dw_kernel, poles):
+    def write(ref, start, to, count):
+        def body(row, carry):
+            total = jnp.concatenate([ref[lane, start + row] for lane in range(tiles)], axis=1)
+            out_ref[to + row] = (cot_ref[to + row].astype(jnp.float32) + total).astype(jnp.bfloat16)
+            return carry
+
+        lax.fori_loop(0, count, body, 0)
+
+    write(sum_ref, 0, 0, 4)
+    write(inner_ref, 0, 4, rows - 8)
+    write(sum_ref, 4, rows - 4, 4)
+
+
+def adjoint_pass(top, band, bottom, inner, cot, dw_kernel, poles):
     rows, cols, chans = cot.shape
     tiles = chans // LANES
     return pl.pallas_call(
         adjoint_kernel,
         out_shape=jax.ShapeDtypeStruct(cot.shape, jnp.bfloat16),
         in_specs=[pl.BlockSpec(memory_space=pltpu.SMEM)]
-        + [pl.BlockSpec(memory_space=pltpu.VMEM)] * 5,
+        + [pl.BlockSpec(memory_space=pltpu.VMEM)] * 8,
         out_specs=pl.BlockSpec(memory_space=pltpu.VMEM),
         scratch_shapes=[
-            pltpu.VMEM((tiles, rows + 6, cols + 6, LANES), jnp.float32),
+            pltpu.VMEM((tiles, 20, cols + 6, LANES), jnp.float32),
             pltpu.VMEM((tiles, 49, SUBLANES, LANES), jnp.float32),
             pltpu.VMEM((2, tiles, 21, SUBLANES, LANES), jnp.float32),
-            pltpu.VMEM((tiles, rows, cols, LANES), jnp.float32),
+            pltpu.VMEM((tiles, 8, cols, LANES), jnp.float32),
         ],
         compiler_params=pltpu.CompilerParams(vmem_limit_bytes=6 << 20),
         cost_estimate=pl.CostEstimate(
-            flops=98 * rows * cols * chans, bytes_accessed=3 << 20, transcendentals=0
+            flops=25 * rows * cols * chans, bytes_accessed=3 << 20, transcendentals=0
         ),
         name="block_adjoint",
-    )(poles, top, wide, bottom, cot, dw_kernel)
+    )(poles, top, *band, bottom, inner, cot, dw_kernel)
 
 
 def local(
@@ -626,16 +659,15 @@
     lat = lax.axis_index("lat")
     poles = jnp.stack([lat == 0, lat == lax.axis_size("lat") - 1]).astype(jnp.int32)
     count, exchange, place = partner_steps()
-    wide = lon_margins(fields)
-    inner = inner_conv(wide, dw_kernel)
-    edges = lat_margins(wide)
+    band = lon_margins(fields)
+    inner = inner_conv(band, dw_kernel, False)
+    edges = lat_margins(band)
     block_out, conv_gradient, keep, give, small = main_pass(
         place,
         edges[0],
-        wide,
+        band,
         edges[1],
         inner,
-        fields.reshape(-1, chans),
         cotangent.reshape(-1, chans),
         dw_kernel,
         (dw_bias, norm_gain, layer_norm_offset, b_project, b_expand),
@@ -646,40 +678,45 @@
     block_out = block_out.reshape(fields.shape)
     conv_gradient = conv_gradient.reshape(fields.shape)
     barrier = lax.optimization_barrier
-    mine, outgoing = halves(keep, within_pair(give))
+    half = hidden_units // 2
+    quarter = half // 2
+    got_far = within_pair(give[half:])
+    got_near = within_pair(give[:half])
+    outgoing = widened_sum(keep[half:], got_far).astype(jnp.bfloat16)
     outgoing, taps_in = barrier((outgoing, conv_gradient))
-    got = exchange(outgoing, 0)
-    small = taps_pass(edges[0], wide, edges[1], taps_in, small, scale_factor)
+    got = exchange(outgoing[quarter:], 0)
+    kept = exchange(outgoing[:quarter], 0)
+    small = taps_pass(edges[0], band, edges[1], taps_in, small, scale_factor)
     got, small, conv_gradient = barrier((got, small, conv_gradient))
-    mine, outgoing = halves(mine, got)
+    outgoing = widened_sum(keep[quarter:half], got_near[quarter:], got).astype(jnp.bfloat16)
     outgoing, conv_gradient = barrier((outgoing, conv_gradient))
     got = exchange(outgoing, 1)
-    wide = lon_margins(conv_gradient)
-    payload = (mine + got.astype(jnp.float32)).astype(jnp.bfloat16)
+    band = lon_margins(conv_gradient)
+    payload = widened_sum(keep[:quarter], got_near[:quarter], kept, got).astype(jnp.bfloat16)
     payload = jnp.concatenate([payload, small], axis=0)
     for at in range(2, count):
         got = exchange(payload, at)
         if at == 2:
-            got, wide = barrier((got, wide))
-            top, bottom = lat_margins(wide)
+            got, band = barrier((got, band))
         payload = rounded_sum(payload, got)
-    if count > 2:
-        payload, top, bottom = barrier((payload, top, bottom))
-    else:
-        top, bottom = lat_margins(wide)
-    for at in (1, 0):
-        if at == 0:
-            payload, top, wide, bottom = barrier((payload, top, wide, bottom))
-            grad_fields = adjoint_pass(top, wide, bottom, cotangent, dw_kernel, poles)
-        got = exchange(payload, at)
-        if at == 0:
-            got, grad_fields = barrier((got, grad_fields))
-        own = payload.shape[0] - small.shape[0]
-        payload = jnp.concatenate(
-            [payload[:own], got[:own], rounded_sum(payload[own:], got[own:])], axis=0
-        )
+    payload, band = barrier((payload, band))
+    top, bottom = lat_margins(band)
+    got = exchange(payload, 1)
+    inner = inner_conv(band, dw_kernel, True)
+    got, inner = barrier((got, inner))
+    across = exchange(payload[:quarter], 0)
+    beside, small = got[:quarter], rounded_sum(payload[quarter:], got[quarter:])
+    sent = jnp.concatenate([beside, small], axis=0)
+    sent, band = barrier((sent, band))
+    got = exchange(sent, 0)
+    grad_fields = adjoint_pass(top, band, bottom, inner, cotangent, dw_kernel, poles)
+    mine = jnp.concatenate([payload[:quarter], beside, across], axis=0)
+    pair = within_pair(mine)
+    got, grad_fields = barrier((got, grad_fields))
+    last = jnp.concatenate([got[:quarter], rounded_sum(small, got[quarter:])], axis=0)
+    pair_last = within_pair(last)
     sum_kern, sum_dwb, sum_gn, sum_sh, sum_exp, sum_bexp, sum_proj, sum_bproj = finish_pass(
-        place, payload, within_pair(payload), hidden_units
+        place, mine, last, pair, pair_last, hidden_units
     )
     return (
         block_out,

time: 72.8 us -> 69.7 us (0.957); the launches traced: 72.6 us -> 68.7 us
  waiting for transfers between devices: 26.6 us -> 18.2 us
  starting transfers between devices: 17.9 us -> 22.4 us
  other arithmetic: 3.68 us -> 1.92 us
  local copies, waits for them, and re-layouts: 0.12 us -> 1.62 us
    ppermute x16 -> x20, waiting for transfers between devices: 26.6 us -> 18.2 us  [send(): return lax.ppermute(value, ('lon', 'lat'), flat_pairs(target))]
    ppermute x16 -> x20, starting transfers between devices: 17.9 us -> 22.4 us  [send(): return lax.ppermute(value, ('lon', 'lat'), flat_pairs(target))]
    pallas_call x1 -> x2, Pallas kernels: 3.26 us -> 6.64 us  [inner_conv(): pl.pallas_call(functools.partial(inner_conv_kernel, flipped), out_shape=j...]
    pallas_call x1, Pallas kernels: 5.94 us -> 2.79 us  [adjoint_pass(): pl.pallas_call(adjoint_kernel, out_shape=jax.ShapeDtypeStruct(cot.shape,...]
    concatenate x4 -> x3, other arithmetic: 1.86 us -> 0.05 us  [the longest x1 0.03 us: local(): mine = jnp.concatenate([payload[:quarter], beside, across], axis=0)]
    slice x4 -> x10, local copies, waits for them, and re-layouts: 0.06 us -> 0.95 us  [the longest x5 0.86 us: lat_margins(): first = jnp.concatenate([part[:3] for part in band], axis=1)]
  transfers between devices with their start and end apart: 16 -> 20, of which waited for: 11 -> 10; matrix products, arithmetic and copies ran while one was open for 1% -> 2% of each run, Pallas kernels for 19% -> 20%
where the time goes in v5:
time: 69.7 us; the launch traced here: 68.7 us
  Pallas kernels  23.6 us (34%)
  starting transfers between devices  22.4 us (32%)
  waiting for transfers between devices  18.2 us (26%)
  other arithmetic  1.92 us (3%)
  local copies, waits for them, and re-layouts  1.62 us (2%)
  between operations  1.01 us (1%)
    ppermute x20, starting transfers between devices, send(): return lax.ppermute(value, ('lon', 'lat'), flat_pairs(target))  22.4 us
    ppermute x20, waiting for transfers between devices, send(): return lax.ppermute(value, ('lon', 'lat'), flat_pairs(target))  18.2 us
    pallas_call x1, Pallas kernels, main_pass(): pl.pallas_call(functools.partial(main_kernel, scale_factor), out_shape=[j...  7.48 us
    pallas_call x2, Pallas kernels, inner_conv(): pl.pallas_call(functools.partial(inner_conv_kernel, flipped), out_shape=j...  6.64 us
    pallas_call x1, Pallas kernels, taps_pass(): pl.pallas_call(functools.partial(taps_kernel, scale_factor), out_shape=ja...  4.59 us
    pallas_call x1, Pallas kernels, adjoint_pass(): pl.pallas_call(adjoint_kernel, out_shape=jax.ShapeDtypeStruct(cot.shape,...  2.79 us
    pallas_call x1, Pallas kernels, finish_pass(): pl.pallas_call(finish_kernel, out_shape=[jax.ShapeDtypeStruct((7, 7, chan...  2.06 us
  transfers between devices with their start and end apart: 20, of which 10 were waited for; matrix products, arithmetic and copies ran while one was open for 2% of the time, Pallas kernels for 20%

profile of v5, /device:TPU:0, one launch (start us, length us, event | category | flops | bytes accessed | tf_op | source)
XLA Modules:
  0.0 68.7 jit_solution(8798408276079955809)
XLA Ops:
  0.7 1.0 %broadcast_select_fusion.7 = (bf16[32,3,256]{2,1,0:T(4,128)(2,1)S(1)}, bf16[32,3,256]{2,1,0:T(4,128)(2,1)S(1)}) fusion(pred[]{:T(512)S(6)} %eq.30, bf16[32,32,256]{2,1,0:T(8,128)(2,1)} %field_ref.3), kind=kLoop, calls=%fused_computation.20 | loop fusion | flops 49152 | bytes 196609 | tf_op jit(solution)/shard_map/jit(_where)/select_n | solution.py:36
  1.7 3.0 %collective-permute-start = (bf16[32,3,256]{2,1,0:T(4,128)(2,1)S(1)}, bf16[32,3,256]{2,1,0:T(4,128)(2,1)S(1)}, u32[]{:S(2)}, u32[]{:S(2)}) collective-permute-start(bf16[32,3,256]{2,1,0:T(4,128)(2,1)S(1)} %get-tuple-element.90), channel_id=1, source_target_pairs={{0,4},{1,5},{2,6},{3,7},{4,0},{5,1},{6,2},{7,3},{8,12},{9,13},{10,... | collective-permute-start | bytes 147464 | tf_op jit(solution)/shard_map/ppermute | solution.py:25
  4.7 3.6 %collective-permute-start.1 = (bf16[32,3,256]{2,1,0:T(4,128)(2,1)S(1)}, bf16[32,3,256]{2,1,0:T(4,128)(2,1)S(1)}, u32[]{:S(2)}, u32[]{:S(2)}) collective-permute-start(bf16[32,3,256]{2,1,0:T(4,128)(2,1)S(1)} %get-tuple-element.91), channel_id=1, source_target_pairs={{0,28},{1,29},{2,30},{3,31},{4,8},{5,9},{6,10},{7,11},{8,4},{9,5},... | collective-permute-start | bytes 147464 | tf_op jit(solution)/shard_map/ppermute | solution.py:25
  8.3 0.8 %fusion.2 = (bf16[3,32,256]{2,1,0:T(8,128)(2,1)S(1)}, bf16[3,32,256]{2,1,0:T(8,128)(2,1)S(1)}) fusion(bf16[32,32,256]{2,1,0:T(8,128)(2,1)} %field_ref.3), kind=kLoop, calls=%fused_computation.37 | loop fusion | bytes 196608 | tf_op jit(solution)/shard_map/slice | solution.py:47
  9.1 2.6 %collective-permute-done.1 = bf16[32,3,256]{2,1,0:T(4,128)(2,1)S(1)} collective-permute-done((bf16[32,3,256]{2,1,0:T(4,128)(2,1)S(1)}, bf16[32,3,256]{2,1,0:T(4,128)(2,1)S(1)}, u32[]{:S(2)}, u32[]{:S(2)}) %collective-permute-start.1) | collective-permute-done | bytes 49184 | tf_op jit(solution)/shard_map/ppermute | solution.py:25
  11.9 0.9 %collective-permute-start.3 = (bf16[3,38,256]{2,1,0:T(8,128)(2,1)S(1)}, bf16[3,38,256]{2,1,0:T(8,128)(2,1)S(1)}, u32[]{:S(2)}, u32[]{:S(2)}) collective-permute-start(bf16[3,38,256]{2,1,0:T(8,128)(2,1)S(1)} %reverse_select_fusion.1), channel_id=1, source_target_pairs={{0,16},{1,2},{2,1},{3,19},{4,20},{5,6},{6,5},{7,23},{8,24},{9,10},... | collective-permute-start | bytes 175112 | tf_op jit(solution)/shard_map/ppermute | solution.py:25
  12.7 0.8 %collective-permute-start.2 = (bf16[3,38,256]{2,1,0:T(8,128)(2,1)S(1)}, bf16[3,38,256]{2,1,0:T(8,128)(2,1)S(1)}, u32[]{:S(2)}, u32[]{:S(2)}) collective-permute-start(bf16[3,38,256]{2,1,0:T(8,128)(2,1)S(1)} %get-tuple-element.105), channel_id=1, source_target_pairs={{0,1},{1,0},{2,3},{3,2},{4,5},{5,4},{6,7},{7,6},{8,9},{9,8},{10,11... | collective-permute-start | bytes 175112 | tf_op jit(solution)/shard_map/ppermute | solution.py:25
  13.7 3.3 %block_inner_conv.2.inner_ref = f32[2,24,32,128]{3,2,1,0:T(8,128)S(1)} custom-call(bf16[32,3,256]{2,1,0:T(4,128)(2,1)S(1)} %get-tuple-element.96.west_ref, bf16[32,32,256]{2,1,0:T(8,128)(2,1)S(1)} %copy-done, bf16[32,3,256]{2,1,0:T(4,128)(2,1)S(1)} %get-tuple-element.97.east_ref, bf16[7,7,256]{2,1,0:T(8,128)(2,1)S(1)} %copy-done.2), custom_call_target="tpu_custom_call" | custom-call | flops 25690112 | bytes 2097152 | tf_op jit(solution)/shard_map/block_inner_conv/pallas_call | solution.py:220
  17.2 0.6 copy-done.9
  17.8 7.5 %block_main.1 = (bf16[1024,256]{1,0:T(8,128)(2,1)}, bf16[1024,256]{1,0:T(8,128)(2,1)S(1)}, f32[1024,256]{1,0:T(8,128)S(1)}, bf16[1024,256]{1,0:T(8,128)(2,1)S(1)}, f32[12,256]{1,0:T(8,128)S(1)}) custom-call(s32[3]{0:T(128)S(1)} %pad_add_fusion.place_ref, bf16[3,38,256]{2,1,0:T(8,128)(2,1)S(1)} %get-tuple-element.103.top_ref, ...), custom_call_target="tpu_custom_call" | custom-call | flops 3221225472 | bytes 8388608 | tf_op jit(solution)/shard_map/block_main/pallas_call | solution.py:381
  25.4 0.5 collective-permute-start.4
  25.9 1.0 %collective-permute-done.5 = bf16[512,256]{1,0:T(8,128)(2,1)S(1)} collective-permute-done((bf16[512,256]{1,0:T(8,128)(2,1)S(1)}, bf16[512,256]{1,0:T(8,128)(2,1)S(1)}, u32[]{:S(2)}, u32[]{:S(2)}) %collective-permute-start.5) | collective-permute-done | bytes 262176 | tf_op jit(solution)/shard_map/ppermute | solution.py:25
  27.1 2.0 %collective-permute-start.6 = (bf16[256,256]{1,0:T(8,128)(2,1)S(1)}, bf16[256,256]{1,0:T(8,128)(2,1)S(1)}, u32[]{:S(2)}, u32[]{:S(2)}) collective-permute-start(bf16[256,256]{1,0:T(8,128)(2,1)S(1)} %get-tuple-element.92), channel_id=1, source_target_pairs={{0,4},{1,3},{2,6},{3,1},{4,0},{5,7},{6,2},{7,5},{8,12},{9,11},{10,... | collective-permute-start | bytes 393224 | tf_op jit(solution)/shard_map/ppermute | solution.py:25
  29.1 4.6 %block_taps.1 = bf16[64,256]{1,0:T(8,128)(2,1)S(1)} custom-call(bf16[3,38,256]{2,1,0:T(8,128)(2,1)S(1)} %get-tuple-element.103.top_ref, bf16[32,3,256]{2,1,0:T(4,128)(2,1)S(1)} %get-tuple-element.96.west_ref, bf16[32,32,256]{2,1,0:T(8,128)(2,1)S(1)} %copy-done, bf16[32,3,256]{2,1,0:T(4,128)(2,1)S(1)} %get-tuple-element.97.east_ref, ...), custom_call_target="tpu_custom_call" | custom-call | flops 25690112 | bytes 3145728 | tf_op jit(solution)/shard_map/block_taps/pallas_call | solution.py:464
  33.8 0.5 collective-permute-start.8
  34.3 3.6 %collective-permute-start.11 = (bf16[32,3,256]{2,1,0:T(4,128)(2,1)S(1)}, bf16[32,3,256]{2,1,0:T(4,128)(2,1)S(1)}, u32[]{:S(2)}, u32[]{:S(2)}) collective-permute-start(bf16[32,3,256]{2,1,0:T(4,128)(2,1)S(1)} %get-tuple-element.84), channel_id=1, source_target_pairs={{0,28},{1,29},{2,30},{3,31},{4,8},{5,9},{6,10},{7,11},{8,4},{9,5},... | collective-permute-start | bytes 147464 | tf_op jit(solution)/shard_map/ppermute | solution.py:25
  37.9 0.8 %collective-permute-done.8 = bf16[256,256]{1,0:T(8,128)(2,1)S(1)} collective-permute-done((bf16[256,256]{1,0:T(8,128)(2,1)S(1)}, bf16[256,256]{1,0:T(8,128)(2,1)S(1)}, u32[]{:S(2)}, u32[]{:S(2)}) %collective-permute-start.8) | collective-permute-done | bytes 131104 | tf_op jit(solution)/shard_map/ppermute | solution.py:25
  38.9 1.3 %collective-permute-start.9 = (bf16[320,256]{1,0:T(8,128)(2,1)S(1)}, bf16[320,256]{1,0:T(8,128)(2,1)S(1)}, u32[]{:S(2)}, u32[]{:S(2)}) collective-permute-start(bf16[320,256]{1,0:T(8,128)(2,1)S(1)} %pad_maximum_fusion.1), channel_id=1, source_target_pairs={{0,8},{1,17},{2,10},{3,19},{4,12},{5,21},{6,14},{7,23},{8,0},{9,25... | collective-permute-start | bytes 491528 | tf_op jit(solution)/shard_map/ppermute | solution.py:25
  40.2 1.2 %collective-permute-done.11 = bf16[32,3,256]{2,1,0:T(4,128)(2,1)S(1)} collective-permute-done((bf16[32,3,256]{2,1,0:T(4,128)(2,1)S(1)}, bf16[32,3,256]{2,1,0:T(4,128)(2,1)S(1)}, u32[]{:S(2)}, u32[]{:S(2)}) %collective-permute-start.11) | collective-permute-done | bytes 49184 | tf_op jit(solution)/shard_map/ppermute | solution.py:25
  41.3 0.9 %collective-permute-done.10 = bf16[32,3,256]{2,1,0:T(4,128)(2,1)S(1)} collective-permute-done((bf16[32,3,256]{2,1,0:T(4,128)(2,1)S(1)}, bf16[32,3,256]{2,1,0:T(4,128)(2,1)S(1)}, u32[]{:S(2)}, u32[]{:S(2)}) %collective-permute-start.10) | collective-permute-done | bytes 49184 | tf_op jit(solution)/shard_map/ppermute | solution.py:25
  42.3 2.6 %collective-permute-done.9 = bf16[320,256]{1,0:T(8,128)(2,1)S(1)} collective-permute-done((bf16[320,256]{1,0:T(8,128)(2,1)S(1)}, bf16[320,256]{1,0:T(8,128)(2,1)S(1)}, u32[]{:S(2)}, u32[]{:S(2)}) %collective-permute-start.9) | collective-permute-done | bytes 163872 | tf_op jit(solution)/shard_map/ppermute | solution.py:25
  44.9 1.6 %collective-permute-start.12 = (bf16[320,256]{1,0:T(8,128)(2,1)S(1)}, bf16[320,256]{1,0:T(8,128)(2,1)S(1)}, u32[]{:S(2)}, u32[]{:S(2)}) collective-permute-start(bf16[320,256]{1,0:T(8,128)(2,1)S(1)} %add_convert_fusion.2), channel_id=1, source_target_pairs={{0,16},{1,9},{2,18},{3,11},{4,20},{5,13},{6,22},{7,15},{8,24},{9,1... | collective-permute-start | bytes 491528 | tf_op jit(solution)/shard_map/ppermute | solution.py:25
  46.6 6.4 %collective-permute-done.12 = bf16[320,256]{1,0:T(8,128)(2,1)S(1)} collective-permute-done((bf16[320,256]{1,0:T(8,128)(2,1)S(1)}, bf16[320,256]{1,0:T(8,128)(2,1)S(1)}, u32[]{:S(2)}, u32[]{:S(2)}) %collective-permute-start.12) | collective-permute-done | bytes 163872 | tf_op jit(solution)/shard_map/ppermute | solution.py:25
  53.0 1.4 %collective-permute-start.13 = (bf16[320,256]{1,0:T(8,128)(2,1)S(1)}, bf16[320,256]{1,0:T(8,128)(2,1)S(1)}, u32[]{:S(2)}, u32[]{:S(2)}) collective-permute-start(bf16[320,256]{1,0:T(8,128)(2,1)S(1)} %add_convert_fusion.1), channel_id=1, source_target_pairs={{0,2},{1,5},{2,0},{3,7},{4,6},{5,1},{6,4},{7,3},{8,10},{9,13},{10,... | collective-permute-start | bytes 491528 | tf_op jit(solution)/shard_map/ppermute | solution.py:25
  54.7 0.8 %collective-permute-start.15 = (bf16[3,38,256]{2,1,0:T(8,128)(2,1)S(1)}, bf16[3,38,256]{2,1,0:T(8,128)(2,1)S(1)}, u32[]{:S(2)}, u32[]{:S(2)}) collective-permute-start(bf16[3,38,256]{2,1,0:T(8,128)(2,1)S(1)} %get-tuple-element.101), channel_id=1, source_target_pairs={{0,1},{1,0},{2,3},{3,2},{4,5},{5,4},{6,7},{7,6},{8,9},{9,8},{10,11... | collective-permute-start | bytes 175112 | tf_op jit(solution)/shard_map/ppermute | solution.py:25
  55.4 0.9 %collective-permute-start.17 = (bf16[256,256]{1,0:T(8,128)(2,1)S(1)}, bf16[256,256]{1,0:T(8,128)(2,1)S(1)}, u32[]{:S(2)}, u32[]{:S(2)}) collective-permute-start(bf16[256,256]{1,0:T(8,128)(2,1)S(1)} %slice.122), channel_id=1, source_target_pairs={{0,4},{1,3},{2,6},{3,1},{4,0},{5,7},{6,2},{7,5},{8,12},{9,11},{10,... | collective-permute-start | bytes 393224 | tf_op jit(solution)/shard_map/ppermute | solution.py:25
  56.4 3.3 %block_inner_conv.3.inner_ref = f32[2,24,32,128]{3,2,1,0:T(8,128)S(1)} custom-call(bf16[32,3,256]{2,1,0:T(4,128)(2,1)S(1)} %get-tuple-element.68.west_ref, bf16[32,32,256]{2,1,0:T(8,128)(2,1)S(1)} %bitcast.11, bf16[32,3,256]{2,1,0:T(4,128)(2,1)S(1)} %get-tuple-element.70.east_ref, bf16[7,7,256]{2,1,0:T(8,128)(2,1)S(1)} %copy-done.2), custom_call_target="tpu_custom_call" | custom-call | flops 25690112 | bytes 2097152 | tf_op jit(solution)/shard_map/block_inner_conv/pallas_call | solution.py:220
  59.8 1.2 %collective-permute-start.14 = (bf16[320,256]{1,0:T(8,128)(2,1)S(1)}, bf16[320,256]{1,0:T(8,128)(2,1)S(1)}, u32[]{:S(2)}, u32[]{:S(2)}) collective-permute-start(bf16[320,256]{1,0:T(8,128)(2,1)S(1)} %pad_maximum_fusion.2), channel_id=1, source_target_pairs={{0,4},{1,3},{2,6},{3,1},{4,0},{5,7},{6,2},{7,5},{8,12},{9,11},{10,... | collective-permute-start | bytes 491528 | tf_op jit(solution)/shard_map/ppermute | solution.py:25
  61.1 2.8 %block_adjoint.1 = bf16[32,32,256]{2,1,0:T(8,128)(2,1)} custom-call(s32[2]{0:T(128)S(1)} %add_convert_fusion.7.poles_ref, bf16[3,38,256]{2,1,0:T(8,128)(2,1)S(1)} %get-tuple-element.99.top_ref, bf16[32,3,256]{2,1,0:T(4,128)(2,1)S(1)} %get-tuple-element.68.west_ref, bf16[32,32,256]{2,1,0:T(8,128)(2,1)S(1)} %bitcast.12, ...), custom_call_target="tpu_custom_call" | custom-call | flops 6553600 | bytes 3145728 | tf_op jit(solution)/shard_map/block_adjoint/pallas_call | solution.py:622
  63.9 1.3 %collective-permute-done.14 = bf16[320,256]{1,0:T(8,128)(2,1)S(1)} collective-permute-done((bf16[320,256]{1,0:T(8,128)(2,1)S(1)}, bf16[320,256]{1,0:T(8,128)(2,1)S(1)}, u32[]{:S(2)}, u32[]{:S(2)}) %collective-permute-start.14) | collective-permute-done | bytes 163872 | tf_op jit(solution)/shard_map/ppermute | solution.py:25
  65.3 1.4 %collective-permute-done.19.pair_last_ref = bf16[320,256]{1,0:T(8,128)(2,1)S(1)} collective-permute-done((bf16[320,256]{1,0:T(8,128)(2,1)S(1)}, bf16[320,256]{1,0:T(8,128)(2,1)S(1)}, u32[]{:S(2)}, u32[]{:S(2)}) %collective-permute-start.19) | collective-permute-done | bytes 163872 | tf_op jit(solution)/shard_map/ppermute | solution.py:25
  66.7 2.1 %block_finish.1 = (f32[7,7,256]{2,1,0:T(8,128)}, f32[256]{0:T(256)}, f32[256]{0:T(256)}, f32[256]{0:T(256)}, f32[256,1024]{1,0:T(8,128)}, /*index=5*/f32[1024]{0:T(1024)}, f32[1024,256]{1,0:T(8,128)}, f32[256]{0:T(256)}) custom-call(s32[3]{0:T(128)S(1)} %pad_add_fusion.place_ref, bf16[768,256]{1,0:T(8,128)(2,1)S(1)} %pad_maximum_fusion.mine_ref, ...), custom_call_target="tpu_custom_call" | custom-call | tf_op jit(solution)/shard_map/block_finish/pallas_call | solution.py:535
  (67 shorter events, 1.5 us)
Async XLA Ops:
  1.7 11.9 %copy-start = (bf16[32,32,256]{2,1,0:T(8,128)(2,1)S(1)}, bf16[32,32,256]{2,1,0:T(8,128)(2,1)}, u32[]{:S(2)}) copy-start(bf16[32,32,256]{2,1,0:T(8,128)(2,1)} %field_ref.3) | copy-start | bytes 1572868
  1.7 7.4 %collective-permute-start = (bf16[32,3,256]{2,1,0:T(4,128)(2,1)S(1)}, bf16[32,3,256]{2,1,0:T(4,128)(2,1)S(1)}, u32[]{:S(2)}, u32[]{:S(2)}) collective-permute-start(bf16[32,3,256]{2,1,0:T(4,128)(2,1)S(1)} %get-tuple-element.90), channel_id=1, source_target_pairs={{0,4},{1,5},{2,6},{3,7},{4,0},{5,1},{6,2},{7,3},{8,12},{9,13},{10,... | collective-permute-start | bytes 147464 | tf_op jit(solution)/shard_map/ppermute | solution.py:25
  4.7 7.0 %collective-permute-start.1 = (bf16[32,3,256]{2,1,0:T(4,128)(2,1)S(1)}, bf16[32,3,256]{2,1,0:T(4,128)(2,1)S(1)}, u32[]{:S(2)}, u32[]{:S(2)}) collective-permute-start(bf16[32,3,256]{2,1,0:T(4,128)(2,1)S(1)} %get-tuple-element.91), channel_id=1, source_target_pairs={{0,28},{1,29},{2,30},{3,31},{4,8},{5,9},{6,10},{7,11},{8,4},{9,5},... | collective-permute-start | bytes 147464 | tf_op jit(solution)/shard_map/ppermute | solution.py:25
  11.8 1.8 %copy-start.2 = (bf16[7,7,256]{2,1,0:T(8,128)(2,1)S(1)}, bf16[7,7,256]{2,1,0:T(8,128)(2,1)}, u32[]{:S(2)}) copy-start(bf16[7,7,256]{2,1,0:T(8,128)(2,1)} %dw_ref.7) | copy-start | bytes 75268
  11.9 5.2 %collective-permute-start.3 = (bf16[3,38,256]{2,1,0:T(8,128)(2,1)S(1)}, bf16[3,38,256]{2,1,0:T(8,128)(2,1)S(1)}, u32[]{:S(2)}, u32[]{:S(2)}) collective-permute-start(bf16[3,38,256]{2,1,0:T(8,128)(2,1)S(1)} %reverse_select_fusion.1), channel_id=1, source_target_pairs={{0,16},{1,2},{2,1},{3,19},{4,20},{5,6},{6,5},{7,23},{8,24},{9,10},... | collective-permute-start | bytes 175112 | tf_op jit(solution)/shard_map/ppermute | solution.py:25
  12.7 4.3 %collective-permute-start.2 = (bf16[3,38,256]{2,1,0:T(8,128)(2,1)S(1)}, bf16[3,38,256]{2,1,0:T(8,128)(2,1)S(1)}, u32[]{:S(2)}, u32[]{:S(2)}) collective-permute-start(bf16[3,38,256]{2,1,0:T(8,128)(2,1)S(1)} %get-tuple-element.105), channel_id=1, source_target_pairs={{0,1},{1,0},{2,3},{3,2},{4,5},{5,4},{6,7},{7,6},{8,9},{9,8},{10,11... | collective-permute-start | bytes 175112 | tf_op jit(solution)/shard_map/ppermute | solution.py:25
  13.6 3.5 %copy-start.1 = (bf16[32,32,256]{2,1,0:T(8,128)(2,1)S(1)}, bf16[32,32,256]{2,1,0:T(8,128)(2,1)}, u32[]{:S(2)}) copy-start(bf16[32,32,256]{2,1,0:T(8,128)(2,1)} %cot_ref.1) | copy-start | bytes 1572868
  13.7 3.5 %copy-start.3 = (bf16[256,1024]{1,0:T(8,128)(2,1)S(1)}, bf16[256,1024]{1,0:T(8,128)(2,1)}, u32[]{:S(2)}) copy-start(bf16[256,1024]{1,0:T(8,128)(2,1)} %w_expand_ref.1) | copy-start | bytes 1572868
  13.7 3.5 %copy-start.4 = (bf16[1024,256]{1,0:T(8,128)(2,1)S(1)}, bf16[1024,256]{1,0:T(8,128)(2,1)}, u32[]{:S(2)}) copy-start(bf16[1024,256]{1,0:T(8,128)(2,1)} %w_project_ref.1) | copy-start | bytes 1572868
  17.1 0.7 copy-start.9
  17.1 0.7 copy-start.5
  17.1 0.7 copy-start.6
  17.1 0.7 copy-start.7
  17.1 0.7 copy-start.8
  25.3 1.6 %collective-permute-start.5 = (bf16[512,256]{1,0:T(8,128)(2,1)S(1)}, bf16[512,256]{1,0:T(8,128)(2,1)S(1)}, u32[]{:S(2)}, u32[]{:S(2)}) collective-permute-start(bf16[512,256]{1,0:T(8,128)(2,1)S(1)} %get-tuple-element.87), channel_id=1, source_target_pairs={{0,1},{1,0},{2,3},{3,2},{4,5},{5,4},{6,7},{7,6},{8,9},{9,8},{10,11... | collective-permute-start | bytes 786440 | tf_op jit(solution)/shard_map/ppermute | solution.py:25
  25.4 8.3 %collective-permute-start.4 = (bf16[512,256]{1,0:T(8,128)(2,1)S(1)}, bf16[512,256]{1,0:T(8,128)(2,1)S(1)}, u32[]{:S(2)}, u32[]{:S(2)}) collective-permute-start(bf16[512,256]{1,0:T(8,128)(2,1)S(1)} %get-tuple-element.86), channel_id=1, source_target_pairs={{0,1},{1,0},{2,3},{3,2},{4,5},{5,4},{6,7},{7,6},{8,9},{9,8},{10,11... | collective-permute-start | bytes 786440 | tf_op jit(solution)/shard_map/ppermute | solution.py:25
  27.0 6.7 %collective-permute-start.7 = (bf16[256,256]{1,0:T(8,128)(2,1)S(1)}, bf16[256,256]{1,0:T(8,128)(2,1)S(1)}, u32[]{:S(2)}, u32[]{:S(2)}) collective-permute-start(bf16[256,256]{1,0:T(8,128)(2,1)S(1)} %get-tuple-element.93), channel_id=1, source_target_pairs={{0,4},{1,3},{2,6},{3,1},{4,0},{5,7},{6,2},{7,5},{8,12},{9,11},{10,... | collective-permute-start | bytes 393224 | tf_op jit(solution)/shard_map/ppermute | solution.py:25
  27.1 10.9 %collective-permute-start.6 = (bf16[256,256]{1,0:T(8,128)(2,1)S(1)}, bf16[256,256]{1,0:T(8,128)(2,1)S(1)}, u32[]{:S(2)}, u32[]{:S(2)}) collective-permute-start(bf16[256,256]{1,0:T(8,128)(2,1)S(1)} %get-tuple-element.92), channel_id=1, source_target_pairs={{0,4},{1,3},{2,6},{3,1},{4,0},{5,7},{6,2},{7,5},{8,12},{9,11},{10,... | collective-permute-start | bytes 393224 | tf_op jit(solution)/shard_map/ppermute | solution.py:25
  33.8 5.0 %collective-permute-start.8 = (bf16[256,256]{1,0:T(8,128)(2,1)S(1)}, bf16[256,256]{1,0:T(8,128)(2,1)S(1)}, u32[]{:S(2)}, u32[]{:S(2)}) collective-permute-start(bf16[256,256]{1,0:T(8,128)(2,1)S(1)} %add_convert_fusion.4), channel_id=1, source_target_pairs={{0,2},{1,5},{2,0},{3,7},{4,6},{5,1},{6,4},{7,3},{8,10},{9,13},{10,... | collective-permute-start | bytes 393224 | tf_op jit(solution)/shard_map/ppermute | solution.py:25
  34.3 7.0 %collective-permute-start.11 = (bf16[32,3,256]{2,1,0:T(4,128)(2,1)S(1)}, bf16[32,3,256]{2,1,0:T(4,128)(2,1)S(1)}, u32[]{:S(2)}, u32[]{:S(2)}) collective-permute-start(bf16[32,3,256]{2,1,0:T(4,128)(2,1)S(1)} %get-tuple-element.84), channel_id=1, source_target_pairs={{0,28},{1,29},{2,30},{3,31},{4,8},{5,9},{6,10},{7,11},{8,4},{9,5},... | collective-permute-start | bytes 147464 | tf_op jit(solution)/shard_map/ppermute | solution.py:25
  37.9 4.3 %collective-permute-start.10 = (bf16[32,3,256]{2,1,0:T(4,128)(2,1)S(1)}, bf16[32,3,256]{2,1,0:T(4,128)(2,1)S(1)}, u32[]{:S(2)}, u32[]{:S(2)}) collective-permute-start(bf16[32,3,256]{2,1,0:T(4,128)(2,1)S(1)} %get-tuple-element.85), channel_id=1, source_target_pairs={{0,4},{1,5},{2,6},{3,7},{4,0},{5,1},{6,2},{7,3},{8,12},{9,13},{10,... | collective-permute-start | bytes 147464 | tf_op jit(solution)/shard_map/ppermute | solution.py:25
  38.9 6.0 %collective-permute-start.9 = (bf16[320,256]{1,0:T(8,128)(2,1)S(1)}, bf16[320,256]{1,0:T(8,128)(2,1)S(1)}, u32[]{:S(2)}, u32[]{:S(2)}) collective-permute-start(bf16[320,256]{1,0:T(8,128)(2,1)S(1)} %pad_maximum_fusion.1), channel_id=1, source_target_pairs={{0,8},{1,17},{2,10},{3,19},{4,12},{5,21},{6,14},{7,23},{8,0},{9,25... | collective-permute-start | bytes 491528 | tf_op jit(solution)/shard_map/ppermute | solution.py:25
  44.9 8.0 %collective-permute-start.12 = (bf16[320,256]{1,0:T(8,128)(2,1)S(1)}, bf16[320,256]{1,0:T(8,128)(2,1)S(1)}, u32[]{:S(2)}, u32[]{:S(2)}) collective-permute-start(bf16[320,256]{1,0:T(8,128)(2,1)S(1)} %add_convert_fusion.2), channel_id=1, source_target_pairs={{0,16},{1,9},{2,18},{3,11},{4,20},{5,13},{6,22},{7,15},{8,24},{9,1... | collective-permute-start | bytes 491528 | tf_op jit(solution)/shard_map/ppermute | solution.py:25
  53.0 6.7 %collective-permute-start.13 = (bf16[320,256]{1,0:T(8,128)(2,1)S(1)}, bf16[320,256]{1,0:T(8,128)(2,1)S(1)}, u32[]{:S(2)}, u32[]{:S(2)}) collective-permute-start(bf16[320,256]{1,0:T(8,128)(2,1)S(1)} %add_convert_fusion.1), channel_id=1, source_target_pairs={{0,2},{1,5},{2,0},{3,7},{4,6},{5,1},{6,4},{7,3},{8,10},{9,13},{10,... | collective-permute-start | bytes 491528 | tf_op jit(solution)/shard_map/ppermute | solution.py:25
  54.6 6.3 %collective-permute-start.16 = (bf16[3,38,256]{2,1,0:T(8,128)(2,1)S(1)}, bf16[3,38,256]{2,1,0:T(8,128)(2,1)S(1)}, u32[]{:S(2)}, u32[]{:S(2)}) collective-permute-start(bf16[3,38,256]{2,1,0:T(8,128)(2,1)S(1)} %reverse_select_fusion), channel_id=1, source_target_pairs={{0,16},{1,2},{2,1},{3,19},{4,20},{5,6},{6,5},{7,23},{8,24},{9,10},... | collective-permute-start | bytes 175112 | tf_op jit(solution)/shard_map/ppermute | solution.py:25
  54.7 6.3 %collective-permute-start.15 = (bf16[3,38,256]{2,1,0:T(8,128)(2,1)S(1)}, bf16[3,38,256]{2,1,0:T(8,128)(2,1)S(1)}, u32[]{:S(2)}, u32[]{:S(2)}) collective-permute-start(bf16[3,38,256]{2,1,0:T(8,128)(2,1)S(1)} %get-tuple-element.101), channel_id=1, source_target_pairs={{0,1},{1,0},{2,3},{3,2},{4,5},{5,4},{6,7},{7,6},{8,9},{9,8},{10,11... | collective-permute-start | bytes 175112 | tf_op jit(solution)/shard_map/ppermute | solution.py:25
  55.4 5.5 %collective-permute-start.17 = (bf16[256,256]{1,0:T(8,128)(2,1)S(1)}, bf16[256,256]{1,0:T(8,128)(2,1)S(1)}, u32[]{:S(2)}, u32[]{:S(2)}) collective-permute-start(bf16[256,256]{1,0:T(8,128)(2,1)S(1)} %slice.122), channel_id=1, source_target_pairs={{0,4},{1,3},{2,6},{3,1},{4,0},{5,7},{6,2},{7,5},{8,12},{9,11},{10,... | collective-permute-start | bytes 393224 | tf_op jit(solution)/shard_map/ppermute | solution.py:25
  59.8 5.4 %collective-permute-start.14 = (bf16[320,256]{1,0:T(8,128)(2,1)S(1)}, bf16[320,256]{1,0:T(8,128)(2,1)S(1)}, u32[]{:S(2)}, u32[]{:S(2)}) collective-permute-start(bf16[320,256]{1,0:T(8,128)(2,1)S(1)} %pad_maximum_fusion.2), channel_id=1, source_target_pairs={{0,4},{1,3},{2,6},{3,1},{4,0},{5,7},{6,2},{7,5},{8,12},{9,11},{10,... | collective-permute-start | bytes 491528 | tf_op jit(solution)/shard_map/ppermute | solution.py:25
  61.0 5.7 %collective-permute-start.18 = (bf16[768,256]{1,0:T(8,128)(2,1)S(1)}, bf16[768,256]{1,0:T(8,128)(2,1)S(1)}, u32[]{:S(2)}, u32[]{:S(2)}) collective-permute-start(bf16[768,256]{1,0:T(8,128)(2,1)S(1)} %pad_maximum_fusion.mine_ref), channel_id=1, source_target_pairs={{0,1},{1,0},{2,3},{3,2},{4,5},{5,4},{6,7},{7,6},{8,9},{9,8},{10,11... | collective-permute-start | bytes 1179656 | tf_op jit(solution)/shard_map/ppermute | solution.py:25
  65.2 1.5 %collective-permute-start.19 = (bf16[320,256]{1,0:T(8,128)(2,1)S(1)}, bf16[320,256]{1,0:T(8,128)(2,1)S(1)}, u32[]{:S(2)}, u32[]{:S(2)}) collective-permute-start(bf16[320,256]{1,0:T(8,128)(2,1)S(1)} %pad_maximum_fusion.3.last_ref), channel_id=1, source_target_pairs={{0,1},{1,0},{2,3},{3,2},{4,5},{5,4},{6,7},{7,6},{8,9},{9,8},{10,11... | collective-permute-start | bytes 491528 | tf_op jit(solution)/shard_map/ppermute | solution.py:25

commit v6 on v5

--- a/solution.py
+++ b/solution.py
@@ -80,7 +80,6 @@
 
 
 def partner_steps():
-    core = lax.axis_index("lat") % 2
     steps = axis_bits()
     other = list(steps)
     for at in range(0, len(steps) - 1, 2):
@@ -89,15 +88,20 @@
     def exchange(value, at):
         return send(value, lambda lon, lat: flip((lon, lat), (other if lat % 2 else steps)[at]))
 
+    return len(steps), exchange
+
+
+def places():
     def order(first):
         high, low = (
-            lax.shift_right_logical(lax.axis_index(axis), bit) & 1 for axis, bit in first[:2]
+            lax.shift_right_logical(lax.axis_index(axis), bit) & 1 for axis, bit in first
         )
         return 2 * high + low
 
-    own, pair = order(steps), order(other)
-    place = jnp.stack([core, jnp.where(core == 0, own, pair), jnp.where(core == 0, pair, own)])
-    return len(steps), exchange, place.astype(jnp.int32)
+    core = lax.axis_index("lat") & 1
+    steps = axis_bits()[:2]
+    plain, turned = order(steps), order(steps[::-1])
+    return core, jnp.where(core == 0, plain, turned), jnp.where(core == 0, turned, plain)
 
 
 def within_pair(value):
@@ -234,9 +238,25 @@
     )(*band, dw_kernel)
 
 
+def pack_kernel(*refs):
+    for at, ref in enumerate(refs[:-1]):
+        refs[-1][at : at + 1, : ref.shape[0]] = ref[...].astype(jnp.float32).reshape(1, -1)
+
+
+def packed(vectors):
+    width = max(vector.shape[0] for vector in vectors)
+    return pl.pallas_call(
+        pack_kernel,
+        out_shape=jax.ShapeDtypeStruct((8, width), jnp.float32),
+        in_specs=[pl.BlockSpec(memory_space=pltpu.VMEM)] * len(vectors),
+        out_specs=pl.BlockSpec(memory_space=pltpu.VMEM),
+        compiler_params=pltpu.CompilerParams(vmem_limit_bytes=1 << 20),
+        name="block_pack",
+    )(*vectors)
+
+
 def main_kernel(
     scale_factor,
-    place_ref,
     top_ref,
     west_ref,
     fields_ref,
@@ -245,11 +265,7 @@
     inner_ref,
     cot_ref,
     dw_ref,
-    dw_bias_ref,
-    gain_ref,
-    offset_ref,
-    b_project_ref,
-    b_expand_ref,
+    vectors_ref,
     w_expand_ref,
     w_project_ref,
     out_ref,
@@ -288,11 +304,8 @@
 
     lax.fori_loop(0, tiles * 2, conv_edge, 0)
     small_ref[...] = jnp.zeros_like(small_ref)
-    dw_bias, gain, offset, b_project = (
-        ref[...].astype(jnp.float32).reshape(1, chans)
-        for ref in (dw_bias_ref, gain_ref, offset_ref, b_project_ref)
-    )
-    b_expand = b_expand_ref[...].astype(jnp.float32).reshape(1, hidden_units)
+    dw_bias, gain, offset, b_project = (vectors_ref[at : at + 1, :chans] for at in range(4))
+    b_expand = vectors_ref[4:5]
 
     conv = jnp.concatenate(
         [
@@ -344,20 +357,21 @@
     dconv_ref[...] = d_conv
     small_ref[...] = small_ref[...] * scale_factor
     quarter = hidden_units // 4
+    place = places()
 
     def finish(mine, other):
         for at in range(4):
             part = slice(at * quarter, (at + 1) * quarter)
-            here = pl.multiple_of((at ^ place_ref[1]) * quarter, quarter)
-            there = pl.multiple_of((at ^ place_ref[2]) * quarter, quarter)
+            here = pl.multiple_of((at ^ place[1]) * quarter, quarter)
+            there = pl.multiple_of((at ^ place[2]) * quarter, quarter)
             keep_ref[pl.ds(here, quarter)] = mine[part] * scale_factor
             give_ref[pl.ds(there, quarter)] = (other[part] * scale_factor).astype(jnp.bfloat16)
 
-    @pl.when(place_ref[0] == 0)
+    @pl.when(place[0] == 0)
     def first():
         finish(expand_ref, project_ref)
 
-    @pl.when(place_ref[0] != 0)
+    @pl.when(place[0] != 0)
     def second():
         finish(project_ref, expand_ref)
 
@@ -372,7 +386,7 @@
 
 
 def main_pass(
-    place, top, band, bottom, inner, cot, dw_kernel, vectors, w_expand, w_project, scale_factor
+    top, band, bottom, inner, cot, dw_kernel, vectors, w_expand, w_project, scale_factor
 ):
     rows, cols, chans = band[1].shape
     hidden_units = w_expand.shape[1]
@@ -387,8 +401,7 @@
             jax.ShapeDtypeStruct((hidden_units, chans), jnp.bfloat16),
             jax.ShapeDtypeStruct((8 + hidden_units // chans, chans), jnp.float32),
         ],
-        in_specs=[pl.BlockSpec(memory_space=pltpu.SMEM)]
-        + [pl.BlockSpec(memory_space=pltpu.VMEM)] * 15,
+        in_specs=[pl.BlockSpec(memory_space=pltpu.VMEM)] * 11,
         out_specs=[pl.BlockSpec(memory_space=pltpu.VMEM)] * 5,
         scratch_shapes=[
             pltpu.VMEM((tiles, 20, cols + 6, LANES), jnp.float32),
@@ -404,7 +417,7 @@
             transcendentals=2 * cells * hidden_units,
         ),
         name="block_main",
-    )(place, top, *band, bottom, inner, cot, dw_kernel, *vectors, w_expand, w_project)
+    )(top, *band, bottom, inner, cot, dw_kernel, vectors, w_expand, w_project)
 
 
 def taps_kernel(
@@ -479,12 +492,75 @@
     )(top, *band, bottom, conv_gradient, small)
 
 
+def write_pieces(
+    mine_ref, pair_ref, first, count, expand_ref, project_ref, held_ref, sems
+):
+    chans = project_ref.shape[1]
+    place = places()
+
+    def write(columns_ref, columns_order, rows_ref, rows_order):
+        copies = []
+        for at in range(count):
+            part = slice(at * chans, (at + 1) * chans)
+            column = pl.multiple_of(((first + at) ^ columns_order) * chans, chans)
+            row = pl.multiple_of(((first + at) ^ rows_order) * chans, chans)
+            held_ref[2 * at] = columns_ref[part].astype(jnp.float32)
+            copies.append(
+                pltpu.make_async_copy(
+                    held_ref.at[2 * at], expand_ref.at[:, pl.ds(column, chans)], sems.at[2 * at]
+                )
+            )
+            copies[-1].start()
+            held_ref[2 * at + 1] = rows_ref[part].astype(jnp.float32)
+            copies.append(
+                pltpu.make_async_copy(
+                    held_ref.at[2 * at + 1], project_ref.at[pl.ds(row, chans)], sems.at[2 * at + 1]
+                )
+            )
+            copies[-1].start()
+        for copy in copies:
+            copy.wait()
+
+    @pl.when(place[0] == 0)
+    def even():
+        write(mine_ref, place[1], pair_ref, place[2])
+
+    @pl.when(place[0] != 0)
+    def odd():
+        write(pair_ref, place[2], mine_ref, place[1])
+
+
+def early_kernel(mine_ref, pair_ref, expand_ref, project_ref, held_ref, sems):
+    count = mine_ref.shape[0] // project_ref.shape[1]
+    write_pieces(mine_ref, pair_ref, 0, count, expand_ref, project_ref, held_ref, sems)
+
+
+def early_pass(mine, pair, hidden_units):
+    chans = mine.shape[1]
+    count = mine.shape[0] // chans
+    return pl.pallas_call(
+        early_kernel,
+        out_shape=[
+            jax.ShapeDtypeStruct((chans, hidden_units), jnp.float32),
+            jax.ShapeDtypeStruct((hidden_units, chans), jnp.float32),
+        ],
+        in_specs=[pl.BlockSpec(memory_space=pltpu.VMEM)] * 2,
+        out_specs=[pl.BlockSpec(memory_space=pl.ANY)] * 2,
+        scratch_shapes=[
+            pltpu.VMEM((2 * count, chans, chans), jnp.float32),
+            pltpu.SemaphoreType.DMA((2 * count,)),
+        ],
+        compiler_params=pltpu.CompilerParams(vmem_limit_bytes=6 << 20),
+        cost_estimate=pl.CostEstimate(flops=0, bytes_accessed=4 << 20, transcendentals=0),
+        name="block_early",
+    )(mine, pair)
+
+
 def finish_kernel(
-    place_ref,
-    mine_ref,
     last_ref,
-    pair_ref,
     pair_last_ref,
+    expand_in_ref,
+    project_in_ref,
     kern_ref,
     dwb_ref,
     gain_ref,
@@ -494,11 +570,13 @@
     project_ref,
     b_project_ref,
     sums_ref,
+    held_ref,
+    sems,
 ):
     hidden_units, chans = project_ref.shape
     pieces = hidden_units // chans
-    early = mine_ref.shape[0] // chans
-    small = slice(hidden_units - early * chans, last_ref.shape[0])
+    count = held_ref.shape[0] // 2
+    small = slice(count * chans, last_ref.shape[0])
     sums_ref[...] = last_ref[small].astype(jnp.float32) + pair_last_ref[small].astype(jnp.float32)
     for row_off in range(7):
         kern_ref[row_off] = sums_ref[row_off * 7 : row_off * 7 + 7]
@@ -508,30 +586,24 @@
     b_project_ref[...] = sums_ref[52]
     for piece in range(pieces):
         b_expand_ref[piece * chans : (piece + 1) * chans] = sums_ref[53 + piece]
-
-    def write(first_refs, first_order, second_refs, second_order):
-        for at in range(pieces):
-            late = at >= early
-            part = pl.ds((at - early if late else at) * chans, chans)
-            columns = pl.multiple_of((at ^ first_order) * chans, chans)
-            expand_ref[:, pl.ds(columns, chans)] = first_refs[late][part].astype(jnp.float32)
-            to = pl.multiple_of((at ^ second_order) * chans, chans)
-            project_ref[pl.ds(to, chans)] = second_refs[late][part].astype(jnp.float32)
-
-    mine_refs, pair_refs = (mine_ref, last_ref), (pair_ref, pair_last_ref)
-
-    @pl.when(place_ref[0] == 0)
-    def first():
-        write(mine_refs, place_ref[1], pair_refs, place_ref[2])
-
-    @pl.when(place_ref[0] != 0)
-    def second():
-        write(pair_refs, place_ref[2], mine_refs, place_ref[1])
-
-
-def finish_pass(place, mine, last, pair, pair_last, hidden_units):
-    chans = mine.shape[1]
+    write_pieces(
+        last_ref,
+        pair_last_ref,
+        pieces - count,
+        count,
+        expand_ref,
+        project_ref,
+        held_ref,
+        sems,
+    )
+
+
+def finish_pass(last, pair_last, expand, project, early):
+    hidden_units, chans = project.shape
+    count = (hidden_units - early) // chans
     one = jax.ShapeDtypeStruct((chans,), jnp.float32)
+    whole = pl.BlockSpec(memory_space=pltpu.VMEM)
+    left = pl.BlockSpec(memory_space=pl.ANY)
     return pl.pallas_call(
         finish_kernel,
         out_shape=[
@@ -544,17 +616,20 @@
             jax.ShapeDtypeStruct((hidden_units, chans), jnp.float32),
             one,
         ],
-        in_specs=[pl.BlockSpec(memory_space=pltpu.SMEM)]
-        + [pl.BlockSpec(memory_space=pltpu.VMEM)] * 4,
-        out_specs=[pl.BlockSpec(memory_space=pltpu.VMEM)] * 8,
-        scratch_shapes=[pltpu.VMEM((mine.shape[0] + last.shape[0] - hidden_units, chans), jnp.float32)],
-        compiler_params=pltpu.CompilerParams(vmem_limit_bytes=8 << 20),
+        in_specs=[whole, whole, left, left],
+        out_specs=[whole, whole, whole, whole, left, whole, left, whole],
+        scratch_shapes=[
+            pltpu.VMEM((last.shape[0] - count * chans, chans), jnp.float32),
+            pltpu.VMEM((2 * count, chans, chans), jnp.float32),
+            pltpu.SemaphoreType.DMA((2 * count,)),
+        ],
+        input_output_aliases={2: 4, 3: 6},
+        compiler_params=pltpu.CompilerParams(vmem_limit_bytes=6 << 20),
         name="block_finish",
-    )(place, mine, last, pair, pair_last)
+    )(last, pair_last, expand, project)
 
 
 def adjoint_kernel(
-    poles_ref,
     top_ref,
     west_ref,
     field_ref,
@@ -578,7 +653,7 @@
     split_band(band_refs, split_ref, start=rows - 7, to=10, count=7)
     split_lanes(bottom_ref, split_ref, to=17)
     for side in range(2):
-        at_pole = poles_ref[side] == 1
+        at_pole = lax.axis_index("lat") == (0 if side == 0 else lax.axis_size("lat") - 1)
         for lane in range(tiles):
             for row_off in range(3):
                 near = row_off if side == 0 else 6 - row_off
@@ -616,14 +691,13 @@
     write(sum_ref, 4, rows - 4, 4)
 
 
-def adjoint_pass(top, band, bottom, inner, cot, dw_kernel, poles):
+def adjoint_pass(top, band, bottom, inner, cot, dw_kernel):
     rows, cols, chans = cot.shape
     tiles = chans // LANES
     return pl.pallas_call(
         adjoint_kernel,
         out_shape=jax.ShapeDtypeStruct(cot.shape, jnp.bfloat16),
-        in_specs=[pl.BlockSpec(memory_space=pltpu.SMEM)]
-        + [pl.BlockSpec(memory_space=pltpu.VMEM)] * 8,
+        in_specs=[pl.BlockSpec(memory_space=pltpu.VMEM)] * 8,
         out_specs=pl.BlockSpec(memory_space=pltpu.VMEM),
         scratch_shapes=[
             pltpu.VMEM((tiles, 20, cols + 6, LANES), jnp.float32),
@@ -636,7 +710,7 @@
             flops=25 * rows * cols * chans, bytes_accessed=3 << 20, transcendentals=0
         ),
         name="block_adjoint",
-    )(poles, top, *band, bottom, inner, cot, dw_kernel)
+    )(top, *band, bottom, inner, cot, dw_kernel)
 
 
 def local(
@@ -656,28 +730,27 @@
     chans = fields.shape[2]
     scale_factor = 1.0 / math.sqrt(rows * cols * lax.axis_size("lat") * lax.axis_size("lon"))
     hidden_units = w_expand.shape[1]
-    lat = lax.axis_index("lat")
-    poles = jnp.stack([lat == 0, lat == lax.axis_size("lat") - 1]).astype(jnp.int32)
-    count, exchange, place = partner_steps()
+    count, exchange = partner_steps()
+    barrier = lax.optimization_barrier
     band = lon_margins(fields)
+    vectors = packed((dw_bias, norm_gain, layer_norm_offset, b_project, b_expand))
+    band, vectors = barrier((band, vectors))
     inner = inner_conv(band, dw_kernel, False)
     edges = lat_margins(band)
     block_out, conv_gradient, keep, give, small = main_pass(
-        place,
         edges[0],
         band,
         edges[1],
         inner,
         cotangent.reshape(-1, chans),
         dw_kernel,
-        (dw_bias, norm_gain, layer_norm_offset, b_project, b_expand),
+        vectors,
         w_expand,
         w_project,
         scale_factor,
     )
     block_out = block_out.reshape(fields.shape)
     conv_gradient = conv_gradient.reshape(fields.shape)
-    barrier = lax.optimization_barrier
     half = hidden_units // 2
     quarter = half // 2
     got_far = within_pair(give[half:])
@@ -709,14 +782,15 @@
     sent = jnp.concatenate([beside, small], axis=0)
     sent, band = barrier((sent, band))
     got = exchange(sent, 0)
-    grad_fields = adjoint_pass(top, band, bottom, inner, cotangent, dw_kernel, poles)
+    grad_fields = adjoint_pass(top, band, bottom, inner, cotangent, dw_kernel)
     mine = jnp.concatenate([payload[:quarter], beside, across], axis=0)
     pair = within_pair(mine)
-    got, grad_fields = barrier((got, grad_fields))
+    written = early_pass(mine, pair, hidden_units)
+    got, grad_fields, written = barrier((got, grad_fields, written))
     last = jnp.concatenate([got[:quarter], rounded_sum(small, got[quarter:])], axis=0)
     pair_last = within_pair(last)
     sum_kern, sum_dwb, sum_gn, sum_sh, sum_exp, sum_bexp, sum_proj, sum_bproj = finish_pass(
-        place, mine, last, pair, pair_last, hidden_units
+        last, pair_last, *written, mine.shape[0]
     )
     return (
         block_out,

time: 69.7 us -> 67.7 us (0.971); the launches traced: 68.7 us -> 67.5 us
  starting transfers between devices: 22.4 us -> 18.6 us
  local copies, waits for them, and re-layouts: 1.62 us -> 3.45 us
  waiting for transfers between devices: 18.2 us -> 19.5 us
    ppermute x20, starting transfers between devices: 22.4 us -> 18.6 us  [send(): return lax.ppermute(value, ('lon', 'lat'), flat_pairs(target))]
    unnamed x20, local copies, waits for them, and re-layouts: 0.67 us -> 3.32 us
    ppermute x20, waiting for transfers between devices: 18.2 us -> 19.5 us  [send(): return lax.ppermute(value, ('lon', 'lat'), flat_pairs(target))]
    pallas_call x0 -> x2, Pallas kernels: none -> 1.22 us  [the longest x1 1.2 us: early_pass(): pl.pallas_call(early_kernel, out_shape=[jax.ShapeDtypeStruct((chans, hidd...]
    select_n x2 -> x0, other arithmetic: 1.11 us -> none  [the longest x1 1.05 us: lon_margins(): inner = send(jnp.where(odd, first, last), lambda lon, lat: (lon ^ 1, lat))]
    select_n x1 -> x2, other arithmetic: 0.08 us -> 1.18 us  [lon_margins(): jnp.where(odd, last, first)]
    slice x5, local copies, waits for them, and re-layouts: 0.86 us -> 0.04 us  [lat_margins(): first = jnp.concatenate([part[:3] for part in band], axis=1)]
  transfers between devices with their start and end apart: 20 -> 20, of which waited for: 10 -> 10; matrix products, arithmetic and copies ran while one was open for 2% -> 1% of each run, Pallas kernels for 20% -> 22%
where the time goes in v6:
time: 67.7 us; the launch traced here: 67.5 us
  Pallas kernels  23.1 us (34%)
  waiting for transfers between devices  19.5 us (29%)
  starting transfers between devices  18.6 us (27%)
  local copies, waits for them, and re-layouts  3.45 us (5%)
  other arithmetic  1.81 us (3%)
  between operations  0.98 us (1%)
    ppermute x20, waiting for transfers between devices, send(): return lax.ppermute(value, ('lon', 'lat'), flat_pairs(target))  19.5 us
    ppermute x20, starting transfers between devices, send(): return lax.ppermute(value, ('lon', 'lat'), flat_pairs(target))  18.6 us
    pallas_call x1, Pallas kernels, main_pass(): pl.pallas_call(functools.partial(main_kernel, scale_factor), out_shape=[j...  6.92 us
    pallas_call x2, Pallas kernels, inner_conv(): pl.pallas_call(functools.partial(inner_conv_kernel, flipped), out_shape=j...  6.64 us
    pallas_call x1, Pallas kernels, taps_pass(): pl.pallas_call(functools.partial(taps_kernel, scale_factor), out_shape=ja...  4.59 us
    unnamed x20, local copies, waits for them, and re-layouts  3.32 us
    pallas_call x1, Pallas kernels, adjoint_pass(): pl.pallas_call(adjoint_kernel, out_shape=jax.ShapeDtypeStruct(cot.shape,...  2.25 us
    pallas_call x1, Pallas kernels, finish_pass(): pl.pallas_call(finish_kernel, out_shape=[jax.ShapeDtypeStruct((7, 7, chan...  1.48 us
  transfers between devices with their start and end apart: 20, of which 10 were waited for; matrix products, arithmetic and copies ran while one was open for 1% of the time, Pallas kernels for 22%

profile of v6, /device:TPU:0, one launch (start us, length us, event | category | flops | bytes accessed | tf_op | source)
XLA Modules:
  0.0 67.5 jit_solution(1739985435728247336)
XLA Ops:
  0.7 1.1 %broadcast_select_fusion.6 = (bf16[32,3,256]{2,1,0:T(4,128)(2,1)S(1)}, bf16[32,3,256]{2,1,0:T(4,128)(2,1)S(1)}) fusion(pred[]{:T(512)S(6)} %eq.22, bf16[32,32,256]{2,1,0:T(8,128)(2,1)} %field_ref.1), kind=kLoop, calls=%fused_computation.19 | loop fusion | flops 49152 | bytes 196609 | tf_op jit(solution)/shard_map/jit(_where)/select_n | solution.py:33
  1.8 6.0 %collective-permute-start.1 = (bf16[32,3,256]{2,1,0:T(4,128)(2,1)S(1)}, bf16[32,3,256]{2,1,0:T(4,128)(2,1)S(1)}, u32[]{:S(2)}, u32[]{:S(2)}) collective-permute-start(bf16[32,3,256]{2,1,0:T(4,128)(2,1)S(1)} %get-tuple-element.106), channel_id=1, source_target_pairs={{0,28},{1,29},{2,30},{3,31},{4,8},{5,9},{6,10},{7,11},{8,4},{9,5},... | collective-permute-start | bytes 147464 | tf_op jit(solution)/shard_map/ppermute | solution.py:25
  7.8 0.7 %copy-done.3 = bf16[1024]{0:T(1024)(128)(2,1)S(1)} copy-done((bf16[1024]{0:T(1024)(128)(2,1)S(1)}, bf16[1024]{0:T(1024)(128)(2,1)}, u32[]{:S(2)}) %copy-start.3) | copy-done | bytes 2072
  8.5 0.7 copy-done.4
  9.2 0.7 copy-done.5
  9.8 0.7 copy-done.6
  10.5 0.7 copy-done.7
  11.1 0.9 %collective-permute-done = bf16[32,3,256]{2,1,0:T(4,128)(2,1)S(1)} collective-permute-done((bf16[32,3,256]{2,1,0:T(4,128)(2,1)S(1)}, bf16[32,3,256]{2,1,0:T(4,128)(2,1)S(1)}, u32[]{:S(2)}, u32[]{:S(2)}) %collective-permute-start) | collective-permute-done | bytes 49184 | tf_op jit(solution)/shard_map/ppermute | solution.py:25
  12.5 1.5 %collective-permute-start.2 = (bf16[3,38,256]{2,1,0:T(8,128)(2,1)S(1)}, bf16[3,38,256]{2,1,0:T(8,128)(2,1)S(1)}, u32[]{:S(2)}, u32[]{:S(2)}) collective-permute-start(bf16[3,38,256]{2,1,0:T(8,128)(2,1)S(1)} %get-tuple-element.121), channel_id=1, source_target_pairs={{0,1},{1,0},{2,3},{3,2},{4,5},{5,4},{6,7},{7,6},{8,9},{9,8},{10,11... | collective-permute-start | bytes 175112 | tf_op jit(solution)/shard_map/ppermute | solution.py:25
  14.0 3.3 %block_inner_conv.2.inner_ref = f32[2,24,32,128]{3,2,1,0:T(8,128)S(1)} custom-call(bf16[32,3,256]{2,1,0:T(4,128)(2,1)S(1)} %get-tuple-element.54.west_ref, bf16[32,32,256]{2,1,0:T(8,128)(2,1)S(1)} %copy-done, bf16[32,3,256]{2,1,0:T(4,128)(2,1)S(1)} %get-tuple-element.56.east_ref, bf16[7,7,256]{2,1,0:T(8,128)(2,1)S(1)} %copy-done.2), custom_call_target="tpu_custom_call" | custom-call | flops 25690112 | bytes 2097152 | tf_op jit(solution)/shard_map/block_inner_conv/pallas_call | solution.py:224
  17.5 6.9 %block_main.1 = (bf16[1024,256]{1,0:T(8,128)(2,1)}, bf16[1024,256]{1,0:T(8,128)(2,1)S(1)}, f32[1024,256]{1,0:T(8,128)S(1)}, bf16[1024,256]{1,0:T(8,128)(2,1)S(1)}, f32[12,256]{1,0:T(8,128)S(1)}) custom-call(bf16[3,38,256]{2,1,0:T(8,128)(2,1)S(1)} %get-tuple-element.119.top_ref, bf16[32,3,256]{2,1,0:T(4,128)(2,1)S(1)} %get-tuple-element.54.west_ref, ...), custom_call_target="tpu_custom_call" | custom-call | flops 3221225472 | bytes 8388608 | tf_op jit(solution)/shard_map/block_main/pallas_call | solution.py:395
  24.6 0.5 collective-permute-start.4
  25.1 1.0 %collective-permute-done.5 = bf16[512,256]{1,0:T(8,128)(2,1)S(1)} collective-permute-done((bf16[512,256]{1,0:T(8,128)(2,1)S(1)}, bf16[512,256]{1,0:T(8,128)(2,1)S(1)}, u32[]{:S(2)}, u32[]{:S(2)}) %collective-permute-start.5) | collective-permute-done | bytes 262176 | tf_op jit(solution)/shard_map/ppermute | solution.py:25
  26.2 1.2 %collective-permute-start.7 = (bf16[256,256]{1,0:T(8,128)(2,1)S(1)}, bf16[256,256]{1,0:T(8,128)(2,1)S(1)}, u32[]{:S(2)}, u32[]{:S(2)}) collective-permute-start(bf16[256,256]{1,0:T(8,128)(2,1)S(1)} %get-tuple-element.109), channel_id=1, source_target_pairs={{0,4},{1,3},{2,6},{3,1},{4,0},{5,7},{6,2},{7,5},{8,12},{9,11},{10,... | collective-permute-start | bytes 393224 | tf_op jit(solution)/shard_map/ppermute | solution.py:25
  27.3 0.9 %collective-permute-start.6 = (bf16[256,256]{1,0:T(8,128)(2,1)S(1)}, bf16[256,256]{1,0:T(8,128)(2,1)S(1)}, u32[]{:S(2)}, u32[]{:S(2)}) collective-permute-start(bf16[256,256]{1,0:T(8,128)(2,1)S(1)} %get-tuple-element.108), channel_id=1, source_target_pairs={{0,4},{1,3},{2,6},{3,1},{4,0},{5,7},{6,2},{7,5},{8,12},{9,11},{10,... | collective-permute-start | bytes 393224 | tf_op jit(solution)/shard_map/ppermute | solution.py:25
  28.3 4.6 %block_taps.1 = bf16[64,256]{1,0:T(8,128)(2,1)S(1)} custom-call(bf16[3,38,256]{2,1,0:T(8,128)(2,1)S(1)} %get-tuple-element.119.top_ref, bf16[32,3,256]{2,1,0:T(4,128)(2,1)S(1)} %get-tuple-element.54.west_ref, bf16[32,32,256]{2,1,0:T(8,128)(2,1)S(1)} %copy-done, bf16[32,3,256]{2,1,0:T(4,128)(2,1)S(1)} %get-tuple-element.56.east_ref, ...), custom_call_target="tpu_custom_call" | custom-call | flops 25690112 | bytes 3145728 | tf_op jit(solution)/shard_map/block_taps/pallas_call | solution.py:477
  33.5 2.8 %collective-permute-start.11 = (bf16[32,3,256]{2,1,0:T(4,128)(2,1)S(1)}, bf16[32,3,256]{2,1,0:T(4,128)(2,1)S(1)}, u32[]{:S(2)}, u32[]{:S(2)}) collective-permute-start(bf16[32,3,256]{2,1,0:T(4,128)(2,1)S(1)} %get-tuple-element.100), channel_id=1, source_target_pairs={{0,28},{1,29},{2,30},{3,31},{4,8},{5,9},{6,10},{7,11},{8,4},{9,5},... | collective-permute-start | bytes 147464 | tf_op jit(solution)/shard_map/ppermute | solution.py:25
  36.2 1.7 %collective-permute-done.8 = bf16[256,256]{1,0:T(8,128)(2,1)S(1)} collective-permute-done((bf16[256,256]{1,0:T(8,128)(2,1)S(1)}, bf16[256,256]{1,0:T(8,128)(2,1)S(1)}, u32[]{:S(2)}, u32[]{:S(2)}) %collective-permute-start.8) | collective-permute-done | bytes 131104 | tf_op jit(solution)/shard_map/ppermute | solution.py:25
  38.4 2.2 %collective-permute-done.11 = bf16[32,3,256]{2,1,0:T(4,128)(2,1)S(1)} collective-permute-done((bf16[32,3,256]{2,1,0:T(4,128)(2,1)S(1)}, bf16[32,3,256]{2,1,0:T(4,128)(2,1)S(1)}, u32[]{:S(2)}, u32[]{:S(2)}) %collective-permute-start.11) | collective-permute-done | bytes 49184 | tf_op jit(solution)/shard_map/ppermute | solution.py:25
  40.6 0.6 collective-permute-done.10
  41.2 3.7 %collective-permute-done.9 = bf16[320,256]{1,0:T(8,128)(2,1)S(1)} collective-permute-done((bf16[320,256]{1,0:T(8,128)(2,1)S(1)}, bf16[320,256]{1,0:T(8,128)(2,1)S(1)}, u32[]{:S(2)}, u32[]{:S(2)}) %collective-permute-start.9) | collective-permute-done | bytes 163872 | tf_op jit(solution)/shard_map/ppermute | solution.py:25
  45.1 6.9 %collective-permute-done.12 = bf16[320,256]{1,0:T(8,128)(2,1)S(1)} collective-permute-done((bf16[320,256]{1,0:T(8,128)(2,1)S(1)}, bf16[320,256]{1,0:T(8,128)(2,1)S(1)}, u32[]{:S(2)}, u32[]{:S(2)}) %collective-permute-start.12) | collective-permute-done | bytes 163872 | tf_op jit(solution)/shard_map/ppermute | solution.py:25
  52.1 1.2 %collective-permute-start.13 = (bf16[320,256]{1,0:T(8,128)(2,1)S(1)}, bf16[320,256]{1,0:T(8,128)(2,1)S(1)}, u32[]{:S(2)}, u32[]{:S(2)}) collective-permute-start(bf16[320,256]{1,0:T(8,128)(2,1)S(1)} %add_convert_fusion.1), channel_id=1, source_target_pairs={{0,2},{1,5},{2,0},{3,7},{4,6},{5,1},{6,4},{7,3},{8,10},{9,13},{10,... | collective-permute-start | bytes 491528 | tf_op jit(solution)/shard_map/ppermute | solution.py:25
  53.3 0.6 collective-permute-start.17
  54.2 1.4 %collective-permute-start.15 = (bf16[3,38,256]{2,1,0:T(8,128)(2,1)S(1)}, bf16[3,38,256]{2,1,0:T(8,128)(2,1)S(1)}, u32[]{:S(2)}, u32[]{:S(2)}) collective-permute-start(bf16[3,38,256]{2,1,0:T(8,128)(2,1)S(1)} %get-tuple-element.117), channel_id=1, source_target_pairs={{0,1},{1,0},{2,3},{3,2},{4,5},{5,4},{6,7},{7,6},{8,9},{9,8},{10,11... | collective-permute-start | bytes 175112 | tf_op jit(solution)/shard_map/ppermute | solution.py:25
  55.6 3.3 %block_inner_conv.3.inner_ref = f32[2,24,32,128]{3,2,1,0:T(8,128)S(1)} custom-call(bf16[32,3,256]{2,1,0:T(4,128)(2,1)S(1)} %get-tuple-element.80.west_ref, bf16[32,32,256]{2,1,0:T(8,128)(2,1)S(1)} %bitcast.6, bf16[32,3,256]{2,1,0:T(4,128)(2,1)S(1)} %get-tuple-element.82.east_ref, bf16[7,7,256]{2,1,0:T(8,128)(2,1)S(1)} %copy-done.2), custom_call_target="tpu_custom_call" | custom-call | flops 25690112 | bytes 2097152 | tf_op jit(solution)/shard_map/block_inner_conv/pallas_call | solution.py:224
  59.1 1.1 %collective-permute-start.14 = (bf16[320,256]{1,0:T(8,128)(2,1)S(1)}, bf16[320,256]{1,0:T(8,128)(2,1)S(1)}, u32[]{:S(2)}, u32[]{:S(2)}) collective-permute-start(bf16[320,256]{1,0:T(8,128)(2,1)S(1)} %pad_maximum_fusion.2), channel_id=1, source_target_pairs={{0,4},{1,3},{2,6},{3,1},{4,0},{5,7},{6,2},{7,5},{8,12},{9,11},{10,... | collective-permute-start | bytes 491528 | tf_op jit(solution)/shard_map/ppermute | solution.py:25
  60.2 2.3 %block_adjoint.1 = bf16[32,32,256]{2,1,0:T(8,128)(2,1)} custom-call(bf16[3,38,256]{2,1,0:T(8,128)(2,1)S(1)} %get-tuple-element.115.top_ref, bf16[32,3,256]{2,1,0:T(4,128)(2,1)S(1)} %get-tuple-element.80.west_ref, bf16[32,32,256]{2,1,0:T(8,128)(2,1)S(1)} %bitcast.7, bf16[32,3,256]{2,1,0:T(4,128)(2,1)S(1)} %get-tuple-element.82.east_ref, ...), custom_call_target="tpu_custom_call" | custom-call | flops 6553600 | bytes 3145728 | tf_op jit(solution)/shard_map/block_adjoint/pallas_call | solution.py:697
  62.4 1.2 %block_early.1 = (f32[256,1024]{1,0:T(8,128)}, f32[1024,256]{1,0:T(8,128)}) custom-call(bf16[768,256]{1,0:T(8,128)(2,1)S(1)} %pad_maximum_fusion.mine_ref, bf16[768,256]{1,0:T(8,128)(2,1)S(1)} %collective-permute-done.18.pair_ref), custom_call_target="tpu_custom_call" | custom-call | bytes 4194304 | tf_op jit(solution)/shard_map/block_early/pallas_call | solution.py:541
  63.6 0.8 %collective-permute-done.14 = bf16[320,256]{1,0:T(8,128)(2,1)S(1)} collective-permute-done((bf16[320,256]{1,0:T(8,128)(2,1)S(1)}, bf16[320,256]{1,0:T(8,128)(2,1)S(1)}, u32[]{:S(2)}, u32[]{:S(2)}) %collective-permute-start.14) | collective-permute-done | bytes 163872 | tf_op jit(solution)/shard_map/ppermute | solution.py:25
  64.6 1.4 %collective-permute-done.19.pair_last_ref = bf16[320,256]{1,0:T(8,128)(2,1)S(1)} collective-permute-done((bf16[320,256]{1,0:T(8,128)(2,1)S(1)}, bf16[320,256]{1,0:T(8,128)(2,1)S(1)}, u32[]{:S(2)}, u32[]{:S(2)}) %collective-permute-start.19) | collective-permute-done | bytes 163872 | tf_op jit(solution)/shard_map/ppermute | solution.py:25
  66.0 1.5 %block_finish.1 = (f32[7,7,256]{2,1,0:T(8,128)}, f32[256]{0:T(256)}, f32[256]{0:T(256)}, f32[256]{0:T(256)}, f32[256,1024]{1,0:T(8,128)}, /*index=5*/f32[1024]{0:T(1024)}, f32[1024,256]{1,0:T(8,128)}, f32[256]{0:T(256)}) custom-call(bf16[320,256]{1,0:T(8,128)(2,1)S(1)} %pad_maximum_fusion.3.last_ref, ...), custom_call_target="tpu_custom_call", output_to_operand_aliasing={{4}: (2, {}), {6}: (3, {})} | custom-call | tf_op jit(solution)/shard_map/block_finish/pallas_call | solution.py:607
  (67 shorter events, 2.6 us)
Async XLA Ops:
  0.6 11.5 %copy-start = (bf16[32,32,256]{2,1,0:T(8,128)(2,1)S(1)}, bf16[32,32,256]{2,1,0:T(8,128)(2,1)}, u32[]{:S(2)}) copy-start(bf16[32,32,256]{2,1,0:T(8,128)(2,1)} %field_ref.1) | copy-start | bytes 1572868
  1.8 9.4 %collective-permute-start.1 = (bf16[32,3,256]{2,1,0:T(4,128)(2,1)S(1)}, bf16[32,3,256]{2,1,0:T(4,128)(2,1)S(1)}, u32[]{:S(2)}, u32[]{:S(2)}) collective-permute-start(bf16[32,3,256]{2,1,0:T(4,128)(2,1)S(1)} %get-tuple-element.106), channel_id=1, source_target_pairs={{0,28},{1,29},{2,30},{3,31},{4,8},{5,9},{6,10},{7,11},{8,4},{9,5},... | collective-permute-start | bytes 147464 | tf_op jit(solution)/shard_map/ppermute | solution.py:25
  7.8 4.3 %collective-permute-start = (bf16[32,3,256]{2,1,0:T(4,128)(2,1)S(1)}, bf16[32,3,256]{2,1,0:T(4,128)(2,1)S(1)}, u32[]{:S(2)}, u32[]{:S(2)}) collective-permute-start(bf16[32,3,256]{2,1,0:T(4,128)(2,1)S(1)} %get-tuple-element.107), channel_id=1, source_target_pairs={{0,4},{1,5},{2,6},{3,7},{4,0},{5,1},{6,2},{7,3},{8,12},{9,13},{10,... | collective-permute-start | bytes 147464 | tf_op jit(solution)/shard_map/ppermute | solution.py:25
  7.8 0.7 %copy-start.3 = (bf16[1024]{0:T(1024)(128)(2,1)S(1)}, bf16[1024]{0:T(1024)(128)(2,1)}, u32[]{:S(2)}) copy-start(bf16[1024]{0:T(1024)(128)(2,1)} %refs_4_.1) | copy-start | bytes 6148
  8.5 0.7 copy-start.4
  9.2 0.7 copy-start.5
  9.8 0.7 copy-start.6
  10.5 0.7 copy-start.7
  12.2 1.7 %copy-start.2 = (bf16[7,7,256]{2,1,0:T(8,128)(2,1)S(1)}, bf16[7,7,256]{2,1,0:T(8,128)(2,1)}, u32[]{:S(2)}) copy-start(bf16[7,7,256]{2,1,0:T(8,128)(2,1)} %dw_ref.7) | copy-start | bytes 75268
  12.3 5.2 %collective-permute-start.3 = (bf16[3,38,256]{2,1,0:T(8,128)(2,1)S(1)}, bf16[3,38,256]{2,1,0:T(8,128)(2,1)S(1)}, u32[]{:S(2)}, u32[]{:S(2)}) collective-permute-start(bf16[3,38,256]{2,1,0:T(8,128)(2,1)S(1)} %reverse_select_fusion.1), channel_id=1, source_target_pairs={{0,16},{1,2},{2,1},{3,19},{4,20},{5,6},{6,5},{7,23},{8,24},{9,10},... | collective-permute-start | bytes 175112 | tf_op jit(solution)/shard_map/ppermute | solution.py:25
  12.5 5.0 %copy-start.1 = (bf16[32,32,256]{2,1,0:T(8,128)(2,1)S(1)}, bf16[32,32,256]{2,1,0:T(8,128)(2,1)}, u32[]{:S(2)}) copy-start(bf16[32,32,256]{2,1,0:T(8,128)(2,1)} %cot_ref.1) | copy-start | bytes 1572868
  12.5 5.0 %copy-start.8 = (bf16[256,1024]{1,0:T(8,128)(2,1)S(1)}, bf16[256,1024]{1,0:T(8,128)(2,1)}, u32[]{:S(2)}) copy-start(bf16[256,1024]{1,0:T(8,128)(2,1)} %w_expand_ref.1) | copy-start | bytes 1572868
  12.5 5.0 %copy-start.9 = (bf16[1024,256]{1,0:T(8,128)(2,1)S(1)}, bf16[1024,256]{1,0:T(8,128)(2,1)}, u32[]{:S(2)}) copy-start(bf16[1024,256]{1,0:T(8,128)(2,1)} %w_project_ref.1) | copy-start | bytes 1572868
  12.5 4.9 %collective-permute-start.2 = (bf16[3,38,256]{2,1,0:T(8,128)(2,1)S(1)}, bf16[3,38,256]{2,1,0:T(8,128)(2,1)S(1)}, u32[]{:S(2)}, u32[]{:S(2)}) collective-permute-start(bf16[3,38,256]{2,1,0:T(8,128)(2,1)S(1)} %get-tuple-element.121), channel_id=1, source_target_pairs={{0,1},{1,0},{2,3},{3,2},{4,5},{5,4},{6,7},{7,6},{8,9},{9,8},{10,11... | collective-permute-start | bytes 175112 | tf_op jit(solution)/shard_map/ppermute | solution.py:25
  24.5 1.6 %collective-permute-start.5 = (bf16[512,256]{1,0:T(8,128)(2,1)S(1)}, bf16[512,256]{1,0:T(8,128)(2,1)S(1)}, u32[]{:S(2)}, u32[]{:S(2)}) collective-permute-start(bf16[512,256]{1,0:T(8,128)(2,1)S(1)} %get-tuple-element.103), channel_id=1, source_target_pairs={{0,1},{1,0},{2,3},{3,2},{4,5},{5,4},{6,7},{7,6},{8,9},{9,8},{10,11... | collective-permute-start | bytes 786440 | tf_op jit(solution)/shard_map/ppermute | solution.py:25
  24.6 8.3 %collective-permute-start.4 = (bf16[512,256]{1,0:T(8,128)(2,1)S(1)}, bf16[512,256]{1,0:T(8,128)(2,1)S(1)}, u32[]{:S(2)}, u32[]{:S(2)}) collective-permute-start(bf16[512,256]{1,0:T(8,128)(2,1)S(1)} %get-tuple-element.102), channel_id=1, source_target_pairs={{0,1},{1,0},{2,3},{3,2},{4,5},{5,4},{6,7},{7,6},{8,9},{9,8},{10,11... | collective-permute-start | bytes 786440 | tf_op jit(solution)/shard_map/ppermute | solution.py:25
  26.2 6.7 %collective-permute-start.7 = (bf16[256,256]{1,0:T(8,128)(2,1)S(1)}, bf16[256,256]{1,0:T(8,128)(2,1)S(1)}, u32[]{:S(2)}, u32[]{:S(2)}) collective-permute-start(bf16[256,256]{1,0:T(8,128)(2,1)S(1)} %get-tuple-element.109), channel_id=1, source_target_pairs={{0,4},{1,3},{2,6},{3,1},{4,0},{5,7},{6,2},{7,5},{8,12},{9,11},{10,... | collective-permute-start | bytes 393224 | tf_op jit(solution)/shard_map/ppermute | solution.py:25
  27.3 8.9 %collective-permute-start.6 = (bf16[256,256]{1,0:T(8,128)(2,1)S(1)}, bf16[256,256]{1,0:T(8,128)(2,1)S(1)}, u32[]{:S(2)}, u32[]{:S(2)}) collective-permute-start(bf16[256,256]{1,0:T(8,128)(2,1)S(1)} %get-tuple-element.108), channel_id=1, source_target_pairs={{0,4},{1,3},{2,6},{3,1},{4,0},{5,7},{6,2},{7,5},{8,12},{9,11},{10,... | collective-permute-start | bytes 393224 | tf_op jit(solution)/shard_map/ppermute | solution.py:25
  32.9 5.0 %collective-permute-start.8 = (bf16[256,256]{1,0:T(8,128)(2,1)S(1)}, bf16[256,256]{1,0:T(8,128)(2,1)S(1)}, u32[]{:S(2)}, u32[]{:S(2)}) collective-permute-start(bf16[256,256]{1,0:T(8,128)(2,1)S(1)} %add_convert_fusion.4), channel_id=1, source_target_pairs={{0,2},{1,5},{2,0},{3,7},{4,6},{5,1},{6,4},{7,3},{8,10},{9,13},{10,... | collective-permute-start | bytes 393224 | tf_op jit(solution)/shard_map/ppermute | solution.py:25
  33.5 7.1 %collective-permute-start.11 = (bf16[32,3,256]{2,1,0:T(4,128)(2,1)S(1)}, bf16[32,3,256]{2,1,0:T(4,128)(2,1)S(1)}, u32[]{:S(2)}, u32[]{:S(2)}) collective-permute-start(bf16[32,3,256]{2,1,0:T(4,128)(2,1)S(1)} %get-tuple-element.100), channel_id=1, source_target_pairs={{0,28},{1,29},{2,30},{3,31},{4,8},{5,9},{6,10},{7,11},{8,4},{9,5},... | collective-permute-start | bytes 147464 | tf_op jit(solution)/shard_map/ppermute | solution.py:25
  36.2 5.0 %collective-permute-start.10 = (bf16[32,3,256]{2,1,0:T(4,128)(2,1)S(1)}, bf16[32,3,256]{2,1,0:T(4,128)(2,1)S(1)}, u32[]{:S(2)}, u32[]{:S(2)}) collective-permute-start(bf16[32,3,256]{2,1,0:T(4,128)(2,1)S(1)} %get-tuple-element.101), channel_id=1, source_target_pairs={{0,4},{1,5},{2,6},{3,7},{4,0},{5,1},{6,2},{7,3},{8,12},{9,13},{10,... | collective-permute-start | bytes 147464 | tf_op jit(solution)/shard_map/ppermute | solution.py:25
  38.1 6.9 %collective-permute-start.9 = (bf16[320,256]{1,0:T(8,128)(2,1)S(1)}, bf16[320,256]{1,0:T(8,128)(2,1)S(1)}, u32[]{:S(2)}, u32[]{:S(2)}) collective-permute-start(bf16[320,256]{1,0:T(8,128)(2,1)S(1)} %pad_maximum_fusion.1), channel_id=1, source_target_pairs={{0,8},{1,17},{2,10},{3,19},{4,12},{5,21},{6,14},{7,23},{8,0},{9,25... | collective-permute-start | bytes 491528 | tf_op jit(solution)/shard_map/ppermute | solution.py:25
  45.0 7.0 %collective-permute-start.12 = (bf16[320,256]{1,0:T(8,128)(2,1)S(1)}, bf16[320,256]{1,0:T(8,128)(2,1)S(1)}, u32[]{:S(2)}, u32[]{:S(2)}) collective-permute-start(bf16[320,256]{1,0:T(8,128)(2,1)S(1)} %add_convert_fusion.2), channel_id=1, source_target_pairs={{0,16},{1,9},{2,18},{3,11},{4,20},{5,13},{6,22},{7,15},{8,24},{9,1... | collective-permute-start | bytes 491528 | tf_op jit(solution)/shard_map/ppermute | solution.py:25
  52.1 6.8 %collective-permute-start.13 = (bf16[320,256]{1,0:T(8,128)(2,1)S(1)}, bf16[320,256]{1,0:T(8,128)(2,1)S(1)}, u32[]{:S(2)}, u32[]{:S(2)}) collective-permute-start(bf16[320,256]{1,0:T(8,128)(2,1)S(1)} %add_convert_fusion.1), channel_id=1, source_target_pairs={{0,2},{1,5},{2,0},{3,7},{4,6},{5,1},{6,4},{7,3},{8,10},{9,13},{10,... | collective-permute-start | bytes 491528 | tf_op jit(solution)/shard_map/ppermute | solution.py:25
  53.3 5.6 %collective-permute-start.17 = (bf16[256,256]{1,0:T(8,128)(2,1)S(1)}, bf16[256,256]{1,0:T(8,128)(2,1)S(1)}, u32[]{:S(2)}, u32[]{:S(2)}) collective-permute-start(bf16[256,256]{1,0:T(8,128)(2,1)S(1)} %slice.122), channel_id=1, source_target_pairs={{0,4},{1,3},{2,6},{3,1},{4,0},{5,7},{6,2},{7,5},{8,12},{9,11},{10,... | collective-permute-start | bytes 393224 | tf_op jit(solution)/shard_map/ppermute | solution.py:25
  54.0 6.2 %collective-permute-start.16 = (bf16[3,38,256]{2,1,0:T(8,128)(2,1)S(1)}, bf16[3,38,256]{2,1,0:T(8,128)(2,1)S(1)}, u32[]{:S(2)}, u32[]{:S(2)}) collective-permute-start(bf16[3,38,256]{2,1,0:T(8,128)(2,1)S(1)} %reverse_select_fusion), channel_id=1, source_target_pairs={{0,16},{1,2},{2,1},{3,19},{4,20},{5,6},{6,5},{7,23},{8,24},{9,10},... | collective-permute-start | bytes 175112 | tf_op jit(solution)/shard_map/ppermute | solution.py:25
  54.2 6.0 %collective-permute-start.15 = (bf16[3,38,256]{2,1,0:T(8,128)(2,1)S(1)}, bf16[3,38,256]{2,1,0:T(8,128)(2,1)S(1)}, u32[]{:S(2)}, u32[]{:S(2)}) collective-permute-start(bf16[3,38,256]{2,1,0:T(8,128)(2,1)S(1)} %get-tuple-element.117), channel_id=1, source_target_pairs={{0,1},{1,0},{2,3},{3,2},{4,5},{5,4},{6,7},{7,6},{8,9},{9,8},{10,11... | collective-permute-start | bytes 175112 | tf_op jit(solution)/shard_map/ppermute | solution.py:25
  59.0 3.5 %collective-permute-start.18 = (bf16[768,256]{1,0:T(8,128)(2,1)S(1)}, bf16[768,256]{1,0:T(8,128)(2,1)S(1)}, u32[]{:S(2)}, u32[]{:S(2)}) collective-permute-start(bf16[768,256]{1,0:T(8,128)(2,1)S(1)} %pad_maximum_fusion.mine_ref), channel_id=1, source_target_pairs={{0,1},{1,0},{2,3},{3,2},{4,5},{5,4},{6,7},{7,6},{8,9},{9,8},{10,11... | collective-permute-start | bytes 1179656 | tf_op jit(solution)/shard_map/ppermute | solution.py:25
  59.1 5.4 %collective-permute-start.14 = (bf16[320,256]{1,0:T(8,128)(2,1)S(1)}, bf16[320,256]{1,0:T(8,128)(2,1)S(1)}, u32[]{:S(2)}, u32[]{:S(2)}) collective-permute-start(bf16[320,256]{1,0:T(8,128)(2,1)S(1)} %pad_maximum_fusion.2), channel_id=1, source_target_pairs={{0,4},{1,3},{2,6},{3,1},{4,0},{5,7},{6,2},{7,5},{8,12},{9,11},{10,... | collective-permute-start | bytes 491528 | tf_op jit(solution)/shard_map/ppermute | solution.py:25
  64.5 1.5 %collective-permute-start.19 = (bf16[320,256]{1,0:T(8,128)(2,1)S(1)}, bf16[320,256]{1,0:T(8,128)(2,1)S(1)}, u32[]{:S(2)}, u32[]{:S(2)}) collective-permute-start(bf16[320,256]{1,0:T(8,128)(2,1)S(1)} %pad_maximum_fusion.3.last_ref), channel_id=1, source_target_pairs={{0,1},{1,0},{2,3},{3,2},{4,5},{5,4},{6,7},{7,6},{8,9},{9,8},{10,11... | collective-permute-start | bytes 491528 | tf_op jit(solution)/shard_map/ppermute | solution.py:25

commit v7 on v6

--- a/solution.py
+++ b/solution.py
@@ -441,28 +441,33 @@
     sums_ref[...] = jnp.zeros_like(sums_ref)
     for lane in range(tiles):
         lanes = slice(lane * LANES, (lane + 1) * LANES)
-        for row_off in range(7):
-
-            def kernel_row(row, totals):
+        for row_off in (0, 2, 4, 6):
+            both = row_off < 6
+
+            def padded_row(row):
+                return tuple(slot_rows(wide_ref, lane, row, place, slots) for place in range(slots + 6))
+
+            def kernel_row(row, carry):
+                totals, low = carry
                 grads = [slot_rows(dwide_ref, lane, row, slot, slots) for slot in range(slots)]
-                loaded = [
-                    slot_rows(wide_ref, lane, row + row_off, place, slots)
-                    for place in range(slots + 6)
-                ]
-                sums = [
-                    totals[col_off] + sum(grads[slot] * loaded[slot + col_off] for slot in range(slots))
-                    for col_off in range(7)
-                ]
-                if row_off == 0:
+                high = padded_row(row + row_off + 1) if both else low
+                low = low if both else padded_row(row + row_off)
+                sums = []
+                for at, loaded in enumerate((low, high) if both else (low,)):
+                    for col_off in range(7):
+                        product = sum(grads[slot] * loaded[slot + col_off] for slot in range(slots))
+                        sums.append(totals[at * 7 + col_off] + product)
+                if row_off == 6:
                     sums.append(totals[7] + sum(grads))
-                return tuple(sums)
-
-            count = 8 if row_off == 0 else 7
+                return tuple(sums), (high if both else ())
+
+            count = 14 if both else 8
             zeros = tuple(jnp.zeros((SUBLANES, LANES), jnp.float32) for unused in range(count))
-            totals = lax.fori_loop(0, rows, kernel_row, zeros, unroll=4)
-            for col_off in range(count):
-                tap = row_off * 7 + col_off if col_off < 7 else 49
-                sums_ref[tap : tap + 1, lanes] = jnp.sum(totals[col_off], axis=0, keepdims=True)
+            start = padded_row(row_off) if both else ()
+            totals, unused = lax.fori_loop(0, rows, kernel_row, (zeros, start), unroll=8)
+            for at in range(count):
+                tap = row_off * 7 + at
+                sums_ref[tap : tap + 1, lanes] = jnp.sum(totals[at], axis=0, keepdims=True)
     sums_ref[...] = sums_ref[...] * scale_factor
     pieces = small_ref.shape[0] - 8
     sums_ref[50:53] = small_ref[0:3]

time: 67.7 us -> 67.2 us (level)
  transfers between devices with their start and end apart: 20 -> 20, of which waited for: 10 -> 10; matrix products, arithmetic and copies ran while one was open for 1% -> 1% of each run, Pallas kernels for 22% -> 21%
where the time goes in v7:
time: 67.2 us; the launch traced here: 67 us
  Pallas kernels  22.6 us (34%)
  waiting for transfers between devices  19.5 us (29%)
  starting transfers between devices  18.6 us (28%)
  local copies, waits for them, and re-layouts  3.45 us (5%)
  other arithmetic  1.81 us (3%)
  between operations  0.98 us (1%)
    ppermute x20, waiting for transfers between devices, send(): return lax.ppermute(value, ('lon', 'lat'), flat_pairs(target))  19.5 us
    ppermute x20, starting transfers between devices, send(): return lax.ppermute(value, ('lon', 'lat'), flat_pairs(target))  18.6 us
    pallas_call x1, Pallas kernels, main_pass(): pl.pallas_call(functools.partial(main_kernel, scale_factor), out_shape=[j...  6.92 us
    pallas_call x2, Pallas kernels, inner_conv(): pl.pallas_call(functools.partial(inner_conv_kernel, flipped), out_shape=j...  6.64 us
    pallas_call x1, Pallas kernels, taps_pass(): pl.pallas_call(functools.partial(taps_kernel, scale_factor), out_shape=ja...  4.13 us
    unnamed x20, local copies, waits for them, and re-layouts  3.32 us
    pallas_call x1, Pallas kernels, adjoint_pass(): pl.pallas_call(adjoint_kernel, out_shape=jax.ShapeDtypeStruct(cot.shape,...  2.25 us
    pallas_call x1, Pallas kernels, finish_pass(): pl.pallas_call(finish_kernel, out_shape=[jax.ShapeDtypeStruct((7, 7, chan...  1.48 us
  transfers between devices with their start and end apart: 20, of which 10 were waited for; matrix products, arithmetic and copies ran while one was open for 1% of the time, Pallas kernels for 21%

profile of v7, /device:TPU:0, one launch (start us, length us, event | category | flops | bytes accessed | tf_op | source)
XLA Modules:
  0.0 67.0 jit_solution(7869941633643774554)
XLA Ops:
  0.7 1.1 %broadcast_select_fusion.6 = (bf16[32,3,256]{2,1,0:T(4,128)(2,1)S(1)}, bf16[32,3,256]{2,1,0:T(4,128)(2,1)S(1)}) fusion(pred[]{:T(512)S(6)} %eq.22, bf16[32,32,256]{2,1,0:T(8,128)(2,1)} %field_ref.1), kind=kLoop, calls=%fused_computation.19 | loop fusion | flops 49152 | bytes 196609 | tf_op jit(solution)/shard_map/jit(_where)/select_n | solution.py:33
  1.8 6.0 %collective-permute-start.1 = (bf16[32,3,256]{2,1,0:T(4,128)(2,1)S(1)}, bf16[32,3,256]{2,1,0:T(4,128)(2,1)S(1)}, u32[]{:S(2)}, u32[]{:S(2)}) collective-permute-start(bf16[32,3,256]{2,1,0:T(4,128)(2,1)S(1)} %get-tuple-element.106), channel_id=1, source_target_pairs={{0,28},{1,29},{2,30},{3,31},{4,8},{5,9},{6,10},{7,11},{8,4},{9,5},... | collective-permute-start | bytes 147464 | tf_op jit(solution)/shard_map/ppermute | solution.py:25
  7.8 0.7 %copy-done.3 = bf16[1024]{0:T(1024)(128)(2,1)S(1)} copy-done((bf16[1024]{0:T(1024)(128)(2,1)S(1)}, bf16[1024]{0:T(1024)(128)(2,1)}, u32[]{:S(2)}) %copy-start.3) | copy-done | bytes 2072
  8.5 0.7 copy-done.4
  9.2 0.7 copy-done.5
  9.8 0.7 copy-done.6
  10.5 0.7 copy-done.7
  11.1 0.9 %collective-permute-done = bf16[32,3,256]{2,1,0:T(4,128)(2,1)S(1)} collective-permute-done((bf16[32,3,256]{2,1,0:T(4,128)(2,1)S(1)}, bf16[32,3,256]{2,1,0:T(4,128)(2,1)S(1)}, u32[]{:S(2)}, u32[]{:S(2)}) %collective-permute-start) | collective-permute-done | bytes 49184 | tf_op jit(solution)/shard_map/ppermute | solution.py:25
  12.5 1.5 %collective-permute-start.2 = (bf16[3,38,256]{2,1,0:T(8,128)(2,1)S(1)}, bf16[3,38,256]{2,1,0:T(8,128)(2,1)S(1)}, u32[]{:S(2)}, u32[]{:S(2)}) collective-permute-start(bf16[3,38,256]{2,1,0:T(8,128)(2,1)S(1)} %get-tuple-element.121), channel_id=1, source_target_pairs={{0,1},{1,0},{2,3},{3,2},{4,5},{5,4},{6,7},{7,6},{8,9},{9,8},{10,11... | collective-permute-start | bytes 175112 | tf_op jit(solution)/shard_map/ppermute | solution.py:25
  14.0 3.3 %block_inner_conv.2.inner_ref = f32[2,24,32,128]{3,2,1,0:T(8,128)S(1)} custom-call(bf16[32,3,256]{2,1,0:T(4,128)(2,1)S(1)} %get-tuple-element.54.west_ref, bf16[32,32,256]{2,1,0:T(8,128)(2,1)S(1)} %copy-done, bf16[32,3,256]{2,1,0:T(4,128)(2,1)S(1)} %get-tuple-element.56.east_ref, bf16[7,7,256]{2,1,0:T(8,128)(2,1)S(1)} %copy-done.2), custom_call_target="tpu_custom_call" | custom-call | flops 25690112 | bytes 2097152 | tf_op jit(solution)/shard_map/block_inner_conv/pallas_call | solution.py:224
  17.5 6.9 %block_main.1 = (bf16[1024,256]{1,0:T(8,128)(2,1)}, bf16[1024,256]{1,0:T(8,128)(2,1)S(1)}, f32[1024,256]{1,0:T(8,128)S(1)}, bf16[1024,256]{1,0:T(8,128)(2,1)S(1)}, f32[12,256]{1,0:T(8,128)S(1)}) custom-call(bf16[3,38,256]{2,1,0:T(8,128)(2,1)S(1)} %get-tuple-element.119.top_ref, bf16[32,3,256]{2,1,0:T(4,128)(2,1)S(1)} %get-tuple-element.54.west_ref, ...), custom_call_target="tpu_custom_call" | custom-call | flops 3221225472 | bytes 8388608 | tf_op jit(solution)/shard_map/block_main/pallas_call | solution.py:395
  24.6 0.5 collective-permute-start.4
  25.1 1.0 %collective-permute-done.5 = bf16[512,256]{1,0:T(8,128)(2,1)S(1)} collective-permute-done((bf16[512,256]{1,0:T(8,128)(2,1)S(1)}, bf16[512,256]{1,0:T(8,128)(2,1)S(1)}, u32[]{:S(2)}, u32[]{:S(2)}) %collective-permute-start.5) | collective-permute-done | bytes 262176 | tf_op jit(solution)/shard_map/ppermute | solution.py:25
  26.2 1.2 %collective-permute-start.7 = (bf16[256,256]{1,0:T(8,128)(2,1)S(1)}, bf16[256,256]{1,0:T(8,128)(2,1)S(1)}, u32[]{:S(2)}, u32[]{:S(2)}) collective-permute-start(bf16[256,256]{1,0:T(8,128)(2,1)S(1)} %get-tuple-element.109), channel_id=1, source_target_pairs={{0,4},{1,3},{2,6},{3,1},{4,0},{5,7},{6,2},{7,5},{8,12},{9,11},{10,... | collective-permute-start | bytes 393224 | tf_op jit(solution)/shard_map/ppermute | solution.py:25
  27.3 0.9 %collective-permute-start.6 = (bf16[256,256]{1,0:T(8,128)(2,1)S(1)}, bf16[256,256]{1,0:T(8,128)(2,1)S(1)}, u32[]{:S(2)}, u32[]{:S(2)}) collective-permute-start(bf16[256,256]{1,0:T(8,128)(2,1)S(1)} %get-tuple-element.108), channel_id=1, source_target_pairs={{0,4},{1,3},{2,6},{3,1},{4,0},{5,7},{6,2},{7,5},{8,12},{9,11},{10,... | collective-permute-start | bytes 393224 | tf_op jit(solution)/shard_map/ppermute | solution.py:25
  28.3 4.1 %block_taps.1 = bf16[64,256]{1,0:T(8,128)(2,1)S(1)} custom-call(bf16[3,38,256]{2,1,0:T(8,128)(2,1)S(1)} %get-tuple-element.119.top_ref, bf16[32,3,256]{2,1,0:T(4,128)(2,1)S(1)} %get-tuple-element.54.west_ref, bf16[32,32,256]{2,1,0:T(8,128)(2,1)S(1)} %copy-done, bf16[32,3,256]{2,1,0:T(4,128)(2,1)S(1)} %get-tuple-element.56.east_ref, ...), custom_call_target="tpu_custom_call" | custom-call | flops 25690112 | bytes 3145728 | tf_op jit(solution)/shard_map/block_taps/pallas_call | solution.py:482
  33.0 2.8 %collective-permute-start.11 = (bf16[32,3,256]{2,1,0:T(4,128)(2,1)S(1)}, bf16[32,3,256]{2,1,0:T(4,128)(2,1)S(1)}, u32[]{:S(2)}, u32[]{:S(2)}) collective-permute-start(bf16[32,3,256]{2,1,0:T(4,128)(2,1)S(1)} %get-tuple-element.100), channel_id=1, source_target_pairs={{0,28},{1,29},{2,30},{3,31},{4,8},{5,9},{6,10},{7,11},{8,4},{9,5},... | collective-permute-start | bytes 147464 | tf_op jit(solution)/shard_map/ppermute | solution.py:25
  35.8 1.7 %collective-permute-done.8 = bf16[256,256]{1,0:T(8,128)(2,1)S(1)} collective-permute-done((bf16[256,256]{1,0:T(8,128)(2,1)S(1)}, bf16[256,256]{1,0:T(8,128)(2,1)S(1)}, u32[]{:S(2)}, u32[]{:S(2)}) %collective-permute-start.8) | collective-permute-done | bytes 131104 | tf_op jit(solution)/shard_map/ppermute | solution.py:25
  37.9 2.2 %collective-permute-done.11 = bf16[32,3,256]{2,1,0:T(4,128)(2,1)S(1)} collective-permute-done((bf16[32,3,256]{2,1,0:T(4,128)(2,1)S(1)}, bf16[32,3,256]{2,1,0:T(4,128)(2,1)S(1)}, u32[]{:S(2)}, u32[]{:S(2)}) %collective-permute-start.11) | collective-permute-done | bytes 49184 | tf_op jit(solution)/shard_map/ppermute | solution.py:25
  40.1 0.6 collective-permute-done.10
  40.8 3.7 %collective-permute-done.9 = bf16[320,256]{1,0:T(8,128)(2,1)S(1)} collective-permute-done((bf16[320,256]{1,0:T(8,128)(2,1)S(1)}, bf16[320,256]{1,0:T(8,128)(2,1)S(1)}, u32[]{:S(2)}, u32[]{:S(2)}) %collective-permute-start.9) | collective-permute-done | bytes 163872 | tf_op jit(solution)/shard_map/ppermute | solution.py:25
  44.6 6.9 %collective-permute-done.12 = bf16[320,256]{1,0:T(8,128)(2,1)S(1)} collective-permute-done((bf16[320,256]{1,0:T(8,128)(2,1)S(1)}, bf16[320,256]{1,0:T(8,128)(2,1)S(1)}, u32[]{:S(2)}, u32[]{:S(2)}) %collective-permute-start.12) | collective-permute-done | bytes 163872 | tf_op jit(solution)/shard_map/ppermute | solution.py:25
  51.6 1.2 %collective-permute-start.13 = (bf16[320,256]{1,0:T(8,128)(2,1)S(1)}, bf16[320,256]{1,0:T(8,128)(2,1)S(1)}, u32[]{:S(2)}, u32[]{:S(2)}) collective-permute-start(bf16[320,256]{1,0:T(8,128)(2,1)S(1)} %add_convert_fusion.1), channel_id=1, source_target_pairs={{0,2},{1,5},{2,0},{3,7},{4,6},{5,1},{6,4},{7,3},{8,10},{9,13},{10,... | collective-permute-start | bytes 491528 | tf_op jit(solution)/shard_map/ppermute | solution.py:25
  52.8 0.6 collective-permute-start.17
  53.7 1.4 %collective-permute-start.15 = (bf16[3,38,256]{2,1,0:T(8,128)(2,1)S(1)}, bf16[3,38,256]{2,1,0:T(8,128)(2,1)S(1)}, u32[]{:S(2)}, u32[]{:S(2)}) collective-permute-start(bf16[3,38,256]{2,1,0:T(8,128)(2,1)S(1)} %get-tuple-element.117), channel_id=1, source_target_pairs={{0,1},{1,0},{2,3},{3,2},{4,5},{5,4},{6,7},{7,6},{8,9},{9,8},{10,11... | collective-permute-start | bytes 175112 | tf_op jit(solution)/shard_map/ppermute | solution.py:25
  55.1 3.3 %block_inner_conv.3.inner_ref = f32[2,24,32,128]{3,2,1,0:T(8,128)S(1)} custom-call(bf16[32,3,256]{2,1,0:T(4,128)(2,1)S(1)} %get-tuple-element.80.west_ref, bf16[32,32,256]{2,1,0:T(8,128)(2,1)S(1)} %bitcast.6, bf16[32,3,256]{2,1,0:T(4,128)(2,1)S(1)} %get-tuple-element.82.east_ref, bf16[7,7,256]{2,1,0:T(8,128)(2,1)S(1)} %copy-done.2), custom_call_target="tpu_custom_call" | custom-call | flops 25690112 | bytes 2097152 | tf_op jit(solution)/shard_map/block_inner_conv/pallas_call | solution.py:224
  58.6 1.1 %collective-permute-start.14 = (bf16[320,256]{1,0:T(8,128)(2,1)S(1)}, bf16[320,256]{1,0:T(8,128)(2,1)S(1)}, u32[]{:S(2)}, u32[]{:S(2)}) collective-permute-start(bf16[320,256]{1,0:T(8,128)(2,1)S(1)} %pad_maximum_fusion.2), channel_id=1, source_target_pairs={{0,4},{1,3},{2,6},{3,1},{4,0},{5,7},{6,2},{7,5},{8,12},{9,11},{10,... | collective-permute-start | bytes 491528 | tf_op jit(solution)/shard_map/ppermute | solution.py:25
  59.7 2.3 %block_adjoint.1 = bf16[32,32,256]{2,1,0:T(8,128)(2,1)} custom-call(bf16[3,38,256]{2,1,0:T(8,128)(2,1)S(1)} %get-tuple-element.115.top_ref, bf16[32,3,256]{2,1,0:T(4,128)(2,1)S(1)} %get-tuple-element.80.west_ref, bf16[32,32,256]{2,1,0:T(8,128)(2,1)S(1)} %bitcast.7, bf16[32,3,256]{2,1,0:T(4,128)(2,1)S(1)} %get-tuple-element.82.east_ref, ...), custom_call_target="tpu_custom_call" | custom-call | flops 6553600 | bytes 3145728 | tf_op jit(solution)/shard_map/block_adjoint/pallas_call | solution.py:702
  62.0 1.2 %block_early.1 = (f32[256,1024]{1,0:T(8,128)}, f32[1024,256]{1,0:T(8,128)}) custom-call(bf16[768,256]{1,0:T(8,128)(2,1)S(1)} %pad_maximum_fusion.mine_ref, bf16[768,256]{1,0:T(8,128)(2,1)S(1)} %collective-permute-done.18.pair_ref), custom_call_target="tpu_custom_call" | custom-call | bytes 4194304 | tf_op jit(solution)/shard_map/block_early/pallas_call | solution.py:546
  63.2 0.8 %collective-permute-done.14 = bf16[320,256]{1,0:T(8,128)(2,1)S(1)} collective-permute-done((bf16[320,256]{1,0:T(8,128)(2,1)S(1)}, bf16[320,256]{1,0:T(8,128)(2,1)S(1)}, u32[]{:S(2)}, u32[]{:S(2)}) %collective-permute-start.14) | collective-permute-done | bytes 163872 | tf_op jit(solution)/shard_map/ppermute | solution.py:25
  64.1 1.4 %collective-permute-done.19.pair_last_ref = bf16[320,256]{1,0:T(8,128)(2,1)S(1)} collective-permute-done((bf16[320,256]{1,0:T(8,128)(2,1)S(1)}, bf16[320,256]{1,0:T(8,128)(2,1)S(1)}, u32[]{:S(2)}, u32[]{:S(2)}) %collective-permute-start.19) | collective-permute-done | bytes 163872 | tf_op jit(solution)/shard_map/ppermute | solution.py:25
  65.5 1.5 %block_finish.1 = (f32[7,7,256]{2,1,0:T(8,128)}, f32[256]{0:T(256)}, f32[256]{0:T(256)}, f32[256]{0:T(256)}, f32[256,1024]{1,0:T(8,128)}, /*index=5*/f32[1024]{0:T(1024)}, f32[1024,256]{1,0:T(8,128)}, f32[256]{0:T(256)}) custom-call(bf16[320,256]{1,0:T(8,128)(2,1)S(1)} %pad_maximum_fusion.3.last_ref, ...), custom_call_target="tpu_custom_call", output_to_operand_aliasing={{4}: (2, {}), {6}: (3, {})} | custom-call | tf_op jit(solution)/shard_map/block_finish/pallas_call | solution.py:612
  (67 shorter events, 2.6 us)
Async XLA Ops:
  0.6 11.5 %copy-start = (bf16[32,32,256]{2,1,0:T(8,128)(2,1)S(1)}, bf16[32,32,256]{2,1,0:T(8,128)(2,1)}, u32[]{:S(2)}) copy-start(bf16[32,32,256]{2,1,0:T(8,128)(2,1)} %field_ref.1) | copy-start | bytes 1572868
  1.8 9.4 %collective-permute-start.1 = (bf16[32,3,256]{2,1,0:T(4,128)(2,1)S(1)}, bf16[32,3,256]{2,1,0:T(4,128)(2,1)S(1)}, u32[]{:S(2)}, u32[]{:S(2)}) collective-permute-start(bf16[32,3,256]{2,1,0:T(4,128)(2,1)S(1)} %get-tuple-element.106), channel_id=1, source_target_pairs={{0,28},{1,29},{2,30},{3,31},{4,8},{5,9},{6,10},{7,11},{8,4},{9,5},... | collective-permute-start | bytes 147464 | tf_op jit(solution)/shard_map/ppermute | solution.py:25
  7.8 4.3 %collective-permute-start = (bf16[32,3,256]{2,1,0:T(4,128)(2,1)S(1)}, bf16[32,3,256]{2,1,0:T(4,128)(2,1)S(1)}, u32[]{:S(2)}, u32[]{:S(2)}) collective-permute-start(bf16[32,3,256]{2,1,0:T(4,128)(2,1)S(1)} %get-tuple-element.107), channel_id=1, source_target_pairs={{0,4},{1,5},{2,6},{3,7},{4,0},{5,1},{6,2},{7,3},{8,12},{9,13},{10,... | collective-permute-start | bytes 147464 | tf_op jit(solution)/shard_map/ppermute | solution.py:25
  7.8 0.7 %copy-start.3 = (bf16[1024]{0:T(1024)(128)(2,1)S(1)}, bf16[1024]{0:T(1024)(128)(2,1)}, u32[]{:S(2)}) copy-start(bf16[1024]{0:T(1024)(128)(2,1)} %refs_4_.1) | copy-start | bytes 6148
  8.5 0.7 copy-start.4
  9.2 0.7 copy-start.5
  9.8 0.7 copy-start.6
  10.5 0.7 copy-start.7
  12.2 1.7 %copy-start.2 = (bf16[7,7,256]{2,1,0:T(8,128)(2,1)S(1)}, bf16[7,7,256]{2,1,0:T(8,128)(2,1)}, u32[]{:S(2)}) copy-start(bf16[7,7,256]{2,1,0:T(8,128)(2,1)} %dw_ref.7) | copy-start | bytes 75268
  12.3 5.2 %collective-permute-start.3 = (bf16[3,38,256]{2,1,0:T(8,128)(2,1)S(1)}, bf16[3,38,256]{2,1,0:T(8,128)(2,1)S(1)}, u32[]{:S(2)}, u32[]{:S(2)}) collective-permute-start(bf16[3,38,256]{2,1,0:T(8,128)(2,1)S(1)} %reverse_select_fusion.1), channel_id=1, source_target_pairs={{0,16},{1,2},{2,1},{3,19},{4,20},{5,6},{6,5},{7,23},{8,24},{9,10},... | collective-permute-start | bytes 175112 | tf_op jit(solution)/shard_map/ppermute | solution.py:25
  12.5 5.0 %copy-start.1 = (bf16[32,32,256]{2,1,0:T(8,128)(2,1)S(1)}, bf16[32,32,256]{2,1,0:T(8,128)(2,1)}, u32[]{:S(2)}) copy-start(bf16[32,32,256]{2,1,0:T(8,128)(2,1)} %cot_ref.1) | copy-start | bytes 1572868
  12.5 5.0 %copy-start.8 = (bf16[256,1024]{1,0:T(8,128)(2,1)S(1)}, bf16[256,1024]{1,0:T(8,128)(2,1)}, u32[]{:S(2)}) copy-start(bf16[256,1024]{1,0:T(8,128)(2,1)} %w_expand_ref.1) | copy-start | bytes 1572868
  12.5 5.0 %copy-start.9 = (bf16[1024,256]{1,0:T(8,128)(2,1)S(1)}, bf16[1024,256]{1,0:T(8,128)(2,1)}, u32[]{:S(2)}) copy-start(bf16[1024,256]{1,0:T(8,128)(2,1)} %w_project_ref.1) | copy-start | bytes 1572868
  12.5 4.9 %collective-permute-start.2 = (bf16[3,38,256]{2,1,0:T(8,128)(2,1)S(1)}, bf16[3,38,256]{2,1,0:T(8,128)(2,1)S(1)}, u32[]{:S(2)}, u32[]{:S(2)}) collective-permute-start(bf16[3,38,256]{2,1,0:T(8,128)(2,1)S(1)} %get-tuple-element.121), channel_id=1, source_target_pairs={{0,1},{1,0},{2,3},{3,2},{4,5},{5,4},{6,7},{7,6},{8,9},{9,8},{10,11... | collective-permute-start | bytes 175112 | tf_op jit(solution)/shard_map/ppermute | solution.py:25
  24.5 1.6 %collective-permute-start.5 = (bf16[512,256]{1,0:T(8,128)(2,1)S(1)}, bf16[512,256]{1,0:T(8,128)(2,1)S(1)}, u32[]{:S(2)}, u32[]{:S(2)}) collective-permute-start(bf16[512,256]{1,0:T(8,128)(2,1)S(1)} %get-tuple-element.103), channel_id=1, source_target_pairs={{0,1},{1,0},{2,3},{3,2},{4,5},{5,4},{6,7},{7,6},{8,9},{9,8},{10,11... | collective-permute-start | bytes 786440 | tf_op jit(solution)/shard_map/ppermute | solution.py:25
  24.6 7.8 %collective-permute-start.4 = (bf16[512,256]{1,0:T(8,128)(2,1)S(1)}, bf16[512,256]{1,0:T(8,128)(2,1)S(1)}, u32[]{:S(2)}, u32[]{:S(2)}) collective-permute-start(bf16[512,256]{1,0:T(8,128)(2,1)S(1)} %get-tuple-element.102), channel_id=1, source_target_pairs={{0,1},{1,0},{2,3},{3,2},{4,5},{5,4},{6,7},{7,6},{8,9},{9,8},{10,11... | collective-permute-start | bytes 786440 | tf_op jit(solution)/shard_map/ppermute | solution.py:25
  26.2 6.2 %collective-permute-start.7 = (bf16[256,256]{1,0:T(8,128)(2,1)S(1)}, bf16[256,256]{1,0:T(8,128)(2,1)S(1)}, u32[]{:S(2)}, u32[]{:S(2)}) collective-permute-start(bf16[256,256]{1,0:T(8,128)(2,1)S(1)} %get-tuple-element.109), channel_id=1, source_target_pairs={{0,4},{1,3},{2,6},{3,1},{4,0},{5,7},{6,2},{7,5},{8,12},{9,11},{10,... | collective-permute-start | bytes 393224 | tf_op jit(solution)/shard_map/ppermute | solution.py:25
  27.3 8.4 %collective-permute-start.6 = (bf16[256,256]{1,0:T(8,128)(2,1)S(1)}, bf16[256,256]{1,0:T(8,128)(2,1)S(1)}, u32[]{:S(2)}, u32[]{:S(2)}) collective-permute-start(bf16[256,256]{1,0:T(8,128)(2,1)S(1)} %get-tuple-element.108), channel_id=1, source_target_pairs={{0,4},{1,3},{2,6},{3,1},{4,0},{5,7},{6,2},{7,5},{8,12},{9,11},{10,... | collective-permute-start | bytes 393224 | tf_op jit(solution)/shard_map/ppermute | solution.py:25
  32.5 5.0 %collective-permute-start.8 = (bf16[256,256]{1,0:T(8,128)(2,1)S(1)}, bf16[256,256]{1,0:T(8,128)(2,1)S(1)}, u32[]{:S(2)}, u32[]{:S(2)}) collective-permute-start(bf16[256,256]{1,0:T(8,128)(2,1)S(1)} %add_convert_fusion.4), channel_id=1, source_target_pairs={{0,2},{1,5},{2,0},{3,7},{4,6},{5,1},{6,4},{7,3},{8,10},{9,13},{10,... | collective-permute-start | bytes 393224 | tf_op jit(solution)/shard_map/ppermute | solution.py:25
  33.0 7.1 %collective-permute-start.11 = (bf16[32,3,256]{2,1,0:T(4,128)(2,1)S(1)}, bf16[32,3,256]{2,1,0:T(4,128)(2,1)S(1)}, u32[]{:S(2)}, u32[]{:S(2)}) collective-permute-start(bf16[32,3,256]{2,1,0:T(4,128)(2,1)S(1)} %get-tuple-element.100), channel_id=1, source_target_pairs={{0,28},{1,29},{2,30},{3,31},{4,8},{5,9},{6,10},{7,11},{8,4},{9,5},... | collective-permute-start | bytes 147464 | tf_op jit(solution)/shard_map/ppermute | solution.py:25
  35.8 5.0 %collective-permute-start.10 = (bf16[32,3,256]{2,1,0:T(4,128)(2,1)S(1)}, bf16[32,3,256]{2,1,0:T(4,128)(2,1)S(1)}, u32[]{:S(2)}, u32[]{:S(2)}) collective-permute-start(bf16[32,3,256]{2,1,0:T(4,128)(2,1)S(1)} %get-tuple-element.101), channel_id=1, source_target_pairs={{0,4},{1,5},{2,6},{3,7},{4,0},{5,1},{6,2},{7,3},{8,12},{9,13},{10,... | collective-permute-start | bytes 147464 | tf_op jit(solution)/shard_map/ppermute | solution.py:25
  37.6 6.9 %collective-permute-start.9 = (bf16[320,256]{1,0:T(8,128)(2,1)S(1)}, bf16[320,256]{1,0:T(8,128)(2,1)S(1)}, u32[]{:S(2)}, u32[]{:S(2)}) collective-permute-start(bf16[320,256]{1,0:T(8,128)(2,1)S(1)} %pad_maximum_fusion.1), channel_id=1, source_target_pairs={{0,8},{1,17},{2,10},{3,19},{4,12},{5,21},{6,14},{7,23},{8,0},{9,25... | collective-permute-start | bytes 491528 | tf_op jit(solution)/shard_map/ppermute | solution.py:25
  44.5 7.0 %collective-permute-start.12 = (bf16[320,256]{1,0:T(8,128)(2,1)S(1)}, bf16[320,256]{1,0:T(8,128)(2,1)S(1)}, u32[]{:S(2)}, u32[]{:S(2)}) collective-permute-start(bf16[320,256]{1,0:T(8,128)(2,1)S(1)} %add_convert_fusion.2), channel_id=1, source_target_pairs={{0,16},{1,9},{2,18},{3,11},{4,20},{5,13},{6,22},{7,15},{8,24},{9,1... | collective-permute-start | bytes 491528 | tf_op jit(solution)/shard_map/ppermute | solution.py:25
  51.6 6.8 %collective-permute-start.13 = (bf16[320,256]{1,0:T(8,128)(2,1)S(1)}, bf16[320,256]{1,0:T(8,128)(2,1)S(1)}, u32[]{:S(2)}, u32[]{:S(2)}) collective-permute-start(bf16[320,256]{1,0:T(8,128)(2,1)S(1)} %add_convert_fusion.1), channel_id=1, source_target_pairs={{0,2},{1,5},{2,0},{3,7},{4,6},{5,1},{6,4},{7,3},{8,10},{9,13},{10,... | collective-permute-start | bytes 491528 | tf_op jit(solution)/shard_map/ppermute | solution.py:25
  52.8 5.6 %collective-permute-start.17 = (bf16[256,256]{1,0:T(8,128)(2,1)S(1)}, bf16[256,256]{1,0:T(8,128)(2,1)S(1)}, u32[]{:S(2)}, u32[]{:S(2)}) collective-permute-start(bf16[256,256]{1,0:T(8,128)(2,1)S(1)} %slice.122), channel_id=1, source_target_pairs={{0,4},{1,3},{2,6},{3,1},{4,0},{5,7},{6,2},{7,5},{8,12},{9,11},{10,... | collective-permute-start | bytes 393224 | tf_op jit(solution)/shard_map/ppermute | solution.py:25
  53.5 6.2 %collective-permute-start.16 = (bf16[3,38,256]{2,1,0:T(8,128)(2,1)S(1)}, bf16[3,38,256]{2,1,0:T(8,128)(2,1)S(1)}, u32[]{:S(2)}, u32[]{:S(2)}) collective-permute-start(bf16[3,38,256]{2,1,0:T(8,128)(2,1)S(1)} %reverse_select_fusion), channel_id=1, source_target_pairs={{0,16},{1,2},{2,1},{3,19},{4,20},{5,6},{6,5},{7,23},{8,24},{9,10},... | collective-permute-start | bytes 175112 | tf_op jit(solution)/shard_map/ppermute | solution.py:25
  53.7 6.0 %collective-permute-start.15 = (bf16[3,38,256]{2,1,0:T(8,128)(2,1)S(1)}, bf16[3,38,256]{2,1,0:T(8,128)(2,1)S(1)}, u32[]{:S(2)}, u32[]{:S(2)}) collective-permute-start(bf16[3,38,256]{2,1,0:T(8,128)(2,1)S(1)} %get-tuple-element.117), channel_id=1, source_target_pairs={{0,1},{1,0},{2,3},{3,2},{4,5},{5,4},{6,7},{7,6},{8,9},{9,8},{10,11... | collective-permute-start | bytes 175112 | tf_op jit(solution)/shard_map/ppermute | solution.py:25
  58.5 3.5 %collective-permute-start.18 = (bf16[768,256]{1,0:T(8,128)(2,1)S(1)}, bf16[768,256]{1,0:T(8,128)(2,1)S(1)}, u32[]{:S(2)}, u32[]{:S(2)}) collective-permute-start(bf16[768,256]{1,0:T(8,128)(2,1)S(1)} %pad_maximum_fusion.mine_ref), channel_id=1, source_target_pairs={{0,1},{1,0},{2,3},{3,2},{4,5},{5,4},{6,7},{7,6},{8,9},{9,8},{10,11... | collective-permute-start | bytes 1179656 | tf_op jit(solution)/shard_map/ppermute | solution.py:25
  58.6 5.4 %collective-permute-start.14 = (bf16[320,256]{1,0:T(8,128)(2,1)S(1)}, bf16[320,256]{1,0:T(8,128)(2,1)S(1)}, u32[]{:S(2)}, u32[]{:S(2)}) collective-permute-start(bf16[320,256]{1,0:T(8,128)(2,1)S(1)} %pad_maximum_fusion.2), channel_id=1, source_target_pairs={{0,4},{1,3},{2,6},{3,1},{4,0},{5,7},{6,2},{7,5},{8,12},{9,11},{10,... | collective-permute-start | bytes 491528 | tf_op jit(solution)/shard_map/ppermute | solution.py:25
  64.0 1.5 %collective-permute-start.19 = (bf16[320,256]{1,0:T(8,128)(2,1)S(1)}, bf16[320,256]{1,0:T(8,128)(2,1)S(1)}, u32[]{:S(2)}, u32[]{:S(2)}) collective-permute-start(bf16[320,256]{1,0:T(8,128)(2,1)S(1)} %pad_maximum_fusion.3.last_ref), channel_id=1, source_target_pairs={{0,1},{1,0},{2,3},{3,2},{4,5},{5,4},{6,7},{7,6},{8,9},{9,8},{10,11... | collective-permute-start | bytes 491528 | tf_op jit(solution)/shard_map/ppermute | solution.py:25

commit v8 on v7

--- a/solution.py
+++ b/solution.py
@@ -174,16 +174,16 @@
     split_lanes(bottom_ref, out_ref, to=3 + band_refs[1].shape[0])
 
 
-def window_sums(source_ref, lane, start, weight_of):
+def window_sums(source_ref, lane, start, weight_of, height=4):
     slots = (source_ref.shape[2] - 6) // SUBLANES
-    totals = [[jnp.zeros((SUBLANES, LANES), jnp.float32)] * slots for unused in range(4)]
-    for row in range(10):
+    totals = [[jnp.zeros((SUBLANES, LANES), jnp.float32)] * slots for unused in range(height)]
+    for row in range(height + 6):
         loaded = [
             slot_rows(source_ref, lane, start + row, place, slots) for place in range(slots + 6)
         ]
         for row_off in range(7):
             to = row - row_off
-            if 0 <= to < 4:
+            if 0 <= to < height:
                 for col_off in range(7):
                     weight = weight_of(row, row_off, col_off)
                     for slot in range(slots):
@@ -193,7 +193,7 @@
 
 def store_sums(totals, out_ref, lane, start):
     slots = len(totals[0])
-    for to in range(4):
+    for to in range(len(totals)):
         for slot in range(slots):
             out_ref[lane, start + to, pl.ds(slot, SUBLANES, stride=slots), :] = totals[to][slot]
 
@@ -206,16 +206,16 @@
     split_band((west_ref, field_ref, east_ref), split_ref)
 
     def body(at, carry):
-        lane, start = at // (rows // 4), (at % (rows // 4)) * 4
+        lane, start = at // (rows // 8), (at % (rows // 8)) * 8
 
         def weight_of(row, row_off, col_off):
             tap = row_off * 7 + col_off
             return spread_ref[lane, 48 - tap if flipped else tap]
 
-        store_sums(window_sums(split_ref, lane, start + 1, weight_of), out_ref, lane, start)
+        store_sums(window_sums(split_ref, lane, start + 1, weight_of, 8), out_ref, lane, start)
         return carry
 
-    lax.fori_loop(0, tiles * (rows // 4), body, 0)
+    lax.fori_loop(0, tiles * (rows // 8), body, 0)
 
 
 def inner_conv(band, dw_kernel, flipped):

time: 67.2 us -> 67.1 us (level)
  no operation moved by 1% of the time
where the time goes in v8:
time: 67.1 us; the launch traced here: 66.9 us
  Pallas kernels  22.4 us (33%)
  waiting for transfers between devices  19.9 us (30%)
  starting transfers between devices  18.3 us (27%)
  local copies, waits for them, and re-layouts  3.45 us (5%)
  other arithmetic  1.81 us (3%)
  between operations  0.97 us (1%)
    ppermute x20, waiting for transfers between devices, send(): return lax.ppermute(value, ('lon', 'lat'), flat_pairs(target))  19.9 us
    ppermute x20, starting transfers between devices, send(): return lax.ppermute(value, ('lon', 'lat'), flat_pairs(target))  18.3 us
    pallas_call x1, Pallas kernels, main_pass(): pl.pallas_call(functools.partial(main_kernel, scale_factor), out_shape=[j...  6.92 us
    pallas_call x2, Pallas kernels, inner_conv(): pl.pallas_call(functools.partial(inner_conv_kernel, flipped), out_shape=j...  6.41 us
    pallas_call x1, Pallas kernels, taps_pass(): pl.pallas_call(functools.partial(taps_kernel, scale_factor), out_shape=ja...  4.13 us
    unnamed x20, local copies, waits for them, and re-layouts  3.32 us
    pallas_call x1, Pallas kernels, adjoint_pass(): pl.pallas_call(adjoint_kernel, out_shape=jax.ShapeDtypeStruct(cot.shape,...  2.25 us
    pallas_call x1, Pallas kernels, finish_pass(): pl.pallas_call(finish_kernel, out_shape=[jax.ShapeDtypeStruct((7, 7, chan...  1.48 us
  transfers between devices with their start and end apart: 20, of which 10 were waited for; matrix products, arithmetic and copies ran while one was open for 1% of the time, Pallas kernels for 21%

profile of v8, /device:TPU:0, one launch (start us, length us, event | category | flops | bytes accessed | tf_op | source)
XLA Modules:
  0.0 66.9 jit_solution(5341704256593098850)
XLA Ops:
  0.7 1.1 %broadcast_select_fusion.6 = (bf16[32,3,256]{2,1,0:T(4,128)(2,1)S(1)}, bf16[32,3,256]{2,1,0:T(4,128)(2,1)S(1)}) fusion(pred[]{:T(512)S(6)} %eq.22, bf16[32,32,256]{2,1,0:T(8,128)(2,1)} %field_ref.1), kind=kLoop, calls=%fused_computation.19 | loop fusion | flops 49152 | bytes 196609 | tf_op jit(solution)/shard_map/jit(_where)/select_n | solution.py:33
  1.8 6.0 %collective-permute-start.1 = (bf16[32,3,256]{2,1,0:T(4,128)(2,1)S(1)}, bf16[32,3,256]{2,1,0:T(4,128)(2,1)S(1)}, u32[]{:S(2)}, u32[]{:S(2)}) collective-permute-start(bf16[32,3,256]{2,1,0:T(4,128)(2,1)S(1)} %get-tuple-element.106), channel_id=1, source_target_pairs={{0,28},{1,29},{2,30},{3,31},{4,8},{5,9},{6,10},{7,11},{8,4},{9,5},... | collective-permute-start | bytes 147464 | tf_op jit(solution)/shard_map/ppermute | solution.py:25
  7.8 0.7 %copy-done.3 = bf16[1024]{0:T(1024)(128)(2,1)S(1)} copy-done((bf16[1024]{0:T(1024)(128)(2,1)S(1)}, bf16[1024]{0:T(1024)(128)(2,1)}, u32[]{:S(2)}) %copy-start.3) | copy-done | bytes 2072
  8.5 0.7 copy-done.4
  9.2 0.7 copy-done.5
  9.8 0.7 copy-done.6
  10.5 0.7 copy-done.7
  11.1 0.9 %collective-permute-done = bf16[32,3,256]{2,1,0:T(4,128)(2,1)S(1)} collective-permute-done((bf16[32,3,256]{2,1,0:T(4,128)(2,1)S(1)}, bf16[32,3,256]{2,1,0:T(4,128)(2,1)S(1)}, u32[]{:S(2)}, u32[]{:S(2)}) %collective-permute-start) | collective-permute-done | bytes 49184 | tf_op jit(solution)/shard_map/ppermute | solution.py:25
  12.5 1.5 %collective-permute-start.2 = (bf16[3,38,256]{2,1,0:T(8,128)(2,1)S(1)}, bf16[3,38,256]{2,1,0:T(8,128)(2,1)S(1)}, u32[]{:S(2)}, u32[]{:S(2)}) collective-permute-start(bf16[3,38,256]{2,1,0:T(8,128)(2,1)S(1)} %get-tuple-element.121), channel_id=1, source_target_pairs={{0,1},{1,0},{2,3},{3,2},{4,5},{5,4},{6,7},{7,6},{8,9},{9,8},{10,11... | collective-permute-start | bytes 175112 | tf_op jit(solution)/shard_map/ppermute | solution.py:25
  14.0 3.2 %block_inner_conv.2.inner_ref = f32[2,24,32,128]{3,2,1,0:T(8,128)S(1)} custom-call(bf16[32,3,256]{2,1,0:T(4,128)(2,1)S(1)} %get-tuple-element.54.west_ref, bf16[32,32,256]{2,1,0:T(8,128)(2,1)S(1)} %copy-done, bf16[32,3,256]{2,1,0:T(4,128)(2,1)S(1)} %get-tuple-element.56.east_ref, bf16[7,7,256]{2,1,0:T(8,128)(2,1)S(1)} %copy-done.2), custom_call_target="tpu_custom_call" | custom-call | flops 25690112 | bytes 2097152 | tf_op jit(solution)/shard_map/block_inner_conv/pallas_call | solution.py:224
  17.5 6.9 %block_main.1 = (bf16[1024,256]{1,0:T(8,128)(2,1)}, bf16[1024,256]{1,0:T(8,128)(2,1)S(1)}, f32[1024,256]{1,0:T(8,128)S(1)}, bf16[1024,256]{1,0:T(8,128)(2,1)S(1)}, f32[12,256]{1,0:T(8,128)S(1)}) custom-call(bf16[3,38,256]{2,1,0:T(8,128)(2,1)S(1)} %get-tuple-element.119.top_ref, bf16[32,3,256]{2,1,0:T(4,128)(2,1)S(1)} %get-tuple-element.54.west_ref, ...), custom_call_target="tpu_custom_call" | custom-call | flops 3221225472 | bytes 8388608 | tf_op jit(solution)/shard_map/block_main/pallas_call | solution.py:395
  24.6 0.5 collective-permute-start.4
  25.1 1.0 %collective-permute-done.5 = bf16[512,256]{1,0:T(8,128)(2,1)S(1)} collective-permute-done((bf16[512,256]{1,0:T(8,128)(2,1)S(1)}, bf16[512,256]{1,0:T(8,128)(2,1)S(1)}, u32[]{:S(2)}, u32[]{:S(2)}) %collective-permute-start.5) | collective-permute-done | bytes 262176 | tf_op jit(solution)/shard_map/ppermute | solution.py:25
  26.2 1.2 %collective-permute-start.7 = (bf16[256,256]{1,0:T(8,128)(2,1)S(1)}, bf16[256,256]{1,0:T(8,128)(2,1)S(1)}, u32[]{:S(2)}, u32[]{:S(2)}) collective-permute-start(bf16[256,256]{1,0:T(8,128)(2,1)S(1)} %get-tuple-element.109), channel_id=1, source_target_pairs={{0,4},{1,3},{2,6},{3,1},{4,0},{5,7},{6,2},{7,5},{8,12},{9,11},{10,... | collective-permute-start | bytes 393224 | tf_op jit(solution)/shard_map/ppermute | solution.py:25
  27.3 0.9 %collective-permute-start.6 = (bf16[256,256]{1,0:T(8,128)(2,1)S(1)}, bf16[256,256]{1,0:T(8,128)(2,1)S(1)}, u32[]{:S(2)}, u32[]{:S(2)}) collective-permute-start(bf16[256,256]{1,0:T(8,128)(2,1)S(1)} %get-tuple-element.108), channel_id=1, source_target_pairs={{0,4},{1,3},{2,6},{3,1},{4,0},{5,7},{6,2},{7,5},{8,12},{9,11},{10,... | collective-permute-start | bytes 393224 | tf_op jit(solution)/shard_map/ppermute | solution.py:25
  28.3 4.1 %block_taps.1 = bf16[64,256]{1,0:T(8,128)(2,1)S(1)} custom-call(bf16[3,38,256]{2,1,0:T(8,128)(2,1)S(1)} %get-tuple-element.119.top_ref, bf16[32,3,256]{2,1,0:T(4,128)(2,1)S(1)} %get-tuple-element.54.west_ref, bf16[32,32,256]{2,1,0:T(8,128)(2,1)S(1)} %copy-done, bf16[32,3,256]{2,1,0:T(4,128)(2,1)S(1)} %get-tuple-element.56.east_ref, ...), custom_call_target="tpu_custom_call" | custom-call | flops 25690112 | bytes 3145728 | tf_op jit(solution)/shard_map/block_taps/pallas_call | solution.py:482
  32.9 2.8 %collective-permute-start.11 = (bf16[32,3,256]{2,1,0:T(4,128)(2,1)S(1)}, bf16[32,3,256]{2,1,0:T(4,128)(2,1)S(1)}, u32[]{:S(2)}, u32[]{:S(2)}) collective-permute-start(bf16[32,3,256]{2,1,0:T(4,128)(2,1)S(1)} %get-tuple-element.100), channel_id=1, source_target_pairs={{0,28},{1,29},{2,30},{3,31},{4,8},{5,9},{6,10},{7,11},{8,4},{9,5},... | collective-permute-start | bytes 147464 | tf_op jit(solution)/shard_map/ppermute | solution.py:25
  35.7 1.8 %collective-permute-done.8 = bf16[256,256]{1,0:T(8,128)(2,1)S(1)} collective-permute-done((bf16[256,256]{1,0:T(8,128)(2,1)S(1)}, bf16[256,256]{1,0:T(8,128)(2,1)S(1)}, u32[]{:S(2)}, u32[]{:S(2)}) %collective-permute-start.8) | collective-permute-done | bytes 131104 | tf_op jit(solution)/shard_map/ppermute | solution.py:25
  37.8 2.2 %collective-permute-done.11 = bf16[32,3,256]{2,1,0:T(4,128)(2,1)S(1)} collective-permute-done((bf16[32,3,256]{2,1,0:T(4,128)(2,1)S(1)}, bf16[32,3,256]{2,1,0:T(4,128)(2,1)S(1)}, u32[]{:S(2)}, u32[]{:S(2)}) %collective-permute-start.11) | collective-permute-done | bytes 49184 | tf_op jit(solution)/shard_map/ppermute | solution.py:25
  40.0 0.6 collective-permute-done.10
  40.7 3.9 %collective-permute-done.9 = bf16[320,256]{1,0:T(8,128)(2,1)S(1)} collective-permute-done((bf16[320,256]{1,0:T(8,128)(2,1)S(1)}, bf16[320,256]{1,0:T(8,128)(2,1)S(1)}, u32[]{:S(2)}, u32[]{:S(2)}) %collective-permute-start.9) | collective-permute-done | bytes 163872 | tf_op jit(solution)/shard_map/ppermute | solution.py:25
  44.7 6.9 %collective-permute-done.12 = bf16[320,256]{1,0:T(8,128)(2,1)S(1)} collective-permute-done((bf16[320,256]{1,0:T(8,128)(2,1)S(1)}, bf16[320,256]{1,0:T(8,128)(2,1)S(1)}, u32[]{:S(2)}, u32[]{:S(2)}) %collective-permute-start.12) | collective-permute-done | bytes 163872 | tf_op jit(solution)/shard_map/ppermute | solution.py:25
  51.7 0.9 %collective-permute-start.13 = (bf16[320,256]{1,0:T(8,128)(2,1)S(1)}, bf16[320,256]{1,0:T(8,128)(2,1)S(1)}, u32[]{:S(2)}, u32[]{:S(2)}) collective-permute-start(bf16[320,256]{1,0:T(8,128)(2,1)S(1)} %add_convert_fusion.1), channel_id=1, source_target_pairs={{0,2},{1,5},{2,0},{3,7},{4,6},{5,1},{6,4},{7,3},{8,10},{9,13},{10,... | collective-permute-start | bytes 491528 | tf_op jit(solution)/shard_map/ppermute | solution.py:25
  52.7 0.7 %collective-permute-start.17 = (bf16[256,256]{1,0:T(8,128)(2,1)S(1)}, bf16[256,256]{1,0:T(8,128)(2,1)S(1)}, u32[]{:S(2)}, u32[]{:S(2)}) collective-permute-start(bf16[256,256]{1,0:T(8,128)(2,1)S(1)} %slice.122), channel_id=1, source_target_pairs={{0,4},{1,3},{2,6},{3,1},{4,0},{5,7},{6,2},{7,5},{8,12},{9,11},{10,... | collective-permute-start | bytes 393224 | tf_op jit(solution)/shard_map/ppermute | solution.py:25
  53.6 1.5 %collective-permute-start.15 = (bf16[3,38,256]{2,1,0:T(8,128)(2,1)S(1)}, bf16[3,38,256]{2,1,0:T(8,128)(2,1)S(1)}, u32[]{:S(2)}, u32[]{:S(2)}) collective-permute-start(bf16[3,38,256]{2,1,0:T(8,128)(2,1)S(1)} %get-tuple-element.117), channel_id=1, source_target_pairs={{0,1},{1,0},{2,3},{3,2},{4,5},{5,4},{6,7},{7,6},{8,9},{9,8},{10,11... | collective-permute-start | bytes 175112 | tf_op jit(solution)/shard_map/ppermute | solution.py:25
  55.1 3.2 %block_inner_conv.3.inner_ref = f32[2,24,32,128]{3,2,1,0:T(8,128)S(1)} custom-call(bf16[32,3,256]{2,1,0:T(4,128)(2,1)S(1)} %get-tuple-element.80.west_ref, bf16[32,32,256]{2,1,0:T(8,128)(2,1)S(1)} %bitcast.6, bf16[32,3,256]{2,1,0:T(4,128)(2,1)S(1)} %get-tuple-element.82.east_ref, bf16[7,7,256]{2,1,0:T(8,128)(2,1)S(1)} %copy-done.2), custom_call_target="tpu_custom_call" | custom-call | flops 25690112 | bytes 2097152 | tf_op jit(solution)/shard_map/block_inner_conv/pallas_call | solution.py:224
  58.5 1.2 %collective-permute-start.14 = (bf16[320,256]{1,0:T(8,128)(2,1)S(1)}, bf16[320,256]{1,0:T(8,128)(2,1)S(1)}, u32[]{:S(2)}, u32[]{:S(2)}) collective-permute-start(bf16[320,256]{1,0:T(8,128)(2,1)S(1)} %pad_maximum_fusion.2), channel_id=1, source_target_pairs={{0,4},{1,3},{2,6},{3,1},{4,0},{5,7},{6,2},{7,5},{8,12},{9,11},{10,... | collective-permute-start | bytes 491528 | tf_op jit(solution)/shard_map/ppermute | solution.py:25
  59.7 2.3 %block_adjoint.1 = bf16[32,32,256]{2,1,0:T(8,128)(2,1)} custom-call(bf16[3,38,256]{2,1,0:T(8,128)(2,1)S(1)} %get-tuple-element.115.top_ref, bf16[32,3,256]{2,1,0:T(4,128)(2,1)S(1)} %get-tuple-element.80.west_ref, bf16[32,32,256]{2,1,0:T(8,128)(2,1)S(1)} %bitcast.7, bf16[32,3,256]{2,1,0:T(4,128)(2,1)S(1)} %get-tuple-element.82.east_ref, ...), custom_call_target="tpu_custom_call" | custom-call | flops 6553600 | bytes 3145728 | tf_op jit(solution)/shard_map/block_adjoint/pallas_call | solution.py:702
  62.0 1.2 %block_early.1 = (f32[256,1024]{1,0:T(8,128)}, f32[1024,256]{1,0:T(8,128)}) custom-call(bf16[768,256]{1,0:T(8,128)(2,1)S(1)} %pad_maximum_fusion.mine_ref, bf16[768,256]{1,0:T(8,128)(2,1)S(1)} %collective-permute-done.18.pair_ref), custom_call_target="tpu_custom_call" | custom-call | bytes 4194304 | tf_op jit(solution)/shard_map/block_early/pallas_call | solution.py:546
  63.2 0.7 %collective-permute-done.14 = bf16[320,256]{1,0:T(8,128)(2,1)S(1)} collective-permute-done((bf16[320,256]{1,0:T(8,128)(2,1)S(1)}, bf16[320,256]{1,0:T(8,128)(2,1)S(1)}, u32[]{:S(2)}, u32[]{:S(2)}) %collective-permute-start.14) | collective-permute-done | bytes 163872 | tf_op jit(solution)/shard_map/ppermute | solution.py:25
  64.0 1.4 %collective-permute-done.19.pair_last_ref = bf16[320,256]{1,0:T(8,128)(2,1)S(1)} collective-permute-done((bf16[320,256]{1,0:T(8,128)(2,1)S(1)}, bf16[320,256]{1,0:T(8,128)(2,1)S(1)}, u32[]{:S(2)}, u32[]{:S(2)}) %collective-permute-start.19) | collective-permute-done | bytes 163872 | tf_op jit(solution)/shard_map/ppermute | solution.py:25
  65.4 1.5 %block_finish.1 = (f32[7,7,256]{2,1,0:T(8,128)}, f32[256]{0:T(256)}, f32[256]{0:T(256)}, f32[256]{0:T(256)}, f32[256,1024]{1,0:T(8,128)}, /*index=5*/f32[1024]{0:T(1024)}, f32[1024,256]{1,0:T(8,128)}, f32[256]{0:T(256)}) custom-call(bf16[320,256]{1,0:T(8,128)(2,1)S(1)} %pad_maximum_fusion.3.last_ref, ...), custom_call_target="tpu_custom_call", output_to_operand_aliasing={{4}: (2, {}), {6}: (3, {})} | custom-call | tf_op jit(solution)/shard_map/block_finish/pallas_call | solution.py:612
  (67 shorter events, 2.4 us)
Async XLA Ops:
  0.6 11.5 %copy-start = (bf16[32,32,256]{2,1,0:T(8,128)(2,1)S(1)}, bf16[32,32,256]{2,1,0:T(8,128)(2,1)}, u32[]{:S(2)}) copy-start(bf16[32,32,256]{2,1,0:T(8,128)(2,1)} %field_ref.1) | copy-start | bytes 1572868
  1.8 9.4 %collective-permute-start.1 = (bf16[32,3,256]{2,1,0:T(4,128)(2,1)S(1)}, bf16[32,3,256]{2,1,0:T(4,128)(2,1)S(1)}, u32[]{:S(2)}, u32[]{:S(2)}) collective-permute-start(bf16[32,3,256]{2,1,0:T(4,128)(2,1)S(1)} %get-tuple-element.106), channel_id=1, source_target_pairs={{0,28},{1,29},{2,30},{3,31},{4,8},{5,9},{6,10},{7,11},{8,4},{9,5},... | collective-permute-start | bytes 147464 | tf_op jit(solution)/shard_map/ppermute | solution.py:25
  7.8 4.3 %collective-permute-start = (bf16[32,3,256]{2,1,0:T(4,128)(2,1)S(1)}, bf16[32,3,256]{2,1,0:T(4,128)(2,1)S(1)}, u32[]{:S(2)}, u32[]{:S(2)}) collective-permute-start(bf16[32,3,256]{2,1,0:T(4,128)(2,1)S(1)} %get-tuple-element.107), channel_id=1, source_target_pairs={{0,4},{1,5},{2,6},{3,7},{4,0},{5,1},{6,2},{7,3},{8,12},{9,13},{10,... | collective-permute-start | bytes 147464 | tf_op jit(solution)/shard_map/ppermute | solution.py:25
  7.8 0.7 %copy-start.3 = (bf16[1024]{0:T(1024)(128)(2,1)S(1)}, bf16[1024]{0:T(1024)(128)(2,1)}, u32[]{:S(2)}) copy-start(bf16[1024]{0:T(1024)(128)(2,1)} %refs_4_.1) | copy-start | bytes 6148
  8.5 0.7 copy-start.4
  9.2 0.7 copy-start.5
  9.8 0.7 copy-start.6
  10.5 0.7 copy-start.7
  12.2 1.7 %copy-start.2 = (bf16[7,7,256]{2,1,0:T(8,128)(2,1)S(1)}, bf16[7,7,256]{2,1,0:T(8,128)(2,1)}, u32[]{:S(2)}) copy-start(bf16[7,7,256]{2,1,0:T(8,128)(2,1)} %dw_ref.7) | copy-start | bytes 75268
  12.3 5.2 %collective-permute-start.3 = (bf16[3,38,256]{2,1,0:T(8,128)(2,1)S(1)}, bf16[3,38,256]{2,1,0:T(8,128)(2,1)S(1)}, u32[]{:S(2)}, u32[]{:S(2)}) collective-permute-start(bf16[3,38,256]{2,1,0:T(8,128)(2,1)S(1)} %reverse_select_fusion.1), channel_id=1, source_target_pairs={{0,16},{1,2},{2,1},{3,19},{4,20},{5,6},{6,5},{7,23},{8,24},{9,10},... | collective-permute-start | bytes 175112 | tf_op jit(solution)/shard_map/ppermute | solution.py:25
  12.5 5.0 %copy-start.1 = (bf16[32,32,256]{2,1,0:T(8,128)(2,1)S(1)}, bf16[32,32,256]{2,1,0:T(8,128)(2,1)}, u32[]{:S(2)}) copy-start(bf16[32,32,256]{2,1,0:T(8,128)(2,1)} %cot_ref.1) | copy-start | bytes 1572868
  12.5 5.0 %copy-start.8 = (bf16[256,1024]{1,0:T(8,128)(2,1)S(1)}, bf16[256,1024]{1,0:T(8,128)(2,1)}, u32[]{:S(2)}) copy-start(bf16[256,1024]{1,0:T(8,128)(2,1)} %w_expand_ref.1) | copy-start | bytes 1572868
  12.5 5.0 %copy-start.9 = (bf16[1024,256]{1,0:T(8,128)(2,1)S(1)}, bf16[1024,256]{1,0:T(8,128)(2,1)}, u32[]{:S(2)}) copy-start(bf16[1024,256]{1,0:T(8,128)(2,1)} %w_project_ref.1) | copy-start | bytes 1572868
  12.5 4.9 %collective-permute-start.2 = (bf16[3,38,256]{2,1,0:T(8,128)(2,1)S(1)}, bf16[3,38,256]{2,1,0:T(8,128)(2,1)S(1)}, u32[]{:S(2)}, u32[]{:S(2)}) collective-permute-start(bf16[3,38,256]{2,1,0:T(8,128)(2,1)S(1)} %get-tuple-element.121), channel_id=1, source_target_pairs={{0,1},{1,0},{2,3},{3,2},{4,5},{5,4},{6,7},{7,6},{8,9},{9,8},{10,11... | collective-permute-start | bytes 175112 | tf_op jit(solution)/shard_map/ppermute | solution.py:25
  24.5 1.6 %collective-permute-start.5 = (bf16[512,256]{1,0:T(8,128)(2,1)S(1)}, bf16[512,256]{1,0:T(8,128)(2,1)S(1)}, u32[]{:S(2)}, u32[]{:S(2)}) collective-permute-start(bf16[512,256]{1,0:T(8,128)(2,1)S(1)} %get-tuple-element.103), channel_id=1, source_target_pairs={{0,1},{1,0},{2,3},{3,2},{4,5},{5,4},{6,7},{7,6},{8,9},{9,8},{10,11... | collective-permute-start | bytes 786440 | tf_op jit(solution)/shard_map/ppermute | solution.py:25
  24.6 7.8 %collective-permute-start.4 = (bf16[512,256]{1,0:T(8,128)(2,1)S(1)}, bf16[512,256]{1,0:T(8,128)(2,1)S(1)}, u32[]{:S(2)}, u32[]{:S(2)}) collective-permute-start(bf16[512,256]{1,0:T(8,128)(2,1)S(1)} %get-tuple-element.102), channel_id=1, source_target_pairs={{0,1},{1,0},{2,3},{3,2},{4,5},{5,4},{6,7},{7,6},{8,9},{9,8},{10,11... | collective-permute-start | bytes 786440 | tf_op jit(solution)/shard_map/ppermute | solution.py:25
  26.2 6.2 %collective-permute-start.7 = (bf16[256,256]{1,0:T(8,128)(2,1)S(1)}, bf16[256,256]{1,0:T(8,128)(2,1)S(1)}, u32[]{:S(2)}, u32[]{:S(2)}) collective-permute-start(bf16[256,256]{1,0:T(8,128)(2,1)S(1)} %get-tuple-element.109), channel_id=1, source_target_pairs={{0,4},{1,3},{2,6},{3,1},{4,0},{5,7},{6,2},{7,5},{8,12},{9,11},{10,... | collective-permute-start | bytes 393224 | tf_op jit(solution)/shard_map/ppermute | solution.py:25
  27.3 8.3 %collective-permute-start.6 = (bf16[256,256]{1,0:T(8,128)(2,1)S(1)}, bf16[256,256]{1,0:T(8,128)(2,1)S(1)}, u32[]{:S(2)}, u32[]{:S(2)}) collective-permute-start(bf16[256,256]{1,0:T(8,128)(2,1)S(1)} %get-tuple-element.108), channel_id=1, source_target_pairs={{0,4},{1,3},{2,6},{3,1},{4,0},{5,7},{6,2},{7,5},{8,12},{9,11},{10,... | collective-permute-start | bytes 393224 | tf_op jit(solution)/shard_map/ppermute | solution.py:25
  32.5 5.0 %collective-permute-start.8 = (bf16[256,256]{1,0:T(8,128)(2,1)S(1)}, bf16[256,256]{1,0:T(8,128)(2,1)S(1)}, u32[]{:S(2)}, u32[]{:S(2)}) collective-permute-start(bf16[256,256]{1,0:T(8,128)(2,1)S(1)} %add_convert_fusion.4), channel_id=1, source_target_pairs={{0,2},{1,5},{2,0},{3,7},{4,6},{5,1},{6,4},{7,3},{8,10},{9,13},{10,... | collective-permute-start | bytes 393224 | tf_op jit(solution)/shard_map/ppermute | solution.py:25
  32.9 7.1 %collective-permute-start.11 = (bf16[32,3,256]{2,1,0:T(4,128)(2,1)S(1)}, bf16[32,3,256]{2,1,0:T(4,128)(2,1)S(1)}, u32[]{:S(2)}, u32[]{:S(2)}) collective-permute-start(bf16[32,3,256]{2,1,0:T(4,128)(2,1)S(1)} %get-tuple-element.100), channel_id=1, source_target_pairs={{0,28},{1,29},{2,30},{3,31},{4,8},{5,9},{6,10},{7,11},{8,4},{9,5},... | collective-permute-start | bytes 147464 | tf_op jit(solution)/shard_map/ppermute | solution.py:25
  35.6 5.0 %collective-permute-start.10 = (bf16[32,3,256]{2,1,0:T(4,128)(2,1)S(1)}, bf16[32,3,256]{2,1,0:T(4,128)(2,1)S(1)}, u32[]{:S(2)}, u32[]{:S(2)}) collective-permute-start(bf16[32,3,256]{2,1,0:T(4,128)(2,1)S(1)} %get-tuple-element.101), channel_id=1, source_target_pairs={{0,4},{1,5},{2,6},{3,7},{4,0},{5,1},{6,2},{7,3},{8,12},{9,13},{10,... | collective-permute-start | bytes 147464 | tf_op jit(solution)/shard_map/ppermute | solution.py:25
  37.6 7.0 %collective-permute-start.9 = (bf16[320,256]{1,0:T(8,128)(2,1)S(1)}, bf16[320,256]{1,0:T(8,128)(2,1)S(1)}, u32[]{:S(2)}, u32[]{:S(2)}) collective-permute-start(bf16[320,256]{1,0:T(8,128)(2,1)S(1)} %pad_maximum_fusion.1), channel_id=1, source_target_pairs={{0,8},{1,17},{2,10},{3,19},{4,12},{5,21},{6,14},{7,23},{8,0},{9,25... | collective-permute-start | bytes 491528 | tf_op jit(solution)/shard_map/ppermute | solution.py:25
  44.7 7.0 %collective-permute-start.12 = (bf16[320,256]{1,0:T(8,128)(2,1)S(1)}, bf16[320,256]{1,0:T(8,128)(2,1)S(1)}, u32[]{:S(2)}, u32[]{:S(2)}) collective-permute-start(bf16[320,256]{1,0:T(8,128)(2,1)S(1)} %add_convert_fusion.2), channel_id=1, source_target_pairs={{0,16},{1,9},{2,18},{3,11},{4,20},{5,13},{6,22},{7,15},{8,24},{9,1... | collective-permute-start | bytes 491528 | tf_op jit(solution)/shard_map/ppermute | solution.py:25
  51.7 6.6 %collective-permute-start.13 = (bf16[320,256]{1,0:T(8,128)(2,1)S(1)}, bf16[320,256]{1,0:T(8,128)(2,1)S(1)}, u32[]{:S(2)}, u32[]{:S(2)}) collective-permute-start(bf16[320,256]{1,0:T(8,128)(2,1)S(1)} %add_convert_fusion.1), channel_id=1, source_target_pairs={{0,2},{1,5},{2,0},{3,7},{4,6},{5,1},{6,4},{7,3},{8,10},{9,13},{10,... | collective-permute-start | bytes 491528 | tf_op jit(solution)/shard_map/ppermute | solution.py:25
  52.7 5.6 %collective-permute-start.17 = (bf16[256,256]{1,0:T(8,128)(2,1)S(1)}, bf16[256,256]{1,0:T(8,128)(2,1)S(1)}, u32[]{:S(2)}, u32[]{:S(2)}) collective-permute-start(bf16[256,256]{1,0:T(8,128)(2,1)S(1)} %slice.122), channel_id=1, source_target_pairs={{0,4},{1,3},{2,6},{3,1},{4,0},{5,7},{6,2},{7,5},{8,12},{9,11},{10,... | collective-permute-start | bytes 393224 | tf_op jit(solution)/shard_map/ppermute | solution.py:25
  53.5 6.2 %collective-permute-start.16 = (bf16[3,38,256]{2,1,0:T(8,128)(2,1)S(1)}, bf16[3,38,256]{2,1,0:T(8,128)(2,1)S(1)}, u32[]{:S(2)}, u32[]{:S(2)}) collective-permute-start(bf16[3,38,256]{2,1,0:T(8,128)(2,1)S(1)} %reverse_select_fusion), channel_id=1, source_target_pairs={{0,16},{1,2},{2,1},{3,19},{4,20},{5,6},{6,5},{7,23},{8,24},{9,10},... | collective-permute-start | bytes 175112 | tf_op jit(solution)/shard_map/ppermute | solution.py:25
  53.6 6.1 %collective-permute-start.15 = (bf16[3,38,256]{2,1,0:T(8,128)(2,1)S(1)}, bf16[3,38,256]{2,1,0:T(8,128)(2,1)S(1)}, u32[]{:S(2)}, u32[]{:S(2)}) collective-permute-start(bf16[3,38,256]{2,1,0:T(8,128)(2,1)S(1)} %get-tuple-element.117), channel_id=1, source_target_pairs={{0,1},{1,0},{2,3},{3,2},{4,5},{5,4},{6,7},{7,6},{8,9},{9,8},{10,11... | collective-permute-start | bytes 175112 | tf_op jit(solution)/shard_map/ppermute | solution.py:25
  58.4 3.6 %collective-permute-start.18 = (bf16[768,256]{1,0:T(8,128)(2,1)S(1)}, bf16[768,256]{1,0:T(8,128)(2,1)S(1)}, u32[]{:S(2)}, u32[]{:S(2)}) collective-permute-start(bf16[768,256]{1,0:T(8,128)(2,1)S(1)} %pad_maximum_fusion.mine_ref), channel_id=1, source_target_pairs={{0,1},{1,0},{2,3},{3,2},{4,5},{5,4},{6,7},{7,6},{8,9},{9,8},{10,11... | collective-permute-start | bytes 1179656 | tf_op jit(solution)/shard_map/ppermute | solution.py:25
  58.5 5.4 %collective-permute-start.14 = (bf16[320,256]{1,0:T(8,128)(2,1)S(1)}, bf16[320,256]{1,0:T(8,128)(2,1)S(1)}, u32[]{:S(2)}, u32[]{:S(2)}) collective-permute-start(bf16[320,256]{1,0:T(8,128)(2,1)S(1)} %pad_maximum_fusion.2), channel_id=1, source_target_pairs={{0,4},{1,3},{2,6},{3,1},{4,0},{5,7},{6,2},{7,5},{8,12},{9,11},{10,... | collective-permute-start | bytes 491528 | tf_op jit(solution)/shard_map/ppermute | solution.py:25
  63.9 1.5 %collective-permute-start.19 = (bf16[320,256]{1,0:T(8,128)(2,1)S(1)}, bf16[320,256]{1,0:T(8,128)(2,1)S(1)}, u32[]{:S(2)}, u32[]{:S(2)}) collective-permute-start(bf16[320,256]{1,0:T(8,128)(2,1)S(1)} %pad_maximum_fusion.3.last_ref), channel_id=1, source_target_pairs={{0,1},{1,0},{2,3},{3,2},{4,5},{5,4},{6,7},{7,6},{8,9},{9,8},{10,11... | collective-permute-start | bytes 491528 | tf_op jit(solution)/shard_map/ppermute | solution.py:25
